TPU v7x, 32 devices: a whole 2x2x4 slice. The times are simulated.
32 devices in a mesh: leaf: 8 (over z, y), fsdp: 4 (over x, core).
Axes of the slice: x: 2, y: 2, z: 4, core: 2. Of those that a mesh axis runs over, the one named last changes fastest.
Arguments:
- hidden: bfloat16 [4, 2048, 768], P('fsdp', 'leaf'), may hold values from -6 to 6
- noise_mask: int32 [4, 2048], P('fsdp', 'leaf'), may hold values 0 or 1
- seg_blocks: int32 [4, 128], P('fsdp'), may hold values from 0 to 12, as said below
- parents: int32 [4, 13], P('fsdp'), may hold values from 0 to 4, as said below
- ln1_gain: bfloat16 [768], P(('leaf', 'fsdp')), may hold values from 0.099609375 to 1.8984375
- w_qkv: bfloat16 [768, 2304], P(('leaf', 'fsdp')), may hold values from -0.21875 to 0.21875
- w_out: bfloat16 [768, 768], P(('leaf', 'fsdp')), may hold values from -3.5 to 3.5
- ln2_gain: bfloat16 [768], P(('leaf', 'fsdp')), may hold values from 0.099609375 to 1.8984375
- w_up: bfloat16 [768, 3072], P(('leaf', 'fsdp')), may hold values from -0.21875 to 0.21875
- up_bias: bfloat16 [3072], P(('leaf', 'fsdp')), may hold values from -3 to 3
- w_down: bfloat16 [3072, 768], P(('leaf', 'fsdp')), may hold values from -0.109375 to 0.109375
- down_bias: bfloat16 [768], P(('leaf', 'fsdp')), may hold values from -2 to 2
- mask_embed: bfloat16 [768], P(('leaf', 'fsdp')), may hold values from -5 to 5
- cotangent: bfloat16 [4, 2, 2048, 768], P('fsdp', None, 'leaf'), may hold values from -6 to 6
Outputs:
- output: bfloat16 [4, 2, 2048, 768], P('fsdp', None, 'leaf')
- grad_hidden: bfloat16 [4, 2048, 768], P('fsdp', 'leaf')
- grad_ln1_gain: float32 [768], P(('leaf', 'fsdp'))
- grad_w_qkv: float32 [768, 2304], P(('leaf', 'fsdp'))
- grad_w_out: float32 [768, 768], P(('leaf', 'fsdp'))
- grad_ln2_gain: float32 [768], P(('leaf', 'fsdp'))
- grad_w_up: float32 [768, 3072], P(('leaf', 'fsdp'))
- grad_up_bias: float32 [3072], P(('leaf', 'fsdp'))
- grad_w_down: float32 [3072, 768], P(('leaf', 'fsdp'))
- grad_down_bias: float32 [768], P(('leaf', 'fsdp'))
- grad_mask_embed: float32 [768], P(('leaf', 'fsdp'))
Inputs may be any that keep to these rules, and one draw needn't show every extreme that they name: `seg_blocks`: segment numbers never fall along a tree; segment 0 holds the first 64 blocks (rounded down); every other segment has one block or more; the last segment ends the tree. `parents`: segment 0 is the trunk with parent 0; segments 1 to 4 have parent 0; each of them is the parent of exactly 2 of the segments above 4.
All inputs are finite; a program needn't handle non-finite values. No bound on the sum of `noise_mask` on one device may be relied on, other than what follows from the above.
Results may differ from a plain program's by a relative error of at most 0.015.
Values may be sent and summed in bfloat16 or wider, within the bound.
No kernel may reach another device: no remote copies, remote signals or barrier semaphores. Data moves between devices by JAX's collectives and lax.ppermute only.
A program may use at most 256 MiB of HBM per device.

v0:
```python
import math

import jax
import jax.numpy as jnp
from jax import lax
from jax.sharding import PartitionSpec as P

HEAD_DIM = 64
BLOCK = 16


NEG_FILL = -1000000000.0
EPSILON = 1e-05


def look_up(table, indices):
    slots = jnp.arange(table.shape[0], dtype=jnp.int32)
    hits = indices[..., None] == slots
    return jnp.sum(jnp.where(hits, table, 0), axis=-1)


def tree_layout(seg_row, parent_row):
    slots = jnp.arange(parent_row.shape[0], dtype=jnp.int32)
    seg_lengths = jnp.sum((seg_row[:, None] == slots).astype(jnp.int32), axis=0)
    seg_starts = jnp.cumsum(seg_lengths) - seg_lengths
    grand_parent = look_up(parent_row, parent_row)
    offsets = jnp.where(slots > 0, look_up(seg_lengths, parent_row), 0) + jnp.where(
        parent_row > 0, look_up(seg_lengths, grand_parent), 0
    )
    block_ids = jnp.arange(seg_row.shape[0], dtype=jnp.int32)
    path_block = look_up(offsets, seg_row) + block_ids - look_up(seg_starts, seg_row)
    return (path_block, look_up(parent_row, seg_row), look_up(grand_parent, seg_row))


def layer_norm(values, gain):
    centred = values - jnp.mean(values, axis=-1, keepdims=True)
    spread = jnp.mean(centred * centred, axis=-1, keepdims=True)
    return centred * lax.rsqrt(spread + EPSILON) * gain


def gelu_tanh(values):
    return jax.nn.gelu(values, approximate=True)


def rotate(values, cosine, sine):
    half = values.shape[-1] // 2
    first = values[..., :half]
    second = values[..., half:]
    return jnp.concatenate(
        [first * cosine - second * sine, second * cosine + first * sine], axis=-1
    )


def to_heads(values, heads):
    return values.reshape(values.shape[0], heads, HEAD_DIM).transpose(1, 0, 2)


def from_heads(values):
    return values.transpose(1, 0, 2).reshape(values.shape[1], values.shape[0] * values.shape[2])


def shards(
    hidden,
    noise_mask,
    seg_blocks,
    parents,
    ln1_gain,
    w_qkv,
    w_out,
    ln2_gain,
    w_up,
    up_bias,
    w_down,
    down_bias,
    mask_embed,
    cotangent,
):
    gathered = (
        lax.all_gather(ln1_gain, ("leaf", "fsdp"), axis=0, tiled=True),
        lax.all_gather(w_qkv, ("leaf", "fsdp"), axis=0, tiled=True),
        lax.all_gather(w_out, ("leaf", "fsdp"), axis=0, tiled=True),
        lax.all_gather(ln2_gain, ("leaf", "fsdp"), axis=0, tiled=True),
        lax.all_gather(w_up, ("leaf", "fsdp"), axis=0, tiled=True),
        lax.all_gather(up_bias, ("leaf", "fsdp"), axis=0, tiled=True),
        lax.all_gather(w_down, ("leaf", "fsdp"), axis=0, tiled=True),
        lax.all_gather(down_bias, ("leaf", "fsdp"), axis=0, tiled=True),
        lax.all_gather(mask_embed, ("leaf", "fsdp"), axis=0, tiled=True),
    )
    gain_one, qkv_w, out_w, gain_two, up_w, up_b, down_w, down_b, embed = gathered
    rows_dev = hidden.shape[1]
    width = hidden.shape[2]
    heads = width // HEAD_DIM
    blocks_dev = rows_dev // BLOCK
    leaf_rank = lax.axis_index("leaf")
    seg_row = seg_blocks[0]
    path_block, first_up, second_up = tree_layout(seg_row, parents[0])
    first_block = leaf_rank * blocks_dev
    own_seg = lax.dynamic_slice_in_dim(seg_row, first_block, blocks_dev)
    own_path = lax.dynamic_slice_in_dim(path_block, first_block, blocks_dev)
    own_first = lax.dynamic_slice_in_dim(first_up, first_block, blocks_dev)
    own_second = lax.dynamic_slice_in_dim(second_up, first_block, blocks_dev)
    related = (
        (seg_row[None, :] == own_seg[:, None])
        | (seg_row[None, :] == own_first[:, None])
        | (seg_row[None, :] == own_second[:, None])
    )
    clean_ok = related & (path_block[None, :] <= own_path[:, None])
    noisy_ok = related & (path_block[None, :] < own_path[:, None])
    clean_tok = jnp.repeat(jnp.repeat(clean_ok, BLOCK, axis=0), BLOCK, axis=1)
    noisy_tok = jnp.repeat(jnp.repeat(noisy_ok, BLOCK, axis=0), BLOCK, axis=1)
    row_block = jnp.arange(rows_dev, dtype=jnp.int32) // BLOCK
    same_block = row_block[:, None] == row_block[None, :]
    mask_all = jnp.concatenate(
        [
            jnp.concatenate([clean_tok, jnp.zeros_like(same_block)], axis=1),
            jnp.concatenate([noisy_tok, same_block], axis=1),
        ],
        axis=0,
    )
    offsets_in = jnp.arange(BLOCK, dtype=jnp.int32)
    positions = (own_path[:, None] * BLOCK + offsets_in).reshape(rows_dev).astype(jnp.float32)
    positions = jnp.concatenate([positions, positions])
    freqs = jnp.exp(
        jnp.arange(HEAD_DIM // 2, dtype=jnp.float32) * (-math.log(10000.0) / (HEAD_DIM // 2))
    )
    angles = positions[:, None, None] * freqs
    cosine = jnp.cos(angles)
    sine = jnp.sin(angles)
    clean = hidden[0].astype(jnp.float32)
    masked = (noise_mask[0] == 1)[:, None]
    noisy = jnp.where(masked, embed.astype(jnp.float32)[None, :], clean)
    stream = jnp.concatenate([clean, noisy], axis=0)
    gain_one_f = gain_one.astype(jnp.float32)
    gain_two_f = gain_two.astype(jnp.float32)
    normed_one = layer_norm(stream, gain_one_f).astype(jnp.bfloat16)
    projected = jnp.dot(normed_one, qkv_w, preferred_element_type=jnp.float32)
    query = rotate(
        projected[:, :width].reshape(2 * rows_dev, heads, HEAD_DIM), cosine, sine
    ).reshape(2 * rows_dev, width)
    keyed = rotate(
        projected[:, width : 2 * width].reshape(2 * rows_dev, heads, HEAD_DIM), cosine, sine
    ).reshape(2 * rows_dev, width)
    query_low = query.astype(jnp.bfloat16)
    key_low = keyed.astype(jnp.bfloat16)
    value_low = projected[:, 2 * width :].astype(jnp.bfloat16)
    tree_keys, tree_values = (
        lax.all_gather(key_low[:rows_dev], "leaf", axis=0, tiled=True),
        lax.all_gather(value_low[:rows_dev], "leaf", axis=0, tiled=True),
    )
    tree_tok = tree_keys.shape[0]
    keys_all = jnp.concatenate([tree_keys, key_low[rows_dev:]], axis=0)
    values_all = jnp.concatenate([tree_values, value_low[rows_dev:]], axis=0)
    q_heads = to_heads(query_low, heads)

    def head_forward(operands):
        q_head, k_head, v_head = operands
        raw = jnp.einsum("qd,kd->qk", q_head, k_head, preferred_element_type=jnp.float32) * 0.125
        scores = jnp.where(mask_all, raw, NEG_FILL)
        top_score = jnp.max(scores, axis=-1, keepdims=True)
        expd = jnp.exp(scores - top_score)
        total = jnp.sum(expd, axis=-1, keepdims=True)
        probs = (expd / total).astype(jnp.bfloat16)
        return (
            jnp.dot(probs, v_head, preferred_element_type=jnp.float32),
            top_score + jnp.log(total),
        )

    attended, log_norm = lax.map(
        head_forward, (q_heads, to_heads(keys_all, heads), to_heads(values_all, heads))
    )
    mixed_low = from_heads(attended).astype(jnp.bfloat16)
    after = stream + jnp.dot(mixed_low, out_w, preferred_element_type=jnp.float32)
    normed_two = layer_norm(after, gain_two_f).astype(jnp.bfloat16)
    pre_act = jnp.dot(normed_two, up_w, preferred_element_type=jnp.float32) + up_b.astype(
        jnp.float32
    )
    activated = gelu_tanh(pre_act).astype(jnp.bfloat16)
    result = (
        after
        + jnp.dot(activated, down_w, preferred_element_type=jnp.float32)
        + down_b.astype(jnp.float32)
    )
    output = result.astype(jnp.bfloat16).reshape(1, 2, rows_dev, width)
    regathered = (
        lax.all_gather(ln1_gain, ("leaf", "fsdp"), axis=0, tiled=True),
        lax.all_gather(w_qkv, ("leaf", "fsdp"), axis=0, tiled=True),
        lax.all_gather(w_out, ("leaf", "fsdp"), axis=0, tiled=True),
        lax.all_gather(ln2_gain, ("leaf", "fsdp"), axis=0, tiled=True),
        lax.all_gather(w_up, ("leaf", "fsdp"), axis=0, tiled=True),
        lax.all_gather(up_bias, ("leaf", "fsdp"), axis=0, tiled=True),
        lax.all_gather(w_down, ("leaf", "fsdp"), axis=0, tiled=True),
        lax.all_gather(down_bias, ("leaf", "fsdp"), axis=0, tiled=True),
        lax.all_gather(mask_embed, ("leaf", "fsdp"), axis=0, tiled=True),
    )
    qkv_back, out_back, up_back, down_back = (
        regathered[1],
        regathered[2],
        regathered[4],
        regathered[6],
    )
    grad_out = cotangent[0].astype(jnp.float32).reshape(2 * rows_dev, width)
    grad_two = grad_out.astype(jnp.bfloat16)
    grad_down_b = jnp.sum(grad_two.astype(jnp.float32), axis=0)
    grad_down_w = jnp.einsum("rf,rd->fd", activated, grad_two, preferred_element_type=jnp.float32)
    grad_act = jnp.einsum("rd,fd->rf", grad_two, down_back, preferred_element_type=jnp.float32)
    gelu_out, gelu_back = jax.vjp(gelu_tanh, pre_act)
    grad_pre = gelu_back(grad_act)[0].astype(jnp.bfloat16)
    grad_up_b = jnp.sum(grad_pre.astype(jnp.float32), axis=0)
    grad_up_w = jnp.einsum("rd,rf->df", normed_two, grad_pre, preferred_element_type=jnp.float32)
    grad_normed_two = jnp.einsum("rf,df->rd", grad_pre, up_back, preferred_element_type=jnp.float32)
    norm_out, norm_back = jax.vjp(layer_norm, after, gain_two_f)
    grad_after_ln, grad_gain_two = norm_back(grad_normed_two)
    grad_after = grad_out + grad_after_ln
    grad_one = grad_after.astype(jnp.bfloat16)
    grad_out_w = jnp.einsum("rd,re->de", mixed_low, grad_one, preferred_element_type=jnp.float32)
    grad_mixed = jnp.einsum(
        "re,de->rd", grad_one, out_back, preferred_element_type=jnp.float32
    ).astype(jnp.bfloat16)
    back_keys, back_values = (
        lax.all_gather(key_low[:rows_dev], "leaf", axis=0, tiled=True),
        lax.all_gather(value_low[:rows_dev], "leaf", axis=0, tiled=True),
    )
    keys_back = jnp.concatenate([back_keys, key_low[rows_dev:]], axis=0)
    values_back = jnp.concatenate([back_values, value_low[rows_dev:]], axis=0)

    def head_backward(operands):
        q_head, k_head, v_head, g_head, norm_head = operands
        raw = jnp.einsum("qd,kd->qk", q_head, k_head, preferred_element_type=jnp.float32) * 0.125
        scores = jnp.where(mask_all, raw, NEG_FILL)
        probs = jnp.exp(scores - norm_head)
        grad_v = jnp.einsum(
            "qk,qd->kd", probs.astype(jnp.bfloat16), g_head, preferred_element_type=jnp.float32
        )
        grad_p = jnp.einsum("qd,kd->qk", g_head, v_head, preferred_element_type=jnp.float32)
        inner = jnp.sum(probs * grad_p, axis=-1, keepdims=True)
        grad_s = (probs * (grad_p - inner)).astype(jnp.bfloat16)
        grad_q = jnp.einsum("qk,kd->qd", grad_s, k_head, preferred_element_type=jnp.float32) * 0.125
        grad_k = jnp.einsum("qk,qd->kd", grad_s, q_head, preferred_element_type=jnp.float32) * 0.125
        return (grad_q, grad_k, grad_v)

    grad_q_heads, grad_k_heads, grad_v_heads = lax.map(
        head_backward,
        (
            q_heads,
            to_heads(keys_back, heads),
            to_heads(values_back, heads),
            to_heads(grad_mixed, heads),
            log_norm,
        ),
    )
    grad_query = from_heads(grad_q_heads)
    grad_keys_all = from_heads(grad_k_heads)
    grad_values_all = from_heads(grad_v_heads)
    own_key_grad, own_value_grad = (
        lax.psum_scatter(
            grad_keys_all[:tree_tok].astype(jnp.bfloat16), "leaf", scatter_dimension=0, tiled=True
        ).astype(jnp.float32),
        lax.psum_scatter(
            grad_values_all[:tree_tok].astype(jnp.bfloat16), "leaf", scatter_dimension=0, tiled=True
        ).astype(jnp.float32),
    )
    grad_key = jnp.concatenate([own_key_grad, grad_keys_all[tree_tok:]], axis=0)
    grad_value = jnp.concatenate([own_value_grad, grad_values_all[tree_tok:]], axis=0)
    grad_query = rotate(grad_query.reshape(2 * rows_dev, heads, HEAD_DIM), cosine, -sine).reshape(
        2 * rows_dev, width
    )
    grad_key = rotate(grad_key.reshape(2 * rows_dev, heads, HEAD_DIM), cosine, -sine).reshape(
        2 * rows_dev, width
    )
    grad_proj = jnp.concatenate([grad_query, grad_key, grad_value], axis=1).astype(jnp.bfloat16)
    grad_qkv_w = jnp.einsum("rd,re->de", normed_one, grad_proj, preferred_element_type=jnp.float32)
    grad_normed_one = jnp.einsum(
        "re,de->rd", grad_proj, qkv_back, preferred_element_type=jnp.float32
    )
    first_out, first_back = jax.vjp(layer_norm, stream, gain_one_f)
    grad_stream_ln, grad_gain_one = first_back(grad_normed_one)
    grad_stream = grad_after + grad_stream_ln
    grad_clean = grad_stream[:rows_dev] + jnp.where(masked, 0.0, grad_stream[rows_dev:])
    grad_embed = jnp.sum(jnp.where(masked, grad_stream[rows_dev:], 0.0), axis=0)
    summed = (
        lax.psum_scatter(grad_gain_one, ("leaf", "fsdp"), scatter_dimension=0, tiled=True),
        lax.psum_scatter(grad_qkv_w, ("leaf", "fsdp"), scatter_dimension=0, tiled=True),
        lax.psum_scatter(grad_out_w, ("leaf", "fsdp"), scatter_dimension=0, tiled=True),
        lax.psum_scatter(grad_gain_two, ("leaf", "fsdp"), scatter_dimension=0, tiled=True),
        lax.psum_scatter(grad_up_w, ("leaf", "fsdp"), scatter_dimension=0, tiled=True),
        lax.psum_scatter(grad_up_b, ("leaf", "fsdp"), scatter_dimension=0, tiled=True),
        lax.psum_scatter(grad_down_w, ("leaf", "fsdp"), scatter_dimension=0, tiled=True),
        lax.psum_scatter(grad_down_b, ("leaf", "fsdp"), scatter_dimension=0, tiled=True),
        lax.psum_scatter(grad_embed, ("leaf", "fsdp"), scatter_dimension=0, tiled=True),
    )
    return (
        output,
        grad_clean.astype(jnp.bfloat16)[None],
        summed[0],
        summed[1],
        summed[2],
        summed[3],
        summed[4],
        summed[5],
        summed[6],
        summed[7],
        summed[8],
    )


def solution(mesh):
    in_specs = (
        P("fsdp", "leaf", None),
        P("fsdp", "leaf"),
        P("fsdp", None),
        P("fsdp", None),
        P(("leaf", "fsdp")),
        P(("leaf", "fsdp"), None),
        P(("leaf", "fsdp"), None),
        P(("leaf", "fsdp")),
        P(("leaf", "fsdp"), None),
        P(("leaf", "fsdp")),
        P(("leaf", "fsdp"), None),
        P(("leaf", "fsdp")),
        P(("leaf", "fsdp")),
        P("fsdp", None, "leaf", None),
    )
    out_specs = (
        P("fsdp", None, "leaf", None),
        P("fsdp", "leaf", None),
        P(("leaf", "fsdp")),
        P(("leaf", "fsdp"), None),
        P(("leaf", "fsdp"), None),
        P(("leaf", "fsdp")),
        P(("leaf", "fsdp"), None),
        P(("leaf", "fsdp")),
        P(("leaf", "fsdp"), None),
        P(("leaf", "fsdp")),
        P(("leaf", "fsdp")),
    )
    return jax.shard_map(shards, mesh=mesh, in_specs=in_specs, out_specs=out_specs, check_vma=False)
```

profile of v0, /device:TPU:0, one launch (start us, length us, event | category | flops | bytes accessed | tf_op | source)
XLA Modules:
  0.0 1241.0 jit_solution(11994550310879820292)
XLA Ops:
  12.2 42.3 %all-reduce.12 = (bf16[768]{0:T(1024)(128)(2,1)S(1)}, bf16[768]{0:T(1024)(128)(2,1)S(1)}, bf16[768]{0:T(1024)(128)(2,1)}, bf16[768]{0:T(1024)(128)(2,1)S(1)}, bf16[3072]{0:T(1024)(128)(2,1)S(1)}) all-reduce(bf16[768]{0:T(1024)(128)(2,1)S(1)} %dynamic-update-slice.1, ...), channel_id=1, replica_groups=mesh['leaf'=8,'fsdp'=4] {'leaf','fsdp'}, use_global_device_ids=true, to_apply=%add.2 | all-reduce | flops 6144 | bytes 24576
  58.5 15.2 %all-gather.7.cloned.1.call-done = bf16[768,2304]{1,0:T(8,128)(2,1)} async-done(((bf16[24,2304]{1,0:T(8,128)(2,1)}), bf16[768,2304]{1,0:T(8,128)(2,1)}) %all-gather.7.cloned.1.call-update) | async-done | bytes 3538960 | tf_op jit(solution)/shard_map/all_gather | solution.py:80
  73.8 6.2 fusion.73
  83.0 3.9 fusion.71
  88.9 3.0 copy.76
  91.9 2.7 subtract_convert_fusion.2
  105.3 35.0 %all-gather.11.cloned.1.call-done = bf16[2048,768]{1,0:T(8,128)(2,1)} async-done(((bf16[256,768]{1,0:T(8,128)(2,1)}), bf16[2048,768]{1,0:T(8,128)(2,1)}) %all-gather.11.cloned.1.call-update) | async-done | bytes 3145744 | tf_op jit(solution)/shard_map/all_gather | solution.py:148
  140.3 4.0 pad_maximum_fusion.1
  144.3 5.9 copy.80
  150.2 53.8 %all-gather.9.cloned.1.call-done = bf16[2048,768]{0,1:T(8,128)(2,1)} async-done(((bf16[256,768]{0,1:T(8,128)(2,1)}), bf16[2048,768]{0,1:T(8,128)(2,1)}) %all-gather.9.cloned.1.call-update) | async-done | bytes 3145744 | tf_op jit(solution)/shard_map/all_gather | solution.py:147
  204.1 4.0 pad_maximum_fusion
  208.1 7.9 copy.82
  216.0 8.0 copy.84
  224.0 69.5 %while.28 = (s32[]{:T(128)}, bf16[12,512,64]{1,2,0:T(8,128)(2,1)S(1)}, f32[12,512,1]{1,2,0:T(1,128)}, bf16[12,512,64]{2,1,0:T(8,128)(2,1)}, bf16[12,2304,64]{2,1...) while((s32[]{:T(128)}, ...), condition=%wide.region_14.15_spmd.clone, body=%wide.region_11.14_spmd.sunk.clone | while | flops 311426560 | bytes 16799832 | solution.py:168
  293.5 2.5 fusion.74
  297.5 27.0 %all-gather.15.cloned.1.call-done = bf16[768,3072]{1,0:T(8,128)(2,1)} async-done(((bf16[24,3072]{1,0:T(8,128)(2,1)}), bf16[768,3072]{1,0:T(8,128)(2,1)}) %all-gather.15.cloned.1.call-update) | async-done | bytes 4718608 | tf_op jit(solution)/shard_map/all_gather | solution.py:83
  324.5 8.2 fusion.64
  332.7 57.0 %all-gather.17.cloned.1.call-done = bf16[3072,768]{1,0:T(8,128)(2,1)} async-done(((bf16[96,768]{1,0:T(8,128)(2,1)}), bf16[3072,768]{1,0:T(8,128)(2,1)}) %all-gather.17.cloned.1.call-update) | async-done | bytes 4718608 | tf_op jit(solution)/shard_map/all_gather | solution.py:85
  389.7 10.2 convert_reduce_fusion
  399.9 3.4 multiply_reduce_fusion.1
  410.3 154.7 %while.29 = (s32[]{:T(128)}, f32[12,512,64]{1,2,0:T(8,128)}, f32[12,2304,64]{1,2,0:T(8,128)}, bf16[12,2304,64]{1,2,0:T(8,128)(2,1)}, bf16[12,512,64]{2,1,0:T(8,1...) while((s32[]{:T(128)}, f32[12,512,64]{1,2,0:T(8,128)}, ...), condition=%wide.region_21.22_spmd.clone, body=%wide.region_19.21_spmd.sunk.clone | while | flops 765771264 | bytes 40057968 | solution.py:241
  412.9 2.8 multiply_reduce_fusion.9
  418.4 2.5 fusion.139
  425.8 2.8 multiply_reduce_fusion.9
  431.2 2.5 fusion.139
  438.7 2.8 multiply_reduce_fusion.9
  444.1 2.6 fusion.139
  451.5 2.8 multiply_reduce_fusion.9
  457.0 2.6 fusion.139
  464.4 2.8 multiply_reduce_fusion.9
  469.9 2.6 fusion.139
  477.3 2.8 multiply_reduce_fusion.9
  482.7 2.6 fusion.139
  485.3 2.3 fusion.140
  490.2 2.8 multiply_reduce_fusion.9
  495.6 2.6 fusion.139
  503.1 2.8 multiply_reduce_fusion.9
  508.5 2.6 fusion.139
  511.1 2.3 fusion.140
  516.0 2.8 multiply_reduce_fusion.9
  521.4 2.6 fusion.139
  528.9 2.8 multiply_reduce_fusion.9
  534.3 2.6 fusion.139
  541.8 2.8 multiply_reduce_fusion.9
  547.2 2.6 fusion.139
  549.7 2.4 fusion.140
  554.7 2.8 multiply_reduce_fusion.9
  560.1 2.6 fusion.139
  562.7 2.3 fusion.140
  565.0 4.9 slice.169
  570.0 3.9 slice.123
  575.1 3.5 fusion.75
  578.6 10.0 fusion.66
  590.1 7.2 fusion.63
  601.3 42.4 %reduce-scatter.7.cloned.1.call-done = bf16[256,768]{0,1:T(8,128)(2,1)} async-done(((bf16[2048,768]{0,1:T(8,128)(2,1)}), bf16[256,768]{0,1:T(8,128)(2,1)}) %reduce-scatter.7.cloned.1.call-update) | async-done | bytes 393232 | tf_op jit(solution)/shard_map/reduce_scatter | solution.py:255
  649.0 72.4 %reduce-scatter.9.cloned.1.call-done = bf16[256,768]{0,1:T(8,128)(2,1)} async-done(((bf16[2048,768]{0,1:T(8,128)(2,1)}), bf16[256,768]{0,1:T(8,128)(2,1)}) %reduce-scatter.9.cloned.1.call-update) | async-done | bytes 393232 | tf_op jit(solution)/shard_map/reduce_scatter | solution.py:258
  721.5 6.7 fusion.52
  730.7 9.3 add_convert_fusion
  740.0 2.4 multiply_reduce_fusion.2
  745.8 40.2 %all-reduce.11 = (f32[768]{0:T(1024)S(1)}, f32[768]{0:T(1024)S(1)}, f32[3072]{0:T(1024)S(1)}, f32[768]{0:T(1024)S(1)}, f32[768]{0:T(1024)S(1)}) all-reduce(f32[768]{0:T(1024)S(1)} %get-tuple-element.195, f32[768]{0:T(1024)S(1)} %copy-done.34, f32[3072]{0:T(1024)S(1)} %copy-done.31, ...), channel_id=4, replica_groups=mesh['leaf'=8,'fsdp'=4] {'leaf','fsdp'}, use_global_device_ids=true, to_apply=%region_27.28.clone | all-reduce | flops 6144 | bytes 49152
  788.9 36.6 %reduce-scatter.13.cloned.1.call-done = f32[24,768]{1,0:T(8,128)} async-done(((f32[768,768]{1,0:T(8,128)}), f32[24,768]{1,0:T(8,128)}) %reduce-scatter.13.cloned.1.call-update) | async-done | bytes 73744 | tf_op jit(solution)/shard_map/reduce_scatter | solution.py:283
  825.6 142.0 %reduce-scatter.17.cloned.1.call-done = f32[96,768]{1,0:T(8,128)} async-done(((f32[3072,768]{1,0:T(8,128)}), f32[96,768]{1,0:T(8,128)}) %reduce-scatter.17.cloned.1.call-update) | async-done | bytes 294928 | tf_op jit(solution)/shard_map/reduce_scatter | solution.py:287
  967.6 140.9 %reduce-scatter.15.cloned.1.call-done = f32[24,3072]{1,0:T(8,128)} async-done(((f32[768,3072]{1,0:T(8,128)}), f32[24,3072]{1,0:T(8,128)}) %reduce-scatter.15.cloned.1.call-update) | async-done | bytes 294928 | tf_op jit(solution)/shard_map/reduce_scatter | solution.py:285
  1108.5 125.4 %reduce-scatter.11.cloned.1.call-done = f32[24,2304]{1,0:T(8,128)} async-done(((f32[768,2304]{1,0:T(8,128)}), f32[24,2304]{1,0:T(8,128)}) %reduce-scatter.11.cloned.1.call-update) | async-done | bytes 221200 | tf_op jit(solution)/shard_map/reduce_scatter | solution.py:282
  (308 shorter events, 203.4 us)
Async XLA Ops:
  7.2 66.6 %all-gather.7.cloned.1.call-start = ((), (), s32[]{:S(2)}) async-start(), calls=%async_computation.6 | async-start | bytes 3649536 | tf_op jit(solution)/shard_map/all_gather | solution.py:80
  7.9 132.4 %all-gather.11.cloned.1.call-start = ((), (), s32[]{:S(2)}) async-start(), calls=%async_computation.8 | async-start | bytes 3538944 | tf_op jit(solution)/shard_map/all_gather | solution.py:148
  54.5 19.2 %copy-start.26 = (f32[768]{0:T(1024)}, f32[768]{0:T(1024)S(1)}, u32[]{:S(2)}) copy-start(f32[768]{0:T(1024)S(1)} %convert_element_type.105) | copy-start | bytes 9220
  55.2 2.7 copy-start.35
  57.6 22.4 %copy-start.22 = (f32[512]{0:T(512)}, f32[512]{0:T(512)S(1)}, u32[]{:S(2)}) copy-start(f32[512]{0:T(512)S(1)} %broadcast_multiply_fusion.1) | copy-start | bytes 6148
  57.9 0.6 copy-start.28
  58.5 21.5 %copy-start.24 = (f32[512]{0:T(512)}, f32[512]{0:T(512)S(1)}, u32[]{:S(2)}) copy-start(f32[512]{0:T(512)S(1)} %fusion.57) | copy-start | bytes 6148
  58.5 22.5 %copy-start.37 = (s32[1,128]{1,0:T(1,128)S(1)}, s32[1,128]{1,0:T(1,128)}, u32[]{:S(2)}) copy-start(s32[1,128]{1,0:T(1,128)} %param.20) | copy-start | bytes 1540
  58.5 22.8 %copy-start.33 = (s32[1,13]{1,0:T(1,128)S(1)}, s32[1,13]{1,0:T(1,128)}, u32[]{:S(2)}) copy-start(s32[1,13]{1,0:T(1,128)} %param.21) | copy-start | bytes 160
  81.0 123.1 %all-gather.9.cloned.1.call-start = ((), (), s32[]{:S(2)}) async-start(), calls=%async_computation.7 | async-start | bytes 3538944 | tf_op jit(solution)/shard_map/all_gather | solution.py:147
  83.0 8.9 copy-start.18
  95.6 197.8 %all-gather.13.cloned.1.call-start = ((), (), s32[]{:S(2)}) async-start(), calls=%async_computation.9 | async-start | bytes 1216512 | tf_op jit(solution)/shard_map/all_gather | solution.py:81
  96.2 228.3 %all-gather.15.cloned.1.call-start = ((), (), s32[]{:S(2)}) async-start(), calls=%async_computation.10 | async-start | bytes 4866048 | tf_op jit(solution)/shard_map/all_gather | solution.py:83
  96.8 292.9 %all-gather.17.cloned.1.call-start = ((), (), s32[]{:S(2)}) async-start(), calls=%async_computation.11 | async-start | bytes 4866048 | tf_op jit(solution)/shard_map/all_gather | solution.py:85
  97.4 546.4 %reduce-scatter.7.cloned.1.call-start = ((), (), s32[]{:S(2)}) async-start(), calls=%async_computation.12 | async-start | bytes 3538944 | tf_op jit(solution)/shard_map/reduce_scatter | solution.py:255
  100.2 3.5 copy-start.14
  100.2 3.5 copy-start.15
  144.3 59.8 %copy-start.13 = (bf16[256,12,64]{0,2,1:T(8,128)(2,1)S(1)}, bf16[256,12,64]{0,2,1:T(8,128)(2,1)}, u32[]{:S(2)}) copy-start(bf16[256,12,64]{0,2,1:T(8,128)(2,1)} %get-tuple-element.274) | copy-start | bytes 1179652
  216.0 8.0 copy-start.8
  293.5 2.5 copy-start.9
  295.9 1.2 copy-start.2
  297.5 92.3 %copy-start.5 = (bf16[1,2,256,768]{3,2,1,0:T(8,128)(2,1)S(1)}, bf16[1,2,256,768]{3,2,1,0:T(8,128)(2,1)}, u32[]{:S(2)}) copy-start(bf16[1,2,256,768]{3,2,1,0:T(8,128)(2,1)} %param.31) | copy-start | bytes 2359300
  389.7 10.2 copy-start.3
  389.7 10.2 copy-start.38
  399.9 3.4 copy-start.12
  404.0 1.2 copy-start
  404.0 2.3 copy-start.39
  405.5 0.9 copy-start.11
  569.9 151.5 %reduce-scatter.9.cloned.1.call-start = ((), (), s32[]{:S(2)}) async-start(), calls=%async_computation.13 | async-start | bytes 3538944 | tf_op jit(solution)/shard_map/reduce_scatter | solution.py:258
  573.9 1.1 copy-start.10
  574.0 4.6 copy-start.32
  574.0 251.6 %reduce-scatter.13.cloned.1.call-start = ((), (), s32[]{:S(2)}) async-start(), calls=%async_computation.15 | async-start | bytes 2433024 | tf_op jit(solution)/shard_map/reduce_scatter | solution.py:283
  578.6 389.0 %reduce-scatter.17.cloned.1.call-start = ((), (), s32[]{:S(2)}) async-start(), calls=%async_computation.17 | async-start | bytes 9732096 | tf_op jit(solution)/shard_map/reduce_scatter | solution.py:287
  588.6 1.4 copy-start.4
  588.7 519.9 %reduce-scatter.15.cloned.1.call-start = ((), (), s32[]{:S(2)}) async-start(), calls=%async_computation.16 | async-start | bytes 9732096 | tf_op jit(solution)/shard_map/reduce_scatter | solution.py:285
  597.2 47.6 %copy-start.19 = (f32[512,32]{0,1:T(8,128)S(1)}, f32[512,32]{0,1:T(8,128)}, u32[]{:S(2)}) copy-start(f32[512,32]{0,1:T(8,128)} %copy-done.18) | copy-start | bytes 196612
  597.2 47.6 %copy-start.21 = (f32[512,32]{0,1:T(8,128)S(1)}, f32[512,32]{0,1:T(8,128)}, u32[]{:S(2)}) copy-start(f32[512,32]{0,1:T(8,128)} %get-tuple-element.281) | copy-start | bytes 196612
  597.3 636.7 %reduce-scatter.11.cloned.1.call-start = ((), (), s32[]{:S(2)}) async-start(), calls=%async_computation.14 | async-start | bytes 7299072 | tf_op jit(solution)/shard_map/reduce_scatter | solution.py:282
  647.1 74.4 %copy-start.20 = (bf16[256,12,64]{0,2,1:T(8,128)(2,1)S(1)}, bf16[256,12,64]{0,2,1:T(8,128)(2,1)}, u32[]{:S(2)}) copy-start(bf16[256,12,64]{0,2,1:T(8,128)(2,1)} %slice.124) | copy-start | bytes 1179652
  647.1 74.4 %copy-start.23 = (f32[512]{0:T(512)S(1)}, f32[512]{0:T(512)}, u32[]{:S(2)}) copy-start(f32[512]{0:T(512)} %copy-done.22) | copy-start | bytes 6148
  647.1 74.4 %copy-start.25 = (f32[512]{0:T(512)S(1)}, f32[512]{0:T(512)}, u32[]{:S(2)}) copy-start(f32[512]{0:T(512)} %copy-done.24) | copy-start | bytes 6148
  647.1 74.4 %copy-start.27 = (f32[768]{0:T(1024)S(1)}, f32[768]{0:T(1024)}, u32[]{:S(2)}) copy-start(f32[768]{0:T(1024)} %copy-done.26) | copy-start | bytes 9220
  730.7 9.3 copy-start.7
  730.7 9.3 copy-start.16
  730.7 9.3 copy-start.17
  730.7 9.3 copy-start.40
  740.0 2.5 copy-start.29
  742.5 1.4 copy-start.1
  742.5 1.6 copy-start.6
  744.2 0.7 copy-start.36
  744.2 1.6 copy-start.30
  744.2 1.6 copy-start.31
  744.2 1.6 copy-start.34
Sparse Core Ops, SparseCore 0:
  10.9 62.7 all-gather.6
  81.1 59.1 all-gather.10
  142.3 61.6 all-gather.8
  206.8 52.2 all-gather.12
  261.9 62.5 all-gather.14
  327.2 62.4 all-gather.16
  570.1 73.6 reduce-scatter.6
  647.3 74.0 reduce-scatter.8
  727.3 98.1 reduce-scatter.12
  832.9 134.6 reduce-scatter.16
  974.1 134.4 reduce-scatter.14
  1115.6 118.3 reduce-scatter.10
where the time goes:
time: 1250 us; the launch traced here: 1240 us
  waiting for transfers between devices  750 us (60%)
  matrix products  265 us (21%)
  blocking collectives  82.6 us (7%)
  local copies, waits for them, and re-layouts  80.2 us (6%)
  other arithmetic  47.1 us (4%)
  between operations  14.9 us (1%)
    reduce_scatter x1, waiting for transfers between devices, shards(): lax.psum_scatter(grad_down_w, ('leaf', 'fsdp'), scatter_dimension=0, tile...  142 us
    reduce_scatter x1, waiting for transfers between devices, shards(): lax.psum_scatter(grad_up_w, ('leaf', 'fsdp'), scatter_dimension=0, tiled=...  141 us
    reduce_scatter x1, waiting for transfers between devices, shards(): lax.psum_scatter(grad_qkv_w, ('leaf', 'fsdp'), scatter_dimension=0, tiled...  125 us
    unnamed x2, blocking collectives  82.6 us
    reduce_scatter x1, waiting for transfers between devices, shards(): lax.psum_scatter(grad_values_all[:tree_tok].astype(jnp.bfloat16), 'leaf',...  72.4 us
    all_gather x1, waiting for transfers between devices, shards(): lax.all_gather(w_down, ('leaf', 'fsdp'), axis=0, tiled=True)  57 us
    all_gather x1, waiting for transfers between devices, shards(): lax.all_gather(key_low[:rows_dev], 'leaf', axis=0, tiled=True)  53.8 us
    reduce_scatter x1, waiting for transfers between devices, shards(): lax.psum_scatter(grad_keys_all[:tree_tok].astype(jnp.bfloat16), 'leaf', s...  42.4 us
  transfers between devices with their start and end apart: 12, of which 11 were waited for; matrix products, arithmetic and copies ran while one was open for 16% of the time, Pallas kernels for 0%

commit v1 on v0

v1 whole, which is shorter than its diff:
```python
import functools
import math

import jax
import jax.numpy as jnp
from jax import lax
from jax.experimental import pallas as pl
from jax.experimental.pallas import tpu as pltpu
from jax.sharding import PartitionSpec as P

HEAD_DIM = 64
BLOCK = 16
NEG_FILL = -1000000000.0
EPSILON = 1e-05
VMEM_LIMIT = 56 * 1024 * 1024
BF = jnp.bfloat16
F32 = jnp.float32


def look_up(table, indices):
    slots = jnp.arange(table.shape[0], dtype=jnp.int32)
    hits = indices[..., None] == slots
    return jnp.sum(jnp.where(hits, table, 0), axis=-1)


def tree_layout(seg_row, parent_row):
    slots = jnp.arange(parent_row.shape[0], dtype=jnp.int32)
    seg_lengths = jnp.sum((seg_row[:, None] == slots).astype(jnp.int32), axis=0)
    seg_starts = jnp.sum((seg_row[:, None] < slots).astype(jnp.int32), axis=0)
    grand_parent = look_up(parent_row, parent_row)
    offsets = jnp.where(slots > 0, look_up(seg_lengths, parent_row), 0) + jnp.where(
        parent_row > 0, look_up(seg_lengths, grand_parent), 0
    )
    block_ids = jnp.arange(seg_row.shape[0], dtype=jnp.int32)
    path_block = look_up(offsets, seg_row) + block_ids - look_up(seg_starts, seg_row)
    return (path_block, look_up(parent_row, seg_row), look_up(grand_parent, seg_row))


class Links:
    def __init__(self):
        leaf = lax.axis_index("leaf")
        fsdp = lax.axis_index("fsdp")
        self.z, self.y = leaf // 2, leaf % 2
        self.x, self.core = fsdp // 2, fsdp % 2

    def swap_core(self, v):
        return lax.ppermute(v, "fsdp", [(i, i ^ 1) for i in range(4)])

    def swap_x(self, v):
        return lax.ppermute(v, "fsdp", [(i, i ^ 2) for i in range(4)])

    def swap_y(self, v, pairs=None):
        return lax.ppermute(v, "leaf", pairs or [(i, i ^ 1) for i in range(8)])

    def up(self, v, first, last):
        return lax.ppermute(v, "leaf", [(i, i + 2) for i in range(2 * first, 2 * last + 2)])

    def down(self, v, first, last):
        return lax.ppermute(v, "leaf", [(i, i - 2) for i in range(2 * first, 2 * last + 2)])


def both(bit, own, other, axis):
    return jnp.where(
        bit == 0, jnp.stack([own, other], axis), jnp.stack([other, own], axis)
    )


def gather_rows(at, block):
    ups, downs = [], []
    cur = block
    for s in (1, 2, 3):
        cur = at.up(cur, s - 1, 2)
        ups.append(cur)
    cur = block
    for s in (1, 2, 3):
        cur = at.down(cur, 1, 4 - s)
        downs.append(cur)
    places = []
    for p in range(4):
        value = block
        for z in range(4):
            if z != p:
                value = jnp.where(at.z == z, ups[z - p - 1] if z > p else downs[p - z - 1], value)
        places.append(value)
    line = jnp.stack(places)
    plane = both(at.y, line, at.swap_y(line), 1)
    plane = plane.reshape((8,) + block.shape)
    return both(at.x, plane, at.swap_x(plane), 1)


def pick(v, index, axis):
    return lax.dynamic_index_in_dim(v, index, axis, keepdims=False)


def choose(bit, v, axis):
    first, second = pick(v, 0, axis), pick(v, 1, axis)
    return jnp.where(bit == 0, first, second), jnp.where(bit == 0, second, first)


def plus(a, b):
    return a.astype(F32) + b.astype(F32)


def reduce_rows(at, own, other):
    g = plus(own, at.swap_core(other)).astype(BF)
    keep, send = choose(at.x, g, 1)
    g = plus(keep, at.swap_x(send)).astype(BF)
    g = g.reshape((4, 2) + g.shape[1:])
    keep, send = choose(at.y, g, 1)
    g = plus(keep, at.swap_y(send)).astype(BF)
    high = None
    for s in (1, 2, 3):
        part = pick(g, jnp.minimum(at.z + 4 - s, 3), 0)
        part = part if high is None else plus(part, high).astype(BF)
        high = at.up(part, 0, s - 1)
    low = None
    for s in (1, 2, 3):
        part = pick(g, jnp.maximum(at.z - 4 + s, 0), 0)
        part = part if low is None else plus(part, low).astype(BF)
        low = at.down(part, 4 - s, 3)
    return plus(pick(g, at.z, 0), high) + low.astype(F32)


def to_column_half(at, half_a, half_b):
    keep = jnp.where(at.core == 0, half_a, half_b)
    send = jnp.where(at.core == 0, half_b, half_a)
    got = at.swap_core(send)
    return both(at.core, keep, got, 0).reshape(2 * keep.shape[0], keep.shape[1])


def from_column_half(at, g):
    g = g.reshape(2, g.shape[0] // 2, g.shape[1])
    keep, send = choose(at.core, g, 0)
    got = at.swap_core(send)
    return jnp.where(at.core == 0, keep, got), jnp.where(at.core == 0, got, keep)


def spec(shape, index_map):
    return pl.BlockSpec(shape, index_map)


def turn(values, cosine, sine):
    lane = lax.broadcasted_iota(jnp.int32, (values.shape[0], 128), 1)
    low_half = (lane % HEAD_DIM) < HEAD_DIM // 2
    groups = []
    for n in range(values.shape[1] // 128):
        part = values[:, n * 128 : (n + 1) * 128]
        swapped = jnp.where(low_half, pltpu.roll(part, 96, 1), pltpu.roll(part, 32, 1))
        groups.append(part * cosine + swapped * sine)
    return groups


def project_kernel(x_ref, gain_ref, own_ref, other_ref, cos_ref, sin_ref, a_ref, q_ref, k_ref, v_ref):
    tile = pl.program_id(0)
    x = x_ref[...].astype(F32)
    centred = x - jnp.mean(x, axis=-1, keepdims=True)
    spread = jnp.mean(centred * centred, axis=-1, keepdims=True)
    a = (centred * lax.rsqrt(spread + EPSILON) * gain_ref[...]).astype(BF)
    a_ref[...] = a
    cosine, sine = cos_ref[...], sin_ref[...]
    half = own_ref.shape[1] // 3
    for n, w_ref in enumerate((own_ref, other_ref)):
        base = n * half
        kv = jnp.dot(a, w_ref[:, half:], preferred_element_type=F32)
        for g, part in enumerate(turn(kv[:, :half], cosine, sine)):
            k_ref[:, base + g * 128 : base + (g + 1) * 128] = part.astype(BF)
        v_ref[:, base : base + half] = kv[:, half:].astype(BF)

        @pl.when(tile < 2)
        def _():
            q = jnp.dot(a, w_ref[:, :half], preferred_element_type=F32)
            for g, part in enumerate(turn(q, cosine, sine)):
                q_ref[:, base + g * 128 : base + (g + 1) * 128] = part.astype(BF)


def project(x_all, gain, own, other, cosine, sine, rows):
    total, width = x_all.shape
    tiles = total // rows
    whole = lambda shape: spec(shape, lambda t: (0, 0))
    out = lambda n: jax.ShapeDtypeStruct((n, width), BF)
    return pl.pallas_call(
        project_kernel,
        grid=(tiles,),
        in_specs=[
            spec((rows, width), lambda t: (t, 0)),
            whole((1, width)),
            whole(own.shape),
            whole(other.shape),
            spec((rows, 128), lambda t: (t, 0)),
            spec((rows, 128), lambda t: (t, 0)),
        ],
        out_specs=[
            spec((rows, width), lambda t: (t, 0)),
            spec((rows, width), lambda t: (jnp.minimum(t, 1), 0)),
            spec((rows, width), lambda t: (t, 0)),
            spec((rows, width), lambda t: (t, 0)),
        ],
        out_shape=[out(total), out(2 * rows), out(total), out(total)],
        compiler_params=pltpu.CompilerParams(vmem_limit_bytes=VMEM_LIMIT),
        cost_estimate=pl.CostEstimate(
            flops=2 * total * width * 2 * width,
            bytes_accessed=2 * (4 * total * width + 3 * width * width),
            transcendentals=0,
        ),
    )(x_all, gain, own, other, cosine, sine)


def matmul_t(a, b):
    return lax.dot_general(a, b, (((1,), (1,)), ((), ())), preferred_element_type=F32)


def attend_kernel(
    rows, tiles, flag_ref, qcol_ref, krow_ref, q_ref, k_ref, v_ref, o_ref, lse_ref,
    bias_ref, s_ref, top_ref, sum_ref, acc_ref,
):
    pair = pl.program_id(0)
    both_rows = 2 * rows

    def span(t):
        return slice(t * rows, (t + 1) * rows)

    def lines(t):
        return slice(rows, both_rows) if t == 1 else slice(0, both_rows)

    @pl.when(pair == 0)
    def _():
        lse_ref[...] = jnp.zeros_like(lse_ref)
        own = qcol_ref[:, 0:1]
        up_one = qcol_ref[:, 1:2]
        up_two = qcol_ref[:, 2:3]
        limit = qcol_ref[:, 3:4]
        for t in range(tiles):
            if t == 1:
                r = lax.broadcasted_iota(jnp.int32, (rows, rows), 0) // BLOCK
                c = lax.broadcasted_iota(jnp.int32, (rows, rows), 1) // BLOCK
                bias_ref[rows:, span(t)] = jnp.where(r == c, 0.0, NEG_FILL)
            else:
                seg = krow_ref[0:1, span(t)]
                index = krow_ref[1:2, span(t)]
                ok = ((seg == own) | (seg == up_one) | (seg == up_two)) & (index < limit)
                bias_ref[:, span(t)] = jnp.where(ok, 0.0, NEG_FILL)

    lane = lax.broadcasted_iota(jnp.int32, (both_rows, 128), 1)
    result = None
    for h in range(2):
        mine = (lane // HEAD_DIM) == h
        q = jnp.where(mine, q_ref[...] * 0.125, 0).astype(BF)
        top_ref[...] = jnp.full_like(top_ref, -3.0e38)
        for t in range(tiles):

            @pl.when(flag_ref[t] > 0)
            def _():
                at = lines(t)
                s = matmul_t(q[at], k_ref[span(t), :]) + bias_ref[at, span(t)]
                s_ref[at, span(t)] = s
                best = top_ref[at, :]
                for c in range(rows // 128):
                    best = jnp.maximum(best, s[:, c * 128 : (c + 1) * 128])
                top_ref[at, :] = best

        top = jnp.max(top_ref[...], axis=-1, keepdims=True)
        sum_ref[...] = jnp.zeros_like(sum_ref)
        acc_ref[...] = jnp.zeros_like(acc_ref)
        for t in range(tiles):

            @pl.when(flag_ref[t] > 0)
            def _():
                at = lines(t)
                p = jnp.exp(s_ref[at, span(t)] - top[at])
                part = sum_ref[at, :]
                for c in range(rows // 128):
                    part = part + p[:, c * 128 : (c + 1) * 128]
                sum_ref[at, :] = part
                acc_ref[at, :] += jnp.dot(p.astype(BF), v_ref[span(t), :], preferred_element_type=F32)

        total = jnp.sum(sum_ref[...], axis=-1, keepdims=True)
        o = acc_ref[...] / total
        lse_ref[...] = jnp.where(lane == 2 * pair + h, top + jnp.log(total), lse_ref[...])
        result = o if result is None else jnp.where(mine, o, result)
    o_ref[...] = result.astype(BF)


def attend(flags, qcol, krow, q, k, v, rows):
    width = q.shape[1]
    total = k.shape[0]
    tiles = total // rows
    pair = lambda n: spec((n, 128), lambda p, f: (0, p))
    fixed = lambda shape: spec(shape, lambda p, f: (0, 0))
    return pl.pallas_call(
        functools.partial(attend_kernel, rows, tiles),
        grid_spec=pltpu.PrefetchScalarGridSpec(
            num_scalar_prefetch=1,
            grid=(width // 128,),
            in_specs=[fixed(qcol.shape), fixed(krow.shape), pair(2 * rows), pair(total), pair(total)],
            out_specs=[pair(2 * rows), fixed((2 * rows, 128))],
            scratch_shapes=[
                pltpu.VMEM((2 * rows, total), F32),
                pltpu.VMEM((2 * rows, total), F32),
                pltpu.VMEM((2 * rows, 128), F32),
                pltpu.VMEM((2 * rows, 128), F32),
                pltpu.VMEM((2 * rows, 128), F32),
            ],
        ),
        out_shape=[
            jax.ShapeDtypeStruct((2 * rows, width), BF),
            jax.ShapeDtypeStruct((2 * rows, 128), F32),
        ],
        compiler_params=pltpu.CompilerParams(vmem_limit_bytes=VMEM_LIMIT),
        cost_estimate=pl.CostEstimate(
            flops=16 * rows * total * width,
            bytes_accessed=4 * (total + rows) * width,
            transcendentals=2 * rows * total * width // HEAD_DIM,
        ),
    )(flags, qcol, krow, q, k, v)


def attend_back_kernel(
    rows, tiles, flag_ref, qrow_ref, kcol_ref, q_ref, k_ref, v_ref, o_ref, g_ref, lse_ref,
    cos_ref, sin_ref, dq_ref, dk_ref, dv_ref, bias_ref, acc_ref,
):
    pair = pl.program_id(0)
    both_rows = 2 * rows

    def span(t):
        return slice(t * rows, (t + 1) * rows)

    def lines(t):
        return slice(rows, both_rows) if t == 1 else slice(0, both_rows)

    @pl.when(pair == 0)
    def _():
        own = qrow_ref[0:1, :]
        up_one = qrow_ref[1:2, :]
        up_two = qrow_ref[2:3, :]
        limit = qrow_ref[3:4, :]
        for t in range(tiles):
            if t == 1:
                r = lax.broadcasted_iota(jnp.int32, (rows, rows), 0) // BLOCK
                c = lax.broadcasted_iota(jnp.int32, (rows, rows), 1) // BLOCK
                bias_ref[span(t), rows:] = jnp.where(r == c, 0.0, NEG_FILL)
            else:
                seg = kcol_ref[span(t), 0:1]
                index = kcol_ref[span(t), 1:2]
                ok = ((seg == own) | (seg == up_one) | (seg == up_two)) & (index < limit)
                bias_ref[span(t), :] = jnp.where(ok, 0.0, NEG_FILL)

    lane = lax.broadcasted_iota(jnp.int32, (both_rows, 128), 1)
    acc_ref[...] = jnp.zeros_like(acc_ref)
    queries, grads, deltas, norms = [], [], [], []
    product = (o_ref[...].astype(F32) * g_ref[...].astype(F32)).T
    for h in range(2):
        mine = (lane // HEAD_DIM) == h
        queries.append(jnp.where(mine, q_ref[...] * 0.125, 0).astype(BF))
        grads.append(jnp.where(mine, g_ref[...], 0).astype(BF))
        deltas.append(jnp.sum(product[h * HEAD_DIM : (h + 1) * HEAD_DIM], axis=0, keepdims=True))
        norms.append(lse_ref[pl.ds(2 * pair + h, 1), :])
    for t in range(tiles):

        @pl.when(flag_ref[t] == 0)
        def _():
            dk_ref[span(t), :] = jnp.zeros((rows, 128), BF)
            dv_ref[span(t), :] = jnp.zeros((rows, 128), BF)

        @pl.when(flag_ref[t] > 0)
        def _():
            at = lines(t)
            keys, values = k_ref[span(t), :], v_ref[span(t), :]
            keys_t = keys.astype(F32).T.astype(BF)
            dk = dv = None
            for h in range(2):
                q, g = queries[h][at], grads[h][at]
                s = matmul_t(keys, q) + bias_ref[span(t), at]
                p = jnp.exp(s - norms[h][:, at])
                dp = matmul_t(values, g)
                ds = (p * (dp - deltas[h][:, at])).astype(BF)
                part_v = jnp.dot(p.astype(BF), g, preferred_element_type=F32)
                part_k = jnp.dot(ds, q, preferred_element_type=F32)
                dv = part_v if dv is None else dv + part_v
                dk = part_k if dk is None else dk + part_k
                half = slice(h * HEAD_DIM, (h + 1) * HEAD_DIM)
                acc_ref[half, at] += jnp.dot(keys_t[half], ds, preferred_element_type=F32)
            [dk] = turn(dk, cos_ref[span(t), :], -sin_ref[span(t), :])
            dk_ref[span(t), :] = dk.astype(BF)
            dv_ref[span(t), :] = dv.astype(BF)

    dq = acc_ref[...].T * 0.125
    [dq] = turn(dq, cos_ref[:both_rows, :], -sin_ref[:both_rows, :])
    dq_ref[...] = dq.astype(BF)


def attend_back(flags, qrow, kcol, q, k, v, o, g, lse, cosine, sine, rows):
    width = q.shape[1]
    total = k.shape[0]
    tiles = total // rows
    pair = lambda n: spec((n, 128), lambda p, f: (0, p))
    fixed = lambda shape: spec(shape, lambda p, f: (0, 0))
    out = lambda n: jax.ShapeDtypeStruct((n, width), BF)
    return pl.pallas_call(
        functools.partial(attend_back_kernel, rows, tiles),
        grid_spec=pltpu.PrefetchScalarGridSpec(
            num_scalar_prefetch=1,
            grid=(width // 128,),
            in_specs=[
                fixed(qrow.shape), fixed(kcol.shape), pair(2 * rows), pair(total), pair(total),
                pair(2 * rows), pair(2 * rows), fixed(lse.shape), fixed(cosine.shape), fixed(sine.shape),
            ],
            out_specs=[pair(2 * rows), pair(total), pair(total)],
            scratch_shapes=[
                pltpu.VMEM((total, 2 * rows), F32),
                pltpu.VMEM((128, 2 * rows), F32),
            ],
        ),
        out_shape=[out(2 * rows), out(total), out(total)],
        compiler_params=pltpu.CompilerParams(vmem_limit_bytes=VMEM_LIMIT),
        cost_estimate=pl.CostEstimate(
            flops=40 * rows * total * width,
            bytes_accessed=8 * (total + rows) * width,
            transcendentals=2 * rows * total * width // HEAD_DIM,
        ),
    )(flags, qrow, kcol, q, k, v, o, g, lse, cosine, sine)


def normalise(values):
    centred = values - jnp.mean(values, axis=-1, keepdims=True)
    spread = jnp.mean(centred * centred, axis=-1, keepdims=True)
    scale = lax.rsqrt(spread + EPSILON)
    return centred * scale, scale


def norm_back(hat, scale, gain, grad):
    scaled = grad * gain
    return scale * (
        scaled
        - jnp.mean(scaled, axis=-1, keepdims=True)
        - hat * jnp.mean(scaled * hat, axis=-1, keepdims=True)
    )


ROOT = math.sqrt(2.0 / math.pi)


def gelu_parts(u):
    t = jnp.tanh(ROOT * (u + 0.044715 * (u * u * u)))
    slope = 0.5 * (1.0 + t) + 0.5 * u * (1.0 - t * t) * (ROOT * (1.0 + 3 * 0.044715 * (u * u)))
    return 0.5 * u * (1.0 + t), slope


def mm(a, b):
    return jnp.dot(a, b, preferred_element_type=F32)


def mm_t(a, b):
    return lax.dot_general(a, b, (((1,), (1,)), ((), ())), preferred_element_type=F32)


def t_mm(a, b):
    return lax.dot_general(a, b, (((0,), (0,)), ((), ())), preferred_element_type=F32)


def halves_of_heads(w):
    w = w.reshape(w.shape[0], 3, 2, -1)
    return w[:, :, 0].reshape(w.shape[0], -1), w[:, :, 1].reshape(w.shape[0], -1)


def heads_of_halves(a, b):
    a, b = a.reshape(a.shape[0], 3, -1), b.reshape(b.shape[0], 3, -1)
    return jnp.stack([a, b], 2).reshape(a.shape[0], -1)


def halves_of_units(w, chunk):
    w = w.reshape(w.shape[0], -1, 2, chunk)
    return w[:, :, 0].reshape(w.shape[0], -1), w[:, :, 1].reshape(w.shape[0], -1)


def units_of_halves(a, b, chunk):
    a, b = a.reshape(a.shape[0], -1, chunk), b.reshape(b.shape[0], -1, chunk)
    return jnp.stack([a, b], 2).reshape(a.shape[0], -1)


class Chain:
    def __init__(self, rows):
        self.at = Links()
        self.rows = rows
        self.core = self.at.core

    def tree(self, hid):
        at = self.at
        chain = []
        cur = hid
        for s in (1, 2, 3):
            cur = at.up(cur, s - 1, 2)
            pairs = [(i, i ^ 1) for i in range(2 * s, 8)]
            chain += [cur, at.swap_y(cur, pairs)]
        chain.append(at.swap_y(hid, [(i, i + 1) for i in range(0, 8, 2)]))
        return chain

    def tile_leaves(self):
        z, y = self.at.z, self.at.y
        found = []
        for s in (1, 2, 3):
            found += [(2 * (z - s) + y, z >= s), (2 * (z - s) + 1 - y, z >= s)]
        found.append((2 * z, y == 1))
        return found

    def tree_sum(self, own, parts):
        at = self.at
        low = [at.swap_y(parts[6], [(i, i - 1) for i in range(1, 8, 2)])]
        for s in (1, 2, 3):
            pairs = [(i, i ^ 1) for i in range(2 * s, 8)]
            low.append(at.swap_y(parts[2 * s - 1], pairs))
        cur = plus(parts[4], low[3])
        for s in (2, 1):
            cur = at.down(cur.astype(BF), s + 1, 3).astype(F32) + plus(parts[2 * s - 2], low[s])
        return own + at.down(cur.astype(BF), 1, 3).astype(F32) + low[0].astype(F32)

    def weights(self, w_qkv, w_out, w_up, w_down, vectors):
        at = self.at
        block = to_column_half(at, *halves_of_heads(w_qkv))
        mine = at.swap_core(vectors)
        row = both(at.core, vectors, mine, 0).reshape(1, -1)
        row = jnp.pad(row, ((0, 7), (0, block.shape[1] - row.shape[1])))
        first = gather_rows(at, jnp.concatenate([block, row], axis=0))
        m = block.shape[0]
        qkv = first[:, :, :m].reshape(16 * m, -1)
        vec = first[:, :, m, : 2 * vectors.shape[0]].reshape(32, -1)
        out_up = jnp.concatenate(
            [
                to_column_half(at, w_out[:, : w_out.shape[1] // 2], w_out[:, w_out.shape[1] // 2 :]),
                to_column_half(at, *halves_of_units(w_up, w_down.shape[0])),
            ],
            axis=1,
        )
        second = gather_rows(at, out_up).reshape(16 * m, -1)
        down = gather_rows(at, w_down).reshape(16 * w_down.shape[0], -1)
        cut = w_out.shape[1] // 2
        out_own = second[:, :cut]
        up_own = second[:, cut:]
        qkv_both = (qkv, at.swap_core(qkv))
        up_both = (up_own, at.swap_core(up_own))
        down_both = (down, at.swap_core(down))
        out = both(at.core, out_own, at.swap_core(out_own), 1).reshape(16 * m, -1)
        half = out.shape[0] // 2
        out = jnp.where(at.core == 0, out, jnp.concatenate([out[half:], out[:half]], axis=0))
        return qkv_both, out, up_both, down_both, vec

    def unit_bias(self, bias, chunk):
        a, b = halves_of_units(bias[None], chunk)
        return jnp.where(self.core == 0, a, b), jnp.where(self.core == 0, b, a)

    def unit_bias_back(self, own, other, chunk):
        a = jnp.where(self.core == 0, own, other)
        b = jnp.where(self.core == 0, other, own)
        return units_of_halves(a, b, chunk)[0]

    def sum_down(self, own, other):
        shape = (8, 2, own.shape[0] // 16, own.shape[1])
        return reduce_rows(self.at, own.reshape(shape), other.reshape(shape))

    def sum_up(self, own, other, chunk):
        shape = (8, 2, own.shape[0] // 16, own.shape[1])
        g = reduce_rows(self.at, own.reshape(shape), other.reshape(shape))
        return units_of_halves(*from_column_half(self.at, g), chunk)

    def sum_out(self, g):
        at = self.at
        half = g.shape[0] // 2
        g = jnp.where(at.core == 0, g, jnp.concatenate([g[half:], g[:half]], axis=0))
        g = g.reshape(8, 2, g.shape[0] // 16, 2, g.shape[1] // 2)
        own, other = choose(at.core, g, 3)
        a, b = from_column_half(at, reduce_rows(at, own, other))
        return jnp.concatenate([a, b], axis=1)

    def sum_qkv(self, own, other, vec):
        at = self.at
        m = own.shape[0] // 16
        shape = (8, 2, m, own.shape[1])
        n = vec.shape[1]
        rows = jnp.pad(vec.astype(BF).reshape(8, 2, 2, 1, n), ((0, 0),) * 3 + ((0, 7), (0, own.shape[1] - n)))
        mine, its = choose(at.core, rows, 2)
        g = reduce_rows(
            at,
            jnp.concatenate([own.reshape(shape), mine], axis=2),
            jnp.concatenate([other.reshape(shape), its], axis=2),
        )
        return heads_of_halves(*from_column_half(at, g[:m])), g[m, :n]


AXES = ("leaf", "fsdp")


class Whole:
    def __init__(self, rows, leaves, devices):
        self.rows, self.leaves, self.devices = rows, leaves, devices
        self.leaf = lax.axis_index("leaf")

    def tree(self, hid):
        every = lax.all_gather(hid, "leaf", axis=0, tiled=False)
        return [pick(every, leaf, 0) for leaf, _ in self.tile_leaves()]

    def tile_leaves(self):
        found = []
        for s in range(1, self.leaves):
            place = self.leaf - s
            found.append((jnp.maximum(place, 0), place >= 0))
        return found

    def tree_sum(self, own, parts):
        every = jnp.stack([own.astype(BF)] + [p for p in parts])
        order = [pick(every, (self.leaf - t) % self.leaves, 0) for t in range(self.leaves)]
        every = jnp.concatenate(order, axis=0)
        return lax.psum_scatter(every, "leaf", scatter_dimension=0, tiled=True).astype(F32)

    def weights(self, w_qkv, w_out, w_up, w_down, vectors):
        every = lambda w: lax.all_gather(w, AXES, axis=0, tiled=True)
        up_w, down_w = every(w_up), every(w_down)
        half = down_w.shape[0] // 2
        return (
            halves_of_heads(every(w_qkv)),
            every(w_out),
            (up_w[:, :half], up_w[:, half:]),
            (down_w[:half], down_w[half:]),
            every(vectors[None]),
        )

    def unit_bias(self, bias, chunk):
        half = bias.shape[0] // 2
        return bias[None, :half], bias[None, half:]

    def unit_bias_back(self, own, other, chunk):
        return jnp.concatenate([own, other], axis=1)[0]

    def scatter(self, g):
        return lax.psum_scatter(g.astype(F32), AXES, scatter_dimension=0, tiled=True)

    def sum_down(self, own, other):
        return self.scatter(jnp.concatenate([own, other], axis=0))

    def sum_up(self, own, other, chunk):
        return self.scatter(jnp.concatenate([own, other], axis=1))

    def sum_out(self, g):
        return self.scatter(g)

    def sum_qkv(self, own, other, vec):
        return self.scatter(heads_of_halves(own, other)), self.scatter(vec)[0]


def shards(
    leaves,
    groups,
    hidden,
    noise_mask,
    seg_blocks,
    parents,
    ln1_gain,
    w_qkv,
    w_out,
    ln2_gain,
    w_up,
    up_bias,
    w_down,
    down_bias,
    mask_embed,
    cotangent,
):
    rows = hidden.shape[1]
    width = hidden.shape[2]
    devices = leaves * groups
    net = Chain(rows) if (leaves, groups) == (8, 4) else Whole(rows, leaves, devices)
    chunk = w_down.shape[0]
    few = ln1_gain.shape[0]

    hid = hidden[0]
    lower = net.tree(hid)
    vectors = jnp.concatenate([ln1_gain, ln2_gain, down_bias, mask_embed, up_bias])
    qkv_w, out_w, up_w, down_w, vec = net.weights(w_qkv, w_out, w_up, w_down, vectors)
    gain_one, gain_two, down_b, embed = (
        vec[:, n * few : (n + 1) * few].reshape(1, width).astype(F32) for n in range(4)
    )
    up_b = net.unit_bias(vec[:, 4 * few :].reshape(-1).astype(F32), chunk)

    blocks = rows // BLOCK
    leaf = lax.axis_index("leaf")
    seg_row = seg_blocks[0]
    path_block, first_up, second_up = tree_layout(seg_row, parents[0])
    table = jnp.stack([seg_row, path_block, jnp.arange(seg_row.shape[0], dtype=jnp.int32), first_up, second_up])
    table = table.reshape(5, leaves, blocks)
    own = pick(table, leaf, 1)
    tiles = [own, own.at[0].set(-1)]
    for place, valid in net.tile_leaves():
        tile = pick(table, jnp.maximum(place, 0), 1)
        tiles.append(tile.at[0].set(jnp.where(valid, tile[0], -1)))
    keys = jnp.stack(tiles, axis=1)
    limit = jnp.concatenate([own[2] + 1, own[2]])
    queries = [jnp.tile(own[n], 2) for n in (0, 3, 4)] + [limit]
    seg_k, index_k = keys[0].reshape(1, -1), keys[2].reshape(1, -1)
    allowed = (
        (seg_k == queries[0][:, None]) | (seg_k == queries[1][:, None]) | (seg_k == queries[2][:, None])
    ) & (index_k < limit[:, None])
    flags = jnp.any(allowed.reshape(2 * blocks, -1, blocks), axis=(0, 2)).astype(jnp.int32)
    flags = flags.at[:2].set(1)
    per_token = lambda v: jnp.repeat(v, BLOCK, axis=-1)
    query_rows = per_token(jnp.stack(queries + queries))
    key_rows = per_token(jnp.concatenate([seg_k, index_k] * 4))
    query_cols = query_rows.T
    key_cols = key_rows.T

    lanes = jnp.arange(128, dtype=jnp.int32)
    exponent = (lanes % (HEAD_DIM // 2)).astype(F32) * (-math.log(10000.0) / (HEAD_DIM // 2))
    positions = (keys[1][:, :, None] * BLOCK + jnp.arange(BLOCK, dtype=jnp.int32)).reshape(-1, 1)
    angles = positions.astype(F32) * jnp.exp(exponent)
    cosine = jnp.cos(angles)
    sine = jnp.sin(angles) * jnp.where((lanes % HEAD_DIM) < HEAD_DIM // 2, -1.0, 1.0)

    masked = (noise_mask[0] == 1)[:, None]
    noisy = jnp.where(masked, embed.astype(BF), hid)
    x_all = jnp.concatenate([hid, noisy] + lower, axis=0)
    stream = jnp.concatenate([hid, noisy], axis=0).astype(F32)
    a_all, query, key, value = project(x_all, gain_one, qkv_w[0], qkv_w[1], cosine, sine, rows)
    mixed, log_norm = attend(flags, query_cols, key_rows, query, key, value, rows)
    after = stream + mm(mixed, out_w)
    hat_two, scale_two = normalise(after)
    normed_two = (hat_two * gain_two).astype(BF)
    act, slope = [], []
    for n in range(2):
        g, s = gelu_parts(mm(normed_two, up_w[n]) + up_b[n])
        act.append(g.astype(BF))
        slope.append(s)
    result = after + (mm(act[0], down_w[0]) + mm(act[1], down_w[1])) + down_b
    output = result.astype(BF).reshape(1, 2, rows, width)

    grad_two = cotangent[0].reshape(2 * rows, width)
    grad_out = grad_two.astype(F32)
    grad_down_b = jnp.sum(grad_out, axis=0)
    grad_down_w = [t_mm(act[n], grad_two).astype(BF) for n in range(2)]
    grad_pre = [(mm_t(grad_two, down_w[n]) * slope[n]).astype(BF) for n in range(2)]
    grad_up_b = [jnp.sum(g.astype(F32), axis=0, keepdims=True) for g in grad_pre]
    grad_up_w = [t_mm(normed_two, g).astype(BF) for g in grad_pre]
    grad_normed = mm_t(grad_pre[0], up_w[0]) + mm_t(grad_pre[1], up_w[1])
    grad_gain_two = jnp.sum(grad_normed * hat_two, axis=0)
    grad_after = grad_out + norm_back(hat_two, scale_two, gain_two, grad_normed)
    sum_down = net.sum_down(*grad_down_w)
    sum_up = net.sum_up(*grad_up_w, chunk)

    grad_one = grad_after.astype(BF)
    grad_out_w = t_mm(mixed, grad_one).astype(BF)
    grad_mixed = mm_t(grad_one, out_w).astype(BF)
    sum_out = net.sum_out(grad_out_w)
    grad_q, grad_k, grad_v = attend_back(
        flags, query_rows, key_cols, query, key, value, mixed, grad_mixed, log_norm.T, cosine, sine, rows
    )
    half = width // 2
    grad_a_kv = None
    grad_a_q = None
    grad_qkv_w = []
    for n in range(2):
        cut = slice(n * half, (n + 1) * half)
        pieces = (grad_k[:, cut], grad_v[:, cut])
        kv = jnp.concatenate(pieces, axis=1)
        part = mm_t(kv, qkv_w[n][:, half:])
        grad_a_kv = part if grad_a_kv is None else grad_a_kv + part
        part = mm_t(grad_q[:, cut], qkv_w[n][:, :half])
        grad_a_q = part if grad_a_q is None else grad_a_q + part
        grad_qkv_w.append(
            jnp.concatenate(
                [t_mm(a_all[: 2 * rows], grad_q[:, cut]).astype(BF), t_mm(a_all, kv).astype(BF)], axis=1
            )
        )
    hat_all, _ = normalise(x_all.astype(F32))
    grad_gain_one = jnp.sum(grad_a_kv * hat_all, axis=0) + jnp.sum(grad_a_q * hat_all[: 2 * rows], axis=0)
    mine = grad_a_kv[: 2 * rows] + grad_a_q
    parts = [grad_a_kv[t * rows : (t + 1) * rows].astype(BF) for t in range(2, len(tiles))]
    hat_noisy, scale_noisy = normalise(stream[rows:])
    stream_noisy = grad_after[rows:] + norm_back(hat_noisy, scale_noisy, gain_one, mine[rows:])
    grad_embed = jnp.sum(jnp.where(masked, stream_noisy, 0.0), axis=0)
    grad_vec = jnp.concatenate(
        [
            v.reshape(devices, -1)
            for v in (
                grad_gain_one, grad_gain_two, grad_down_b, grad_embed,
                net.unit_bias_back(grad_up_b[0], grad_up_b[1], chunk),
            )
        ],
        axis=1,
    )
    sum_qkv, sum_vec = net.sum_qkv(*grad_qkv_w, grad_vec)
    clean = net.tree_sum(mine[:rows], parts)
    hat_clean, scale_clean = normalise(stream[:rows])
    stream_clean = grad_after[:rows] + norm_back(hat_clean, scale_clean, gain_one, clean)
    grad_hidden = (stream_clean + jnp.where(masked, 0.0, stream_noisy)).astype(BF)[None]
    piece = lambda n: sum_vec[n * few : (n + 1) * few]
    return (
        output,
        grad_hidden,
        piece(0),
        sum_qkv,
        sum_out,
        piece(1),
        sum_up,
        sum_vec[4 * few :],
        sum_down,
        piece(2),
        piece(3),
    )


def solution(mesh):
    split = ("leaf", "fsdp")
    in_specs = (
        P("fsdp", "leaf", None),
        P("fsdp", "leaf"),
        P("fsdp", None),
        P("fsdp", None),
        P(split),
        P(split, None),
        P(split, None),
        P(split),
        P(split, None),
        P(split),
        P(split, None),
        P(split),
        P(split),
        P("fsdp", None, "leaf", None),
    )
    out_specs = (
        P("fsdp", None, "leaf", None),
        P("fsdp", "leaf", None),
        P(split),
        P(split, None),
        P(split, None),
        P(split),
        P(split, None),
        P(split),
        P(split, None),
        P(split),
        P(split),
    )
    body = functools.partial(shards, mesh.shape["leaf"], mesh.shape["fsdp"])
    return jax.shard_map(body, mesh=mesh, in_specs=in_specs, out_specs=out_specs, check_vma=False)
```

time: 1250 us -> 646 us (0.52)
  waiting for transfers between devices: 750 us -> 123 us
  starting transfers between devices: 0.83 us -> 223 us
  matrix products: 265 us -> 80.5 us
  blocking collectives: 82.6 us -> 0 us
  Pallas kernels: 0 us -> 59.5 us
  other arithmetic: 47.1 us -> 69.5 us
    reduce_scatter x6 -> x0, waiting for transfers between devices: 560 us -> none  [the longest x1 142 us: shards(): lax.psum_scatter(grad_down_w, ('leaf', 'fsdp'), scatter_dimension=0, tile...]
    ppermute x0 -> x85, starting transfers between devices: none -> 223 us  [the longest x24 152 us: up(): lax.ppermute(v, 'leaf', [(i, i + 2) for i in range(2 * first, 2 * last +...]
    all_gather x6 -> x0, waiting for transfers between devices: 188 us -> none  [the longest x1 57 us: shards(): lax.all_gather(w_down, ('leaf', 'fsdp'), axis=0, tiled=True)]
    dot_general x96 -> x23, matrix products: 265 us -> 80.5 us  [the longest x9 38.7 us: mm_t(): lax.dot_general(a, b, (((1,), (1,)), ((), ())), preferred_element_type=F32)]
    ppermute x0 -> x85, waiting for transfers between devices: none -> 123 us  [the longest x7 68 us: swap_x(): return lax.ppermute(v, 'fsdp', [(i, i ^ 2) for i in range(4)])]
    unnamed x2 -> x0, blocking collectives: 82.6 us -> none
    pallas_call x0 -> x3, Pallas kernels: none -> 59.5 us  [the longest x1 20.7 us: attend_back(): pl.pallas_call(functools.partial(attend_back_kernel, rows, tiles), grid_s...]
    while x4 -> x0, local copies, waits for them, and re-layouts: 18.8 us -> none  [shards(): lax.map(head_forward, (q_heads, to_heads(keys_all, heads), to_heads(value...]
  transfers between devices with their start and end apart: 12 -> 85, of which waited for: 11 -> 21; matrix products, arithmetic and copies ran while one was open for 16% -> 28% of each run, Pallas kernels for 0% -> 6%
where the time goes in v1:
time: 646 us; the launch traced here: 636 us
  starting transfers between devices  223 us (35%)
  waiting for transfers between devices  123 us (19%)
  matrix products  80.5 us (12%)
  local copies, waits for them, and re-layouts  77.7 us (12%)
  other arithmetic  69.5 us (11%)
  Pallas kernels  59.5 us (9%)
    ppermute x24, starting transfers between devices, up(): lax.ppermute(v, 'leaf', [(i, i + 2) for i in range(2 * first, 2 * last +...  152 us
    ppermute x7, waiting for transfers between devices, swap_x(): return lax.ppermute(v, 'fsdp', [(i, i ^ 2) for i in range(4)])  68 us
    dot_general x9, matrix products, mm_t(): lax.dot_general(a, b, (((1,), (1,)), ((), ())), preferred_element_type=F32)  38.7 us
    ppermute x15, starting transfers between devices, swap_y(): return lax.ppermute(v, 'leaf', pairs or [(i, i ^ 1) for i in range(8)])  35.7 us
    dot_general x9, matrix products, t_mm(): lax.dot_general(a, b, (((0,), (0,)), ((), ())), preferred_element_type=F32)  27 us
    ppermute x24, starting transfers between devices, down(): lax.ppermute(v, 'leaf', [(i, i - 2) for i in range(2 * first, 2 * last +...  26.2 us
    ppermute x24, waiting for transfers between devices, down(): lax.ppermute(v, 'leaf', [(i, i - 2) for i in range(2 * first, 2 * last +...  25.8 us
    ppermute x15, waiting for transfers between devices, swap_y(): return lax.ppermute(v, 'leaf', pairs or [(i, i ^ 1) for i in range(8)])  22.4 us
  transfers between devices with their start and end apart: 85, of which 21 were waited for; matrix products, arithmetic and copies ran while one was open for 28% of the time, Pallas kernels for 6%

profile of v1, /device:TPU:0, one launch (start us, length us, event | category | flops | bytes accessed | tf_op | source)
XLA Modules:
  0.0 636.4 jit_solution(15962934388507204001)
XLA Ops:
  0.6 4.9 collective-permute-start.29
  6.9 3.4 concatenate.88
  24.2 5.2 collective-permute-start.2
  33.2 5.9 fusion.34
  39.1 8.1 %collective-permute-start.20 = (bf16[48,1920]{1,0:T(8,128)(2,1)S(1)}, bf16[48,1920]{1,0:T(8,128)(2,1)S(1)}, u32[]{:S(2)}, u32[]{:S(2)}) collective-permute-start(bf16[48,1920]{1,0:T(8,128)(2,1)S(1)} %pad_maximum_fusion.18), channel_id=1, source_target_pairs={{0,8},{4,12},{8,16},{12,20},{16,24},{20,28},{1,9},{5,13},{9,17},{1... | collective-permute-start | bytes 552968 | tf_op jit(solution)/shard_map/ppermute | solution.py:56
  51.6 4.2 collective-permute-start.16
  60.1 9.2 %collective-permute-start.10 = (bf16[256,768]{1,0:T(8,128)(2,1)}, bf16[256,768]{1,0:T(8,128)(2,1)}, u32[]{:S(2)}, u32[]{:S(2)}) collective-permute-start(bf16[256,768]{1,0:T(8,128)(2,1)} %bitcast), channel_id=1, source_target_pairs={{0,8},{4,12},{8,16},{12,20},{16,24},{20,28},{1,9},{5,13},{9,17},{1... | collective-permute-start | bytes 1179656 | tf_op jit(solution)/shard_map/ppermute | solution.py:56
  72.6 4.2 collective-permute-done.25
  80.4 3.7 collective-permute-done.8
  98.3 2.8 maximum_select_fusion.6
  101.1 7.7 %collective-permute-done.26 = bf16[4,48,1920]{2,1,0:T(8,128)(2,1)} collective-permute-done((bf16[4,48,1920]{2,1,0:T(8,128)(2,1)}, bf16[4,48,1920]{2,1,0:T(8,128)(2,1)}, u32[]{:S(2)}, u32[]{:S(2)}) %collective-permute-start.26) | collective-permute-done | bytes 737312 | tf_op jit(solution)/shard_map/ppermute | solution.py:53
  110.2 3.2 maximum_select_fusion.3
  116.5 2.5 maximum_select_fusion.2
  127.9 2.8 slice.486
  132.1 2.8 copy.221
  152.3 19.0 %collective-permute-done.27 = bf16[8,48,1920]{2,1,0:T(8,128)(2,1)S(1)} collective-permute-done((bf16[8,48,1920]{2,1,0:T(8,128)(2,1)}, bf16[8,48,1920]{2,1,0:T(8,128)(2,1)S(1)}, u32[]{:S(2)}, u32[]{:S(2)}) %collective-permute-start.27) | collective-permute-done | bytes 1474592 | tf_op jit(solution)/shard_map/ppermute | solution.py:50
  173.0 2.9 maximum_select_fusion.1
  183.3 18.4 %shard_map.221 = (bf16[2304,768]{1,0:T(8,128)(2,1)}, bf16[512,768]{1,0:T(8,128)(2,1)}, bf16[2304,768]{1,0:T(8,128)(2,1)}, bf16[2304,768]{1,0:T(8,128)(2,1)}) custom-call(bf16[2304,768]{1,0:T(8,128)(2,1)} %copy-done.2, f32[1,768]{1,0:T(1,128)} %reshape.1087.gain_ref, bf16[768,1152]{1,0:T(8,128)(2,1)} %bitcast.410, bf16[768,1152]{1,0:T(8,128)(2,1)} %copy-done.27, ...), custom_call_target="tpu_custom_call" | custom-call | flops 5435817984 | bytes 17694720 | tf_op jit(solution)/shard_map/pallas_call | solution.py:181
  201.8 20.3 %shard_map.222 = (bf16[512,768]{1,0:T(8,128)(2,1)}, f32[512,128]{1,0:T(8,128)}) custom-call(s32[9]{0:T(128)} %copy-done.62, s32[512,8]{1,0:T(8,128)} %bitcast.440, s32[8,2304]{1,0:T(8,128)} %copy.222.krow_ref, bf16[512,768]{1,0:T(8,128)(2,1)} %get-tuple-element.128.q_ref, bf16[2304,768]{1,0:T(8,128)(2,1)} %get-tuple-element.129.k_ref, ...), custom_call_target="tpu_custom_call" | custom-call | flops 7247757312 | bytes 7864320 | tf_op jit(solution)/shard_map/pallas_call | solution.py:289
  226.4 6.4 %convert_reduce_fusion.2 = (bf16[1536]{0:T(1024)(128)(2,1)S(1)}, bf16[512,1536]{1,0:T(8,128)(2,1)}) fusion(f32[512,1536]{1,0:T(8,128)S(1)} %convolution_add_fusion.2, bf16[1536,768]{1,0:T(8,128)(2,1)} %bitcast.53, bf16[512,768]{1,0:T(8,128)(2,1)S(1)} %bitcast.414), kind=kOutput, calls=%fused_computation.45 | convolution fusion | flops 1223686656 | bytes 7867392 | tf_op jit(solution)/shard_map/dot_general | solution.py:453
  233.7 4.4 convolution_convert_fusion.3
  240.0 3.2 convolution_convert_fusion.1
  243.2 3.0 convolution_add_fusion.1
  246.2 3.2 convolution_convert_fusion
  249.4 4.6 convert_reduce_fusion.1
  254.0 2.8 convolution_convert_fusion.2
  256.8 4.1 multiply_reduce_fusion.1
  265.2 20.7 %shard_map.223 = (bf16[512,768]{1,0:T(8,128)(2,1)}, bf16[2304,768]{1,0:T(8,128)(2,1)}, bf16[2304,768]{1,0:T(8,128)(2,1)}) custom-call(s32[9]{0:T(128)} %copy-done.62, s32[8,512]{1,0:T(8,128)} %copy-done.47, s32[2304,8]{1,0:T(8,128)} %bitcast.409, bf16[512,768]{1,0:T(8,128)(2,1)} %get-tuple-element.128.q_ref, bf16[2304,768]{1,0:T(8,128)(2,1)} %get-tuple-element.129.k_ref, ...), custom_call_target="tpu_custom_call" | custom-call | flops 18119393280 | bytes 15728640 | tf_op jit(solution)/shard_map/pallas_call | solution.py:398
  285.9 2.7 convolution_convert_fusion.7
  288.6 2.7 convolution_convert_fusion.6
  298.4 4.1 fusion.32
  302.5 5.0 fusion.29
  311.0 3.8 reshape.1080
  314.8 4.2 fusion.124
  320.7 3.1 fusion.33
  323.9 9.6 %multiply_reduce_fusion = (f32[768]{0:T(1024)S(1)}, bf16[2304,768]{1,0:T(8,128)(2,1)S(1)}, f32[2304,768]{1,0:T(8,128)}, f32[2304,768]{1,0:T(8,128)}) fusion(f32[2304]{0:T(1024)S(1)} %add_rsqrt_fusion, f32[2304]{0:T(1024)S(1)} %broadcast_multiply_fusion, bf16[2304,768]{1,0:T(8,128)(2,1)S(1)} %copy-done.3, f32[2304,768]{1,0:T(8,128)} %fusion.29, ...), kind=kOutput, calls=%fused_computation.5 | convolution fusion | flops 2737372416 | bytes 33051648 | tf_op jit(solution)/shard_map/dot_general | solution.py:453
  337.3 3.6 fusion.118
  341.0 4.0 fusion.31
  345.0 4.6 add_convert_fusion.1
  351.8 8.5 %collective-permute-done.57 = bf16[8,48,384]{2,1,0:T(8,128)(2,1)S(1)} collective-permute-done((bf16[8,48,384]{2,1,0:T(8,128)(2,1)S(1)}, bf16[8,48,384]{2,1,0:T(8,128)(2,1)S(1)}, u32[]{:S(2)}, u32[]{:S(2)}) %collective-permute-start.57) | collective-permute-done | bytes 294944 | tf_op jit(solution)/shard_map/ppermute | solution.py:50
  360.5 13.0 %collective-permute-start.58 = (bf16[4,48,384]{2,1,0:T(8,128)(2,1)S(1)}, bf16[4,48,384]{2,1,0:T(8,128)(2,1)S(1)}, u32[]{:S(2)}, u32[]{:S(2)}) collective-permute-start(bf16[4,48,384]{2,1,0:T(8,128)(2,1)S(1)} %fusion.86), channel_id=1, source_target_pairs={{0,4},{4,0},{8,12},{12,8},{16,20},{20,16},{24,28},{28,24},{1,5},{5... | collective-permute-start | bytes 442376 | tf_op jit(solution)/shard_map/ppermute | solution.py:53
  377.0 25.4 %collective-permute-start.59 = (bf16[48,384]{1,0:T(8,128)(2,1)S(1)}, bf16[48,384]{1,0:T(8,128)(2,1)S(1)}, u32[]{:S(2)}, u32[]{:S(2)}) collective-permute-start(bf16[48,384]{1,0:T(8,128)(2,1)S(1)} %get-tuple-element.230), channel_id=1, source_target_pairs={{0,8},{4,12},{1,9},{5,13},{2,10},{6,14},{3,11},{7,15}} | collective-permute-start | bytes 110600 | tf_op jit(solution)/shard_map/ppermute | solution.py:56
  404.7 4.2 collective-permute-start.60
  415.4 52.6 %collective-permute-start.61 = (bf16[48,384]{1,0:T(8,128)(2,1)S(1)}, bf16[48,384]{1,0:T(8,128)(2,1)S(1)}, u32[]{:S(2)}, u32[]{:S(2)}) collective-permute-start(bf16[48,384]{1,0:T(8,128)(2,1)S(1)} %get-tuple-element.228), channel_id=1, source_target_pairs={{0,8},{4,12},{8,16},{12,20},{16,24},{20,28},{1,9},{5,13},{9,17},{1... | collective-permute-start | bytes 110600 | tf_op jit(solution)/shard_map/ppermute | solution.py:56
  471.5 5.2 collective-permute-done.64
  484.5 4.0 copy.240
  489.3 11.9 %collective-permute-done.44 = bf16[256,768]{1,0:T(8,128)(2,1)} collective-permute-done((bf16[256,768]{1,0:T(8,128)(2,1)}, bf16[256,768]{1,0:T(8,128)(2,1)}, u32[]{:S(2)}, u32[]{:S(2)}) %collective-permute-start.44) | collective-permute-done | bytes 393248 | tf_op jit(solution)/shard_map/ppermute | solution.py:59
  501.3 3.1 fusion.49
  512.3 2.4 fusion.3
  517.1 22.6 %collective-permute-done.77 = bf16[8,96,768]{2,1,0:T(8,128)(2,1)S(1)} collective-permute-done((bf16[8,96,768]{2,1,0:T(8,128)(2,1)S(1)}, bf16[8,96,768]{2,1,0:T(8,128)(2,1)S(1)}, u32[]{:S(2)}, u32[]{:S(2)}) %collective-permute-start.77) | collective-permute-done | bytes 1179680 | tf_op jit(solution)/shard_map/ppermute | solution.py:50
  542.4 17.8 %collective-permute-done.67 = bf16[8,48,1536]{2,1,0:T(8,128)(2,1)S(1)} collective-permute-done((bf16[8,48,1536]{2,1,0:T(8,128)(2,1)S(1)}, bf16[8,48,1536]{2,1,0:T(8,128)(2,1)S(1)}, u32[]{:S(2)}, u32[]{:S(2)}) %collective-permute-start.67) | collective-permute-done | bytes 1179680 | tf_op jit(solution)/shard_map/ppermute | solution.py:50
  560.7 3.2 collective-permute-start.68
  565.3 3.9 collective-permute-start.79
  570.0 3.7 collective-permute-done.68
  573.9 3.9 collective-permute-start.69
  580.6 4.4 collective-permute-start.70
  585.1 3.5 collective-permute-start.81
  589.4 3.9 collective-permute-start.71
  599.2 4.4 collective-permute-done.48
  603.8 5.2 collective-permute-start.49
  611.5 4.4 collective-permute-start.50
  616.0 2.4 collective-permute-done.50
  619.9 5.0 collective-permute-start.51
  628.9 4.0 collective-permute-done.54
  (513 shorter events, 179.3 us)
Async XLA Ops:
  0.6 38.5 %collective-permute-start.29 = (bf16[96,768]{1,0:T(8,128)(2,1)}, bf16[96,768]{1,0:T(8,128)(2,1)S(1)}, u32[]{:S(2)}, u32[]{:S(2)}) collective-permute-start(bf16[96,768]{1,0:T(8,128)(2,1)} %param.42), channel_id=1, source_target_pairs={{0,8},{4,12},{8,16},{12,20},{16,24},{20,28},{1,9},{5,13},{9,17},{1... | collective-permute-start | bytes 442376 | tf_op jit(solution)/shard_map/ppermute | solution.py:56
  5.6 41.6 %collective-permute-start.32 = (bf16[96,768]{1,0:T(8,128)(2,1)}, bf16[96,768]{1,0:T(8,128)(2,1)S(1)}, u32[]{:S(2)}, u32[]{:S(2)}) collective-permute-start(bf16[96,768]{1,0:T(8,128)(2,1)} %param.42), channel_id=1, source_target_pairs={{8,0},{12,4},{16,8},{20,12},{24,16},{28,20},{9,1},{13,5},{17,9},{2... | collective-permute-start | bytes 442376 | tf_op jit(solution)/shard_map/ppermute | solution.py:59
  10.3 11.9 %collective-permute-start.1 = (bf16[192]{0:T(256)(128)(2,1)S(1)}, bf16[192]{0:T(256)(128)(2,1)S(1)}, u32[]{:S(2)}, u32[]{:S(2)}) collective-permute-start(bf16[192]{0:T(256)(128)(2,1)S(1)} %concatenate.88), channel_id=1, source_target_pairs={{0,1},{1,0},{2,3},{3,2},{4,5},{5,4},{6,7},{7,6},{8,9},{9,8},{10,11... | collective-permute-start | bytes 1160 | tf_op jit(solution)/shard_map/ppermute | solution.py:47
  11.1 11.7 %collective-permute-start.18 = (bf16[24,384]{1,0:T(8,128)(2,1)S(1)}, bf16[24,384]{1,0:T(8,128)(2,1)S(1)}, u32[]{:S(2)}, u32[]{:S(2)}) collective-permute-start(bf16[24,384]{1,0:T(8,128)(2,1)S(1)} %get-tuple-element.242), channel_id=1, source_target_pairs={{0,1},{1,0},{2,3},{3,2},{4,5},{5,4},{6,7},{7,6},{8,9},{9,8},{10,11... | collective-permute-start | bytes 55304 | tf_op jit(solution)/shard_map/ppermute | solution.py:47
  12.8 10.1 %collective-permute-start = (bf16[24,1152]{1,0:T(8,128)(2,1)S(1)}, bf16[24,1152]{1,0:T(8,128)(2,1)S(1)}, u32[]{:S(2)}, u32[]{:S(2)}) collective-permute-start(bf16[24,1152]{1,0:T(8,128)(2,1)S(1)} %bitcast.444), channel_id=1, source_target_pairs={{0,1},{1,0},{2,3},{3,2},{4,5},{5,4},{6,7},{7,6},{8,9},{9,8},{10,11... | collective-permute-start | bytes 165896 | tf_op jit(solution)/shard_map/ppermute | solution.py:47
  22.9 8.2 %collective-permute-start.5 = (bf16[56,1152]{1,0:T(8,128)(2,1)S(1)}, bf16[56,1152]{1,0:T(8,128)(2,1)S(1)}, u32[]{:S(2)}, u32[]{:S(2)}) collective-permute-start(bf16[56,1152]{1,0:T(8,128)(2,1)S(1)} %fusion.88), channel_id=1, source_target_pairs={{8,0},{12,4},{16,8},{20,12},{24,16},{28,20},{9,1},{13,5},{17,9},{2... | collective-permute-start | bytes 387080 | tf_op jit(solution)/shard_map/ppermute | solution.py:59
  24.2 8.2 %collective-permute-start.2 = (bf16[56,1152]{1,0:T(8,128)(2,1)S(1)}, bf16[56,1152]{1,0:T(8,128)(2,1)S(1)}, u32[]{:S(2)}, u32[]{:S(2)}) collective-permute-start(bf16[56,1152]{1,0:T(8,128)(2,1)S(1)} %fusion.88), channel_id=1, source_target_pairs={{0,8},{4,12},{8,16},{12,20},{16,24},{20,28},{1,9},{5,13},{9,17},{1... | collective-permute-start | bytes 387080 | tf_op jit(solution)/shard_map/ppermute | solution.py:56
  29.5 18.4 %collective-permute-start.23 = (bf16[48,1920]{1,0:T(8,128)(2,1)S(1)}, bf16[48,1920]{1,0:T(8,128)(2,1)S(1)}, u32[]{:S(2)}, u32[]{:S(2)}) collective-permute-start(bf16[48,1920]{1,0:T(8,128)(2,1)S(1)} %pad_maximum_fusion.18), channel_id=1, source_target_pairs={{8,0},{12,4},{16,8},{20,12},{24,16},{28,20},{9,1},{13,5},{17,9},{2... | collective-permute-start | bytes 552968 | tf_op jit(solution)/shard_map/ppermute | solution.py:59
  31.2 18.0 %collective-permute-start.6 = (bf16[56,1152]{1,0:T(8,128)(2,1)S(1)}, bf16[56,1152]{1,0:T(8,128)(2,1)S(1)}, u32[]{:S(2)}, u32[]{:S(2)}) collective-permute-start(bf16[56,1152]{1,0:T(8,128)(2,1)S(1)} %collective-permute-done.5), channel_id=1, source_target_pairs={{8,0},{12,4},{16,8},{20,12},{9,1},{13,5},{17,9},{21,13},{10,2},{14... | collective-permute-start | bytes 387080 | tf_op jit(solution)/shard_map/ppermute | solution.py:59
  32.5 18.0 %collective-permute-start.3 = (bf16[56,1152]{1,0:T(8,128)(2,1)S(1)}, bf16[56,1152]{1,0:T(8,128)(2,1)S(1)}, u32[]{:S(2)}, u32[]{:S(2)}) collective-permute-start(bf16[56,1152]{1,0:T(8,128)(2,1)S(1)} %collective-permute-done.2), channel_id=1, source_target_pairs={{8,16},{12,20},{16,24},{20,28},{9,17},{13,21},{17,25},{21,29},{10,... | collective-permute-start | bytes 387080 | tf_op jit(solution)/shard_map/ppermute | solution.py:56
  39.1 12.5 %collective-permute-start.20 = (bf16[48,1920]{1,0:T(8,128)(2,1)S(1)}, bf16[48,1920]{1,0:T(8,128)(2,1)S(1)}, u32[]{:S(2)}, u32[]{:S(2)}) collective-permute-start(bf16[48,1920]{1,0:T(8,128)(2,1)S(1)} %pad_maximum_fusion.18), channel_id=1, source_target_pairs={{0,8},{4,12},{8,16},{12,20},{16,24},{20,28},{1,9},{5,13},{9,17},{1... | collective-permute-start | bytes 552968 | tf_op jit(solution)/shard_map/ppermute | solution.py:56
  47.2 8.6 %collective-permute-start.30 = (bf16[96,768]{1,0:T(8,128)(2,1)S(1)}, bf16[96,768]{1,0:T(8,128)(2,1)S(1)}, u32[]{:S(2)}, u32[]{:S(2)}) collective-permute-start(bf16[96,768]{1,0:T(8,128)(2,1)S(1)} %collective-permute-done.29), channel_id=1, source_target_pairs={{8,16},{12,20},{16,24},{20,28},{9,17},{13,21},{17,25},{21,29},{10,... | collective-permute-start | bytes 442376 | tf_op jit(solution)/shard_map/ppermute | solution.py:56
  47.9 9.2 %collective-permute-start.33 = (bf16[96,768]{1,0:T(8,128)(2,1)S(1)}, bf16[96,768]{1,0:T(8,128)(2,1)S(1)}, u32[]{:S(2)}, u32[]{:S(2)}) collective-permute-start(bf16[96,768]{1,0:T(8,128)(2,1)S(1)} %collective-permute-done.32), channel_id=1, source_target_pairs={{8,0},{12,4},{16,8},{20,12},{9,1},{13,5},{17,9},{21,13},{10,2},{14... | collective-permute-start | bytes 442376 | tf_op jit(solution)/shard_map/ppermute | solution.py:59
  49.2 8.6 %collective-permute-start.7 = (bf16[56,1152]{1,0:T(8,128)(2,1)S(1)}, bf16[56,1152]{1,0:T(8,128)(2,1)S(1)}, u32[]{:S(2)}, u32[]{:S(2)}) collective-permute-start(bf16[56,1152]{1,0:T(8,128)(2,1)S(1)} %collective-permute-done.6), channel_id=1, source_target_pairs={{8,0},{12,4},{9,1},{13,5},{10,2},{14,6},{11,3},{15,7}} | collective-permute-start | bytes 387080 | tf_op jit(solution)/shard_map/ppermute | solution.py:59
  51.6 96.8 %collective-permute-start.16 = (bf16[256,768]{1,0:T(8,128)(2,1)}, bf16[256,768]{1,0:T(8,128)(2,1)}, u32[]{:S(2)}, u32[]{:S(2)}) collective-permute-start(bf16[256,768]{1,0:T(8,128)(2,1)} %bitcast), channel_id=1, source_target_pairs={{0,4},{8,12},{16,20},{24,28},{1,5},{9,13},{17,21},{25,29},{2,6},{1... | collective-permute-start | bytes 1179656 | tf_op jit(solution)/shard_map/ppermute | solution.py:53
  55.8 13.6 %collective-permute-start.24 = (bf16[48,1920]{1,0:T(8,128)(2,1)S(1)}, bf16[48,1920]{1,0:T(8,128)(2,1)S(1)}, u32[]{:S(2)}, u32[]{:S(2)}) collective-permute-start(bf16[48,1920]{1,0:T(8,128)(2,1)S(1)} %collective-permute-done.23), channel_id=1, source_target_pairs={{8,0},{12,4},{16,8},{20,12},{9,1},{13,5},{17,9},{21,13},{10,2},{14... | collective-permute-start | bytes 552968 | tf_op jit(solution)/shard_map/ppermute | solution.py:59
  57.1 13.6 %collective-permute-start.21 = (bf16[48,1920]{1,0:T(8,128)(2,1)S(1)}, bf16[48,1920]{1,0:T(8,128)(2,1)S(1)}, u32[]{:S(2)}, u32[]{:S(2)}) collective-permute-start(bf16[48,1920]{1,0:T(8,128)(2,1)S(1)} %collective-permute-done.20), channel_id=1, source_target_pairs={{8,16},{12,20},{16,24},{20,28},{9,17},{13,21},{17,25},{21,29},{10,... | collective-permute-start | bytes 552968 | tf_op jit(solution)/shard_map/ppermute | solution.py:56
  58.5 10.9 %collective-permute-start.34 = (bf16[96,768]{1,0:T(8,128)(2,1)S(1)}, bf16[96,768]{1,0:T(8,128)(2,1)S(1)}, u32[]{:S(2)}, u32[]{:S(2)}) collective-permute-start(bf16[96,768]{1,0:T(8,128)(2,1)S(1)} %collective-permute-done.33), channel_id=1, source_target_pairs={{8,0},{12,4},{9,1},{13,5},{10,2},{14,6},{11,3},{15,7}} | collective-permute-start | bytes 442376 | tf_op jit(solution)/shard_map/ppermute | solution.py:59
  60.1 27.2 %collective-permute-start.10 = (bf16[256,768]{1,0:T(8,128)(2,1)}, bf16[256,768]{1,0:T(8,128)(2,1)}, u32[]{:S(2)}, u32[]{:S(2)}) collective-permute-start(bf16[256,768]{1,0:T(8,128)(2,1)} %bitcast), channel_id=1, source_target_pairs={{0,8},{4,12},{8,16},{12,20},{16,24},{20,28},{1,9},{5,13},{9,17},{1... | collective-permute-start | bytes 1179656 | tf_op jit(solution)/shard_map/ppermute | solution.py:56
  69.4 14.7 %collective-permute-start.8 = (bf16[4,56,1152]{2,1,0:T(8,128)(2,1)S(1)}, bf16[4,56,1152]{2,1,0:T(8,128)(2,1)S(1)}, u32[]{:S(2)}, u32[]{:S(2)}) collective-permute-start(bf16[4,56,1152]{2,1,0:T(8,128)(2,1)S(1)} %get-tuple-element.205), channel_id=1, source_target_pairs={{0,4},{4,0},{8,12},{12,8},{16,20},{20,16},{24,28},{28,24},{1,5},{5... | collective-permute-start | bytes 1548296 | tf_op jit(solution)/shard_map/ppermute | solution.py:53
  70.7 8.1 %collective-permute-start.22 = (bf16[48,1920]{1,0:T(8,128)(2,1)S(1)}, bf16[48,1920]{1,0:T(8,128)(2,1)S(1)}, u32[]{:S(2)}, u32[]{:S(2)}) collective-permute-start(bf16[48,1920]{1,0:T(8,128)(2,1)S(1)} %collective-permute-done.21), channel_id=1, source_target_pairs={{16,24},{20,28},{17,25},{21,29},{18,26},{22,30},{19,27},{23,31}} | collective-permute-start | bytes 552968 | tf_op jit(solution)/shard_map/ppermute | solution.py:56
  76.9 20.0 %collective-permute-start.35 = (bf16[4,96,768]{2,1,0:T(8,128)(2,1)}, bf16[4,96,768]{2,1,0:T(8,128)(2,1)}, u32[]{:S(2)}, u32[]{:S(2)}) collective-permute-start(bf16[4,96,768]{2,1,0:T(8,128)(2,1)} %get-tuple-element.195), channel_id=1, source_target_pairs={{0,4},{4,0},{8,12},{12,8},{16,20},{20,16},{24,28},{28,24},{1,5},{5... | collective-permute-start | bytes 1769480 | tf_op jit(solution)/shard_map/ppermute | solution.py:53
  80.4 28.4 %collective-permute-start.26 = (bf16[4,48,1920]{2,1,0:T(8,128)(2,1)}, bf16[4,48,1920]{2,1,0:T(8,128)(2,1)}, u32[]{:S(2)}, u32[]{:S(2)}) collective-permute-start(bf16[4,48,1920]{2,1,0:T(8,128)(2,1)} %get-tuple-element.185), channel_id=1, source_target_pairs={{0,4},{4,0},{8,12},{12,8},{16,20},{20,16},{24,28},{28,24},{1,5},{5... | collective-permute-start | bytes 2211848 | tf_op jit(solution)/shard_map/ppermute | solution.py:53
  85.4 29.5 %collective-permute-start.9 = (bf16[8,56,1152]{2,1,0:T(8,128)(2,1)}, bf16[8,56,1152]{2,1,0:T(8,128)(2,1)}, u32[]{:S(2)}, u32[]{:S(2)}) collective-permute-start(bf16[8,56,1152]{2,1,0:T(8,128)(2,1)} %bitcast.10), channel_id=1, source_target_pairs={{0,2},{1,3},{2,0},{3,1},{4,6},{5,7},{6,4},{7,5},{8,10},{9,11},{10,... | collective-permute-start | bytes 3096584 | tf_op jit(solution)/shard_map/ppermute | solution.py:50
  94.8 46.1 %collective-permute-start.11 = (bf16[256,768]{1,0:T(8,128)(2,1)}, bf16[256,768]{1,0:T(8,128)(2,1)}, u32[]{:S(2)}, u32[]{:S(2)}) collective-permute-start(bf16[256,768]{1,0:T(8,128)(2,1)} %collective-permute-done.10), channel_id=1, source_target_pairs={{8,12},{12,8},{16,20},{20,16},{24,28},{28,24},{9,13},{13,9},{17,21... | collective-permute-start | bytes 1179656 | tf_op jit(solution)/shard_map/ppermute | solution.py:53
  96.9 16.6 %collective-permute-start.14 = (bf16[256,768]{1,0:T(8,128)(2,1)}, bf16[256,768]{1,0:T(8,128)(2,1)}, u32[]{:S(2)}, u32[]{:S(2)}) collective-permute-start(bf16[256,768]{1,0:T(8,128)(2,1)} %collective-permute-done.12), channel_id=1, source_target_pairs={{16,24},{20,28},{17,25},{21,29},{18,26},{22,30},{19,27},{23,31}} | collective-permute-start | bytes 1179656 | tf_op jit(solution)/shard_map/ppermute | solution.py:56
  108.8 34.7 %collective-permute-start.13 = (bf16[256,768]{1,0:T(8,128)(2,1)}, bf16[256,768]{1,0:T(8,128)(2,1)}, u32[]{:S(2)}, u32[]{:S(2)}) collective-permute-start(bf16[256,768]{1,0:T(8,128)(2,1)} %collective-permute-done.12), channel_id=1, source_target_pairs={{16,20},{20,16},{24,28},{28,24},{17,21},{21,17},{25,29},{29,25},{1... | collective-permute-start | bytes 1179656 | tf_op jit(solution)/shard_map/ppermute | solution.py:53
  113.5 59.5 %collective-permute-start.36 = (bf16[8,96,768]{2,1,0:T(8,128)(2,1)}, bf16[8,96,768]{2,1,0:T(8,128)(2,1)}, u32[]{:S(2)}, u32[]{:S(2)}) collective-permute-start(bf16[8,96,768]{2,1,0:T(8,128)(2,1)} %bitcast.51), channel_id=1, source_target_pairs={{0,2},{1,3},{2,0},{3,1},{4,6},{5,7},{6,4},{7,5},{8,10},{9,11},{10,... | collective-permute-start | bytes 3538952 | tf_op jit(solution)/shard_map/ppermute | solution.py:50
  115.0 31.9 %collective-permute-start.15 = (bf16[256,768]{1,0:T(8,128)(2,1)}, bf16[256,768]{1,0:T(8,128)(2,1)}, u32[]{:S(2)}, u32[]{:S(2)}) collective-permute-start(bf16[256,768]{1,0:T(8,128)(2,1)} %collective-permute-done.14), channel_id=1, source_target_pairs={{24,28},{28,24},{25,29},{29,25},{26,30},{30,26},{27,31},{31,27}} | collective-permute-start | bytes 1179656 | tf_op jit(solution)/shard_map/ppermute | solution.py:53
  140.9 30.4 %collective-permute-start.27 = (bf16[8,48,1920]{2,1,0:T(8,128)(2,1)}, bf16[8,48,1920]{2,1,0:T(8,128)(2,1)S(1)}, u32[]{:S(2)}, u32[]{:S(2)}) collective-permute-start(bf16[8,48,1920]{2,1,0:T(8,128)(2,1)} %bitcast.406), channel_id=1, source_target_pairs={{0,2},{1,3},{2,0},{3,1},{4,6},{5,7},{6,4},{7,5},{8,10},{9,11},{10,... | collective-permute-start | bytes 4423688 | tf_op jit(solution)/shard_map/ppermute | solution.py:50
  143.6 38.5 %collective-permute-start.17 = (bf16[768,1152]{1,0:T(8,128)(2,1)S(1)}, bf16[768,1152]{1,0:T(8,128)(2,1)S(1)}, u32[]{:S(2)}, u32[]{:S(2)}) collective-permute-start(bf16[768,1152]{1,0:T(8,128)(2,1)S(1)} %bitcast.411), channel_id=1, source_target_pairs={{0,1},{1,0},{2,3},{3,2},{4,5},{5,4},{6,7},{7,6},{8,9},{9,8},{10,11... | collective-permute-start | bytes 5308424 | tf_op jit(solution)/shard_map/ppermute | solution.py:47
  177.5 72.0 %collective-permute-start.38 = (bf16[1536,768]{1,0:T(8,128)(2,1)}, bf16[1536,768]{1,0:T(8,128)(2,1)}, u32[]{:S(2)}, u32[]{:S(2)}) collective-permute-start(bf16[1536,768]{1,0:T(8,128)(2,1)} %bitcast.53), channel_id=1, source_target_pairs={{0,1},{1,0},{2,3},{3,2},{4,5},{5,4},{6,7},{7,6},{8,9},{9,8},{10,11... | collective-permute-start | bytes 7077896 | tf_op jit(solution)/shard_map/ppermute | solution.py:47
  179.4 63.8 %collective-permute-start.37 = (bf16[768,1536]{1,0:T(8,128)(2,1)}, bf16[768,1536]{1,0:T(8,128)(2,1)}, u32[]{:S(2)}, u32[]{:S(2)}) collective-permute-start(bf16[768,1536]{1,0:T(8,128)(2,1)} %slice.494), channel_id=1, source_target_pairs={{0,1},{1,0},{2,3},{3,2},{4,5},{5,4},{6,7},{7,6},{8,9},{9,8},{10,11... | collective-permute-start | bytes 7077896 | tf_op jit(solution)/shard_map/ppermute | solution.py:47
  309.1 202.4 %collective-permute-start.66 = (bf16[8,2,48,1536]{3,2,1,0:T(8,128)(2,1)}, bf16[8,2,48,1536]{3,2,1,0:T(8,128)(2,1)}, u32[]{:S(2)}, u32[]{:S(2)}) collective-permute-start(bf16[8,2,48,1536]{3,2,1,0:T(8,128)(2,1)} %bitcast.103), channel_id=1, source_target_pairs={{0,1},{1,0},{2,3},{3,2},{4,5},{5,4},{6,7},{7,6},{8,9},{9,8},{10,11... | collective-permute-start | bytes 7077896 | tf_op jit(solution)/shard_map/ppermute | solution.py:47
  309.4 198.6 %collective-permute-start.76 = (bf16[8,2,96,768]{3,2,0,1:T(8,128)(2,1)}, bf16[8,2,96,768]{3,2,0,1:T(8,128)(2,1)}, u32[]{:S(2)}, u32[]{:S(2)}) collective-permute-start(bf16[8,2,96,768]{3,2,0,1:T(8,128)(2,1)} %copy.264), channel_id=1, source_target_pairs={{0,1},{1,0},{2,3},{3,2},{4,5},{5,4},{6,7},{7,6},{8,9},{9,8},{10,11... | collective-permute-start | bytes 7077896 | tf_op jit(solution)/shard_map/ppermute | solution.py:47
  320.0 29.5 %collective-permute-start.56 = (bf16[8,2,48,384]{3,2,1,0:T(8,128)(2,1)}, bf16[8,2,48,384]{3,2,1,0:T(8,128)(2,1)}, u32[]{:S(2)}, u32[]{:S(2)}) collective-permute-start(bf16[8,2,48,384]{3,2,1,0:T(8,128)(2,1)} %select_bitcast_fusion.2), channel_id=1, source_target_pairs={{0,1},{1,0},{2,3},{3,2},{4,5},{5,4},{6,7},{7,6},{8,9},{9,8},{10,11... | collective-permute-start | bytes 1769480 | tf_op jit(solution)/shard_map/ppermute | solution.py:47
  334.5 70.3 %collective-permute-start.39 = (bf16[256,768]{1,0:T(8,128)(2,1)S(1)}, bf16[256,768]{1,0:T(8,128)(2,1)S(1)}, u32[]{:S(2)}, u32[]{:S(2)}) collective-permute-start(bf16[256,768]{1,0:T(8,128)(2,1)S(1)} %get-tuple-element.166), channel_id=1, source_target_pairs={{24,28},{28,24},{25,29},{29,25},{26,30},{30,26},{27,31},{31,27}} | collective-permute-start | bytes 1179656 | tf_op jit(solution)/shard_map/ppermute | solution.py:53
  335.3 80.1 %collective-permute-start.41 = (bf16[256,768]{1,0:T(8,128)(2,1)}, bf16[256,768]{1,0:T(8,128)(2,1)}, u32[]{:S(2)}, u32[]{:S(2)}) collective-permute-start(bf16[256,768]{1,0:T(8,128)(2,1)} %get-tuple-element.169), channel_id=1, source_target_pairs={{16,20},{20,16},{24,28},{28,24},{17,21},{21,17},{25,29},{29,25},{1... | collective-permute-start | bytes 1179656 | tf_op jit(solution)/shard_map/ppermute | solution.py:53
  351.1 9.3 %collective-permute-start.57 = (bf16[8,48,384]{2,1,0:T(8,128)(2,1)S(1)}, bf16[8,48,384]{2,1,0:T(8,128)(2,1)S(1)}, u32[]{:S(2)}, u32[]{:S(2)}) collective-permute-start(bf16[8,48,384]{2,1,0:T(8,128)(2,1)S(1)} %fusion.67), channel_id=1, source_target_pairs={{0,2},{1,3},{2,0},{3,1},{4,6},{5,7},{6,4},{7,5},{8,10},{9,11},{10,... | collective-permute-start | bytes 884744 | tf_op jit(solution)/shard_map/ppermute | solution.py:50
  360.5 16.5 %collective-permute-start.58 = (bf16[4,48,384]{2,1,0:T(8,128)(2,1)S(1)}, bf16[4,48,384]{2,1,0:T(8,128)(2,1)S(1)}, u32[]{:S(2)}, u32[]{:S(2)}) collective-permute-start(bf16[4,48,384]{2,1,0:T(8,128)(2,1)S(1)} %fusion.86), channel_id=1, source_target_pairs={{0,4},{4,0},{8,12},{12,8},{16,20},{20,16},{24,28},{28,24},{1,5},{5... | collective-permute-start | bytes 442376 | tf_op jit(solution)/shard_map/ppermute | solution.py:53
  377.0 27.0 %collective-permute-start.59 = (bf16[48,384]{1,0:T(8,128)(2,1)S(1)}, bf16[48,384]{1,0:T(8,128)(2,1)S(1)}, u32[]{:S(2)}, u32[]{:S(2)}) collective-permute-start(bf16[48,384]{1,0:T(8,128)(2,1)S(1)} %get-tuple-element.230), channel_id=1, source_target_pairs={{0,8},{4,12},{1,9},{5,13},{2,10},{6,14},{3,11},{7,15}} | collective-permute-start | bytes 110600 | tf_op jit(solution)/shard_map/ppermute | solution.py:56
  409.8 58.2 %collective-permute-start.40 = (bf16[256,768]{1,0:T(8,128)(2,1)}, bf16[256,768]{1,0:T(8,128)(2,1)}, u32[]{:S(2)}, u32[]{:S(2)}) collective-permute-start(bf16[256,768]{1,0:T(8,128)(2,1)} %add_convert_fusion.4), channel_id=1, source_target_pairs={{24,16},{28,20},{25,17},{29,21},{26,18},{30,22},{27,19},{31,23}} | collective-permute-start | bytes 1179656 | tf_op jit(solution)/shard_map/ppermute | solution.py:59
  413.3 76.0 %collective-permute-start.45 = (bf16[256,768]{1,0:T(8,128)(2,1)}, bf16[256,768]{1,0:T(8,128)(2,1)}, u32[]{:S(2)}, u32[]{:S(2)}) collective-permute-start(bf16[256,768]{1,0:T(8,128)(2,1)} %get-tuple-element.167), channel_id=1, source_target_pairs={{4,0},{12,8},{20,16},{28,24},{5,1},{13,9},{21,17},{29,25},{6,2},{1... | collective-permute-start | bytes 1179656 | tf_op jit(solution)/shard_map/ppermute | solution.py:53
  415.4 55.3 %collective-permute-start.61 = (bf16[48,384]{1,0:T(8,128)(2,1)S(1)}, bf16[48,384]{1,0:T(8,128)(2,1)S(1)}, u32[]{:S(2)}, u32[]{:S(2)}) collective-permute-start(bf16[48,384]{1,0:T(8,128)(2,1)S(1)} %get-tuple-element.228), channel_id=1, source_target_pairs={{0,8},{4,12},{8,16},{12,20},{16,24},{20,28},{1,9},{5,13},{9,17},{1... | collective-permute-start | bytes 110600 | tf_op jit(solution)/shard_map/ppermute | solution.py:56
  468.1 8.6 %collective-permute-start.64 = (bf16[48,384]{1,0:T(8,128)(2,1)S(1)}, bf16[48,384]{1,0:T(8,128)(2,1)S(1)}, u32[]{:S(2)}, u32[]{:S(2)}) collective-permute-start(bf16[48,384]{1,0:T(8,128)(2,1)S(1)} %fusion.90), channel_id=1, source_target_pairs={{8,0},{12,4},{16,8},{20,12},{24,16},{28,20},{9,1},{13,5},{17,9},{2... | collective-permute-start | bytes 110600 | tf_op jit(solution)/shard_map/ppermute | solution.py:59
  478.0 10.7 %collective-permute-start.65 = (f32[24,384]{1,0:T(8,128)S(1)}, f32[24,384]{1,0:T(8,128)S(1)}, u32[]{:S(2)}, u32[]{:S(2)}) collective-permute-start(f32[24,384]{1,0:T(8,128)S(1)} %slice_select_fusion.4), channel_id=1, source_target_pairs={{0,1},{1,0},{2,3},{3,2},{4,5},{5,4},{6,7},{7,6},{8,9},{9,8},{10,11... | collective-permute-start | bytes 110600 | tf_op jit(solution)/shard_map/ppermute | solution.py:47
  480.0 21.3 %collective-permute-start.44 = (bf16[256,768]{1,0:T(8,128)(2,1)}, bf16[256,768]{1,0:T(8,128)(2,1)}, u32[]{:S(2)}, u32[]{:S(2)}) collective-permute-start(bf16[256,768]{1,0:T(8,128)(2,1)} %add_convert_fusion.2), channel_id=1, source_target_pairs={{8,0},{12,4},{16,8},{20,12},{24,16},{28,20},{9,1},{13,5},{17,9},{2... | collective-permute-start | bytes 1179656 | tf_op jit(solution)/shard_map/ppermute | solution.py:59
  510.8 29.0 %collective-permute-start.77 = (bf16[8,96,768]{2,1,0:T(8,128)(2,1)S(1)}, bf16[8,96,768]{2,1,0:T(8,128)(2,1)S(1)}, u32[]{:S(2)}, u32[]{:S(2)}) collective-permute-start(bf16[8,96,768]{2,1,0:T(8,128)(2,1)S(1)} %select_bitcast_fusion), channel_id=1, source_target_pairs={{0,2},{1,3},{2,0},{3,1},{4,6},{5,7},{6,4},{7,5},{8,10},{9,11},{10,... | collective-permute-start | bytes 3538952 | tf_op jit(solution)/shard_map/ppermute | solution.py:50
  514.8 45.3 %collective-permute-start.67 = (bf16[8,48,1536]{2,1,0:T(8,128)(2,1)S(1)}, bf16[8,48,1536]{2,1,0:T(8,128)(2,1)S(1)}, u32[]{:S(2)}, u32[]{:S(2)}) collective-permute-start(bf16[8,48,1536]{2,1,0:T(8,128)(2,1)S(1)} %fusion.35), channel_id=1, source_target_pairs={{0,2},{1,3},{2,0},{3,1},{4,6},{5,7},{6,4},{7,5},{8,10},{9,11},{10,... | collective-permute-start | bytes 3538952 | tf_op jit(solution)/shard_map/ppermute | solution.py:50
  515.5 48.4 %collective-permute-start.46 = (bf16[8,2,56,1152]{3,2,1,0:T(8,128)(2,1)S(1)}, bf16[8,2,56,1152]{3,2,1,0:T(8,128)(2,1)S(1)}, u32[]{:S(2)}, u32[]{:S(2)}) collective-permute-start(bf16[8,2,56,1152]{3,2,1,0:T(8,128)(2,1)S(1)} %pad_maximum_fusion.6), channel_id=1, source_target_pairs={{0,1},{1,0},{2,3},{3,2},{4,5},{5,4},{6,7},{7,6},{8,9},{9,8},{10,11... | collective-permute-start | bytes 6193160 | tf_op jit(solution)/shard_map/ppermute | solution.py:47
  540.3 24.8 %collective-permute-start.78 = (bf16[4,96,768]{2,1,0:T(8,128)(2,1)S(1)}, bf16[4,96,768]{2,1,0:T(8,128)(2,1)S(1)}, u32[]{:S(2)}, u32[]{:S(2)}) collective-permute-start(bf16[4,96,768]{2,1,0:T(8,128)(2,1)S(1)} %fusion.51), channel_id=1, source_target_pairs={{0,4},{4,0},{8,12},{12,8},{16,20},{20,16},{24,28},{28,24},{1,5},{5... | collective-permute-start | bytes 1769480 | tf_op jit(solution)/shard_map/ppermute | solution.py:53
  560.7 13.0 %collective-permute-start.68 = (bf16[4,48,1536]{2,1,0:T(8,128)(2,1)S(1)}, bf16[4,48,1536]{2,1,0:T(8,128)(2,1)S(1)}, u32[]{:S(2)}, u32[]{:S(2)}) collective-permute-start(bf16[4,48,1536]{2,1,0:T(8,128)(2,1)S(1)} %fusion.50), channel_id=1, source_target_pairs={{0,4},{4,0},{8,12},{12,8},{16,20},{20,16},{24,28},{28,24},{1,5},{5... | collective-permute-start | bytes 1769480 | tf_op jit(solution)/shard_map/ppermute | solution.py:53
  564.5 29.5 %collective-permute-start.47 = (bf16[8,56,1152]{2,1,0:T(8,128)(2,1)S(1)}, bf16[8,56,1152]{2,1,0:T(8,128)(2,1)S(1)}, u32[]{:S(2)}, u32[]{:S(2)}) collective-permute-start(bf16[8,56,1152]{2,1,0:T(8,128)(2,1)S(1)} %select_bitcast_fusion.1), channel_id=1, source_target_pairs={{0,2},{1,3},{2,0},{3,1},{4,6},{5,7},{6,4},{7,5},{8,10},{9,11},{10,... | collective-permute-start | bytes 3096584 | tf_op jit(solution)/shard_map/ppermute | solution.py:50
  565.3 13.2 %collective-permute-start.79 = (bf16[96,768]{1,0:T(8,128)(2,1)S(1)}, bf16[96,768]{1,0:T(8,128)(2,1)S(1)}, u32[]{:S(2)}, u32[]{:S(2)}) collective-permute-start(bf16[96,768]{1,0:T(8,128)(2,1)S(1)} %get-tuple-element.188), channel_id=1, source_target_pairs={{0,8},{4,12},{1,9},{5,13},{2,10},{6,14},{3,11},{7,15}} | collective-permute-start | bytes 442376 | tf_op jit(solution)/shard_map/ppermute | solution.py:56
  569.3 15.7 %collective-permute-start.82 = (bf16[96,768]{1,0:T(8,128)(2,1)S(1)}, bf16[96,768]{1,0:T(8,128)(2,1)S(1)}, u32[]{:S(2)}, u32[]{:S(2)}) collective-permute-start(bf16[96,768]{1,0:T(8,128)(2,1)S(1)} %get-tuple-element.189), channel_id=1, source_target_pairs={{24,16},{28,20},{25,17},{29,21},{26,18},{30,22},{27,19},{31,23}} | collective-permute-start | bytes 442376 | tf_op jit(solution)/shard_map/ppermute | solution.py:59
  577.9 11.4 %collective-permute-start.72 = (bf16[48,1536]{1,0:T(8,128)(2,1)S(1)}, bf16[48,1536]{1,0:T(8,128)(2,1)S(1)}, u32[]{:S(2)}, u32[]{:S(2)}) collective-permute-start(bf16[48,1536]{1,0:T(8,128)(2,1)S(1)} %get-tuple-element.193), channel_id=1, source_target_pairs={{24,16},{28,20},{25,17},{29,21},{26,18},{30,22},{27,19},{31,23}} | collective-permute-start | bytes 442376 | tf_op jit(solution)/shard_map/ppermute | solution.py:59
  580.6 8.7 %collective-permute-start.70 = (bf16[48,1536]{1,0:T(8,128)(2,1)S(1)}, bf16[48,1536]{1,0:T(8,128)(2,1)S(1)}, u32[]{:S(2)}, u32[]{:S(2)}) collective-permute-start(bf16[48,1536]{1,0:T(8,128)(2,1)S(1)} %fusion.76), channel_id=1, source_target_pairs={{0,8},{4,12},{8,16},{12,20},{1,9},{5,13},{9,17},{13,21},{2,10},{6,... | collective-permute-start | bytes 442376 | tf_op jit(solution)/shard_map/ppermute | solution.py:56
  585.1 34.1 %collective-permute-start.81 = (bf16[96,768]{1,0:T(8,128)(2,1)S(1)}, bf16[96,768]{1,0:T(8,128)(2,1)S(1)}, u32[]{:S(2)}, u32[]{:S(2)}) collective-permute-start(bf16[96,768]{1,0:T(8,128)(2,1)S(1)} %get-tuple-element.186), channel_id=1, source_target_pairs={{0,8},{4,12},{8,16},{12,20},{16,24},{20,28},{1,9},{5,13},{9,17},{1... | collective-permute-start | bytes 442376 | tf_op jit(solution)/shard_map/ppermute | solution.py:56
  589.4 19.6 %collective-permute-start.71 = (bf16[48,1536]{1,0:T(8,128)(2,1)S(1)}, bf16[48,1536]{1,0:T(8,128)(2,1)S(1)}, u32[]{:S(2)}, u32[]{:S(2)}) collective-permute-start(bf16[48,1536]{1,0:T(8,128)(2,1)S(1)} %get-tuple-element.190), channel_id=1, source_target_pairs={{0,8},{4,12},{8,16},{12,20},{16,24},{20,28},{1,9},{5,13},{9,17},{1... | collective-permute-start | bytes 442376 | tf_op jit(solution)/shard_map/ppermute | solution.py:56
  594.4 9.2 %collective-permute-start.48 = (bf16[4,56,1152]{2,1,0:T(8,128)(2,1)S(1)}, bf16[4,56,1152]{2,1,0:T(8,128)(2,1)S(1)}, u32[]{:S(2)}, u32[]{:S(2)}) collective-permute-start(bf16[4,56,1152]{2,1,0:T(8,128)(2,1)S(1)} %fusion.58), channel_id=1, source_target_pairs={{0,4},{4,0},{8,12},{12,8},{16,20},{20,16},{24,28},{28,24},{1,5},{5... | collective-permute-start | bytes 1548296 | tf_op jit(solution)/shard_map/ppermute | solution.py:53
  596.5 22.6 %collective-permute-start.84 = (bf16[96,768]{1,0:T(8,128)(2,1)S(1)}, bf16[96,768]{1,0:T(8,128)(2,1)S(1)}, u32[]{:S(2)}, u32[]{:S(2)}) collective-permute-start(bf16[96,768]{1,0:T(8,128)(2,1)S(1)} %fusion.70), channel_id=1, source_target_pairs={{8,0},{12,4},{16,8},{20,12},{24,16},{28,20},{9,1},{13,5},{17,9},{2... | collective-permute-start | bytes 442376 | tf_op jit(solution)/shard_map/ppermute | solution.py:59
  597.9 11.2 %collective-permute-start.74 = (bf16[48,1536]{1,0:T(8,128)(2,1)S(1)}, bf16[48,1536]{1,0:T(8,128)(2,1)S(1)}, u32[]{:S(2)}, u32[]{:S(2)}) collective-permute-start(bf16[48,1536]{1,0:T(8,128)(2,1)S(1)} %fusion.75), channel_id=1, source_target_pairs={{8,0},{12,4},{16,8},{20,12},{24,16},{28,20},{9,1},{13,5},{17,9},{2... | collective-permute-start | bytes 442376 | tf_op jit(solution)/shard_map/ppermute | solution.py:59
  615.9 10.3 %collective-permute-start.75 = (f32[24,1536]{1,0:T(8,128)S(1)}, f32[24,1536]{1,0:T(8,128)S(1)}, u32[]{:S(2)}, u32[]{:S(2)}) collective-permute-start(f32[24,1536]{1,0:T(8,128)S(1)} %slice_select_fusion), channel_id=1, source_target_pairs={{0,1},{1,0},{2,3},{3,2},{4,5},{5,4},{6,7},{7,6},{8,9},{9,8},{10,11... | collective-permute-start | bytes 442376 | tf_op jit(solution)/shard_map/ppermute | solution.py:47
  619.9 9.0 %collective-permute-start.51 = (bf16[56,1152]{1,0:T(8,128)(2,1)S(1)}, bf16[56,1152]{1,0:T(8,128)(2,1)S(1)}, u32[]{:S(2)}, u32[]{:S(2)}) collective-permute-start(bf16[56,1152]{1,0:T(8,128)(2,1)S(1)} %get-tuple-element.200), channel_id=1, source_target_pairs={{0,8},{4,12},{8,16},{12,20},{16,24},{20,28},{1,9},{5,13},{9,17},{1... | collective-permute-start | bytes 387080 | tf_op jit(solution)/shard_map/ppermute | solution.py:56
  (92 other events, 729.0 us)

commit v2 on v1

--- a/solution.py
+++ b/solution.py
@@ -52,6 +52,9 @@
     def swap_y(self, v, pairs=None):
         return lax.ppermute(v, "leaf", pairs or [(i, i ^ 1) for i in range(8)])
 
+    def swap_z(self, v, n):
+        return lax.ppermute(v, "leaf", [(i, i ^ (2 * n)) for i in range(8)])
+
     def up(self, v, first, last):
         return lax.ppermute(v, "leaf", [(i, i + 2) for i in range(2 * first, 2 * last + 2)])
 
@@ -65,27 +68,13 @@
     )
 
 
-def gather_rows(at, block):
-    ups, downs = [], []
-    cur = block
-    for s in (1, 2, 3):
-        cur = at.up(cur, s - 1, 2)
-        ups.append(cur)
-    cur = block
-    for s in (1, 2, 3):
-        cur = at.down(cur, 1, 4 - s)
-        downs.append(cur)
-    places = []
-    for p in range(4):
-        value = block
-        for z in range(4):
-            if z != p:
-                value = jnp.where(at.z == z, ups[z - p - 1] if z > p else downs[p - z - 1], value)
-        places.append(value)
-    line = jnp.stack(places)
-    plane = both(at.y, line, at.swap_y(line), 1)
-    plane = plane.reshape((8,) + block.shape)
-    return both(at.x, plane, at.swap_x(plane), 1)
+def after(values, done):
+    values, done = list(values), list(done)
+    return lax.optimization_barrier(tuple(values + done))[: len(values)]
+
+
+def z_gather(at, block):
+    return jnp.concatenate([block] + [at.swap_z(block, n) for n in (1, 2, 3)], axis=0)
 
 
 def pick(v, index, axis):
@@ -101,24 +90,27 @@
     return a.astype(F32) + b.astype(F32)
 
 
-def reduce_rows(at, own, other):
+def z_reduce(at, g):
+    got = [at.swap_z(pick(g, at.z ^ n, 0), n) for n in (1, 2, 3)]
+    return plus(pick(g, at.z, 0), got[0]) + plus(got[1], got[2])
+
+
+def reduce_x_first(at, own, other):
     g = plus(own, at.swap_core(other)).astype(BF)
     keep, send = choose(at.x, g, 1)
     g = plus(keep, at.swap_x(send)).astype(BF)
     g = g.reshape((4, 2) + g.shape[1:])
     keep, send = choose(at.y, g, 1)
-    g = plus(keep, at.swap_y(send)).astype(BF)
-    high = None
-    for s in (1, 2, 3):
-        part = pick(g, jnp.minimum(at.z + 4 - s, 3), 0)
-        part = part if high is None else plus(part, high).astype(BF)
-        high = at.up(part, 0, s - 1)
-    low = None
-    for s in (1, 2, 3):
-        part = pick(g, jnp.maximum(at.z - 4 + s, 0), 0)
-        part = part if low is None else plus(part, low).astype(BF)
-        low = at.down(part, 4 - s, 3)
-    return plus(pick(g, at.z, 0), high) + low.astype(F32)
+    return z_reduce(at, plus(keep, at.swap_y(send)).astype(BF))
+
+
+def reduce_y_first(at, own, other):
+    g = plus(own, at.swap_core(other)).astype(BF)
+    g = g.reshape((4, 2) + g.shape[1:])
+    keep, send = choose(at.y, g, 1)
+    g = z_reduce(at, plus(keep, at.swap_y(send)).astype(BF)).astype(BF)
+    keep, send = choose(at.x, g, 0)
+    return plus(keep, at.swap_x(send))
 
 
 def to_column_half(at, half_a, half_b):
@@ -150,9 +142,35 @@
     return groups
 
 
-def project_kernel(x_ref, gain_ref, own_ref, other_ref, cos_ref, sin_ref, a_ref, q_ref, k_ref, v_ref):
+def fetch(pieces, sems):
+    copies = [pltpu.make_async_copy(src, dst, sems.at[n]) for n, (src, dst) in enumerate(pieces)]
+    for copy in copies:
+        copy.start()
+    return copies
+
+
+def placed(ref, count, size, table, row):
+    return [
+        ref.at[pl.ds(pl.multiple_of(table[row, n] * size, size), size), :] for n in range(count)
+    ]
+
+
+def project_kernel(
+    count, size, first_rows, table_ref, x_ref, mask_ref, embed_ref, gain_ref, own_hbm, other_hbm, cos_ref, sin_ref,
+    a_ref, q_ref, k_ref, v_ref, own_ref, other_ref, sems,
+):
     tile = pl.program_id(0)
-    x = x_ref[...].astype(F32)
+
+    @pl.when(tile == 0)
+    def _():
+        pieces = []
+        for hbm, ref in ((own_hbm, own_ref), (other_hbm, other_ref)):
+            spots = placed(ref, count, size, table_ref, 0)
+            pieces += [(hbm.at[n, pl.ds(0, size), :], spots[n]) for n in range(count)]
+        for copy in fetch(pieces, sems):
+            copy.wait()
+
+    x = jnp.where(mask_ref[...] > 0, embed_ref[...], x_ref[...].astype(F32))
     centred = x - jnp.mean(x, axis=-1, keepdims=True)
     spread = jnp.mean(centred * centred, axis=-1, keepdims=True)
     a = (centred * lax.rsqrt(spread + EPSILON) * gain_ref[...]).astype(BF)
@@ -161,48 +179,157 @@
     half = own_ref.shape[1] // 3
     for n, w_ref in enumerate((own_ref, other_ref)):
         base = n * half
-        kv = jnp.dot(a, w_ref[:, half:], preferred_element_type=F32)
-        for g, part in enumerate(turn(kv[:, :half], cosine, sine)):
+        keys = jnp.dot(a, w_ref[:, half : 2 * half], preferred_element_type=F32)
+        for g, part in enumerate(turn(keys, cosine, sine)):
             k_ref[:, base + g * 128 : base + (g + 1) * 128] = part.astype(BF)
-        v_ref[:, base : base + half] = kv[:, half:].astype(BF)
-
-        @pl.when(tile < 2)
-        def _():
-            q = jnp.dot(a, w_ref[:, :half], preferred_element_type=F32)
-            for g, part in enumerate(turn(q, cosine, sine)):
+        values = jnp.dot(a, w_ref[:, 2 * half :], preferred_element_type=F32)
+        v_ref[:, base : base + half] = values.astype(BF)
+
+    @pl.when(tile * x_ref.shape[0] < first_rows)
+    def _():
+        rows = q_ref.shape[0]
+        for n, w_ref in enumerate((own_ref, other_ref)):
+            base = n * half
+            q = jnp.dot(a[:rows], w_ref[:, :half], preferred_element_type=F32)
+            for g, part in enumerate(turn(q, cosine[:rows], sine[:rows])):
                 q_ref[:, base + g * 128 : base + (g + 1) * 128] = part.astype(BF)
 
 
-def project(x_all, gain, own, other, cosine, sine, rows):
+def project(table, x_all, mask, embed, gain, own, other, cosine, sine, rows):
     total, width = x_all.shape
-    tiles = total // rows
-    whole = lambda shape: spec(shape, lambda t: (0, 0))
+    step = next(n for n in (3 * rows, 2 * rows, rows) if total % n == 0)
+    q_step = min(step, 2 * rows)
+    last_q = 2 * rows // q_step - 1
+    count = own.shape[0]
+    size = width // count
+    columns = own.shape[2]
+    whole = lambda shape: spec(shape, lambda t, i: (0, 0))
+    moved = lambda n: spec((step, n), lambda t, i: (t, 0))
     out = lambda n: jax.ShapeDtypeStruct((n, width), BF)
+    anywhere = pl.BlockSpec(memory_space=pl.ANY)
     return pl.pallas_call(
-        project_kernel,
-        grid=(tiles,),
-        in_specs=[
-            spec((rows, width), lambda t: (t, 0)),
-            whole((1, width)),
-            whole(own.shape),
-            whole(other.shape),
-            spec((rows, 128), lambda t: (t, 0)),
-            spec((rows, 128), lambda t: (t, 0)),
-        ],
-        out_specs=[
-            spec((rows, width), lambda t: (t, 0)),
-            spec((rows, width), lambda t: (jnp.minimum(t, 1), 0)),
-            spec((rows, width), lambda t: (t, 0)),
-            spec((rows, width), lambda t: (t, 0)),
-        ],
+        functools.partial(project_kernel, count, size, 2 * rows),
+        grid_spec=pltpu.PrefetchScalarGridSpec(
+            num_scalar_prefetch=1,
+            grid=(total // step,),
+            in_specs=[
+                moved(width), moved(1), whole((1, width)), whole((1, width)), anywhere, anywhere, moved(128), moved(128),
+            ],
+            out_specs=[
+                moved(width),
+                spec((q_step, width), lambda t, i: (jnp.minimum(t, last_q), 0)),
+                moved(width),
+                moved(width),
+            ],
+            scratch_shapes=[
+                pltpu.VMEM((width, columns), BF),
+                pltpu.VMEM((width, columns), BF),
+                pltpu.SemaphoreType.DMA((2 * count,)),
+            ],
+        ),
         out_shape=[out(total), out(2 * rows), out(total), out(total)],
         compiler_params=pltpu.CompilerParams(vmem_limit_bytes=VMEM_LIMIT),
         cost_estimate=pl.CostEstimate(
-            flops=2 * total * width * 2 * width,
+            flops=2 * total * width * 2 * width + 4 * rows * width * width,
             bytes_accessed=2 * (4 * total * width + 3 * width * width),
             transcendentals=0,
         ),
-    )(x_all, gain, own, other, cosine, sine)
+    )(table, x_all, mask, embed, gain, own, other, cosine, sine)
+
+
+def middle_kernel(
+    count, size, chunk, table_ref, o_ref, x_ref, dy_ref, gain_ref, up_b_ref, down_b_ref,
+    one_own, one_other, two_own, two_other,
+    y_ref, b_ref, g_ref, du_ref, dh_low_ref, do_ref, dh_ref, dgain_ref, dup_b_ref, ddown_b_ref,
+    out_ref, up_ref, down_ref, sems,
+):
+    cut = out_ref.shape[1] // 2
+    units = up_ref.shape[2]
+    pieces_out, pieces_up, pieces_down = [], [], []
+    for n, (one, two) in enumerate(((one_own, two_own), (one_other, two_other))):
+        column = pl.multiple_of(table_ref[3, n] * cut, cut)
+        for j in range(count):
+            spot = pl.multiple_of(table_ref[1, j] * size, size)
+            pieces_out.append(
+                (one.at[j, :, pl.ds(0, cut)], out_ref.at[pl.ds(spot, size), pl.ds(column, cut)])
+            )
+            spot = pl.multiple_of(table_ref[0, j] * size, size)
+            pieces_up.append((one.at[j, :, pl.ds(cut, units)], up_ref.at[n, pl.ds(spot, size), :]))
+            spot = pl.multiple_of(table_ref[2, j] * chunk, chunk)
+            pieces_down.append((two.at[j], down_ref.at[n, pl.ds(spot, chunk), :]))
+    copies = fetch(pieces_out + pieces_up + pieces_down, sems)
+    for copy in copies[: 2 * count]:
+        copy.wait()
+    h = x_ref[...].astype(F32) + jnp.dot(o_ref[...], out_ref[...], preferred_element_type=F32)
+    centred = h - jnp.mean(h, axis=-1, keepdims=True)
+    spread = jnp.mean(centred * centred, axis=-1, keepdims=True)
+    scale = lax.rsqrt(spread + EPSILON)
+    hat = centred * scale
+    b = (hat * gain_ref[...]).astype(BF)
+    b_ref[...] = b
+    dy = dy_ref[...]
+    ddown_b_ref[...] = jnp.sum(dy.astype(F32), axis=0, keepdims=True)
+    for copy in copies[2 * count :]:
+        copy.wait()
+    y = h + down_b_ref[...]
+    db = None
+    wide = next(n for n in (768, 512, 384, 256, 128) if units % n == 0)
+    for n in range(2):
+        for c in range(0, units, wide):
+            at = slice(c, c + wide)
+            to = slice(n * units + c, n * units + c + wide)
+            u = jnp.dot(b, up_ref[n, :, at], preferred_element_type=F32) + up_b_ref[n : n + 1, at]
+            g, slope = gelu_parts(u)
+            g = g.astype(BF)
+            g_ref[:, to] = g
+            y = y + jnp.dot(g, down_ref[n, at, :], preferred_element_type=F32)
+            du = (matmul_t(dy, down_ref[n, at, :]) * slope).astype(BF)
+            du_ref[:, to] = du
+            dup_b_ref[n : n + 1, at] = jnp.sum(du.astype(F32), axis=0, keepdims=True)
+            part = matmul_t(du, up_ref[n, :, at])
+            db = part if db is None else db + part
+    y_ref[...] = y.astype(BF)
+    dgain_ref[...] = jnp.sum(db * hat, axis=0, keepdims=True)
+    dh = dy.astype(F32) + norm_back(hat, scale, gain_ref[...], db)
+    dh_ref[...] = dh
+    low = dh.astype(BF)
+    dh_low_ref[...] = low
+    do_ref[...] = matmul_t(low, out_ref[...]).astype(BF)
+
+
+def middle(table, o, x, dy, gain, up_b, down_b, one, two):
+    rows, width = o.shape
+    count, size, columns = one[0].shape
+    chunk = two[0].shape[1]
+    units = columns - width // 2
+    anywhere = pl.BlockSpec(memory_space=pl.ANY)
+    full = lambda shape: spec(shape, lambda t, i: (0, 0))
+    shapes = [
+        ((rows, width), BF), ((rows, width), BF), ((rows, 2 * units), BF), ((rows, 2 * units), BF), ((rows, width), BF),
+        ((rows, width), BF), ((rows, width), F32), ((1, width), F32), ((2, units), F32), ((1, width), F32),
+    ]
+    return pl.pallas_call(
+        functools.partial(middle_kernel, count, size, chunk),
+        grid_spec=pltpu.PrefetchScalarGridSpec(
+            num_scalar_prefetch=1,
+            grid=(1,),
+            in_specs=[full(v.shape) for v in (o, x, dy, gain, up_b, down_b)] + [anywhere] * 4,
+            out_specs=[full(shape) for shape, _ in shapes],
+            scratch_shapes=[
+                pltpu.VMEM((width, width), BF),
+                pltpu.VMEM((2, width, units), BF),
+                pltpu.VMEM((2, units, width), BF),
+                pltpu.SemaphoreType.DMA((6 * count,)),
+            ],
+        ),
+        out_shape=[jax.ShapeDtypeStruct(shape, kind) for shape, kind in shapes],
+        compiler_params=pltpu.CompilerParams(vmem_limit_bytes=VMEM_LIMIT),
+        cost_estimate=pl.CostEstimate(
+            flops=2 * rows * width * (2 * width + 8 * units),
+            bytes_accessed=4 * (width * width + 4 * units * width),
+            transcendentals=2 * rows * units,
+        ),
+    )(table, o, x, dy, gain, up_b, down_b, one[0], one[1], two[0], two[1])
 
 
 def matmul_t(a, b):
@@ -241,43 +368,46 @@
                 bias_ref[:, span(t)] = jnp.where(ok, 0.0, NEG_FILL)
 
     lane = lax.broadcasted_iota(jnp.int32, (both_rows, 128), 1)
-    result = None
-    for h in range(2):
-        mine = (lane // HEAD_DIM) == h
-        q = jnp.where(mine, q_ref[...] * 0.125, 0).astype(BF)
-        top_ref[...] = jnp.full_like(top_ref, -3.0e38)
-        for t in range(tiles):
-
-            @pl.when(flag_ref[t] > 0)
-            def _():
-                at = lines(t)
-                s = matmul_t(q[at], k_ref[span(t), :]) + bias_ref[at, span(t)]
-                s_ref[at, span(t)] = s
-                best = top_ref[at, :]
+    queries = [jnp.where((lane // HEAD_DIM) == h, q_ref[...] * 0.125, 0).astype(BF) for h in range(2)]
+    top_ref[...] = jnp.full_like(top_ref, -3.0e38)
+    for t in range(tiles):
+
+        @pl.when(flag_ref[t] > 0)
+        def _():
+            at = lines(t)
+            keys, bias = k_ref[span(t), :], bias_ref[at, span(t)]
+            for h in range(2):
+                s = matmul_t(queries[h][at], keys) + bias
+                s_ref[h, at, span(t)] = s
+                best = top_ref[h, at, :]
                 for c in range(rows // 128):
                     best = jnp.maximum(best, s[:, c * 128 : (c + 1) * 128])
-                top_ref[at, :] = best
-
-        top = jnp.max(top_ref[...], axis=-1, keepdims=True)
-        sum_ref[...] = jnp.zeros_like(sum_ref)
-        acc_ref[...] = jnp.zeros_like(acc_ref)
-        for t in range(tiles):
-
-            @pl.when(flag_ref[t] > 0)
-            def _():
-                at = lines(t)
-                p = jnp.exp(s_ref[at, span(t)] - top[at])
-                part = sum_ref[at, :]
+                top_ref[h, at, :] = best
+
+    tops = [jnp.max(top_ref[h], axis=-1, keepdims=True) for h in range(2)]
+    sum_ref[...] = jnp.zeros_like(sum_ref)
+    acc_ref[...] = jnp.zeros_like(acc_ref)
+    for t in range(tiles):
+
+        @pl.when(flag_ref[t] > 0)
+        def _():
+            at = lines(t)
+            values = v_ref[span(t), :]
+            for h in range(2):
+                p = jnp.exp(s_ref[h, at, span(t)] - tops[h][at])
+                part = sum_ref[h, at, :]
                 for c in range(rows // 128):
                     part = part + p[:, c * 128 : (c + 1) * 128]
-                sum_ref[at, :] = part
-                acc_ref[at, :] += jnp.dot(p.astype(BF), v_ref[span(t), :], preferred_element_type=F32)
-
-        total = jnp.sum(sum_ref[...], axis=-1, keepdims=True)
-        o = acc_ref[...] / total
-        lse_ref[...] = jnp.where(lane == 2 * pair + h, top + jnp.log(total), lse_ref[...])
-        result = o if result is None else jnp.where(mine, o, result)
-    o_ref[...] = result.astype(BF)
+                sum_ref[h, at, :] = part
+                acc_ref[h, at, :] += jnp.dot(p.astype(BF), values, preferred_element_type=F32)
+
+    outs, norms = [], lse_ref[...]
+    for h in range(2):
+        total = jnp.sum(sum_ref[h], axis=-1, keepdims=True)
+        outs.append(acc_ref[h] / total)
+        norms = jnp.where(lane == 2 * pair + h, tops[h] + jnp.log(total), norms)
+    lse_ref[...] = norms
+    o_ref[...] = jnp.where(lane < HEAD_DIM, outs[0], outs[1]).astype(BF)
 
 
 def attend(flags, qcol, krow, q, k, v, rows):
@@ -295,10 +425,10 @@
             out_specs=[pair(2 * rows), fixed((2 * rows, 128))],
             scratch_shapes=[
                 pltpu.VMEM((2 * rows, total), F32),
-                pltpu.VMEM((2 * rows, total), F32),
-                pltpu.VMEM((2 * rows, 128), F32),
-                pltpu.VMEM((2 * rows, 128), F32),
-                pltpu.VMEM((2 * rows, 128), F32),
+                pltpu.VMEM((2, 2 * rows, total), F32),
+                pltpu.VMEM((2, 2 * rows, 128), F32),
+                pltpu.VMEM((2, 2 * rows, 128), F32),
+                pltpu.VMEM((2, 2 * rows, 128), F32),
             ],
         ),
         out_shape=[
@@ -483,16 +613,64 @@
         self.rows = rows
         self.core = self.at.core
 
-    def tree(self, hid):
+    def places(self):
         at = self.at
-        chain = []
-        cur = hid
-        for s in (1, 2, 3):
-            cur = at.up(cur, s - 1, 2)
-            pairs = [(i, i ^ 1) for i in range(2 * s, 8)]
-            chain += [cur, at.swap_y(cur, pairs)]
-        chain.append(at.swap_y(hid, [(i, i + 1) for i in range(0, 8, 2)]))
-        return chain
+        n = jnp.arange(4)
+        zyx = ((at.z ^ n)[None, None, :] * 2 + (at.y ^ n[:2])[None, :, None]) * 2 + (at.x ^ n[:2])[:, None, None]
+        yzx = ((at.z ^ n)[None, :, None] * 2 + (at.y ^ n[:2])[:, None, None]) * 2 + (at.x ^ n[:2])[None, None, :]
+        first = zyx.reshape(16)
+        columns = jnp.where(jnp.arange(16) % 2 == 0, at.core, 1 - at.core)
+        return jnp.stack([first, first ^ (8 * at.core), yzx.reshape(16), columns]).astype(jnp.int32)
+
+    def gather(self, hid, w_qkv, w_out, w_up, w_down, vectors):
+        at = self.at
+        chunk, cut = w_down.shape[0], w_out.shape[1] // 2
+        up_a, up_b = halves_of_units(w_up, chunk)
+        one_a = jnp.concatenate([w_out[:, :cut], up_a], axis=1)
+        one_b = jnp.concatenate([w_out[:, cut:], up_b], axis=1)
+        qkv_a, qkv_b = halves_of_heads(w_qkv)
+        row = jnp.pad(vectors[None], ((0, 7), (0, qkv_a.shape[1] - vectors.shape[0])))
+        qkv_a, qkv_b = (jnp.concatenate([v, row], axis=0) for v in (qkv_a, qkv_b))
+        block = to_column_half(at, qkv_a, qkv_b)
+        few = w_qkv.shape[0]
+        block = jnp.concatenate(
+            [block[:few], block[few + 8 : 2 * few + 8], block[few : few + 8], block[2 * few + 8 :]], axis=0
+        )[None]
+        beside = at.swap_y(hid, [(i, i + 1) for i in range(0, 8, 2)])
+        down_two = jnp.stack([w_down, at.swap_x(w_down)])[None]
+        one = to_column_half(at, one_a, one_b)[None]
+        line = z_gather(at, block)
+        [cur] = after([hid], [line])
+        hops = [at.up(cur, 0, 2)]
+        plane = jnp.concatenate([line, at.swap_y(line)], axis=0)
+        [cur, plane] = after([hops[0], plane], [beside])
+        hops.append(at.up(cur, 1, 2))
+        across = [at.swap_y(cur, [(i, i ^ 1) for i in range(2, 8)])]
+        qkv = jnp.concatenate([plane, at.swap_x(plane)], axis=0)
+        [cur] = after([hops[1]], [across[0]])
+        hops.append(at.up(cur, 2, 2))
+        across.append(at.swap_y(cur, [(i, i ^ 1) for i in range(4, 8)]))
+        [last, one, qkv] = after([hops[2], one, qkv], [across[1]])
+        across.append(at.swap_y(last, [(i, i ^ 1) for i in range(6, 8)]))
+        qkv_both = (qkv, at.swap_core(qkv))
+        line = z_gather(at, one)
+        [line, down_two] = after([line, down_two], [across[2], qkv_both[1]])
+        plane = jnp.concatenate([line, at.swap_y(line)], axis=0)
+        down_line = z_gather(at, down_two)
+        [plane, down_line] = after([plane, down_line], [plane, down_line])
+        one = jnp.concatenate([plane, at.swap_x(plane)], axis=0)
+        down = jnp.concatenate([down_line, at.swap_y(down_line)], axis=0)
+        down = down.reshape((16,) + w_down.shape)
+        one_both = (one, at.swap_core(one))
+        down_both = (down, at.swap_core(down))
+        m = 2 * few
+        vec = jnp.concatenate([qkv[:, m, : vectors.shape[0]], qkv[:, m + 8, : vectors.shape[0]]], axis=1)
+        order = (self.places()[0][None, :] == jnp.arange(16)[:, None]).astype(BF)
+        vec = mm(order, vec).reshape(32, -1)
+        lower = []
+        for n in range(3):
+            lower += [hops[n], across[n]]
+        return lower + [beside], qkv_both, one_both, down_both, vec
 
     def tile_leaves(self):
         z, y = self.at.z, self.at.y
@@ -513,36 +691,6 @@
             cur = at.down(cur.astype(BF), s + 1, 3).astype(F32) + plus(parts[2 * s - 2], low[s])
         return own + at.down(cur.astype(BF), 1, 3).astype(F32) + low[0].astype(F32)
 
-    def weights(self, w_qkv, w_out, w_up, w_down, vectors):
-        at = self.at
-        block = to_column_half(at, *halves_of_heads(w_qkv))
-        mine = at.swap_core(vectors)
-        row = both(at.core, vectors, mine, 0).reshape(1, -1)
-        row = jnp.pad(row, ((0, 7), (0, block.shape[1] - row.shape[1])))
-        first = gather_rows(at, jnp.concatenate([block, row], axis=0))
-        m = block.shape[0]
-        qkv = first[:, :, :m].reshape(16 * m, -1)
-        vec = first[:, :, m, : 2 * vectors.shape[0]].reshape(32, -1)
-        out_up = jnp.concatenate(
-            [
-                to_column_half(at, w_out[:, : w_out.shape[1] // 2], w_out[:, w_out.shape[1] // 2 :]),
-                to_column_half(at, *halves_of_units(w_up, w_down.shape[0])),
-            ],
-            axis=1,
-        )
-        second = gather_rows(at, out_up).reshape(16 * m, -1)
-        down = gather_rows(at, w_down).reshape(16 * w_down.shape[0], -1)
-        cut = w_out.shape[1] // 2
-        out_own = second[:, :cut]
-        up_own = second[:, cut:]
-        qkv_both = (qkv, at.swap_core(qkv))
-        up_both = (up_own, at.swap_core(up_own))
-        down_both = (down, at.swap_core(down))
-        out = both(at.core, out_own, at.swap_core(out_own), 1).reshape(16 * m, -1)
-        half = out.shape[0] // 2
-        out = jnp.where(at.core == 0, out, jnp.concatenate([out[half:], out[:half]], axis=0))
-        return qkv_both, out, up_both, down_both, vec
-
     def unit_bias(self, bias, chunk):
         a, b = halves_of_units(bias[None], chunk)
         return jnp.where(self.core == 0, a, b), jnp.where(self.core == 0, b, a)
@@ -554,11 +702,11 @@
 
     def sum_down(self, own, other):
         shape = (8, 2, own.shape[0] // 16, own.shape[1])
-        return reduce_rows(self.at, own.reshape(shape), other.reshape(shape))
+        return reduce_x_first(self.at, own.reshape(shape), other.reshape(shape))
 
     def sum_up(self, own, other, chunk):
         shape = (8, 2, own.shape[0] // 16, own.shape[1])
-        g = reduce_rows(self.at, own.reshape(shape), other.reshape(shape))
+        g = reduce_y_first(self.at, own.reshape(shape), other.reshape(shape))
         return units_of_halves(*from_column_half(self.at, g), chunk)
 
     def sum_out(self, g):
@@ -567,7 +715,7 @@
         g = jnp.where(at.core == 0, g, jnp.concatenate([g[half:], g[:half]], axis=0))
         g = g.reshape(8, 2, g.shape[0] // 16, 2, g.shape[1] // 2)
         own, other = choose(at.core, g, 3)
-        a, b = from_column_half(at, reduce_rows(at, own, other))
+        a, b = from_column_half(at, reduce_x_first(at, own, other))
         return jnp.concatenate([a, b], axis=1)
 
     def sum_qkv(self, own, other, vec):
@@ -577,7 +725,7 @@
         n = vec.shape[1]
         rows = jnp.pad(vec.astype(BF).reshape(8, 2, 2, 1, n), ((0, 0),) * 3 + ((0, 7), (0, own.shape[1] - n)))
         mine, its = choose(at.core, rows, 2)
-        g = reduce_rows(
+        g = reduce_x_first(
             at,
             jnp.concatenate([own.reshape(shape), mine], axis=2),
             jnp.concatenate([other.reshape(shape), its], axis=2),
@@ -588,14 +736,24 @@
 AXES = ("leaf", "fsdp")
 
 
+def in_place(places, w, rows):
+    count = w.shape[0]
+    if count == 1:
+        return w[0]
+    size = rows // count
+    out = jnp.zeros((rows, w.shape[2]), w.dtype)
+    for n in range(count):
+        out = lax.dynamic_update_slice(out, w[n, :size], (places[n] * size, 0))
+    return out
+
+
 class Whole:
     def __init__(self, rows, leaves, devices):
         self.rows, self.leaves, self.devices = rows, leaves, devices
         self.leaf = lax.axis_index("leaf")
 
-    def tree(self, hid):
-        every = lax.all_gather(hid, "leaf", axis=0, tiled=False)
-        return [pick(every, leaf, 0) for leaf, _ in self.tile_leaves()]
+    def places(self):
+        return jnp.array([[0, 0], [0, 0], [0, 0], [0, 1]], jnp.int32)
 
     def tile_leaves(self):
         found = []
@@ -610,15 +768,20 @@
         every = jnp.concatenate(order, axis=0)
         return lax.psum_scatter(every, "leaf", scatter_dimension=0, tiled=True).astype(F32)
 
-    def weights(self, w_qkv, w_out, w_up, w_down, vectors):
+    def gather(self, hid, w_qkv, w_out, w_up, w_down, vectors):
+        tree = lax.all_gather(hid, "leaf", axis=0, tiled=False)
+        lower = [pick(tree, leaf, 0) for leaf, _ in self.tile_leaves()]
         every = lambda w: lax.all_gather(w, AXES, axis=0, tiled=True)
-        up_w, down_w = every(w_up), every(w_down)
-        half = down_w.shape[0] // 2
+        up_w, down_w, out_w = every(w_up), every(w_down), every(w_out)
+        half, cut = down_w.shape[0] // 2, out_w.shape[1] // 2
         return (
-            halves_of_heads(every(w_qkv)),
-            every(w_out),
-            (up_w[:, :half], up_w[:, half:]),
-            (down_w[:half], down_w[half:]),
+            lower,
+            tuple(v[None] for v in halves_of_heads(every(w_qkv))),
+            tuple(
+                jnp.concatenate([out_w[:, n * cut : (n + 1) * cut], up_w[:, n * half : (n + 1) * half]], axis=1)[None]
+                for n in range(2)
+            ),
+            tuple(down_w[None, n * half : (n + 1) * half] for n in range(2)),
             every(vectors[None]),
         )
 
@@ -671,9 +834,9 @@
     few = ln1_gain.shape[0]
 
     hid = hidden[0]
-    lower = net.tree(hid)
     vectors = jnp.concatenate([ln1_gain, ln2_gain, down_bias, mask_embed, up_bias])
-    qkv_w, out_w, up_w, down_w, vec = net.weights(w_qkv, w_out, w_up, w_down, vectors)
+    lower, qkv_w, one_w, down_w, vec = net.gather(hid, w_qkv, w_out, w_up, w_down, vectors)
+    places = net.places()
     gain_one, gain_two, down_b, embed = (
         vec[:, n * few : (n + 1) * few].reshape(1, width).astype(F32) for n in range(4)
     )
@@ -713,43 +876,34 @@
     sine = jnp.sin(angles) * jnp.where((lanes % HEAD_DIM) < HEAD_DIM // 2, -1.0, 1.0)
 
     masked = (noise_mask[0] == 1)[:, None]
+    x_all = jnp.concatenate([hid, hid] + lower, axis=0)
+    swapped = jnp.pad(noise_mask[0][:, None], ((rows, x_all.shape[0] - 2 * rows), (0, 0)))
+    a_all, query, key, value = project(
+        places, x_all, swapped, embed, gain_one, qkv_w[0], qkv_w[1], cosine, sine, rows
+    )
+    mixed, log_norm = attend(flags, query_cols, key_rows, query, key, value, rows)
     noisy = jnp.where(masked, embed.astype(BF), hid)
-    x_all = jnp.concatenate([hid, noisy] + lower, axis=0)
-    stream = jnp.concatenate([hid, noisy], axis=0).astype(F32)
-    a_all, query, key, value = project(x_all, gain_one, qkv_w[0], qkv_w[1], cosine, sine, rows)
-    mixed, log_norm = attend(flags, query_cols, key_rows, query, key, value, rows)
-    after = stream + mm(mixed, out_w)
-    hat_two, scale_two = normalise(after)
-    normed_two = (hat_two * gain_two).astype(BF)
-    act, slope = [], []
-    for n in range(2):
-        g, s = gelu_parts(mm(normed_two, up_w[n]) + up_b[n])
-        act.append(g.astype(BF))
-        slope.append(s)
-    result = after + (mm(act[0], down_w[0]) + mm(act[1], down_w[1])) + down_b
-    output = result.astype(BF).reshape(1, 2, rows, width)
-
+    stream_low = jnp.concatenate([hid, noisy], axis=0)
+    stream = stream_low.astype(F32)
     grad_two = cotangent[0].reshape(2 * rows, width)
-    grad_out = grad_two.astype(F32)
-    grad_down_b = jnp.sum(grad_out, axis=0)
-    grad_down_w = [t_mm(act[n], grad_two).astype(BF) for n in range(2)]
-    grad_pre = [(mm_t(grad_two, down_w[n]) * slope[n]).astype(BF) for n in range(2)]
-    grad_up_b = [jnp.sum(g.astype(F32), axis=0, keepdims=True) for g in grad_pre]
-    grad_up_w = [t_mm(normed_two, g).astype(BF) for g in grad_pre]
-    grad_normed = mm_t(grad_pre[0], up_w[0]) + mm_t(grad_pre[1], up_w[1])
-    grad_gain_two = jnp.sum(grad_normed * hat_two, axis=0)
-    grad_after = grad_out + norm_back(hat_two, scale_two, gain_two, grad_normed)
+    (
+        output, normed_two, act, grad_pre, grad_one, grad_mixed, grad_after, grad_gain_two, grad_up_b, grad_down_b,
+    ) = middle(places, mixed, stream_low, grad_two, gain_two, jnp.concatenate(up_b, axis=0), down_b, one_w, down_w)
+    output = output.reshape(1, 2, rows, width)
+    units = act.shape[1] // 2
+    two = lambda v: (v[:, :units], v[:, units:])
+    grad_down_w = [t_mm(v, grad_two).astype(BF) for v in two(act)]
+    grad_up_w = [t_mm(normed_two, v).astype(BF) for v in two(grad_pre)]
     sum_down = net.sum_down(*grad_down_w)
     sum_up = net.sum_up(*grad_up_w, chunk)
 
-    grad_one = grad_after.astype(BF)
     grad_out_w = t_mm(mixed, grad_one).astype(BF)
-    grad_mixed = mm_t(grad_one, out_w).astype(BF)
     sum_out = net.sum_out(grad_out_w)
     grad_q, grad_k, grad_v = attend_back(
         flags, query_rows, key_cols, query, key, value, mixed, grad_mixed, log_norm.T, cosine, sine, rows
     )
     half = width // 2
+    qkv_w = [in_place(places[0], w, width) for w in qkv_w]
     grad_a_kv = None
     grad_a_q = None
     grad_qkv_w = []
@@ -766,7 +920,7 @@
                 [t_mm(a_all[: 2 * rows], grad_q[:, cut]).astype(BF), t_mm(a_all, kv).astype(BF)], axis=1
             )
         )
-    hat_all, _ = normalise(x_all.astype(F32))
+    hat_all, _ = normalise(jnp.concatenate([stream_low] + lower, axis=0).astype(F32))
     grad_gain_one = jnp.sum(grad_a_kv * hat_all, axis=0) + jnp.sum(grad_a_q * hat_all[: 2 * rows], axis=0)
     mine = grad_a_kv[: 2 * rows] + grad_a_q
     parts = [grad_a_kv[t * rows : (t + 1) * rows].astype(BF) for t in range(2, len(tiles))]
@@ -778,7 +932,7 @@
             v.reshape(devices, -1)
             for v in (
                 grad_gain_one, grad_gain_two, grad_down_b, grad_embed,
-                net.unit_bias_back(grad_up_b[0], grad_up_b[1], chunk),
+                net.unit_bias_back(grad_up_b[:1], grad_up_b[1:], chunk),
             )
         ],
         axis=1,

time: 646 us -> 635 us (0.983)
  starting transfers between devices: 223 us -> 153 us
  local copies, waits for them, and re-layouts: 77.7 us -> 134 us
  matrix products: 80.5 us -> 44.8 us
  waiting for transfers between devices: 123 us -> 144 us
  Pallas kernels: 59.5 us -> 78.3 us
  other arithmetic: 69.5 us -> 58.2 us
  between operations: 3.18 us -> 12.8 us
    ppermute x24 -> x3, starting transfers between devices: 152 us -> 4.75 us  [up(): lax.ppermute(v, 'leaf', [(i, i + 2) for i in range(2 * first, 2 * last +...]
    ppermute x0 -> x21, starting transfers between devices: none -> 108 us  [swap_z(): return lax.ppermute(v, 'leaf', [(i, i ^ 2 * n) for i in range(8)])]
    ppermute x0 -> x21, waiting for transfers between devices: none -> 36.5 us  [swap_z(): return lax.ppermute(v, 'leaf', [(i, i ^ 2 * n) for i in range(8)])]
    dynamic_update_slice x0 -> x32, local copies, waits for them, and re-layouts: none -> 25.1 us  [in_place(): out = lax.dynamic_update_slice(out, w[n, :size], (places[n] * size, 0))]
    ppermute x24 -> x3, starting transfers between devices: 26.2 us -> 2.82 us  [down(): lax.ppermute(v, 'leaf', [(i, i - 2) for i in range(2 * first, 2 * last +...]
    pallas_call x1 -> x2, Pallas kernels: 18.4 us -> 41.4 us  [the longest x1 22.2 us: middle(): pl.pallas_call(functools.partial(middle_kernel, count, size, chunk), grid...]
    dot_general x9 -> x4, matrix products: 38.7 us -> 19.3 us  [mm_t(): lax.dot_general(a, b, (((1,), (1,)), ((), ())), preferred_element_type=F32)]
    dot_general x5 -> x1, matrix products: 14.7 us -> 0.79 us  [mm(): return jnp.dot(a, b, preferred_element_type=F32)]
  transfers between devices with their start and end apart: 85 -> 61, of which waited for: 21 -> 19; matrix products, arithmetic and copies ran while one was open for 28% -> 27% of each run, Pallas kernels for 6% -> 6%
where the time goes in v2:
time: 635 us; the launch traced here: 626 us
  starting transfers between devices  153 us (24%)
  waiting for transfers between devices  144 us (23%)
  local copies, waits for them, and re-layouts  134 us (21%)
  Pallas kernels  78.3 us (12%)
  other arithmetic  58.2 us (9%)
  matrix products  44.8 us (7%)
  between operations  12.8 us (2%)
    ppermute x21, starting transfers between devices, swap_z(): return lax.ppermute(v, 'leaf', [(i, i ^ 2 * n) for i in range(8)])  108 us
    ppermute x7, waiting for transfers between devices, swap_x(): return lax.ppermute(v, 'fsdp', [(i, i ^ 2) for i in range(4)])  54.8 us
    ppermute x21, waiting for transfers between devices, swap_z(): return lax.ppermute(v, 'leaf', [(i, i ^ 2 * n) for i in range(8)])  36.5 us
    ppermute x15, waiting for transfers between devices, swap_y(): return lax.ppermute(v, 'leaf', pairs or [(i, i ^ 1) for i in range(8)])  34.6 us
    ppermute x15, starting transfers between devices, swap_y(): return lax.ppermute(v, 'leaf', pairs or [(i, i ^ 1) for i in range(8)])  26.9 us
    dynamic_update_slice x32, local copies, waits for them, and re-layouts, in_place(): out = lax.dynamic_update_slice(out, w[n, :size], (places[n] * size, 0))  25.1 us
    dot_general x9, matrix products, t_mm(): lax.dot_general(a, b, (((0,), (0,)), ((), ())), preferred_element_type=F32)  24.7 us
    unnamed x186, local copies, waits for them, and re-layouts  24.4 us
  transfers between devices with their start and end apart: 61, of which 19 were waited for; matrix products, arithmetic and copies ran while one was open for 27% of the time, Pallas kernels for 6%

profile of v2, /device:TPU:0, one launch (start us, length us, event | category | flops | bytes accessed | tf_op | source)
XLA Modules:
  0.0 625.9 jit_solution(10864463795417482713)
XLA Ops:
  0.7 3.5 concatenate.182
  7.1 2.5 collective-permute-start.18
  30.6 3.7 collective-permute-start.3
  35.7 3.5 collective-permute-done.3
  39.2 3.4 collective-permute-start.6
  42.7 4.5 collective-permute-done.2
  48.9 2.7 collective-permute-start.4
  53.6 9.2 %collective-permute-done.5 = bf16[4,64,1152]{2,1,0:T(8,128)(2,1)S(1)} collective-permute-done((bf16[4,64,1152]{2,1,0:T(8,128)(2,1)S(1)}, bf16[4,64,1152]{2,1,0:T(8,128)(2,1)S(1)}, u32[]{:S(2)}, u32[]{:S(2)}) %collective-permute-start.5) | collective-permute-done | bytes 589856 | tf_op jit(solution)/shard_map/ppermute | solution.py:53
  64.4 5.9 fusion.18
  98.7 2.0 pad.31.mask_ref
  100.7 2.0 broadcast_in_dim.159
  102.6 2.2 copy.158.krow_ref
  109.8 1.9 pad_maximum_fusion.2.own_hbm
  119.9 14.2 %collective-permute-start.17 = (bf16[1,48,1920]{2,1,0:T(8,128)(2,1)}, bf16[1,48,1920]{2,1,0:T(8,128)(2,1)}, u32[]{:S(2)}, u32[]{:S(2)}) collective-permute-start(bf16[1,48,1920]{2,1,0:T(8,128)(2,1)} %bitcast.423), channel_id=1, source_target_pairs={{0,24},{4,28},{8,16},{12,20},{16,8},{20,12},{24,0},{28,4},{1,25},{... | collective-permute-start | bytes 552968 | tf_op jit(solution)/shard_map/ppermute | solution.py:56
  134.1 2.1 collective-permute-start.16
  145.0 2.1 fusion.95
  170.4 3.2 collective-permute-start.22
  185.1 19.2 %shard_map.221 = (bf16[2304,768]{1,0:T(8,128)(2,1)}, bf16[512,768]{1,0:T(8,128)(2,1)}, bf16[2304,768]{1,0:T(8,128)(2,1)}, bf16[2304,768]{1,0:T(8,128)(2,1)}) custom-call(s32[4,16]{1,0:T(4,128)} %pad_add_fusion.table_ref, bf16[2304,768]{1,0:T(8,128)(2,1)} %get-tuple-element.235.x_ref, s32[2304,1]{1,0:T(8,128)} %pad.31.mask_ref, ...), custom_call_target="tpu_custom_call" | custom-call | flops 6039797760 | bytes 17694720 | tf_op jit(solution)/shard_map/pallas_call | solution.py:210
  210.4 15.7 %shard_map.222 = (bf16[512,768]{1,0:T(8,128)(2,1)}, f32[512,128]{1,0:T(8,128)}) custom-call(s32[9]{0:T(128)} %copy-done.75, s32[512,8]{1,0:T(8,128)} %bitcast.431, s32[8,2304]{1,0:T(8,128)} %copy.158.krow_ref, bf16[512,768]{1,0:T(8,128)(2,1)} %get-tuple-element.155.q_ref, bf16[2304,768]{1,0:T(8,128)(2,1)} %get-tuple-element.156.k_ref, ...), custom_call_target="tpu_custom_call" | custom-call | flops 7247757312 | bytes 7864320 | tf_op jit(solution)/shard_map/pallas_call | solution.py:419
  226.1 4.5 collective-permute-start.25
  233.4 8.0 %collective-permute-done.23 = bf16[8,48,1920]{2,1,0:T(8,128)(2,1)S(1)} collective-permute-done((bf16[8,48,1920]{2,1,0:T(8,128)(2,1)S(1)}, bf16[8,48,1920]{2,1,0:T(8,128)(2,1)S(1)}, u32[]{:S(2)}, u32[]{:S(2)}) %collective-permute-start.23) | collective-permute-done | bytes 1474592 | tf_op jit(solution)/shard_map/ppermute | solution.py:50
  244.2 11.7 %collective-permute-done.25 = bf16[4,2,96,768]{3,2,1,0:T(8,128)(2,1)S(1)} collective-permute-done((bf16[4,2,96,768]{3,2,1,0:T(8,128)(2,1)S(1)}, bf16[4,2,96,768]{3,2,1,0:T(8,128)(2,1)S(1)}, u32[]{:S(2)}, u32[]{:S(2)}) %collective-permute-start.25) | collective-permute-done | bytes 1179680 | tf_op jit(solution)/shard_map/ppermute | solution.py:53
  268.6 22.2 %shard_map.223 = (bf16[512,768]{1,0:T(8,128)(2,1)}, bf16[512,768]{1,0:T(8,128)(2,1)}, bf16[512,3072]{1,0:T(8,128)(2,1)}, bf16[512,3072]{1,0:T(8,128)(2,1)}, bf16...) custom-call(s32[4,16]{1,0:T(4,128)} %pad_add_fusion.table_ref, ...), custom_call_target="tpu_custom_call" | custom-call | flops 10871635968 | bytes 21233664 | tf_op jit(solution)/shard_map/pallas_call | solution.py:311
  290.8 21.2 %shard_map.224 = (bf16[512,768]{1,0:T(8,128)(2,1)}, bf16[2304,768]{1,0:T(8,128)(2,1)}, bf16[2304,768]{1,0:T(8,128)(2,1)}) custom-call(s32[9]{0:T(128)} %copy-done.75, s32[8,512]{1,0:T(8,128)} %reshape.1124.qrow_ref, s32[2304,8]{1,0:T(8,128)} %bitcast.417, bf16[512,768]{1,0:T(8,128)(2,1)} %get-tuple-element.155.q_ref, ...), custom_call_target="tpu_custom_call" | custom-call | flops 18119393280 | bytes 15728640 | tf_op jit(solution)/shard_map/pallas_call | solution.py:528
  312.1 2.5 convolution_convert_fusion.6
  315.9 2.9 convolution_convert_fusion.2
  318.8 2.8 convolution_convert_fusion.3
  321.6 2.9 convolution_convert_fusion
  324.5 2.9 convolution_convert_fusion.1
  332.6 4.0 fusion.16
  336.6 5.4 fusion.9
  344.7 2.2 convolution_convert_fusion.4
  348.3 3.6 reshape.1139
  351.9 4.0 fusion.102
  360.5 9.3 %multiply_reduce_fusion = (f32[768]{0:T(1024)S(1)}, bf16[2304,768]{1,0:T(8,128)(2,1)S(1)}, f32[2304,768]{1,0:T(8,128)}, f32[2304,768]{1,0:T(8,128)}) fusion(f32[2304]{0:T(1024)S(1)} %copy-done.41, f32[2304]{0:T(1024)S(1)} %broadcast_multiply_fusion, bf16[2304,768]{1,0:T(8,128)(2,1)S(1)} %get-tuple-element.234, f32[2304,768]{1,0:T(8,128)} %fusion.9, ...), kind=kOutput, calls=%fused_computation.5 | convolution fusion | flops 2737372416 | bytes 33051648 | tf_op jit(solution)/shard_map/dot_general | solution.py:583
  373.7 2.9 fusion.11
  376.8 3.2 fusion.17
  382.8 7.0 %collective-permute-done.42 = bf16[8,48,384]{2,1,0:T(8,128)(2,1)S(1)} collective-permute-done((bf16[8,48,384]{2,1,0:T(8,128)(2,1)S(1)}, bf16[8,48,384]{2,1,0:T(8,128)(2,1)S(1)}, u32[]{:S(2)}, u32[]{:S(2)}) %collective-permute-start.42) | collective-permute-done | bytes 294944 | tf_op jit(solution)/shard_map/ppermute | solution.py:50
  389.9 7.8 %collective-permute-start.43 = (bf16[4,48,384]{2,1,0:T(8,128)(2,1)S(1)}, bf16[4,48,384]{2,1,0:T(8,128)(2,1)S(1)}, u32[]{:S(2)}, u32[]{:S(2)}) collective-permute-start(bf16[4,48,384]{2,1,0:T(8,128)(2,1)S(1)} %fusion.51), channel_id=1, source_target_pairs={{0,4},{4,0},{8,12},{12,8},{16,20},{20,16},{24,28},{28,24},{1,5},{5... | collective-permute-start | bytes 442376 | tf_op jit(solution)/shard_map/ppermute | solution.py:53
  398.7 2.7 collective-permute-done.43
  401.5 19.9 %collective-permute-start.44 = (bf16[48,384]{1,0:T(8,128)(2,1)S(1)}, bf16[48,384]{1,0:T(8,128)(2,1)S(1)}, u32[]{:S(2)}, u32[]{:S(2)}) collective-permute-start(bf16[48,384]{1,0:T(8,128)(2,1)S(1)} %get-tuple-element.256), channel_id=1, source_target_pairs={{0,8},{4,12},{8,0},{12,4},{16,24},{20,28},{24,16},{28,20},{1,9},{5... | collective-permute-start | bytes 110600 | tf_op jit(solution)/shard_map/ppermute | solution.py:56
  421.4 43.7 %collective-permute-start.46 = (bf16[48,384]{1,0:T(8,128)(2,1)S(1)}, bf16[48,384]{1,0:T(8,128)(2,1)S(1)}, u32[]{:S(2)}, u32[]{:S(2)}) collective-permute-start(bf16[48,384]{1,0:T(8,128)(2,1)S(1)} %get-tuple-element.257), channel_id=1, source_target_pairs={{0,24},{4,28},{8,16},{12,20},{16,8},{20,12},{24,0},{28,4},{1,25},{... | collective-permute-start | bytes 110600 | tf_op jit(solution)/shard_map/ppermute | solution.py:56
  465.1 7.5 %collective-permute-start.45 = (bf16[48,384]{1,0:T(8,128)(2,1)S(1)}, bf16[48,384]{1,0:T(8,128)(2,1)S(1)}, u32[]{:S(2)}, u32[]{:S(2)}) collective-permute-start(bf16[48,384]{1,0:T(8,128)(2,1)S(1)} %get-tuple-element.258), channel_id=1, source_target_pairs={{0,16},{4,20},{8,24},{12,28},{16,0},{20,4},{24,8},{28,12},{1,17},{... | collective-permute-start | bytes 110600 | tf_op jit(solution)/shard_map/ppermute | solution.py:56
  478.1 2.2 copy.164
  480.4 4.0 copy.171
  485.9 17.6 %collective-permute-done.32 = bf16[256,768]{1,0:T(8,128)(2,1)} collective-permute-done((bf16[256,768]{1,0:T(8,128)(2,1)}, bf16[256,768]{1,0:T(8,128)(2,1)}, u32[]{:S(2)}, u32[]{:S(2)}) %collective-permute-start.32) | collective-permute-done | bytes 393248 | tf_op jit(solution)/shard_map/ppermute | solution.py:62
  503.6 2.6 fusion.30
  510.1 2.3 fusion.4
  514.1 2.4 fusion.3
  519.5 21.3 %collective-permute-done.56 = bf16[8,96,768]{2,1,0:T(8,128)(2,1)S(1)} collective-permute-done((bf16[8,96,768]{2,1,0:T(8,128)(2,1)S(1)}, bf16[8,96,768]{2,1,0:T(8,128)(2,1)S(1)}, u32[]{:S(2)}, u32[]{:S(2)}) %collective-permute-start.56) | collective-permute-done | bytes 1179680 | tf_op jit(solution)/shard_map/ppermute | solution.py:50
  541.3 4.2 collective-permute-done.49
  546.1 2.0 collective-permute-start.50
  548.1 2.6 collective-permute-start.52
  551.2 5.1 collective-permute-done.50
  556.3 8.7 %collective-permute-done.52 = bf16[2,48,1536]{2,1,0:T(8,128)(2,1)S(1)} collective-permute-done((bf16[2,48,1536]{2,1,0:T(8,128)(2,1)S(1)}, bf16[2,48,1536]{2,1,0:T(8,128)(2,1)S(1)}, u32[]{:S(2)}, u32[]{:S(2)}) %collective-permute-start.52) | collective-permute-done | bytes 294944 | tf_op jit(solution)/shard_map/ppermute | solution.py:56
  565.0 9.0 %collective-permute-done.51 = bf16[2,48,1536]{2,1,0:T(8,128)(2,1)S(1)} collective-permute-done((bf16[2,48,1536]{2,1,0:T(8,128)(2,1)S(1)}, bf16[2,48,1536]{2,1,0:T(8,128)(2,1)S(1)}, u32[]{:S(2)}, u32[]{:S(2)}) %collective-permute-start.51) | collective-permute-done | bytes 294944 | tf_op jit(solution)/shard_map/ppermute | solution.py:56
  576.5 4.6 collective-permute-done.53
  582.4 2.6 collective-permute-start.60
  585.9 14.0 %collective-permute-done.35 = bf16[8,56,1152]{2,1,0:T(8,128)(2,1)S(1)} collective-permute-done((bf16[8,56,1152]{2,1,0:T(8,128)(2,1)S(1)}, bf16[8,56,1152]{2,1,0:T(8,128)(2,1)S(1)}, u32[]{:S(2)}, u32[]{:S(2)}) %collective-permute-start.35) | collective-permute-done | bytes 1032224 | tf_op jit(solution)/shard_map/ppermute | solution.py:50
  604.3 6.8 %collective-permute-done.36 = bf16[4,56,1152]{2,1,0:T(8,128)(2,1)S(1)} collective-permute-done((bf16[4,56,1152]{2,1,0:T(8,128)(2,1)S(1)}, bf16[4,56,1152]{2,1,0:T(8,128)(2,1)S(1)}, u32[]{:S(2)}, u32[]{:S(2)}) %collective-permute-start.36) | collective-permute-done | bytes 516128 | tf_op jit(solution)/shard_map/ppermute | solution.py:53
  611.3 2.8 collective-permute-start.39
  614.8 1.9 fusion.48
  616.7 2.3 collective-permute-done.37
  619.0 3.3 collective-permute-done.38
  (511 shorter events, 182.7 us)
Async XLA Ops:
  6.7 22.9 %collective-permute-start = (bf16[32,1152]{1,0:T(8,128)(2,1)}, bf16[32,1152]{1,0:T(8,128)(2,1)}, u32[]{:S(2)}, u32[]{:S(2)}) collective-permute-start(bf16[32,1152]{1,0:T(8,128)(2,1)} %fusion.69), channel_id=1, source_target_pairs={{0,1},{1,0},{2,3},{3,2},{4,5},{5,4},{6,7},{7,6},{8,9},{9,8},{10,11... | collective-permute-start | bytes 221192 | tf_op jit(solution)/shard_map/ppermute | solution.py:47
  7.1 100.9 %collective-permute-start.18 = (bf16[96,768]{1,0:T(8,128)(2,1)}, bf16[96,768]{1,0:T(8,128)(2,1)}, u32[]{:S(2)}, u32[]{:S(2)}) collective-permute-start(bf16[96,768]{1,0:T(8,128)(2,1)} %param.42), channel_id=1, source_target_pairs={{0,2},{1,3},{2,0},{3,1},{4,6},{5,7},{6,4},{7,5},{8,10},{9,11},{10,... | collective-permute-start | bytes 442376 | tf_op jit(solution)/shard_map/ppermute | solution.py:50
  12.5 92.4 %collective-permute-start.11 = (bf16[24,1920]{1,0:T(8,128)(2,1)}, bf16[24,1920]{1,0:T(8,128)(2,1)}, u32[]{:S(2)}, u32[]{:S(2)}) collective-permute-start(bf16[24,1920]{1,0:T(8,128)(2,1)} %maximum_select_fusion.4), channel_id=1, source_target_pairs={{0,1},{1,0},{2,3},{3,2},{4,5},{5,4},{6,7},{7,6},{8,9},{9,8},{10,11... | collective-permute-start | bytes 276488 | tf_op jit(solution)/shard_map/ppermute | solution.py:47
  26.9 36.8 %copy-start.11 = (bf16[2304,768]{1,0:T(8,128)(2,1)}, bf16[2304,768]{1,0:T(8,128)(2,1)S(1)}, u32[]{:S(2)}) copy-start(bf16[2304,768]{1,0:T(8,128)(2,1)S(1)} %constant_dynamic-update-slice_fusion.17) | copy-start | bytes 10616836
  30.6 8.6 %collective-permute-start.3 = (bf16[1,64,1152]{2,1,0:T(8,128)(2,1)S(1)}, bf16[1,64,1152]{2,1,0:T(8,128)(2,1)S(1)}, u32[]{:S(2)}, u32[]{:S(2)}) collective-permute-start(bf16[1,64,1152]{2,1,0:T(8,128)(2,1)S(1)} %maximum_bitcast_fusion.1), channel_id=1, source_target_pairs={{0,24},{4,28},{8,16},{12,20},{16,8},{20,12},{24,0},{28,4},{1,25},{... | collective-permute-start | bytes 442376 | tf_op jit(solution)/shard_map/ppermute | solution.py:56
  34.3 12.9 %collective-permute-start.2 = (bf16[1,64,1152]{2,1,0:T(8,128)(2,1)S(1)}, bf16[1,64,1152]{2,1,0:T(8,128)(2,1)S(1)}, u32[]{:S(2)}, u32[]{:S(2)}) collective-permute-start(bf16[1,64,1152]{2,1,0:T(8,128)(2,1)S(1)} %maximum_bitcast_fusion.1), channel_id=1, source_target_pairs={{0,16},{4,20},{8,24},{12,28},{16,0},{20,4},{24,8},{28,12},{1,17},{... | collective-permute-start | bytes 442376 | tf_op jit(solution)/shard_map/ppermute | solution.py:56
  34.3 12.9 %collective-permute-start.1 = (bf16[1,64,1152]{2,1,0:T(8,128)(2,1)S(1)}, bf16[1,64,1152]{2,1,0:T(8,128)(2,1)S(1)}, u32[]{:S(2)}, u32[]{:S(2)}) collective-permute-start(bf16[1,64,1152]{2,1,0:T(8,128)(2,1)S(1)} %maximum_bitcast_fusion.1), channel_id=1, source_target_pairs={{0,8},{4,12},{8,0},{12,4},{16,24},{20,28},{24,16},{28,20},{1,9},{5... | collective-permute-start | bytes 442376 | tf_op jit(solution)/shard_map/ppermute | solution.py:56
  39.2 24.4 %collective-permute-start.6 = (bf16[256,768]{1,0:T(8,128)(2,1)S(1)}, bf16[256,768]{1,0:T(8,128)(2,1)S(1)}, u32[]{:S(2)}, u32[]{:S(2)}) collective-permute-start(bf16[256,768]{1,0:T(8,128)(2,1)S(1)} %bitcast.414), channel_id=1, source_target_pairs={{0,4},{8,12},{16,20},{24,28},{1,5},{9,13},{17,21},{25,29},{2,6},{1... | collective-permute-start | bytes 1179656 | tf_op jit(solution)/shard_map/ppermute | solution.py:53
  47.3 15.4 %collective-permute-start.5 = (bf16[4,64,1152]{2,1,0:T(8,128)(2,1)S(1)}, bf16[4,64,1152]{2,1,0:T(8,128)(2,1)S(1)}, u32[]{:S(2)}, u32[]{:S(2)}) collective-permute-start(bf16[4,64,1152]{2,1,0:T(8,128)(2,1)S(1)} %pad_maximum_fusion.19), channel_id=1, source_target_pairs={{0,4},{4,0},{8,12},{12,8},{16,20},{20,16},{24,28},{28,24},{1,5},{5... | collective-permute-start | bytes 1769480 | tf_op jit(solution)/shard_map/ppermute | solution.py:53
  48.9 14.7 %collective-permute-start.4 = (bf16[256,768]{1,0:T(8,128)(2,1)S(1)}, bf16[256,768]{1,0:T(8,128)(2,1)}, u32[]{:S(2)}, u32[]{:S(2)}) collective-permute-start(bf16[256,768]{1,0:T(8,128)(2,1)S(1)} %bitcast.415), channel_id=1, source_target_pairs={{0,8},{4,12},{8,16},{12,20},{16,24},{20,28},{1,9},{5,13},{9,17},{1... | collective-permute-start | bytes 1179656 | tf_op jit(solution)/shard_map/ppermute | solution.py:59
  63.6 46.1 %collective-permute-start.12 = (bf16[8,64,1152]{2,1,0:T(8,128)(2,1)}, bf16[8,64,1152]{2,1,0:T(8,128)(2,1)}, u32[]{:S(2)}, u32[]{:S(2)}) collective-permute-start(bf16[8,64,1152]{2,1,0:T(8,128)(2,1)} %constant_dynamic-update-slice_fusion.5), channel_id=1, source_target_pairs={{0,2},{1,3},{2,0},{3,1},{4,6},{5,7},{6,4},{7,5},{8,10},{9,11},{10,... | collective-permute-start | bytes 3538952 | tf_op jit(solution)/shard_map/ppermute | solution.py:50
  70.3 36.3 %collective-permute-start.8 = (bf16[256,768]{1,0:T(8,128)(2,1)}, bf16[256,768]{1,0:T(8,128)(2,1)}, u32[]{:S(2)}, u32[]{:S(2)}) collective-permute-start(bf16[256,768]{1,0:T(8,128)(2,1)} %collective-permute-done.4), channel_id=1, source_target_pairs={{8,16},{12,20},{16,24},{20,28},{9,17},{13,21},{17,25},{21,29},{10,... | collective-permute-start | bytes 1179656 | tf_op jit(solution)/shard_map/ppermute | solution.py:59
  71.7 34.9 %collective-permute-start.7 = (bf16[256,768]{1,0:T(8,128)(2,1)}, bf16[256,768]{1,0:T(8,128)(2,1)}, u32[]{:S(2)}, u32[]{:S(2)}) collective-permute-start(bf16[256,768]{1,0:T(8,128)(2,1)} %collective-permute-done.4), channel_id=1, source_target_pairs={{8,12},{12,8},{16,20},{20,16},{24,28},{28,24},{9,13},{13,9},{17,21... | collective-permute-start | bytes 1179656 | tf_op jit(solution)/shard_map/ppermute | solution.py:53
  106.7 5.0 collective-permute-start.10
  107.3 4.3 collective-permute-start.9
  119.9 44.3 %collective-permute-start.17 = (bf16[1,48,1920]{2,1,0:T(8,128)(2,1)}, bf16[1,48,1920]{2,1,0:T(8,128)(2,1)}, u32[]{:S(2)}, u32[]{:S(2)}) collective-permute-start(bf16[1,48,1920]{2,1,0:T(8,128)(2,1)} %bitcast.423), channel_id=1, source_target_pairs={{0,24},{4,28},{8,16},{12,20},{16,8},{20,12},{24,0},{28,4},{1,25},{... | collective-permute-start | bytes 552968 | tf_op jit(solution)/shard_map/ppermute | solution.py:56
  134.1 30.0 %collective-permute-start.16 = (bf16[1,48,1920]{2,1,0:T(8,128)(2,1)}, bf16[1,48,1920]{2,1,0:T(8,128)(2,1)}, u32[]{:S(2)}, u32[]{:S(2)}) collective-permute-start(bf16[1,48,1920]{2,1,0:T(8,128)(2,1)} %bitcast.424), channel_id=1, source_target_pairs={{0,16},{4,20},{8,24},{12,28},{16,0},{20,4},{24,8},{28,12},{1,17},{... | collective-permute-start | bytes 552968 | tf_op jit(solution)/shard_map/ppermute | solution.py:56
  136.2 27.9 %collective-permute-start.15 = (bf16[1,48,1920]{2,1,0:T(8,128)(2,1)}, bf16[1,48,1920]{2,1,0:T(8,128)(2,1)}, u32[]{:S(2)}, u32[]{:S(2)}) collective-permute-start(bf16[1,48,1920]{2,1,0:T(8,128)(2,1)} %bitcast.425), channel_id=1, source_target_pairs={{0,8},{4,12},{8,0},{12,4},{16,24},{20,28},{24,16},{28,20},{1,9},{5... | collective-permute-start | bytes 552968 | tf_op jit(solution)/shard_map/ppermute | solution.py:56
  136.8 33.6 %collective-permute-start.14 = (bf16[16,64,1152]{2,1,0:T(8,128)(2,1)}, bf16[16,64,1152]{2,1,0:T(8,128)(2,1)}, u32[]{:S(2)}, u32[]{:S(2)}) collective-permute-start(bf16[16,64,1152]{2,1,0:T(8,128)(2,1)} %copy-done.2), channel_id=1, source_target_pairs={{0,1},{1,0},{2,3},{3,2},{4,5},{5,4},{6,7},{7,6},{8,9},{9,8},{10,11... | collective-permute-start | bytes 7077896 | tf_op jit(solution)/shard_map/ppermute | solution.py:47
  142.3 23.2 %collective-permute-start.13 = (bf16[256,768]{1,0:T(8,128)(2,1)}, bf16[256,768]{1,0:T(8,128)(2,1)}, u32[]{:S(2)}, u32[]{:S(2)}) collective-permute-start(bf16[256,768]{1,0:T(8,128)(2,1)} %copy-done.30), channel_id=1, source_target_pairs={{24,28},{28,24},{25,29},{29,25},{26,30},{30,26},{27,31},{31,27}} | collective-permute-start | bytes 1179656 | tf_op jit(solution)/shard_map/ppermute | solution.py:53
  170.4 37.0 %collective-permute-start.22 = (bf16[1,2,96,768]{3,2,1,0:T(8,128)(2,1)S(1)}, bf16[1,2,96,768]{3,2,1,0:T(8,128)(2,1)S(1)}, u32[]{:S(2)}, u32[]{:S(2)}) collective-permute-start(bf16[1,2,96,768]{3,2,1,0:T(8,128)(2,1)S(1)} %copy-done.22), channel_id=1, source_target_pairs={{0,24},{4,28},{8,16},{12,20},{16,8},{20,12},{24,0},{28,4},{1,25},{... | collective-permute-start | bytes 884744 | tf_op jit(solution)/shard_map/ppermute | solution.py:56
  173.6 33.8 %collective-permute-start.21 = (bf16[1,2,96,768]{3,2,1,0:T(8,128)(2,1)S(1)}, bf16[1,2,96,768]{3,2,1,0:T(8,128)(2,1)S(1)}, u32[]{:S(2)}, u32[]{:S(2)}) collective-permute-start(bf16[1,2,96,768]{3,2,1,0:T(8,128)(2,1)S(1)} %copy-done.22), channel_id=1, source_target_pairs={{0,16},{4,20},{8,24},{12,28},{16,0},{20,4},{24,8},{28,12},{1,17},{... | collective-permute-start | bytes 884744 | tf_op jit(solution)/shard_map/ppermute | solution.py:56
  173.6 33.8 %collective-permute-start.20 = (bf16[1,2,96,768]{3,2,1,0:T(8,128)(2,1)S(1)}, bf16[1,2,96,768]{3,2,1,0:T(8,128)(2,1)S(1)}, u32[]{:S(2)}, u32[]{:S(2)}) collective-permute-start(bf16[1,2,96,768]{3,2,1,0:T(8,128)(2,1)S(1)} %copy-done.22), channel_id=1, source_target_pairs={{0,8},{4,12},{8,0},{12,4},{16,24},{20,28},{24,16},{28,20},{1,9},{5... | collective-permute-start | bytes 884744 | tf_op jit(solution)/shard_map/ppermute | solution.py:56
  174.8 32.8 %collective-permute-start.19 = (bf16[4,48,1920]{2,1,0:T(8,128)(2,1)S(1)}, bf16[4,48,1920]{2,1,0:T(8,128)(2,1)S(1)}, u32[]{:S(2)}, u32[]{:S(2)}) collective-permute-start(bf16[4,48,1920]{2,1,0:T(8,128)(2,1)S(1)} %pad_maximum_fusion.18), channel_id=1, source_target_pairs={{0,4},{4,0},{8,12},{12,8},{16,20},{20,16},{24,28},{28,24},{1,5},{5... | collective-permute-start | bytes 2211848 | tf_op jit(solution)/shard_map/ppermute | solution.py:53
  207.8 33.6 %collective-permute-start.23 = (bf16[8,48,1920]{2,1,0:T(8,128)(2,1)S(1)}, bf16[8,48,1920]{2,1,0:T(8,128)(2,1)S(1)}, u32[]{:S(2)}, u32[]{:S(2)}) collective-permute-start(bf16[8,48,1920]{2,1,0:T(8,128)(2,1)S(1)} %pad_maximum_fusion.15), channel_id=1, source_target_pairs={{0,2},{1,3},{2,0},{3,1},{4,6},{5,7},{6,4},{7,5},{8,10},{9,11},{10,... | collective-permute-start | bytes 4423688 | tf_op jit(solution)/shard_map/ppermute | solution.py:50
  226.1 29.8 %collective-permute-start.25 = (bf16[4,2,96,768]{3,2,1,0:T(8,128)(2,1)S(1)}, bf16[4,2,96,768]{3,2,1,0:T(8,128)(2,1)S(1)}, u32[]{:S(2)}, u32[]{:S(2)}) collective-permute-start(bf16[4,2,96,768]{3,2,1,0:T(8,128)(2,1)S(1)} %pad_maximum_fusion.16), channel_id=1, source_target_pairs={{0,4},{4,0},{8,12},{12,8},{16,20},{20,16},{24,28},{28,24},{1,5},{5... | collective-permute-start | bytes 3538952 | tf_op jit(solution)/shard_map/ppermute | solution.py:53
  242.6 26.0 %collective-permute-start.24 = (bf16[16,48,1920]{2,1,0:T(8,128)(2,1)}, bf16[16,48,1920]{2,1,0:T(8,128)(2,1)}, u32[]{:S(2)}, u32[]{:S(2)}) collective-permute-start(bf16[16,48,1920]{2,1,0:T(8,128)(2,1)} %constant_dynamic-update-slice_fusion.19.one_own), channel_id=1, source_target_pairs={{0,1},{1,0},{2,3},{3,2},{4,5},{5,4},{6,7},{7,6},{8,9},{9,8},{10,11... | collective-permute-start | bytes 8847368 | tf_op jit(solution)/shard_map/ppermute | solution.py:47
  257.5 11.1 %collective-permute-start.26 = (bf16[16,96,768]{2,1,0:T(8,128)(2,1)}, bf16[16,96,768]{2,1,0:T(8,128)(2,1)}, u32[]{:S(2)}, u32[]{:S(2)}) collective-permute-start(bf16[16,96,768]{2,1,0:T(8,128)(2,1)} %bitcast.27.two_own), channel_id=1, source_target_pairs={{0,1},{1,0},{2,3},{3,2},{4,5},{5,4},{6,7},{7,6},{8,9},{9,8},{10,11... | collective-permute-start | bytes 7077896 | tf_op jit(solution)/shard_map/ppermute | solution.py:47
  290.8 25.1 %copy-start.80 = (bf16[512,768]{1,0:T(8,128)(2,1)S(1)}, bf16[512,768]{1,0:T(8,128)(2,1)}, u32[]{:S(2)}) copy-start(bf16[512,768]{1,0:T(8,128)(2,1)} %get-tuple-element.176) | copy-start | bytes 2359300
  356.1 23.8 %collective-permute-start.41 = (bf16[8,2,48,384]{3,2,1,0:T(8,128)(2,1)S(1)}, bf16[8,2,48,384]{3,2,1,0:T(8,128)(2,1)S(1)}, u32[]{:S(2)}, u32[]{:S(2)}) collective-permute-start(bf16[8,2,48,384]{3,2,1,0:T(8,128)(2,1)S(1)} %select_bitcast_fusion.2), channel_id=1, source_target_pairs={{0,1},{1,0},{2,3},{3,2},{4,5},{5,4},{6,7},{7,6},{8,9},{9,8},{10,11... | collective-permute-start | bytes 1769480 | tf_op jit(solution)/shard_map/ppermute | solution.py:47
  359.2 150.6 %collective-permute-start.55 = (bf16[8,2,96,768]{3,2,0,1:T(8,128)(2,1)}, bf16[8,2,96,768]{3,2,0,1:T(8,128)(2,1)}, u32[]{:S(2)}, u32[]{:S(2)}) collective-permute-start(bf16[8,2,96,768]{3,2,0,1:T(8,128)(2,1)} %copy.191), channel_id=1, source_target_pairs={{0,1},{1,0},{2,3},{3,2},{4,5},{5,4},{6,7},{7,6},{8,9},{9,8},{10,11... | collective-permute-start | bytes 7077896 | tf_op jit(solution)/shard_map/ppermute | solution.py:47
  359.7 153.9 %collective-permute-start.48 = (bf16[8,2,48,1536]{3,2,1,0:T(8,128)(2,1)}, bf16[8,2,48,1536]{3,2,1,0:T(8,128)(2,1)}, u32[]{:S(2)}, u32[]{:S(2)}) collective-permute-start(bf16[8,2,48,1536]{3,2,1,0:T(8,128)(2,1)} %bitcast.116), channel_id=1, source_target_pairs={{0,1},{1,0},{2,3},{3,2},{4,5},{5,4},{6,7},{7,6},{8,9},{9,8},{10,11... | collective-permute-start | bytes 7077896 | tf_op jit(solution)/shard_map/ppermute | solution.py:47
  370.6 27.1 %collective-permute-start.27 = (bf16[256,768]{1,0:T(8,128)(2,1)S(1)}, bf16[256,768]{1,0:T(8,128)(2,1)S(1)}, u32[]{:S(2)}, u32[]{:S(2)}) collective-permute-start(bf16[256,768]{1,0:T(8,128)(2,1)S(1)} %get-tuple-element.205), channel_id=1, source_target_pairs={{24,28},{28,24},{25,29},{29,25},{26,30},{30,26},{27,31},{31,27}} | collective-permute-start | bytes 1179656 | tf_op jit(solution)/shard_map/ppermute | solution.py:53
  371.3 50.1 %collective-permute-start.29 = (bf16[256,768]{1,0:T(8,128)(2,1)S(1)}, bf16[256,768]{1,0:T(8,128)(2,1)S(1)}, u32[]{:S(2)}, u32[]{:S(2)}) collective-permute-start(bf16[256,768]{1,0:T(8,128)(2,1)S(1)} %get-tuple-element.208), channel_id=1, source_target_pairs={{16,20},{20,16},{24,28},{28,24},{17,21},{21,17},{25,29},{29,25},{1... | collective-permute-start | bytes 1179656 | tf_op jit(solution)/shard_map/ppermute | solution.py:53
  380.3 9.5 %collective-permute-start.42 = (bf16[8,48,384]{2,1,0:T(8,128)(2,1)S(1)}, bf16[8,48,384]{2,1,0:T(8,128)(2,1)S(1)}, u32[]{:S(2)}, u32[]{:S(2)}) collective-permute-start(bf16[8,48,384]{2,1,0:T(8,128)(2,1)S(1)} %fusion.46), channel_id=1, source_target_pairs={{0,2},{1,3},{2,0},{3,1},{4,6},{5,7},{6,4},{7,5},{8,10},{9,11},{10,... | collective-permute-start | bytes 884744 | tf_op jit(solution)/shard_map/ppermute | solution.py:50
  389.9 11.5 %collective-permute-start.43 = (bf16[4,48,384]{2,1,0:T(8,128)(2,1)S(1)}, bf16[4,48,384]{2,1,0:T(8,128)(2,1)S(1)}, u32[]{:S(2)}, u32[]{:S(2)}) collective-permute-start(bf16[4,48,384]{2,1,0:T(8,128)(2,1)S(1)} %fusion.51), channel_id=1, source_target_pairs={{0,4},{4,0},{8,12},{12,8},{16,20},{20,16},{24,28},{28,24},{1,5},{5... | collective-permute-start | bytes 442376 | tf_op jit(solution)/shard_map/ppermute | solution.py:53
  397.8 67.3 %collective-permute-start.28 = (bf16[256,768]{1,0:T(8,128)(2,1)S(1)}, bf16[256,768]{1,0:T(8,128)(2,1)S(1)}, u32[]{:S(2)}, u32[]{:S(2)}) collective-permute-start(bf16[256,768]{1,0:T(8,128)(2,1)S(1)} %add_convert_fusion.4), channel_id=1, source_target_pairs={{24,16},{28,20},{25,17},{29,21},{26,18},{30,22},{27,19},{31,23}} | collective-permute-start | bytes 1179656 | tf_op jit(solution)/shard_map/ppermute | solution.py:62
  401.5 76.3 %copy-start.58 = (f32[1,768]{1,0:T(1,128)S(1)}, f32[1,768]{1,0:T(1,128)}, u32[]{:S(2)}) copy-start(f32[1,768]{1,0:T(1,128)} %get-tuple-element.173) | copy-start | bytes 9220
  401.5 71.2 %collective-permute-start.44 = (bf16[48,384]{1,0:T(8,128)(2,1)S(1)}, bf16[48,384]{1,0:T(8,128)(2,1)S(1)}, u32[]{:S(2)}, u32[]{:S(2)}) collective-permute-start(bf16[48,384]{1,0:T(8,128)(2,1)S(1)} %get-tuple-element.256), channel_id=1, source_target_pairs={{0,8},{4,12},{8,0},{12,4},{16,24},{20,28},{24,16},{28,20},{1,9},{5... | collective-permute-start | bytes 110600 | tf_op jit(solution)/shard_map/ppermute | solution.py:56
  421.4 52.7 %collective-permute-start.46 = (bf16[48,384]{1,0:T(8,128)(2,1)S(1)}, bf16[48,384]{1,0:T(8,128)(2,1)S(1)}, u32[]{:S(2)}, u32[]{:S(2)}) collective-permute-start(bf16[48,384]{1,0:T(8,128)(2,1)S(1)} %get-tuple-element.257), channel_id=1, source_target_pairs={{0,24},{4,28},{8,16},{12,20},{16,8},{20,12},{24,0},{28,4},{1,25},{... | collective-permute-start | bytes 110600 | tf_op jit(solution)/shard_map/ppermute | solution.py:56
  465.1 9.7 %collective-permute-start.45 = (bf16[48,384]{1,0:T(8,128)(2,1)S(1)}, bf16[48,384]{1,0:T(8,128)(2,1)S(1)}, u32[]{:S(2)}, u32[]{:S(2)}) collective-permute-start(bf16[48,384]{1,0:T(8,128)(2,1)S(1)} %get-tuple-element.258), channel_id=1, source_target_pairs={{0,16},{4,20},{8,24},{12,28},{16,0},{20,4},{24,8},{28,12},{1,17},{... | collective-permute-start | bytes 110600 | tf_op jit(solution)/shard_map/ppermute | solution.py:56
  472.8 13.1 %collective-permute-start.33 = (bf16[256,768]{1,0:T(8,128)(2,1)}, bf16[256,768]{1,0:T(8,128)(2,1)}, u32[]{:S(2)}, u32[]{:S(2)}) collective-permute-start(bf16[256,768]{1,0:T(8,128)(2,1)} %get-tuple-element.206), channel_id=1, source_target_pairs={{4,0},{12,8},{20,16},{28,24},{5,1},{13,9},{21,17},{29,25},{6,2},{1... | collective-permute-start | bytes 1179656 | tf_op jit(solution)/shard_map/ppermute | solution.py:53
  474.1 1.4 collective-permute-start.31
  474.8 0.8 collective-permute-start.30
  475.5 8.9 %collective-permute-start.47 = (f32[24,384]{1,0:T(8,128)S(1)}, f32[24,384]{1,0:T(8,128)}, u32[]{:S(2)}, u32[]{:S(2)}) collective-permute-start(f32[24,384]{1,0:T(8,128)S(1)} %slice_select_fusion.4), channel_id=1, source_target_pairs={{0,1},{1,0},{2,3},{3,2},{4,5},{5,4},{6,7},{7,6},{8,9},{9,8},{10,11... | collective-permute-start | bytes 110600 | tf_op jit(solution)/shard_map/ppermute | solution.py:47
  476.5 26.9 %collective-permute-start.32 = (bf16[256,768]{1,0:T(8,128)(2,1)}, bf16[256,768]{1,0:T(8,128)(2,1)}, u32[]{:S(2)}, u32[]{:S(2)}) collective-permute-start(bf16[256,768]{1,0:T(8,128)(2,1)} %add_convert_fusion.2), channel_id=1, source_target_pairs={{8,0},{12,4},{16,8},{20,12},{24,16},{28,20},{9,1},{13,5},{17,9},{2... | collective-permute-start | bytes 1179656 | tf_op jit(solution)/shard_map/ppermute | solution.py:62
  509.7 41.0 %collective-permute-start.34 = (bf16[8,2,56,1152]{3,2,1,0:T(8,128)(2,1)S(1)}, bf16[8,2,56,1152]{3,2,1,0:T(8,128)(2,1)S(1)}, u32[]{:S(2)}, u32[]{:S(2)}) collective-permute-start(bf16[8,2,56,1152]{3,2,1,0:T(8,128)(2,1)S(1)} %pad_maximum_fusion.8), channel_id=1, source_target_pairs={{0,1},{1,0},{2,3},{3,2},{4,5},{5,4},{6,7},{7,6},{8,9},{9,8},{10,11... | collective-permute-start | bytes 6193160 | tf_op jit(solution)/shard_map/ppermute | solution.py:47
  512.6 28.1 %collective-permute-start.56 = (bf16[8,96,768]{2,1,0:T(8,128)(2,1)S(1)}, bf16[8,96,768]{2,1,0:T(8,128)(2,1)S(1)}, u32[]{:S(2)}, u32[]{:S(2)}) collective-permute-start(bf16[8,96,768]{2,1,0:T(8,128)(2,1)S(1)} %select_bitcast_fusion), channel_id=1, source_target_pairs={{0,2},{1,3},{2,0},{3,1},{4,6},{5,7},{6,4},{7,5},{8,10},{9,11},{10,... | collective-permute-start | bytes 3538952 | tf_op jit(solution)/shard_map/ppermute | solution.py:50
  516.7 28.9 %collective-permute-start.49 = (bf16[4,2,48,1536]{3,2,1,0:T(8,128)(2,1)S(1)}, bf16[4,2,48,1536]{3,2,1,0:T(8,128)(2,1)S(1)}, u32[]{:S(2)}, u32[]{:S(2)}) collective-permute-start(bf16[4,2,48,1536]{3,2,1,0:T(8,128)(2,1)S(1)} %fusion.19), channel_id=1, source_target_pairs={{0,4},{4,0},{8,12},{12,8},{16,20},{20,16},{24,28},{28,24},{1,5},{5... | collective-permute-start | bytes 3538952 | tf_op jit(solution)/shard_map/ppermute | solution.py:53
  541.3 40.0 %collective-permute-start.57 = (bf16[4,96,768]{2,1,0:T(8,128)(2,1)S(1)}, bf16[4,96,768]{2,1,0:T(8,128)(2,1)S(1)}, u32[]{:S(2)}, u32[]{:S(2)}) collective-permute-start(bf16[4,96,768]{2,1,0:T(8,128)(2,1)S(1)} %fusion.31), channel_id=1, source_target_pairs={{0,4},{4,0},{8,12},{12,8},{16,20},{20,16},{24,28},{28,24},{1,5},{5... | collective-permute-start | bytes 1769480 | tf_op jit(solution)/shard_map/ppermute | solution.py:53
  546.1 10.2 %collective-permute-start.50 = (bf16[2,48,1536]{2,1,0:T(8,128)(2,1)S(1)}, bf16[2,48,1536]{2,1,0:T(8,128)(2,1)S(1)}, u32[]{:S(2)}, u32[]{:S(2)}) collective-permute-start(bf16[2,48,1536]{2,1,0:T(8,128)(2,1)S(1)} %get-tuple-element.217), channel_id=1, source_target_pairs={{0,8},{4,12},{8,0},{12,4},{16,24},{20,28},{24,16},{28,20},{1,9},{5... | collective-permute-start | bytes 884744 | tf_op jit(solution)/shard_map/ppermute | solution.py:56
  548.1 17.0 %collective-permute-start.52 = (bf16[2,48,1536]{2,1,0:T(8,128)(2,1)S(1)}, bf16[2,48,1536]{2,1,0:T(8,128)(2,1)S(1)}, u32[]{:S(2)}, u32[]{:S(2)}) collective-permute-start(bf16[2,48,1536]{2,1,0:T(8,128)(2,1)S(1)} %get-tuple-element.218), channel_id=1, source_target_pairs={{0,24},{4,28},{8,16},{12,20},{16,8},{20,12},{24,0},{28,4},{1,25},{... | collective-permute-start | bytes 884744 | tf_op jit(solution)/shard_map/ppermute | solution.py:56
  550.7 23.4 %collective-permute-start.51 = (bf16[2,48,1536]{2,1,0:T(8,128)(2,1)S(1)}, bf16[2,48,1536]{2,1,0:T(8,128)(2,1)S(1)}, u32[]{:S(2)}, u32[]{:S(2)}) collective-permute-start(bf16[2,48,1536]{2,1,0:T(8,128)(2,1)S(1)} %get-tuple-element.219), channel_id=1, source_target_pairs={{0,16},{4,20},{8,24},{12,28},{16,0},{20,4},{24,8},{28,12},{1,17},{... | collective-permute-start | bytes 884744 | tf_op jit(solution)/shard_map/ppermute | solution.py:56
  574.3 6.8 %collective-permute-start.53 = (bf16[48,1536]{1,0:T(8,128)(2,1)S(1)}, bf16[48,1536]{1,0:T(8,128)(2,1)S(1)}, u32[]{:S(2)}, u32[]{:S(2)}) collective-permute-start(bf16[48,1536]{1,0:T(8,128)(2,1)S(1)} %select_bitcast_fusion.5), channel_id=1, source_target_pairs={{0,2},{1,3},{2,0},{3,1},{4,6},{5,7},{6,4},{7,5},{8,10},{9,11},{10,... | collective-permute-start | bytes 442376 | tf_op jit(solution)/shard_map/ppermute | solution.py:50
  575.4 24.5 %collective-permute-start.35 = (bf16[8,56,1152]{2,1,0:T(8,128)(2,1)S(1)}, bf16[8,56,1152]{2,1,0:T(8,128)(2,1)S(1)}, u32[]{:S(2)}, u32[]{:S(2)}) collective-permute-start(bf16[8,56,1152]{2,1,0:T(8,128)(2,1)S(1)} %select_bitcast_fusion.1), channel_id=1, source_target_pairs={{0,2},{1,3},{2,0},{3,1},{4,6},{5,7},{6,4},{7,5},{8,10},{9,11},{10,... | collective-permute-start | bytes 3096584 | tf_op jit(solution)/shard_map/ppermute | solution.py:50
  581.2 20.4 %collective-permute-start.54 = (f32[24,1536]{1,0:T(8,128)S(1)}, f32[24,1536]{1,0:T(8,128)S(1)}, u32[]{:S(2)}, u32[]{:S(2)}) collective-permute-start(f32[24,1536]{1,0:T(8,128)S(1)} %slice_select_fusion), channel_id=1, source_target_pairs={{0,1},{1,0},{2,3},{3,2},{4,5},{5,4},{6,7},{7,6},{8,9},{9,8},{10,11... | collective-permute-start | bytes 442376 | tf_op jit(solution)/shard_map/ppermute | solution.py:47
  582.4 31.7 %collective-permute-start.58 = (bf16[96,768]{1,0:T(8,128)(2,1)}, bf16[96,768]{1,0:T(8,128)(2,1)}, u32[]{:S(2)}, u32[]{:S(2)}) collective-permute-start(bf16[96,768]{1,0:T(8,128)(2,1)} %get-tuple-element.226), channel_id=1, source_target_pairs={{0,8},{4,12},{8,0},{12,4},{16,24},{20,28},{24,16},{28,20},{1,9},{5... | collective-permute-start | bytes 442376 | tf_op jit(solution)/shard_map/ppermute | solution.py:56
  582.4 32.4 %collective-permute-start.60 = (bf16[96,768]{1,0:T(8,128)(2,1)}, bf16[96,768]{1,0:T(8,128)(2,1)}, u32[]{:S(2)}, u32[]{:S(2)}) collective-permute-start(bf16[96,768]{1,0:T(8,128)(2,1)} %get-tuple-element.227), channel_id=1, source_target_pairs={{0,24},{4,28},{8,16},{12,20},{16,8},{20,12},{24,0},{28,4},{1,25},{... | collective-permute-start | bytes 442376 | tf_op jit(solution)/shard_map/ppermute | solution.py:56
  585.0 29.8 %collective-permute-start.59 = (bf16[96,768]{1,0:T(8,128)(2,1)}, bf16[96,768]{1,0:T(8,128)(2,1)}, u32[]{:S(2)}, u32[]{:S(2)}) collective-permute-start(bf16[96,768]{1,0:T(8,128)(2,1)} %get-tuple-element.228), channel_id=1, source_target_pairs={{0,16},{4,20},{8,24},{12,28},{16,0},{20,4},{24,8},{28,12},{1,17},{... | collective-permute-start | bytes 442376 | tf_op jit(solution)/shard_map/ppermute | solution.py:56
  600.3 10.7 %collective-permute-start.36 = (bf16[4,56,1152]{2,1,0:T(8,128)(2,1)S(1)}, bf16[4,56,1152]{2,1,0:T(8,128)(2,1)S(1)}, u32[]{:S(2)}, u32[]{:S(2)}) collective-permute-start(bf16[4,56,1152]{2,1,0:T(8,128)(2,1)S(1)} %fusion.39), channel_id=1, source_target_pairs={{0,4},{4,0},{8,12},{12,8},{16,20},{20,16},{24,28},{28,24},{1,5},{5... | collective-permute-start | bytes 1548296 | tf_op jit(solution)/shard_map/ppermute | solution.py:53
  611.3 7.8 %collective-permute-start.37 = (bf16[56,1152]{1,0:T(8,128)(2,1)S(1)}, bf16[56,1152]{1,0:T(8,128)(2,1)S(1)}, u32[]{:S(2)}, u32[]{:S(2)}) collective-permute-start(bf16[56,1152]{1,0:T(8,128)(2,1)S(1)} %get-tuple-element.229), channel_id=1, source_target_pairs={{0,8},{4,12},{8,0},{12,4},{16,24},{20,28},{24,16},{28,20},{1,9},{5... | collective-permute-start | bytes 387080 | tf_op jit(solution)/shard_map/ppermute | solution.py:56
  611.3 7.7 %collective-permute-start.39 = (bf16[56,1152]{1,0:T(8,128)(2,1)S(1)}, bf16[56,1152]{1,0:T(8,128)(2,1)S(1)}, u32[]{:S(2)}, u32[]{:S(2)}) collective-permute-start(bf16[56,1152]{1,0:T(8,128)(2,1)S(1)} %get-tuple-element.230), channel_id=1, source_target_pairs={{0,24},{4,28},{8,16},{12,20},{16,8},{20,12},{24,0},{28,4},{1,25},{... | collective-permute-start | bytes 387080 | tf_op jit(solution)/shard_map/ppermute | solution.py:56
  614.1 8.3 %collective-permute-start.38 = (bf16[56,1152]{1,0:T(8,128)(2,1)S(1)}, bf16[56,1152]{1,0:T(8,128)(2,1)S(1)}, u32[]{:S(2)}, u32[]{:S(2)}) collective-permute-start(bf16[56,1152]{1,0:T(8,128)(2,1)S(1)} %get-tuple-element.231), channel_id=1, source_target_pairs={{0,16},{4,20},{8,24},{12,28},{16,0},{20,4},{24,8},{28,12},{1,17},{... | collective-permute-start | bytes 387080 | tf_op jit(solution)/shard_map/ppermute | solution.py:56
  623.0 1.4 collective-permute-start.40
  (78 other events, 375.7 us)

commit v3 on v2

--- a/solution.py
+++ b/solution.py
@@ -17,25 +17,6 @@
 F32 = jnp.float32
 
 
-def look_up(table, indices):
-    slots = jnp.arange(table.shape[0], dtype=jnp.int32)
-    hits = indices[..., None] == slots
-    return jnp.sum(jnp.where(hits, table, 0), axis=-1)
-
-
-def tree_layout(seg_row, parent_row):
-    slots = jnp.arange(parent_row.shape[0], dtype=jnp.int32)
-    seg_lengths = jnp.sum((seg_row[:, None] == slots).astype(jnp.int32), axis=0)
-    seg_starts = jnp.sum((seg_row[:, None] < slots).astype(jnp.int32), axis=0)
-    grand_parent = look_up(parent_row, parent_row)
-    offsets = jnp.where(slots > 0, look_up(seg_lengths, parent_row), 0) + jnp.where(
-        parent_row > 0, look_up(seg_lengths, grand_parent), 0
-    )
-    block_ids = jnp.arange(seg_row.shape[0], dtype=jnp.int32)
-    path_block = look_up(offsets, seg_row) + block_ids - look_up(seg_starts, seg_row)
-    return (path_block, look_up(parent_row, seg_row), look_up(grand_parent, seg_row))
-
-
 class Links:
     def __init__(self):
         leaf = lax.axis_index("leaf")
@@ -68,9 +49,9 @@
     )
 
 
-def after(values, done):
-    values, done = list(values), list(done)
-    return lax.optimization_barrier(tuple(values + done))[: len(values)]
+def tie(*values):
+    flat, tree = jax.tree.flatten(values)
+    return jax.tree.unflatten(tree, lax.optimization_barrier(tuple(flat)))
 
 
 def z_gather(at, block):
@@ -82,35 +63,23 @@
 
 
 def choose(bit, v, axis):
-    first, second = pick(v, 0, axis), pick(v, 1, axis)
-    return jnp.where(bit == 0, first, second), jnp.where(bit == 0, second, first)
+    return pick(v, bit, axis), pick(v, 1 - bit, axis)
 
 
 def plus(a, b):
     return a.astype(F32) + b.astype(F32)
 
 
-def z_reduce(at, g):
-    got = [at.swap_z(pick(g, at.z ^ n, 0), n) for n in (1, 2, 3)]
-    return plus(pick(g, at.z, 0), got[0]) + plus(got[1], got[2])
-
-
-def reduce_x_first(at, own, other):
-    g = plus(own, at.swap_core(other)).astype(BF)
-    keep, send = choose(at.x, g, 1)
-    g = plus(keep, at.swap_x(send)).astype(BF)
-    g = g.reshape((4, 2) + g.shape[1:])
-    keep, send = choose(at.y, g, 1)
-    return z_reduce(at, plus(keep, at.swap_y(send)).astype(BF))
-
-
-def reduce_y_first(at, own, other):
-    g = plus(own, at.swap_core(other)).astype(BF)
-    g = g.reshape((4, 2) + g.shape[1:])
-    keep, send = choose(at.y, g, 1)
-    g = z_reduce(at, plus(keep, at.swap_y(send)).astype(BF)).astype(BF)
-    keep, send = choose(at.x, g, 0)
-    return plus(keep, at.swap_x(send))
+def z_parts(at, g):
+    return pick(g, at.z, 0), [pick(g, at.z ^ n, 0) for n in (1, 2, 3)]
+
+
+def z_move(at, parts):
+    return [at.swap_z(part, n) for n, part in zip((1, 2, 3), parts)]
+
+
+def z_total(keep, got):
+    return plus(keep, got[0]) + plus(got[1], got[2])
 
 
 def to_column_half(at, half_a, half_b):
@@ -140,6 +109,85 @@
         swapped = jnp.where(low_half, pltpu.roll(part, 96, 1), pltpu.roll(part, 32, 1))
         groups.append(part * cosine + swapped * sine)
     return groups
+
+
+def column(row):
+    return jnp.broadcast_to(row, (8, row.shape[1])).T[:, :1]
+
+
+def tables_kernel(places, rows, leaf_ref, seg_ref, parent_ref, qcol_ref, qrow_ref, kcol_ref, krow_ref, flag_ref, pad_ref):
+    leaf = leaf_ref[0]
+    blocks = rows // BLOCK
+    slots = 16
+    seg = column(seg_ref[...].astype(F32))
+    lane = lax.broadcasted_iota(jnp.int32, (seg.shape[0], 128), 1).astype(F32)
+    length = jnp.sum(jnp.where(seg == lane, 1.0, 0.0), axis=0, keepdims=True)
+    start = jnp.sum(jnp.where(seg < lane, 1.0, 0.0), axis=0, keepdims=True)
+    pad_ref[...] = jnp.zeros_like(pad_ref)
+    pad_ref[0:1, 0 : parent_ref.shape[1]] = parent_ref[...].astype(F32)
+    parent_row = pad_ref[0:1, :]
+    lane = lax.broadcasted_iota(jnp.int32, (slots, 128), 1).astype(F32)
+    slot = lax.broadcasted_iota(jnp.int32, (slots, 1), 0).astype(F32)
+    parent = column(parent_row)[:slots]
+    look = lambda index, row: jnp.sum(jnp.where(index == lane, row, 0.0), axis=1, keepdims=True)
+    grand = look(parent, parent_row)
+    start = look(slot, start)
+    shift = jnp.where(slot > 0, look(parent, length), 0.0) + jnp.where(parent > 0, look(grand, length), 0.0) - start
+
+    def facts(block):
+        own = jnp.sum(jnp.where(block >= start, 1.0, 0.0), axis=0, keepdims=True) - 1.0
+        take = lambda col: jnp.sum(jnp.where(slot == own, col, 0.0), axis=0, keepdims=True)
+        return own, take(parent), take(grand), take(shift)
+
+    token = lax.broadcasted_iota(jnp.int32, (1, rows), 1)
+    zero = jnp.zeros((1, rows), F32)
+    tiles = [(leaf, leaf >= 0), (leaf, leaf < 0)] + places(leaf)
+    for t, (place, valid) in enumerate(tiles):
+        first = jnp.maximum(place, 0) * blocks
+        block = (first + lax.shift_right_logical(token, 4)).astype(F32)
+        own, one, two, move = facts(block)
+        position = (move + block) * BLOCK + (token & (BLOCK - 1)).astype(F32)
+        at = slice(t * rows, (t + 1) * rows)
+        if t < 2:
+            limit = block + (1.0 if t == 0 else 0.0)
+            lines = jnp.concatenate([own, one, two, limit, zero, zero, zero, zero], axis=0)
+            qrow_ref[:, at] = lines
+            qcol_ref[at, :] = lines.T
+        lines = jnp.concatenate(
+            [jnp.where(valid, own, -1.0), block, position, zero, zero, zero, zero, zero], axis=0
+        )
+        krow_ref[:, at] = lines
+        kcol_ref[at, :] = lines.T
+    queries = qcol_ref[pl.ds(0, 2 * blocks, stride=BLOCK), :]
+    lane = lax.broadcasted_iota(jnp.int32, (1, 128), 1)
+    for t, (place, valid) in enumerate(tiles):
+        if t < 2:
+            flag_ref[t] = 1
+            continue
+        block = (jnp.maximum(place, 0) * blocks + lane).astype(F32)
+        own = facts(block)[0]
+        allowed = (
+            ((own == queries[:, 0:1]) | (own == queries[:, 1:2]) | (own == queries[:, 2:3]))
+            & (block < queries[:, 3:4])
+            & (lane < blocks)
+            & valid
+        )
+        flag_ref[t] = jnp.max(jnp.where(allowed, 1.0, 0.0)).astype(jnp.int32)
+
+
+def tables(places, leaf, seg, parent, rows):
+    tiles = 2 + len(places(leaf))
+    total = tiles * rows
+    smem = pl.BlockSpec(memory_space=pltpu.SMEM)
+    vmem = pl.BlockSpec(memory_space=pltpu.VMEM)
+    shapes = [(2 * rows, 8), (8, 2 * rows), (total, 8), (8, total)]
+    return pl.pallas_call(
+        functools.partial(tables_kernel, places, rows),
+        in_specs=[smem, vmem, vmem],
+        out_specs=[vmem] * 4 + [smem],
+        out_shape=[jax.ShapeDtypeStruct(shape, F32) for shape in shapes] + [jax.ShapeDtypeStruct((tiles,), jnp.int32)],
+        scratch_shapes=[pltpu.VMEM((8, 128), F32)],
+    )(leaf.reshape(1), seg, parent)
 
 
 def fetch(pieces, sems):
@@ -238,7 +286,7 @@
 
 
 def middle_kernel(
-    count, size, chunk, table_ref, o_ref, x_ref, dy_ref, gain_ref, up_b_ref, down_b_ref,
+    count, size, chunk, table_ref, o_ref, x_ref, mask_ref, embed_ref, dy_ref, gain_ref, up_b_ref, down_b_ref,
     one_own, one_other, two_own, two_other,
     y_ref, b_ref, g_ref, du_ref, dh_low_ref, do_ref, dh_ref, dgain_ref, dup_b_ref, ddown_b_ref,
     out_ref, up_ref, down_ref, sems,
@@ -260,7 +308,8 @@
     copies = fetch(pieces_out + pieces_up + pieces_down, sems)
     for copy in copies[: 2 * count]:
         copy.wait()
-    h = x_ref[...].astype(F32) + jnp.dot(o_ref[...], out_ref[...], preferred_element_type=F32)
+    x = jnp.where(mask_ref[...] > 0, embed_ref[...], x_ref[...].astype(F32))
+    h = x + jnp.dot(o_ref[...], out_ref[...], preferred_element_type=F32)
     centred = h - jnp.mean(h, axis=-1, keepdims=True)
     spread = jnp.mean(centred * centred, axis=-1, keepdims=True)
     scale = lax.rsqrt(spread + EPSILON)
@@ -297,7 +346,7 @@
     do_ref[...] = matmul_t(low, out_ref[...]).astype(BF)
 
 
-def middle(table, o, x, dy, gain, up_b, down_b, one, two):
+def middle(table, o, x, mask, embed, dy, gain, up_b, down_b, one, two):
     rows, width = o.shape
     count, size, columns = one[0].shape
     chunk = two[0].shape[1]
@@ -313,7 +362,8 @@
         grid_spec=pltpu.PrefetchScalarGridSpec(
             num_scalar_prefetch=1,
             grid=(1,),
-            in_specs=[full(v.shape) for v in (o, x, dy, gain, up_b, down_b)] + [anywhere] * 4,
+            in_specs=[full((rows, v.shape[1]) if v is x or v is mask else v.shape) for v in (o, x, mask, embed, dy, gain, up_b, down_b)]
+            + [anywhere] * 4,
             out_specs=[full(shape) for shape, _ in shapes],
             scratch_shapes=[
                 pltpu.VMEM((width, width), BF),
@@ -329,7 +379,7 @@
             bytes_accessed=4 * (width * width + 4 * units * width),
             transcendentals=2 * rows * units,
         ),
-    )(table, o, x, dy, gain, up_b, down_b, one[0], one[1], two[0], two[1])
+    )(table, o, x, mask, embed, dy, gain, up_b, down_b, one[0], one[1], two[0], two[1])
 
 
 def matmul_t(a, b):
@@ -445,9 +495,13 @@
 
 
 def attend_back_kernel(
-    rows, tiles, flag_ref, qrow_ref, kcol_ref, q_ref, k_ref, v_ref, o_ref, g_ref, lse_ref,
-    cos_ref, sin_ref, dq_ref, dk_ref, dv_ref, bias_ref, acc_ref,
+    rows, first, last, flag_ref, qrow_ref, kcol_ref, q_ref, k_ref, v_ref, o_ref, g_ref, lse_ref, *refs,
 ):
+    refs = list(refs)
+    near = first == 0
+    cos_ref, sin_ref = refs[:2]
+    part_ref = refs[2] if near else None
+    dq_ref, dk_ref, dv_ref, bias_ref, acc_ref = refs[-5:]
     pair = pl.program_id(0)
     both_rows = 2 * rows
 
@@ -463,19 +517,19 @@
         up_one = qrow_ref[1:2, :]
         up_two = qrow_ref[2:3, :]
         limit = qrow_ref[3:4, :]
-        for t in range(tiles):
+        for t in range(first, last):
             if t == 1:
                 r = lax.broadcasted_iota(jnp.int32, (rows, rows), 0) // BLOCK
                 c = lax.broadcasted_iota(jnp.int32, (rows, rows), 1) // BLOCK
-                bias_ref[span(t), rows:] = jnp.where(r == c, 0.0, NEG_FILL)
+                bias_ref[span(t - first), rows:] = jnp.where(r == c, 0.0, NEG_FILL)
             else:
                 seg = kcol_ref[span(t), 0:1]
                 index = kcol_ref[span(t), 1:2]
                 ok = ((seg == own) | (seg == up_one) | (seg == up_two)) & (index < limit)
-                bias_ref[span(t), :] = jnp.where(ok, 0.0, NEG_FILL)
+                bias_ref[span(t - first), :] = jnp.where(ok, 0.0, NEG_FILL)
 
     lane = lax.broadcasted_iota(jnp.int32, (both_rows, 128), 1)
-    acc_ref[...] = jnp.zeros_like(acc_ref)
+    acc_ref[...] = part_ref[...] if near else jnp.zeros_like(acc_ref)
     queries, grads, deltas, norms = [], [], [], []
     product = (o_ref[...].astype(F32) * g_ref[...].astype(F32)).T
     for h in range(2):
@@ -484,12 +538,13 @@
         grads.append(jnp.where(mine, g_ref[...], 0).astype(BF))
         deltas.append(jnp.sum(product[h * HEAD_DIM : (h + 1) * HEAD_DIM], axis=0, keepdims=True))
         norms.append(lse_ref[pl.ds(2 * pair + h, 1), :])
-    for t in range(tiles):
+    for t in range(first, last):
+        to = span(t - first)
 
         @pl.when(flag_ref[t] == 0)
         def _():
-            dk_ref[span(t), :] = jnp.zeros((rows, 128), BF)
-            dv_ref[span(t), :] = jnp.zeros((rows, 128), BF)
+            dk_ref[to, :] = jnp.zeros((rows, 128), BF)
+            dv_ref[to, :] = jnp.zeros((rows, 128), BF)
 
         @pl.when(flag_ref[t] > 0)
         def _():
@@ -499,7 +554,7 @@
             dk = dv = None
             for h in range(2):
                 q, g = queries[h][at], grads[h][at]
-                s = matmul_t(keys, q) + bias_ref[span(t), at]
+                s = matmul_t(keys, q) + bias_ref[to, at]
                 p = jnp.exp(s - norms[h][:, at])
                 dp = matmul_t(values, g)
                 ds = (p * (dp - deltas[h][:, at])).astype(BF)
@@ -510,44 +565,149 @@
                 half = slice(h * HEAD_DIM, (h + 1) * HEAD_DIM)
                 acc_ref[half, at] += jnp.dot(keys_t[half], ds, preferred_element_type=F32)
             [dk] = turn(dk, cos_ref[span(t), :], -sin_ref[span(t), :])
-            dk_ref[span(t), :] = dk.astype(BF)
-            dv_ref[span(t), :] = dv.astype(BF)
-
-    dq = acc_ref[...].T * 0.125
-    [dq] = turn(dq, cos_ref[:both_rows, :], -sin_ref[:both_rows, :])
-    dq_ref[...] = dq.astype(BF)
-
-
-def attend_back(flags, qrow, kcol, q, k, v, o, g, lse, cosine, sine, rows):
+            dk_ref[to, :] = dk.astype(BF)
+            dv_ref[to, :] = dv.astype(BF)
+
+    if near:
+        dq = acc_ref[...].T * 0.125
+        [dq] = turn(dq, cos_ref[:both_rows, :], -sin_ref[:both_rows, :])
+        dq_ref[...] = dq.astype(BF)
+    else:
+        dq_ref[...] = acc_ref[...]
+
+
+def attend_back(first, last, flags, qrow, kcol, q, k, v, o, g, lse, cosine, sine, rows, part=None):
     width = q.shape[1]
     total = k.shape[0]
-    tiles = total // rows
+    there = (last - first) * rows
+    near = first == 0
     pair = lambda n: spec((n, 128), lambda p, f: (0, p))
+    turned = spec((128, 2 * rows), lambda p, f: (p, 0))
     fixed = lambda shape: spec(shape, lambda p, f: (0, 0))
     out = lambda n: jax.ShapeDtypeStruct((n, width), BF)
     return pl.pallas_call(
-        functools.partial(attend_back_kernel, rows, tiles),
+        functools.partial(attend_back_kernel, rows, first, last),
         grid_spec=pltpu.PrefetchScalarGridSpec(
             num_scalar_prefetch=1,
             grid=(width // 128,),
             in_specs=[
                 fixed(qrow.shape), fixed(kcol.shape), pair(2 * rows), pair(total), pair(total),
                 pair(2 * rows), pair(2 * rows), fixed(lse.shape), fixed(cosine.shape), fixed(sine.shape),
-            ],
-            out_specs=[pair(2 * rows), pair(total), pair(total)],
+            ] + ([turned] if near else []),
+            out_specs=[pair(2 * rows) if near else turned, pair(there), pair(there)],
             scratch_shapes=[
-                pltpu.VMEM((total, 2 * rows), F32),
+                pltpu.VMEM((there, 2 * rows), F32),
                 pltpu.VMEM((128, 2 * rows), F32),
             ],
         ),
-        out_shape=[out(2 * rows), out(total), out(total)],
+        out_shape=[out(2 * rows) if near else jax.ShapeDtypeStruct((width, 2 * rows), F32), out(there), out(there)],
         compiler_params=pltpu.CompilerParams(vmem_limit_bytes=VMEM_LIMIT),
         cost_estimate=pl.CostEstimate(
-            flops=40 * rows * total * width,
-            bytes_accessed=8 * (total + rows) * width,
-            transcendentals=2 * rows * total * width // HEAD_DIM,
+            flops=40 * rows * there * width,
+            bytes_accessed=8 * (there + rows) * width,
+            transcendentals=2 * rows * there * width // HEAD_DIM,
         ),
-    )(flags, qrow, kcol, q, k, v, o, g, lse, cosine, sine)
+    )(flags, qrow, kcol, q, k, v, o, g, lse, cosine, sine, *([part] if near else []))
+
+
+def fold_kernel(
+    count, size, rows, first, table_ref, dk_ref, dv_ref, x_ref, mask_ref, embed_ref, gain_ref, own_hbm, other_hbm, *refs,
+):
+    near = first == 0
+    refs = list(refs)
+    dq_ref, dh_ref = refs[:2] if near else (None, None)
+    outs = refs[2:] if near else refs
+    if near:
+        da_ref, dgain_ref, clean_ref, noisy_ref, dembed_ref, acc_ref, own_ref, other_ref, sems = outs
+    else:
+        da_ref, dgain_ref, acc_ref, own_ref, other_ref, sems = outs
+    tile = pl.program_id(0)
+
+    @pl.when(tile == 0)
+    def _():
+        pieces = []
+        for hbm, ref in ((own_hbm, own_ref), (other_hbm, other_ref)):
+            spots = placed(ref, count, size, table_ref, 0)
+            pieces += [(hbm.at[n, pl.ds(0, size), :], spots[n]) for n in range(count)]
+        for copy in fetch(pieces, sems):
+            copy.wait()
+        dgain_ref[...] = jnp.zeros_like(dgain_ref)
+
+    half = own_ref.shape[1] // 3
+    cuts = [slice(n * half, (n + 1) * half) for n in range(3)]
+    da = None
+    for n, w_ref in enumerate((own_ref, other_ref)):
+        part = matmul_t(dk_ref[:, cuts[n]], w_ref[:, cuts[1]]) + matmul_t(dv_ref[:, cuts[n]], w_ref[:, cuts[2]])
+        da = part if da is None else da + part
+    acc_ref[...] = da
+    if near:
+
+        @pl.when(tile < 2)
+        def _():
+            acc_ref[...] += matmul_t(dq_ref[:, cuts[0]], own_ref[:, cuts[0]]) + matmul_t(
+                dq_ref[:, cuts[1]], other_ref[:, cuts[0]]
+            )
+
+    da = acc_ref[...]
+    da_ref[...] = da.astype(BF)
+    x = jnp.where(mask_ref[...] > 0, embed_ref[...], x_ref[...].astype(F32))
+    centred = x - jnp.mean(x, axis=-1, keepdims=True)
+    scale = lax.rsqrt(jnp.mean(centred * centred, axis=-1, keepdims=True) + EPSILON)
+    hat = centred * scale
+    dgain_ref[...] += jnp.sum(da * hat, axis=0, keepdims=True)
+    if near:
+
+        @pl.when(tile == 0)
+        def _():
+            clean_ref[...] = da
+
+        @pl.when(tile == 1)
+        def _():
+            noisy = dh_ref[...] + norm_back(hat, scale, gain_ref[...], da)
+            noisy_ref[...] = noisy
+            dembed_ref[...] = jnp.sum(jnp.where(mask_ref[...] > 0, noisy, 0.0), axis=0, keepdims=True)
+
+
+def fold(table, first, last, dk, dv, x_all, mask, embed, gain, own, other, rows, dq=None, dh=None):
+    width = x_all.shape[1]
+    there = (last - first) * rows
+    near = first == 0
+    count = own.shape[0]
+    size = width // count
+    columns = own.shape[2]
+    whole = lambda shape: spec(shape, lambda t, i: (0, 0))
+    moved = lambda n: spec((rows, n), lambda t, i: (t, 0))
+    shifted = lambda n: spec((rows, n), lambda t, i: (t + first, 0))
+    early = lambda n: spec((rows, n), lambda t, i: (jnp.minimum(t, 1), 0))
+    second = lambda n: spec((rows, n), lambda t, i: (1, 0))
+    anywhere = pl.BlockSpec(memory_space=pl.ANY)
+    line = jax.ShapeDtypeStruct((1, width), F32)
+    tile = jax.ShapeDtypeStruct((rows, width), F32)
+    return pl.pallas_call(
+        functools.partial(fold_kernel, count, size, rows, first),
+        grid_spec=pltpu.PrefetchScalarGridSpec(
+            num_scalar_prefetch=1,
+            grid=(last - first,),
+            in_specs=[
+                moved(width), moved(width), shifted(width), shifted(1), whole((1, width)), whole((1, width)), anywhere, anywhere,
+            ] + ([early(width), second(width)] if near else []),
+            out_specs=[moved(width), whole((1, width))]
+            + ([whole((rows, width)), whole((rows, width)), whole((1, width))] if near else []),
+            scratch_shapes=[
+                pltpu.VMEM((rows, width), F32),
+                pltpu.VMEM((width, columns), BF),
+                pltpu.VMEM((width, columns), BF),
+                pltpu.SemaphoreType.DMA((2 * count,)),
+            ],
+        ),
+        out_shape=[jax.ShapeDtypeStruct((there, width), BF), line] + ([tile, tile, line] if near else []),
+        compiler_params=pltpu.CompilerParams(vmem_limit_bytes=VMEM_LIMIT),
+        cost_estimate=pl.CostEstimate(
+            flops=4 * there * width * width,
+            bytes_accessed=2 * (4 * there * width + 3 * width * width),
+            transcendentals=0,
+        ),
+    )(table, dk, dv, x_all, mask, embed, gain, own, other, *([dq, dh] if near else []))
 
 
 def normalise(values):
@@ -607,11 +767,22 @@
     return jnp.stack([a, b], 2).reshape(a.shape[0], -1)
 
 
+def lower_in_chain(leaf):
+    z, y = lax.shift_right_logical(leaf, 1), leaf & 1
+    below = [((2 * (z - s) + at), z >= s) for s in (1, 2, 3) for at in (y, 1 - y)]
+    return below[:2] + [(2 * z, y == 1)] + below[2:]
+
+
 class Chain:
+    near = 5
+
     def __init__(self, rows):
         self.at = Links()
         self.rows = rows
         self.core = self.at.core
+
+    def lower(self, leaf):
+        return lower_in_chain(leaf)
 
     def places(self):
         at = self.at
@@ -622,74 +793,62 @@
         columns = jnp.where(jnp.arange(16) % 2 == 0, at.core, 1 - at.core)
         return jnp.stack([first, first ^ (8 * at.core), yzx.reshape(16), columns]).astype(jnp.int32)
 
-    def gather(self, hid, w_qkv, w_out, w_up, w_down, vectors):
+    def first_gather(self, hid, w_qkv, w_out, w_up, w_down, vectors):
         at = self.at
-        chunk, cut = w_down.shape[0], w_out.shape[1] // 2
-        up_a, up_b = halves_of_units(w_up, chunk)
-        one_a = jnp.concatenate([w_out[:, :cut], up_a], axis=1)
-        one_b = jnp.concatenate([w_out[:, cut:], up_b], axis=1)
+        few, chunk, cut = w_qkv.shape[0], w_down.shape[0], w_out.shape[1] // 2
         qkv_a, qkv_b = halves_of_heads(w_qkv)
         row = jnp.pad(vectors[None], ((0, 7), (0, qkv_a.shape[1] - vectors.shape[0])))
         qkv_a, qkv_b = (jnp.concatenate([v, row], axis=0) for v in (qkv_a, qkv_b))
         block = to_column_half(at, qkv_a, qkv_b)
-        few = w_qkv.shape[0]
         block = jnp.concatenate(
             [block[:few], block[few + 8 : 2 * few + 8], block[few : few + 8], block[2 * few + 8 :]], axis=0
         )[None]
         beside = at.swap_y(hid, [(i, i + 1) for i in range(0, 8, 2)])
-        down_two = jnp.stack([w_down, at.swap_x(w_down)])[None]
+        down_two = at.swap_x(w_down)
+        block, hid_up = tie(block, hid)
+        line = z_gather(at, block)
+        line, hid_up = tie(line, hid_up)
+        first_hop = at.up(hid_up, 0, 2)
+        plane = jnp.concatenate([line, at.swap_y(line)], axis=0)
+        up_a, up_b = halves_of_units(w_up, chunk)
+        one_a = jnp.concatenate([w_out[:, :cut], up_a], axis=1)
+        one_b = jnp.concatenate([w_out[:, cut:], up_b], axis=1)
         one = to_column_half(at, one_a, one_b)[None]
-        line = z_gather(at, block)
-        [cur] = after([hid], [line])
-        hops = [at.up(cur, 0, 2)]
-        plane = jnp.concatenate([line, at.swap_y(line)], axis=0)
-        [cur, plane] = after([hops[0], plane], [beside])
-        hops.append(at.up(cur, 1, 2))
-        across = [at.swap_y(cur, [(i, i ^ 1) for i in range(2, 8)])]
-        qkv = jnp.concatenate([plane, at.swap_x(plane)], axis=0)
-        [cur] = after([hops[1]], [across[0]])
-        hops.append(at.up(cur, 2, 2))
-        across.append(at.swap_y(cur, [(i, i ^ 1) for i in range(4, 8)]))
-        [last, one, qkv] = after([hops[2], one, qkv], [across[1]])
-        across.append(at.swap_y(last, [(i, i ^ 1) for i in range(6, 8)]))
+        down_two = jnp.stack([w_down, down_two])[None]
+        first_hop, plane, beside, one, down_two = tie(first_hop, plane, beside, one, down_two)
+        other = at.swap_x(plane)
+        second_hop = at.up(first_hop, 1, 2)
+        first_over = at.swap_y(first_hop, [(i, i ^ 1) for i in range(2, 8)])
+        second_hop, first_over, one = tie(second_hop, first_over, one)
+        third_hop = at.up(second_hop, 2, 2)
+        second_over = at.swap_y(second_hop, [(i, i ^ 1) for i in range(4, 8)])
+        qkv = jnp.concatenate([plane, other], axis=0)
+        third_hop, second_over, qkv, one = tie(third_hop, second_over, qkv, one)
+        third_over = at.swap_y(third_hop, [(i, i ^ 1) for i in range(6, 8)])
         qkv_both = (qkv, at.swap_core(qkv))
         line = z_gather(at, one)
-        [line, down_two] = after([line, down_two], [across[2], qkv_both[1]])
-        plane = jnp.concatenate([line, at.swap_y(line)], axis=0)
-        down_line = z_gather(at, down_two)
-        [plane, down_line] = after([plane, down_line], [plane, down_line])
-        one = jnp.concatenate([plane, at.swap_x(plane)], axis=0)
-        down = jnp.concatenate([down_line, at.swap_y(down_line)], axis=0)
-        down = down.reshape((16,) + w_down.shape)
-        one_both = (one, at.swap_core(one))
-        down_both = (down, at.swap_core(down))
+        third_over, qkv_both, line = tie(third_over, qkv_both, line)
         m = 2 * few
         vec = jnp.concatenate([qkv[:, m, : vectors.shape[0]], qkv[:, m + 8, : vectors.shape[0]]], axis=1)
         order = (self.places()[0][None, :] == jnp.arange(16)[:, None]).astype(BF)
         vec = mm(order, vec).reshape(32, -1)
-        lower = []
-        for n in range(3):
-            lower += [hops[n], across[n]]
-        return lower + [beside], qkv_both, one_both, down_both, vec
-
-    def tile_leaves(self):
-        z, y = self.at.z, self.at.y
-        found = []
-        for s in (1, 2, 3):
-            found += [(2 * (z - s) + y, z >= s), (2 * (z - s) + 1 - y, z >= s)]
-        found.append((2 * z, y == 1))
-        return found
-
-    def tree_sum(self, own, parts):
+        lower = [first_hop, first_over, beside, second_hop, second_over, third_hop, third_over]
+        return lower, qkv_both, vec, (line, down_two)
+
+    def second_start(self, state):
+        line, down_two = state
+        return jnp.concatenate([line, self.at.swap_y(line)], axis=0), z_gather(self.at, down_two)
+
+    def second_go_on(self, state):
+        plane, line = state
         at = self.at
-        low = [at.swap_y(parts[6], [(i, i - 1) for i in range(1, 8, 2)])]
-        for s in (1, 2, 3):
-            pairs = [(i, i ^ 1) for i in range(2 * s, 8)]
-            low.append(at.swap_y(parts[2 * s - 1], pairs))
-        cur = plus(parts[4], low[3])
-        for s in (2, 1):
-            cur = at.down(cur.astype(BF), s + 1, 3).astype(F32) + plus(parts[2 * s - 2], low[s])
-        return own + at.down(cur.astype(BF), 1, 3).astype(F32) + low[0].astype(F32)
+        one = jnp.concatenate([plane, at.swap_x(plane)], axis=0)
+        down = jnp.concatenate([line, at.swap_y(line)], axis=0)
+        return one, down.reshape((16,) + down.shape[2:])
+
+    def second_end(self, state):
+        one, down = state
+        return (one, self.at.swap_core(one)), (down, self.at.swap_core(down))
 
     def unit_bias(self, bias, chunk):
         a, b = halves_of_units(bias[None], chunk)
@@ -700,90 +859,156 @@
         b = jnp.where(self.core == 0, other, own)
         return units_of_halves(a, b, chunk)[0]
 
-    def sum_down(self, own, other):
-        shape = (8, 2, own.shape[0] // 16, own.shape[1])
-        return reduce_x_first(self.at, own.reshape(shape), other.reshape(shape))
-
-    def sum_up(self, own, other, chunk):
-        shape = (8, 2, own.shape[0] // 16, own.shape[1])
-        g = reduce_y_first(self.at, own.reshape(shape), other.reshape(shape))
+    def backward(self, run):
+        at = self.at
+        rows = self.rows
+        cores = lambda g: (8, 2, g.shape[0] // 16, g.shape[1])
+        down_other, up_other = run.feed_other()
+        down_got, up_got = at.swap_core(down_other), at.swap_core(up_other)
+        down_own, up_own, out_own, out_other = run.feed_own(self)
+        down = plus(down_own, down_got).astype(BF).reshape(cores(down_own))
+        up = plus(up_own, up_got).astype(BF)
+        up = up.reshape((4, 2, 2, up.shape[0] // 16, up.shape[1]))
+        down_keep, down_send = choose(at.x, down, 1)
+        up_keep, up_send = choose(at.y, up, 1)
+        (down_keep, down_send, up_keep, up_send, out_own, out_other, run.grad_mixed) = tie(
+            down_keep, down_send, up_keep, up_send, out_own, out_other, run.grad_mixed
+        )
+        down_got, up_got, out_got = at.swap_x(down_send), at.swap_y(up_send), at.swap_core(out_other)
+        far = run.far_tiles()
+        down_got, up_got, out_got, far = tie(down_got, up_got, out_got, far)
+        far_da, far_gain = run.far_fold(far)
+        down = plus(down_keep, down_got).astype(BF)
+        down = down.reshape((4, 2) + down.shape[1:])
+        down_keep, down_send = choose(at.y, down, 1)
+        up = plus(up_keep, up_got).astype(BF)
+        up_keep, up_send = z_parts(at, up)
+        out = plus(out_own, out_got).astype(BF)
+        out_keep, out_send = choose(at.x, out, 1)
+        tiles = [far_da[n * rows : (n + 1) * rows] for n in range(4)]
+        (down_keep, down_send, up_keep, up_send, out_keep, out_send, tiles, far) = tie(
+            down_keep, down_send, up_keep, up_send, out_keep, out_send, tiles, far
+        )
+        down_got, up_got, out_got = at.swap_y(down_send), z_move(at, up_send), at.swap_x(out_send)
+        third = at.swap_y(tiles[3], [(i, i ^ 1) for i in range(6, 8)])
+        second = at.swap_y(tiles[1], [(i, i ^ 1) for i in range(4, 8)])
+        near = run.near_tiles(far)
+        down_got, up_got, out_got, third, second, near, tiles = tie(
+            down_got, up_got, out_got, third, second, near, tiles
+        )
+        down = plus(down_keep, down_got).astype(BF)
+        down_keep, down_send = z_parts(at, down)
+        up = z_total(up_keep, up_got).astype(BF)
+        up_keep, up_send = choose(at.x, up, 0)
+        out = plus(out_keep, out_got).astype(BF)
+        out = out.reshape((4, 2) + out.shape[1:])
+        out_keep, out_send = choose(at.y, out, 1)
+        cur = plus(tiles[2], third).astype(BF)
+        (down_keep, down_send, up_keep, up_send, out_keep, out_send, cur, near) = tie(
+            down_keep, down_send, up_keep, up_send, out_keep, out_send, cur, near
+        )
+        cur = at.down(cur, 3, 3)
+        down_got, up_got, out_got = z_move(at, down_send), at.swap_x(up_send), at.swap_y(out_send)
+        near_da, clean, vec = run.near_fold(near, far_gain)
+        near_da, clean, vec, cur = tie(near_da, clean, vec, cur)
+        first = at.swap_y(near_da[3 * rows : 4 * rows], [(i, i ^ 1) for i in range(2, 8)])
+        beside = at.swap_y(near_da[4 * rows : 5 * rows], [(i, i - 1) for i in range(1, 8, 2)])
+        cur = (plus(tiles[0], second) + cur.astype(F32)).astype(BF)
+        other = run.qkv_other(vec, self)
+        other, cur = tie(other, cur)
+        cur = at.down(cur, 2, 3)
+        other_got = [at.swap_core(v) for v in other]
+        own = run.qkv_own(vec, self)
+        other_got, own, first, cur, beside, down_got, up_got, out_got = tie(
+            other_got, own, first, cur, beside, down_got, up_got, out_got
+        )
+        a, b = (plus(v, got).astype(BF) for v, got in zip(own, other_got))
+        b = b.reshape((4, 2) + b.shape[1:])
+        a_keep, a_send = choose(at.x, a, 1)
+        b_keep, b_send = choose(at.y, b, 1)
+        cur = (plus(near_da[2 * rows : 3 * rows], first) + cur.astype(F32)).astype(BF)
+        out = plus(out_keep, out_got).astype(BF)
+        out_keep, out_send = z_parts(at, out)
+        a_keep, a_send, b_keep, b_send, cur, out_send = tie(a_keep, a_send, b_keep, b_send, cur, out_send)
+        a_got, b_got, cur, out_got = at.swap_x(a_send), at.swap_y(b_send), at.down(cur, 1, 3), z_move(at, out_send)
+        sum_down = z_total(down_keep, down_got)
+        sum_up = self.join_units(plus(up_keep, up_got), run.chunk)
+        a_got, b_got, cur, out_got = tie(a_got, b_got, cur, out_got)
+        a = plus(a_keep, a_got).astype(BF)
+        a = a.reshape((4, 2) + a.shape[1:])
+        a_keep, a_send = choose(at.y, a, 1)
+        b_keep, b_send = z_parts(at, plus(b_keep, b_got).astype(BF))
+        a_keep, a_send, b_keep, b_send = tie(a_keep, a_send, b_keep, b_send)
+        a_got, b_got = at.swap_y(a_send), z_move(at, b_send)
+        grad_hidden = run.last(clean + cur.astype(F32) + beside.astype(F32))
+        sum_out = jnp.concatenate(from_column_half(at, z_total(out_keep, out_got)), axis=1)
+        a_got, b_got = tie(a_got, b_got)
+        a_keep, a_send = z_parts(at, plus(a_keep, a_got).astype(BF))
+        b_keep, b_send = choose(at.x, z_total(b_keep, b_got).astype(BF), 0)
+        a_keep, a_send, b_keep, b_send = tie(a_keep, a_send, b_keep, b_send)
+        a_got, b_got = z_move(at, a_send), at.swap_x(b_send)
+        a_got, b_got = tie(a_got, b_got)
+        m = run.few * 2
+        a, b = z_total(a_keep, a_got), plus(b_keep, b_got)
+        rest = jnp.concatenate([a[:m], b], axis=1)
+        sum_qkv = heads_of_halves(*from_column_half(at, rest))
+        return sum_down, sum_up, sum_out, sum_qkv, a[m, : run.vectors], grad_hidden
+
+    def join_units(self, g, chunk):
         return units_of_halves(*from_column_half(self.at, g), chunk)
 
-    def sum_out(self, g):
-        at = self.at
+    def out_pieces(self, g):
         half = g.shape[0] // 2
-        g = jnp.where(at.core == 0, g, jnp.concatenate([g[half:], g[:half]], axis=0))
+        g = jnp.where(self.core == 0, g, jnp.concatenate([g[half:], g[:half]], axis=0))
         g = g.reshape(8, 2, g.shape[0] // 16, 2, g.shape[1] // 2)
-        own, other = choose(at.core, g, 3)
-        a, b = from_column_half(at, reduce_x_first(at, own, other))
-        return jnp.concatenate([a, b], axis=1)
-
-    def sum_qkv(self, own, other, vec):
-        at = self.at
-        m = own.shape[0] // 16
-        shape = (8, 2, m, own.shape[1])
+        return choose(self.core, g, 3)
+
+    def qkv_pieces(self, q, k, v, vec, other):
+        m = q.shape[0] // 16
+        a = jnp.concatenate([q, k[:, : k.shape[1] // 3]], axis=1).reshape(8, 2, m, -1)
+        b = jnp.concatenate([k[:, k.shape[1] // 3 :], v], axis=1).reshape(8, 2, m, -1)
         n = vec.shape[1]
-        rows = jnp.pad(vec.astype(BF).reshape(8, 2, 2, 1, n), ((0, 0),) * 3 + ((0, 7), (0, own.shape[1] - n)))
-        mine, its = choose(at.core, rows, 2)
-        g = reduce_x_first(
-            at,
-            jnp.concatenate([own.reshape(shape), mine], axis=2),
-            jnp.concatenate([other.reshape(shape), its], axis=2),
-        )
-        return heads_of_halves(*from_column_half(at, g[:m])), g[m, :n]
+        rows = pick(vec.astype(BF).reshape(8, 2, 2, n), 1 - self.core if other else self.core, 2)[:, :, None]
+        rows = jnp.pad(rows, ((0, 0), (0, 0), (0, 7), (0, a.shape[3] - n)))
+        return [jnp.concatenate([a, rows], axis=2), b]
 
 
 AXES = ("leaf", "fsdp")
-
-
-def in_place(places, w, rows):
-    count = w.shape[0]
-    if count == 1:
-        return w[0]
-    size = rows // count
-    out = jnp.zeros((rows, w.shape[2]), w.dtype)
-    for n in range(count):
-        out = lax.dynamic_update_slice(out, w[n, :size], (places[n] * size, 0))
-    return out
 
 
 class Whole:
     def __init__(self, rows, leaves, devices):
         self.rows, self.leaves, self.devices = rows, leaves, devices
         self.leaf = lax.axis_index("leaf")
+        self.near = 2 + (leaves - 1) // 2
+
+    def lower(self, leaf):
+        return [(leaf - s, leaf >= s) for s in range(1, self.leaves)]
 
     def places(self):
         return jnp.array([[0, 0], [0, 0], [0, 0], [0, 1]], jnp.int32)
 
-    def tile_leaves(self):
-        found = []
-        for s in range(1, self.leaves):
-            place = self.leaf - s
-            found.append((jnp.maximum(place, 0), place >= 0))
-        return found
-
-    def tree_sum(self, own, parts):
-        every = jnp.stack([own.astype(BF)] + [p for p in parts])
-        order = [pick(every, (self.leaf - t) % self.leaves, 0) for t in range(self.leaves)]
-        every = jnp.concatenate(order, axis=0)
-        return lax.psum_scatter(every, "leaf", scatter_dimension=0, tiled=True).astype(F32)
-
-    def gather(self, hid, w_qkv, w_out, w_up, w_down, vectors):
+    def first_gather(self, hid, w_qkv, w_out, w_up, w_down, vectors):
         tree = lax.all_gather(hid, "leaf", axis=0, tiled=False)
-        lower = [pick(tree, leaf, 0) for leaf, _ in self.tile_leaves()]
+        lower = [pick(tree, jnp.maximum(leaf, 0), 0) for leaf, _ in self.lower(self.leaf)]
         every = lambda w: lax.all_gather(w, AXES, axis=0, tiled=True)
-        up_w, down_w, out_w = every(w_up), every(w_down), every(w_out)
+        qkv = tuple(v[None] for v in halves_of_heads(every(w_qkv)))
+        return lower, qkv, every(vectors[None]), (every(w_out), every(w_up), every(w_down))
+
+    def second_start(self, state):
+        return state
+
+    def second_go_on(self, state):
+        return state
+
+    def second_end(self, state):
+        out_w, up_w, down_w = state
         half, cut = down_w.shape[0] // 2, out_w.shape[1] // 2
-        return (
-            lower,
-            tuple(v[None] for v in halves_of_heads(every(w_qkv))),
-            tuple(
-                jnp.concatenate([out_w[:, n * cut : (n + 1) * cut], up_w[:, n * half : (n + 1) * half]], axis=1)[None]
-                for n in range(2)
-            ),
-            tuple(down_w[None, n * half : (n + 1) * half] for n in range(2)),
-            every(vectors[None]),
+        one = tuple(
+            jnp.concatenate([out_w[:, n * cut : (n + 1) * cut], up_w[:, n * half : (n + 1) * half]], axis=1)[None]
+            for n in range(2)
         )
+        return one, tuple(down_w[None, n * half : (n + 1) * half] for n in range(2))
 
     def unit_bias(self, bias, chunk):
         half = bias.shape[0] // 2
@@ -795,17 +1020,38 @@
     def scatter(self, g):
         return lax.psum_scatter(g.astype(F32), AXES, scatter_dimension=0, tiled=True)
 
-    def sum_down(self, own, other):
-        return self.scatter(jnp.concatenate([own, other], axis=0))
-
-    def sum_up(self, own, other, chunk):
-        return self.scatter(jnp.concatenate([own, other], axis=1))
-
-    def sum_out(self, g):
-        return self.scatter(g)
-
-    def sum_qkv(self, own, other, vec):
-        return self.scatter(heads_of_halves(own, other)), self.scatter(vec)[0]
+    def out_pieces(self, g):
+        return g, g
+
+    def qkv_pieces(self, q, k, v, vec, other):
+        return [jnp.concatenate([q, k, v], axis=1), vec]
+
+    def backward(self, run):
+        rows = self.rows
+        down_other, up_other = run.feed_other()
+        down_own, up_own, out, _ = run.feed_own(self)
+        far = run.far_tiles()
+        far_da, far_gain = run.far_fold(far)
+        near = run.near_tiles(far)
+        near_da, clean, vec = run.near_fold(near, far_gain)
+        own, vec = run.qkv_own(vec, self)
+        other, _ = run.qkv_other(vec, self)
+        tiles = jnp.concatenate([near_da[:rows], near_da[2 * rows :], far_da], axis=0)
+        tiles = tiles.reshape((self.leaves, rows) + tiles.shape[1:])
+        order = [pick(tiles, (self.leaf - n) % self.leaves, 0) for n in range(self.leaves)]
+        total = lax.psum_scatter(jnp.concatenate(order, axis=0), "leaf", scatter_dimension=0, tiled=True)
+        return (
+            self.scatter(jnp.concatenate([down_own, down_other], axis=0)),
+            self.scatter(jnp.concatenate([up_own, up_other], axis=1)),
+            self.scatter(out),
+            self.scatter(heads_of_halves(own, other)),
+            self.scatter(vec)[0],
+            run.last(total.astype(F32)),
+        )
+
+
+class Backward:
+    pass
 
 
 def shards(
@@ -828,120 +1074,102 @@
 ):
     rows = hidden.shape[1]
     width = hidden.shape[2]
+    half = width // 2
     devices = leaves * groups
     net = Chain(rows) if (leaves, groups) == (8, 4) else Whole(rows, leaves, devices)
     chunk = w_down.shape[0]
     few = ln1_gain.shape[0]
+    leaf = lax.axis_index("leaf")
 
     hid = hidden[0]
+    query_cols, query_rows, key_cols, key_rows, flags = tables(net.lower, leaf, seg_blocks, parents, rows)
+    tiles = flags.shape[0]
+    lanes = jnp.arange(128, dtype=jnp.int32)
+    exponent = (lanes % (HEAD_DIM // 2)).astype(F32) * (-math.log(10000.0) / (HEAD_DIM // 2))
+    angles = key_cols[:, 2:3] * jnp.exp(exponent)
+    cosine = jnp.cos(angles)
+    sine = jnp.sin(angles) * jnp.where((lanes % HEAD_DIM) < HEAD_DIM // 2, -1.0, 1.0)
+    places = net.places()
+    mask = jnp.pad(noise_mask[0].astype(F32)[:, None], ((rows, (tiles - 2) * rows), (0, 0)))
+
     vectors = jnp.concatenate([ln1_gain, ln2_gain, down_bias, mask_embed, up_bias])
-    lower, qkv_w, one_w, down_w, vec = net.gather(hid, w_qkv, w_out, w_up, w_down, vectors)
-    places = net.places()
+    lower, qkv_w, vec, coming = net.first_gather(hid, w_qkv, w_out, w_up, w_down, vectors)
     gain_one, gain_two, down_b, embed = (
         vec[:, n * few : (n + 1) * few].reshape(1, width).astype(F32) for n in range(4)
     )
-    up_b = net.unit_bias(vec[:, 4 * few :].reshape(-1).astype(F32), chunk)
-
-    blocks = rows // BLOCK
-    leaf = lax.axis_index("leaf")
-    seg_row = seg_blocks[0]
-    path_block, first_up, second_up = tree_layout(seg_row, parents[0])
-    table = jnp.stack([seg_row, path_block, jnp.arange(seg_row.shape[0], dtype=jnp.int32), first_up, second_up])
-    table = table.reshape(5, leaves, blocks)
-    own = pick(table, leaf, 1)
-    tiles = [own, own.at[0].set(-1)]
-    for place, valid in net.tile_leaves():
-        tile = pick(table, jnp.maximum(place, 0), 1)
-        tiles.append(tile.at[0].set(jnp.where(valid, tile[0], -1)))
-    keys = jnp.stack(tiles, axis=1)
-    limit = jnp.concatenate([own[2] + 1, own[2]])
-    queries = [jnp.tile(own[n], 2) for n in (0, 3, 4)] + [limit]
-    seg_k, index_k = keys[0].reshape(1, -1), keys[2].reshape(1, -1)
-    allowed = (
-        (seg_k == queries[0][:, None]) | (seg_k == queries[1][:, None]) | (seg_k == queries[2][:, None])
-    ) & (index_k < limit[:, None])
-    flags = jnp.any(allowed.reshape(2 * blocks, -1, blocks), axis=(0, 2)).astype(jnp.int32)
-    flags = flags.at[:2].set(1)
-    per_token = lambda v: jnp.repeat(v, BLOCK, axis=-1)
-    query_rows = per_token(jnp.stack(queries + queries))
-    key_rows = per_token(jnp.concatenate([seg_k, index_k] * 4))
-    query_cols = query_rows.T
-    key_cols = key_rows.T
-
-    lanes = jnp.arange(128, dtype=jnp.int32)
-    exponent = (lanes % (HEAD_DIM // 2)).astype(F32) * (-math.log(10000.0) / (HEAD_DIM // 2))
-    positions = (keys[1][:, :, None] * BLOCK + jnp.arange(BLOCK, dtype=jnp.int32)).reshape(-1, 1)
-    angles = positions.astype(F32) * jnp.exp(exponent)
-    cosine = jnp.cos(angles)
-    sine = jnp.sin(angles) * jnp.where((lanes % HEAD_DIM) < HEAD_DIM // 2, -1.0, 1.0)
-
-    masked = (noise_mask[0] == 1)[:, None]
+    up_b = jnp.concatenate(net.unit_bias(vec[:, 4 * few :].reshape(-1).astype(F32), chunk), axis=0)
     x_all = jnp.concatenate([hid, hid] + lower, axis=0)
-    swapped = jnp.pad(noise_mask[0][:, None], ((rows, x_all.shape[0] - 2 * rows), (0, 0)))
+    x_all, coming, cosine, sine = tie(x_all, coming, cosine, sine)
+    coming = net.second_start(coming)
     a_all, query, key, value = project(
-        places, x_all, swapped, embed, gain_one, qkv_w[0], qkv_w[1], cosine, sine, rows
+        places, x_all, mask, embed, gain_one, qkv_w[0], qkv_w[1], cosine, sine, rows
     )
+    coming, query, a_all = tie(coming, query, a_all)
+    coming = net.second_go_on(coming)
     mixed, log_norm = attend(flags, query_cols, key_rows, query, key, value, rows)
-    noisy = jnp.where(masked, embed.astype(BF), hid)
-    stream_low = jnp.concatenate([hid, noisy], axis=0)
-    stream = stream_low.astype(F32)
+    coming, mixed = tie(coming, mixed)
+    one_w, down_w = net.second_end(coming)
+    norm_rows = log_norm.T
     grad_two = cotangent[0].reshape(2 * rows, width)
     (
         output, normed_two, act, grad_pre, grad_one, grad_mixed, grad_after, grad_gain_two, grad_up_b, grad_down_b,
-    ) = middle(places, mixed, stream_low, grad_two, gain_two, jnp.concatenate(up_b, axis=0), down_b, one_w, down_w)
+    ) = middle(places, mixed, x_all, mask, embed, grad_two, gain_two, up_b, down_b, one_w, down_w)
     output = output.reshape(1, 2, rows, width)
     units = act.shape[1] // 2
-    two = lambda v: (v[:, :units], v[:, units:])
-    grad_down_w = [t_mm(v, grad_two).astype(BF) for v in two(act)]
-    grad_up_w = [t_mm(normed_two, v).astype(BF) for v in two(grad_pre)]
-    sum_down = net.sum_down(*grad_down_w)
-    sum_up = net.sum_up(*grad_up_w, chunk)
-
-    grad_out_w = t_mm(mixed, grad_one).astype(BF)
-    sum_out = net.sum_out(grad_out_w)
-    grad_q, grad_k, grad_v = attend_back(
-        flags, query_rows, key_cols, query, key, value, mixed, grad_mixed, log_norm.T, cosine, sine, rows
-    )
-    half = width // 2
-    qkv_w = [in_place(places[0], w, width) for w in qkv_w]
-    grad_a_kv = None
-    grad_a_q = None
-    grad_qkv_w = []
-    for n in range(2):
-        cut = slice(n * half, (n + 1) * half)
-        pieces = (grad_k[:, cut], grad_v[:, cut])
-        kv = jnp.concatenate(pieces, axis=1)
-        part = mm_t(kv, qkv_w[n][:, half:])
-        grad_a_kv = part if grad_a_kv is None else grad_a_kv + part
-        part = mm_t(grad_q[:, cut], qkv_w[n][:, :half])
-        grad_a_q = part if grad_a_q is None else grad_a_q + part
-        grad_qkv_w.append(
-            jnp.concatenate(
-                [t_mm(a_all[: 2 * rows], grad_q[:, cut]).astype(BF), t_mm(a_all, kv).astype(BF)], axis=1
-            )
+
+    run = Backward()
+    run.chunk, run.few, run.vectors, run.grad_mixed = chunk, few, vectors.shape[0], grad_mixed
+    cut = net.near
+
+    def feed_other():
+        return t_mm(act[:, units:], grad_two).astype(BF), t_mm(normed_two, grad_pre[:, units:]).astype(BF)
+
+    def feed_own(net):
+        down, up = t_mm(act[:, :units], grad_two).astype(BF), t_mm(normed_two, grad_pre[:, :units]).astype(BF)
+        return (down, up) + tuple(net.out_pieces(t_mm(mixed, grad_one).astype(BF)))
+
+    def far_tiles():
+        return attend_back(
+            cut, tiles, flags, query_rows, key_cols, query, key, value, mixed, run.grad_mixed, norm_rows, cosine, sine, rows
         )
-    hat_all, _ = normalise(jnp.concatenate([stream_low] + lower, axis=0).astype(F32))
-    grad_gain_one = jnp.sum(grad_a_kv * hat_all, axis=0) + jnp.sum(grad_a_q * hat_all[: 2 * rows], axis=0)
-    mine = grad_a_kv[: 2 * rows] + grad_a_q
-    parts = [grad_a_kv[t * rows : (t + 1) * rows].astype(BF) for t in range(2, len(tiles))]
-    hat_noisy, scale_noisy = normalise(stream[rows:])
-    stream_noisy = grad_after[rows:] + norm_back(hat_noisy, scale_noisy, gain_one, mine[rows:])
-    grad_embed = jnp.sum(jnp.where(masked, stream_noisy, 0.0), axis=0)
-    grad_vec = jnp.concatenate(
-        [
-            v.reshape(devices, -1)
-            for v in (
-                grad_gain_one, grad_gain_two, grad_down_b, grad_embed,
-                net.unit_bias_back(grad_up_b[:1], grad_up_b[1:], chunk),
-            )
-        ],
-        axis=1,
-    )
-    sum_qkv, sum_vec = net.sum_qkv(*grad_qkv_w, grad_vec)
-    clean = net.tree_sum(mine[:rows], parts)
-    hat_clean, scale_clean = normalise(stream[:rows])
-    stream_clean = grad_after[:rows] + norm_back(hat_clean, scale_clean, gain_one, clean)
-    grad_hidden = (stream_clean + jnp.where(masked, 0.0, stream_noisy)).astype(BF)[None]
+
+    def far_fold(far):
+        run.far = far
+        return fold(places, cut, tiles, far[1], far[2], x_all, mask, embed, gain_one, qkv_w[0], qkv_w[1], rows)
+
+    def near_tiles(far):
+        run.far = far
+        return attend_back(
+            0, cut, flags, query_rows, key_cols, query, key, value, mixed, run.grad_mixed, norm_rows, cosine, sine, rows, far[0]
+        )
+
+    def near_fold(near, far_gain):
+        run.near = near
+        da, gain, clean, run.noisy, grad_embed = fold(
+            places, 0, cut, near[1], near[2], x_all, mask, embed, gain_one, qkv_w[0], qkv_w[1], rows, near[0], grad_after
+        )
+        parts = (gain + far_gain, grad_gain_two, grad_down_b, grad_embed, net.unit_bias_back(grad_up_b[:1], grad_up_b[1:], chunk))
+        vec = jnp.concatenate([v.reshape(devices, -1) for v in parts], axis=1)
+        run.keys, run.values = (jnp.concatenate([run.near[n], run.far[n]], axis=0) for n in (1, 2))
+        return da, clean, vec
+
+    def qkv_half(n, vec, net):
+        at = slice(n * half, (n + 1) * half)
+        q = t_mm(a_all[: 2 * rows], run.near[0][:, at]).astype(BF)
+        k, v = (t_mm(a_all, g[:, at]).astype(BF) for g in (run.keys, run.values))
+        return net.qkv_pieces(q, k, v, vec, n == 1)
+
+    def last(total):
+        hat, scale = normalise(hid.astype(F32))
+        masked = (noise_mask[0] == 1)[:, None]
+        clean = grad_after[:rows] + norm_back(hat, scale, gain_one, total)
+        return (clean + jnp.where(masked, 0.0, run.noisy)).astype(BF)[None]
+
+    run.feed_other, run.feed_own, run.far_tiles, run.far_fold = feed_other, feed_own, far_tiles, far_fold
+    run.near_tiles, run.near_fold, run.last = near_tiles, near_fold, last
+    run.qkv_own = lambda vec, net: qkv_half(0, vec, net)
+    run.qkv_other = lambda vec, net: qkv_half(1, vec, net)
+    sum_down, sum_up, sum_out, sum_qkv, sum_vec, grad_hidden = net.backward(run)
     piece = lambda n: sum_vec[n * few : (n + 1) * few]
     return (
         output,

time: 635 us -> 511 us (0.80)
  local copies, waits for them, and re-layouts: 134 us -> 59.8 us
  Pallas kernels: 78.3 us -> 115 us
  starting transfers between devices: 153 us -> 120 us
  matrix products: 44.8 us -> 30.8 us
  waiting for transfers between devices: 144 us -> 131 us
  other arithmetic: 58.2 us -> 46.5 us
  between operations: 12.8 us -> 2.71 us
    pallas_call x1 -> x5, Pallas kernels: 21.2 us -> 57.4 us  [the longest x2 29.9 us: attend_back(): pl.pallas_call(functools.partial(attend_back_kernel, rows, first, last),...]
    ppermute x21 -> x24, starting transfers between devices: 108 us -> 77.4 us  [swap_z(): return lax.ppermute(v, 'leaf', [(i, i ^ 2 * n) for i in range(8)])]
    ppermute x21 -> x24, waiting for transfers between devices: 36.5 us -> 64.7 us  [swap_z(): return lax.ppermute(v, 'leaf', [(i, i ^ 2 * n) for i in range(8)])]
    dynamic_update_slice x32 -> x0, local copies, waits for them, and re-layouts: 25.1 us -> none  [in_place(): out = lax.dynamic_update_slice(out, w[n, :size], (places[n] * size, 0))]
    dot_general x4 -> x0, matrix products: 19.3 us -> none  [mm_t(): lax.dot_general(a, b, (((1,), (1,)), ((), ())), preferred_element_type=F32)]
    ppermute x7 -> x8, waiting for transfers between devices: 54.8 us -> 35.7 us  [swap_x(): return lax.ppermute(v, 'fsdp', [(i, i ^ 2) for i in range(4)])]
    ppermute x3, waiting for transfers between devices: 17.6 us -> 0.14 us  [down(): lax.ppermute(v, 'leaf', [(i, i - 2) for i in range(2 * first, 2 * last +...]
    ppermute x15 -> x16, waiting for transfers between devices: 34.6 us -> 22.8 us  [swap_y(): return lax.ppermute(v, 'leaf', pairs or [(i, i ^ 1) for i in range(8)])]
  transfers between devices with their start and end apart: 61 -> 67, of which waited for: 19 -> 24; matrix products, arithmetic and copies ran while one was open for 27% -> 16% of each run, Pallas kernels for 6% -> 13%
where the time goes in v3:
time: 511 us; the launch traced here: 505 us
  waiting for transfers between devices  131 us (26%)
  starting transfers between devices  120 us (23%)
  Pallas kernels  115 us (23%)
  local copies, waits for them, and re-layouts  59.8 us (12%)
  other arithmetic  46.5 us (9%)
  matrix products  30.8 us (6%)
    ppermute x24, starting transfers between devices, swap_z(): return lax.ppermute(v, 'leaf', [(i, i ^ 2 * n) for i in range(8)])  77.4 us
    ppermute x24, waiting for transfers between devices, swap_z(): return lax.ppermute(v, 'leaf', [(i, i ^ 2 * n) for i in range(8)])  64.7 us
    ppermute x8, waiting for transfers between devices, swap_x(): return lax.ppermute(v, 'fsdp', [(i, i ^ 2) for i in range(4)])  35.7 us
    dot_general x11, matrix products, t_mm(): lax.dot_general(a, b, (((0,), (0,)), ((), ())), preferred_element_type=F32)  30.6 us
    pallas_call x2, Pallas kernels, attend_back(): pl.pallas_call(functools.partial(attend_back_kernel, rows, first, last),...  29.9 us
    pallas_call x2, Pallas kernels, fold(): pl.pallas_call(functools.partial(fold_kernel, count, size, rows, first),...  24.8 us
    ppermute x16, waiting for transfers between devices, swap_y(): return lax.ppermute(v, 'leaf', pairs or [(i, i ^ 1) for i in range(8)])  22.8 us
    pallas_call x1, Pallas kernels, middle(): pl.pallas_call(functools.partial(middle_kernel, count, size, chunk), grid...  22.3 us
  transfers between devices with their start and end apart: 67, of which 24 were waited for; matrix products, arithmetic and copies ran while one was open for 16% of the time, Pallas kernels for 13%

profile of v3, /device:TPU:0, one launch (start us, length us, event | category | flops | bytes accessed | tf_op | source)
XLA Modules:
  0.0 505.1 jit_solution(2245569714299931648)
XLA Ops:
  0.7 3.5 concatenate.138
  5.9 2.6 collective-permute-start.8
  8.5 3.4 collective-permute-start.6
  13.6 3.7 collective-permute-start.3
  18.1 4.1 collective-permute-done.3
  22.3 7.6 %collective-permute-done.2 = bf16[1,64,1152]{2,1,0:T(8,128)(2,1)S(1)} collective-permute-done((bf16[1,64,1152]{2,1,0:T(8,128)(2,1)S(1)}, bf16[1,64,1152]{2,1,0:T(8,128)(2,1)S(1)}, u32[]{:S(2)}, u32[]{:S(2)}) %collective-permute-start.2) | collective-permute-done | bytes 147488 | tf_op jit(solution)/shard_map/ppermute | solution.py:37
  31.6 2.7 shard_map.221
  34.4 1.7 collective-permute-start.4
  36.1 1.7 maximum_bitcast_fusion
  37.8 6.6 %collective-permute-done.5 = bf16[4,64,1152]{2,1,0:T(8,128)(2,1)S(1)} collective-permute-done((bf16[4,64,1152]{2,1,0:T(8,128)(2,1)S(1)}, bf16[4,64,1152]{2,1,0:T(8,128)(2,1)S(1)}, u32[]{:S(2)}, u32[]{:S(2)}) %collective-permute-start.5) | collective-permute-done | bytes 589856 | tf_op jit(solution)/shard_map/ppermute | solution.py:34
  51.5 19.2 %collective-permute-done.13 = bf16[8,64,1152]{2,1,0:T(8,128)(2,1)S(1)} collective-permute-done((bf16[8,64,1152]{2,1,0:T(8,128)(2,1)S(1)}, bf16[8,64,1152]{2,1,0:T(8,128)(2,1)S(1)}, u32[]{:S(2)}, u32[]{:S(2)}) %collective-permute-start.13) | collective-permute-done | bytes 1179680 | tf_op jit(solution)/shard_map/ppermute | solution.py:31
  71.0 6.0 %fusion.26 = (f32[2304,128]{1,0:T(8,128)}, f32[2304,128]{1,0:T(8,128)}) fusion(f32[128]{0:T(128)S(1)} %get-tuple-element.447, f32[128]{0:T(128)S(1)} %get-tuple-element.448, f32[2304]{0:T(1024)S(1)} %slice_reduce_fusion), kind=kLoop, calls=%fused_computation.38 | loop fusion | flops 589824 | bytes 2369536 | tf_op jit(solution)/shard_map/mul | solution.py:1091
  80.1 6.2 %collective-permute-start.18 = (bf16[1,48,1920]{2,1,0:T(8,128)(2,1)S(1)}, bf16[1,48,1920]{2,1,0:T(8,128)(2,1)S(1)}, u32[]{:S(2)}, u32[]{:S(2)}) collective-permute-start(bf16[1,48,1920]{2,1,0:T(8,128)(2,1)S(1)} %bitcast.231), channel_id=1, source_target_pairs={{0,24},{4,28},{8,16},{12,20},{16,8},{20,12},{24,0},{28,4},{1,25},{... | collective-permute-start | bytes 552968 | tf_op jit(solution)/shard_map/ppermute | solution.py:37
  89.6 1.8 constant_dynamic-update-slice_fusion.1
  92.0 9.7 %collective-permute-done.17 = bf16[1,48,1920]{2,1,0:T(8,128)(2,1)S(1)} collective-permute-done((bf16[1,48,1920]{2,1,0:T(8,128)(2,1)S(1)}, bf16[1,48,1920]{2,1,0:T(8,128)(2,1)S(1)}, u32[]{:S(2)}, u32[]{:S(2)}) %collective-permute-start.17) | collective-permute-done | bytes 184352 | tf_op jit(solution)/shard_map/ppermute | solution.py:37
  103.7 1.8 constant_dynamic-update-slice_fusion.x_ref
  108.8 2.7 collective-permute-start.22
  111.4 1.7 collective-permute-start.20
  113.2 19.3 %shard_map.222 = (bf16[2304,768]{1,0:T(8,128)(2,1)}, bf16[512,768]{1,0:T(8,128)(2,1)}, bf16[2304,768]{1,0:T(8,128)(2,1)}, bf16[2304,768]{1,0:T(8,128)(2,1)}) custom-call(s32[4,16]{1,0:T(4,128)} %pad_add_fusion.table_ref, bf16[2304,768]{1,0:T(8,128)(2,1)} %constant_dynamic-update-slice_fusion.x_ref, f32[2304,1]{1,0:T(8,128)} %pad.16.mask_ref, ...), custom_call_target="tpu_custom_call" | custom-call | flops 6039797760 | bytes 17694720 | tf_op jit(solution)/shard_map/pallas_call | solution.py:258
  132.4 3.1 collective-permute-done.21
  138.2 15.6 %shard_map.223 = (bf16[512,768]{1,0:T(8,128)(2,1)}, f32[512,128]{1,0:T(8,128)}) custom-call(s32[9]{0:T(128)} %get-tuple-element.212.flag_ref, f32[512,8]{1,0:T(8,128)} %get-tuple-element.213.qcol_ref, f32[8,2304]{1,0:T(8,128)} %get-tuple-element.214.krow_ref, bf16[512,768]{1,0:T(8,128)(2,1)} %get-tuple-element.215.q_ref, ...), custom_call_target="tpu_custom_call" | custom-call | flops 7247757312 | bytes 7864320 | tf_op jit(solution)/shard_map/pallas_call | solution.py:469
  153.8 9.5 %collective-permute-done.24 = bf16[4,2,96,768]{3,2,1,0:T(8,128)(2,1)} collective-permute-done((bf16[4,2,96,768]{3,2,1,0:T(8,128)(2,1)S(1)}, bf16[4,2,96,768]{3,2,1,0:T(8,128)(2,1)}, u32[]{:S(2)}, u32[]{:S(2)}) %collective-permute-start.24) | collective-permute-done | bytes 1179680 | tf_op jit(solution)/shard_map/ppermute | solution.py:34
  164.8 3.7 collective-permute-done.23
  168.5 1.9 pad_maximum_fusion.one_own
  173.2 5.8 %collective-permute-done.26.two_other = bf16[16,96,768]{2,1,0:T(8,128)(2,1)} collective-permute-done((bf16[16,96,768]{2,1,0:T(8,128)(2,1)S(1)}, bf16[16,96,768]{2,1,0:T(8,128)(2,1)}, u32[]{:S(2)}, u32[]{:S(2)}) %collective-permute-start.26) | collective-permute-done | bytes 2359328 | tf_op jit(solution)/shard_map/ppermute | solution.py:28
  179.6 22.3 %shard_map.224 = (bf16[512,768]{1,0:T(8,128)(2,1)}, bf16[512,768]{1,0:T(8,128)(2,1)}, bf16[512,3072]{1,0:T(8,128)(2,1)}, bf16[512,3072]{1,0:T(8,128)(2,1)}, bf16...) custom-call(s32[4,16]{1,0:T(4,128)} %pad_add_fusion.table_ref, ...), custom_call_target="tpu_custom_call" | custom-call | flops 10871635968 | bytes 21233664 | tf_op jit(solution)/shard_map/pallas_call | solution.py:360
  201.9 4.5 convolution_convert_fusion
  206.7 4.4 convolution_convert_fusion.2
  213.0 2.7 constant_dynamic-slice_fusion.2
  221.5 2.3 add_convert_fusion
  225.0 2.3 add_convert_fusion.1
  231.7 1.8 copy.58
  233.5 10.8 %shard_map.225 = (f32[768,512]{1,0:T(8,128)}, bf16[1024,768]{1,0:T(8,128)(2,1)}, bf16[1024,768]{1,0:T(8,128)(2,1)}) custom-call(s32[9]{0:T(128)} %get-tuple-element.212.flag_ref, f32[8,512]{1,0:T(8,128)} %get-tuple-element.233.qrow_ref, f32[2304,8]{1,0:T(8,128)} %get-tuple-element.200.kcol_ref, bf16[512,768]{1,0:T(8,128)(2,1)} %get-tuple-element.215.q_ref, ...), custom_call_target="tpu_custom_call" | custom-call | flops 8053063680 | bytes 7864320 | tf_op jit(solution)/shard_map/pallas_call | solution.py:588
  244.3 12.5 %collective-permute-done.29 = bf16[8,96,768]{2,1,0:T(8,128)(2,1)} collective-permute-done((bf16[8,96,768]{2,1,0:T(8,128)(2,1)}, bf16[8,96,768]{2,1,0:T(8,128)(2,1)}, u32[]{:S(2)}, u32[]{:S(2)}) %collective-permute-start.29) | collective-permute-done | bytes 1179680 | tf_op jit(solution)/shard_map/ppermute | solution.py:31
  261.4 9.6 %shard_map.226 = (bf16[1024,768]{1,0:T(8,128)(2,1)}, f32[1,768]{1,0:T(1,128)}) custom-call(s32[4,16]{1,0:T(4,128)} %pad_add_fusion.table_ref, bf16[1024,768]{1,0:T(8,128)(2,1)} %get-tuple-element.288.dk_ref, bf16[1024,768]{1,0:T(8,128)(2,1)} %get-tuple-element.290.dv_ref, bf16[2304,768]{1,0:T(8,128)(2,1)} %constant_dynamic-update-slice_fusion.x_ref, ...), custom_call_target="tpu_custom_call" | custom-call | flops 2415919104 | bytes 9830400 | tf_op jit(solution)/shard_map/pallas_call | solution.py:686
  271.0 2.4 fusion.62
  275.8 20.1 %collective-permute-start.34 = (bf16[2,48,1536]{2,1,0:T(8,128)(2,1)S(1)}, bf16[2,48,1536]{2,1,0:T(8,128)(2,1)}, u32[]{:S(2)}, u32[]{:S(2)}) collective-permute-start(bf16[2,48,1536]{2,1,0:T(8,128)(2,1)S(1)} %get-tuple-element.251), channel_id=1, source_target_pairs={{0,16},{4,20},{8,24},{12,28},{16,0},{20,4},{24,8},{28,12},{1,17},{... | collective-permute-start | bytes 884744 | tf_op jit(solution)/shard_map/ppermute | solution.py:37
  300.8 15.7 %collective-permute-done.34 = bf16[2,48,1536]{2,1,0:T(8,128)(2,1)} collective-permute-done((bf16[2,48,1536]{2,1,0:T(8,128)(2,1)S(1)}, bf16[2,48,1536]{2,1,0:T(8,128)(2,1)}, u32[]{:S(2)}, u32[]{:S(2)}) %collective-permute-start.34) | collective-permute-done | bytes 294944 | tf_op jit(solution)/shard_map/ppermute | solution.py:37
  316.5 19.2 %shard_map.227 = (bf16[512,768]{1,0:T(8,128)(2,1)}, bf16[1280,768]{1,0:T(8,128)(2,1)}, bf16[1280,768]{1,0:T(8,128)(2,1)}) custom-call(s32[9]{0:T(128)} %get-tuple-element.212.flag_ref, f32[8,512]{1,0:T(8,128)} %get-tuple-element.233.qrow_ref, f32[2304,8]{1,0:T(8,128)} %get-tuple-element.200.kcol_ref, bf16[512,768]{1,0:T(8,128)(2,1)} %get-tuple-element.215.q_ref, ...), custom_call_target="tpu_custom_call" | custom-call | flops 10066329600 | bytes 9437184 | tf_op jit(solution)/shard_map/pallas_call | solution.py:588
  342.7 1.7 fusion.14
  347.9 15.2 %shard_map.228 = (bf16[1280,768]{1,0:T(8,128)(2,1)}, f32[1,768]{1,0:T(1,128)}, f32[256,768]{1,0:T(8,128)}, f32[256,768]{1,0:T(8,128)}, f32[1,768]{1,0:T(1,128)}) custom-call(s32[4,16]{1,0:T(4,128)} %pad_add_fusion.table_ref, bf16[1280,768]{1,0:T(8,128)(2,1)} %get-tuple-element.274.dk_ref, bf16[1280,768]{1,0:T(8,128)(2,1)} %get-tuple-element.275.dv_ref, ...), custom_call_target="tpu_custom_call" | custom-call | flops 3019898880 | bytes 11403264 | tf_op jit(solution)/shard_map/pallas_call | solution.py:686
  366.1 1.6 collective-permute-start.39
  369.3 4.2 fusion.17
  375.0 4.1 fusion.20
  380.8 1.9 add_convert_fusion.11
  382.8 5.1 %fusion.23 = bf16[768,384]{0,1:T(8,128)(2,1)} fusion(bf16[2304,768]{1,0:T(8,128)(2,1)} %get-tuple-element.287, bf16[2304,768]{1,0:T(8,128)(2,1)} %constant_dynamic-update-slice_fusion.11), kind=kOutput, calls=%fused_computation.35 | convolution fusion | flops 1359249408 | bytes 5898240 | tf_op jit(solution)/shard_map/dot_general | solution.py:747
  387.9 11.3 %collective-permute-start.45 = (bf16[96,768]{1,0:T(8,128)(2,1)S(1)}, bf16[96,768]{1,0:T(8,128)(2,1)S(1)}, u32[]{:S(2)}, u32[]{:S(2)}) collective-permute-start(bf16[96,768]{1,0:T(8,128)(2,1)S(1)} %copy-done.31), channel_id=1, source_target_pairs={{0,8},{4,12},{8,0},{12,4},{16,24},{20,28},{24,16},{28,20},{1,9},{5... | collective-permute-start | bytes 442376 | tf_op jit(solution)/shard_map/ppermute | solution.py:37
  399.3 4.1 collective-permute-start.46
  403.4 1.6 convolution_convert_fusion.5
  406.3 8.0 %collective-permute-done.46 = bf16[96,768]{1,0:T(8,128)(2,1)S(1)} collective-permute-done((bf16[96,768]{1,0:T(8,128)(2,1)S(1)}, bf16[96,768]{1,0:T(8,128)(2,1)S(1)}, u32[]{:S(2)}, u32[]{:S(2)}) %collective-permute-start.46) | collective-permute-done | bytes 147488 | tf_op jit(solution)/shard_map/ppermute | solution.py:37
  414.3 7.9 %collective-permute-start.49 = (bf16[4,48,384]{2,1,0:T(8,128)(2,1)S(1)}, bf16[4,48,384]{2,1,0:T(8,128)(2,1)S(1)}, u32[]{:S(2)}, u32[]{:S(2)}) collective-permute-start(bf16[4,48,384]{2,1,0:T(8,128)(2,1)S(1)} %copy-done.42), channel_id=1, source_target_pairs={{0,4},{4,0},{8,12},{12,8},{16,20},{20,16},{24,28},{28,24},{1,5},{5... | collective-permute-start | bytes 442376 | tf_op jit(solution)/shard_map/ppermute | solution.py:34
  422.3 2.1 fusion.61
  430.9 3.5 collective-permute-done.44
  440.0 2.3 add_convert_fusion.10
  442.3 10.1 %collective-permute-start.53 = (bf16[48,384]{1,0:T(8,128)(2,1)}, bf16[48,384]{1,0:T(8,128)(2,1)S(1)}, u32[]{:S(2)}, u32[]{:S(2)}) collective-permute-start(bf16[48,384]{1,0:T(8,128)(2,1)} %get-tuple-element.314), channel_id=1, source_target_pairs={{0,8},{4,12},{8,0},{12,4},{16,24},{20,28},{24,16},{28,20},{1,9},{5... | collective-permute-start | bytes 110600 | tf_op jit(solution)/shard_map/ppermute | solution.py:37
  452.4 3.4 collective-permute-start.54
  460.3 2.9 collective-permute-start.55
  464.8 4.7 collective-permute-done.55
  470.0 2.2 collective-permute-done.51
  477.3 2.4 collective-permute-start.57
  484.7 7.4 %collective-permute-done.58 = bf16[2,48,640]{2,1,0:T(8,128)(2,1)S(1)} collective-permute-done((bf16[2,48,640]{2,1,0:T(8,128)(2,1)S(1)}, bf16[2,48,640]{2,1,0:T(8,128)(2,1)S(1)}, u32[]{:S(2)}, u32[]{:S(2)}) %collective-permute-start.58) | collective-permute-done | bytes 122912 | tf_op jit(solution)/shard_map/ppermute | solution.py:37
  492.3 2.5 collective-permute-start.60
  494.8 2.4 collective-permute-start.62
  498.7 2.7 collective-permute-done.61
  (430 shorter events, 111.2 us)
Async XLA Ops:
  5.4 8.1 %collective-permute-start = (bf16[32,1152]{1,0:T(8,128)(2,1)S(1)}, bf16[32,1152]{1,0:T(8,128)(2,1)S(1)}, u32[]{:S(2)}, u32[]{:S(2)}) collective-permute-start(bf16[32,1152]{1,0:T(8,128)(2,1)S(1)} %fusion.45), channel_id=1, source_target_pairs={{0,1},{1,0},{2,3},{3,2},{4,5},{5,4},{6,7},{7,6},{8,9},{9,8},{10,11... | collective-permute-start | bytes 221192 | tf_op jit(solution)/shard_map/ppermute | solution.py:28
  5.9 30.2 %collective-permute-start.8 = (bf16[96,768]{1,0:T(8,128)(2,1)}, bf16[96,768]{1,0:T(8,128)(2,1)}, u32[]{:S(2)}, u32[]{:S(2)}) collective-permute-start(bf16[96,768]{1,0:T(8,128)(2,1)} %param.24), channel_id=1, source_target_pairs={{0,2},{1,3},{2,0},{3,1},{4,6},{5,7},{6,4},{7,5},{8,10},{9,11},{10,... | collective-permute-start | bytes 442376 | tf_op jit(solution)/shard_map/ppermute | solution.py:31
  8.5 36.0 %collective-permute-start.6 = (bf16[256,768]{1,0:T(8,128)(2,1)}, bf16[256,768]{1,0:T(8,128)(2,1)S(1)}, u32[]{:S(2)}, u32[]{:S(2)}) collective-permute-start(bf16[256,768]{1,0:T(8,128)(2,1)} %bitcast.213), channel_id=1, source_target_pairs={{0,4},{8,12},{16,20},{24,28},{1,5},{9,13},{17,21},{25,29},{2,6},{1... | collective-permute-start | bytes 1179656 | tf_op jit(solution)/shard_map/ppermute | solution.py:34
  13.6 8.6 %collective-permute-start.3 = (bf16[1,64,1152]{2,1,0:T(8,128)(2,1)S(1)}, bf16[1,64,1152]{2,1,0:T(8,128)(2,1)S(1)}, u32[]{:S(2)}, u32[]{:S(2)}) collective-permute-start(bf16[1,64,1152]{2,1,0:T(8,128)(2,1)S(1)} %maximum_bitcast_fusion.1), channel_id=1, source_target_pairs={{0,24},{4,28},{8,16},{12,20},{16,8},{20,12},{24,0},{28,4},{1,25},{... | collective-permute-start | bytes 442376 | tf_op jit(solution)/shard_map/ppermute | solution.py:37
  17.3 12.5 %collective-permute-start.2 = (bf16[1,64,1152]{2,1,0:T(8,128)(2,1)S(1)}, bf16[1,64,1152]{2,1,0:T(8,128)(2,1)S(1)}, u32[]{:S(2)}, u32[]{:S(2)}) collective-permute-start(bf16[1,64,1152]{2,1,0:T(8,128)(2,1)S(1)} %maximum_bitcast_fusion.1), channel_id=1, source_target_pairs={{0,16},{4,20},{8,24},{12,28},{16,0},{20,4},{24,8},{28,12},{1,17},{... | collective-permute-start | bytes 442376 | tf_op jit(solution)/shard_map/ppermute | solution.py:37
  17.3 12.5 %collective-permute-start.1 = (bf16[1,64,1152]{2,1,0:T(8,128)(2,1)S(1)}, bf16[1,64,1152]{2,1,0:T(8,128)(2,1)S(1)}, u32[]{:S(2)}, u32[]{:S(2)}) collective-permute-start(bf16[1,64,1152]{2,1,0:T(8,128)(2,1)S(1)} %maximum_bitcast_fusion.1), channel_id=1, source_target_pairs={{0,8},{4,12},{8,0},{12,4},{16,24},{20,28},{24,16},{28,20},{1,9},{5... | collective-permute-start | bytes 442376 | tf_op jit(solution)/shard_map/ppermute | solution.py:37
  22.2 12.0 %collective-permute-start.7 = (bf16[24,1920]{1,0:T(8,128)(2,1)S(1)}, bf16[24,1920]{1,0:T(8,128)(2,1)S(1)}, u32[]{:S(2)}, u32[]{:S(2)}) collective-permute-start(bf16[24,1920]{1,0:T(8,128)(2,1)S(1)} %maximum_select_fusion.4), channel_id=1, source_target_pairs={{0,1},{1,0},{2,3},{3,2},{4,5},{5,4},{6,7},{7,6},{8,9},{9,8},{10,11... | collective-permute-start | bytes 276488 | tf_op jit(solution)/shard_map/ppermute | solution.py:28
  29.9 14.5 %collective-permute-start.5 = (bf16[4,64,1152]{2,1,0:T(8,128)(2,1)S(1)}, bf16[4,64,1152]{2,1,0:T(8,128)(2,1)S(1)}, u32[]{:S(2)}, u32[]{:S(2)}) collective-permute-start(bf16[4,64,1152]{2,1,0:T(8,128)(2,1)S(1)} %pad_maximum_fusion.11), channel_id=1, source_target_pairs={{0,4},{4,0},{8,12},{12,8},{16,20},{20,16},{24,28},{28,24},{1,5},{5... | collective-permute-start | bytes 1769480 | tf_op jit(solution)/shard_map/ppermute | solution.py:34
  34.4 10.1 %collective-permute-start.4 = (bf16[256,768]{1,0:T(8,128)(2,1)S(1)}, bf16[256,768]{1,0:T(8,128)(2,1)S(1)}, u32[]{:S(2)}, u32[]{:S(2)}) collective-permute-start(bf16[256,768]{1,0:T(8,128)(2,1)S(1)} %bitcast.214), channel_id=1, source_target_pairs={{0,8},{4,12},{8,16},{12,20},{16,24},{20,28},{1,9},{5,13},{9,17},{1... | collective-permute-start | bytes 1179656 | tf_op jit(solution)/shard_map/ppermute | solution.py:40
  44.5 26.2 %collective-permute-start.13 = (bf16[8,64,1152]{2,1,0:T(8,128)(2,1)S(1)}, bf16[8,64,1152]{2,1,0:T(8,128)(2,1)S(1)}, u32[]{:S(2)}, u32[]{:S(2)}) collective-permute-start(bf16[8,64,1152]{2,1,0:T(8,128)(2,1)S(1)} %pad_maximum_fusion.4), channel_id=1, source_target_pairs={{0,2},{1,3},{2,0},{3,1},{4,6},{5,7},{6,4},{7,5},{8,10},{9,11},{10,... | collective-permute-start | bytes 3538952 | tf_op jit(solution)/shard_map/ppermute | solution.py:31
  49.4 21.6 %collective-permute-start.12 = (bf16[256,768]{1,0:T(8,128)(2,1)S(1)}, bf16[256,768]{1,0:T(8,128)(2,1)S(1)}, u32[]{:S(2)}, u32[]{:S(2)}) collective-permute-start(bf16[256,768]{1,0:T(8,128)(2,1)S(1)} %collective-permute-done.9), channel_id=1, source_target_pairs={{16,20},{20,16},{24,28},{28,24},{17,21},{21,17},{25,29},{29,25},{1... | collective-permute-start | bytes 1179656 | tf_op jit(solution)/shard_map/ppermute | solution.py:34
  50.0 20.9 %collective-permute-start.11 = (bf16[256,768]{1,0:T(8,128)(2,1)S(1)}, bf16[256,768]{1,0:T(8,128)(2,1)}, u32[]{:S(2)}, u32[]{:S(2)}) collective-permute-start(bf16[256,768]{1,0:T(8,128)(2,1)S(1)} %collective-permute-done.9), channel_id=1, source_target_pairs={{16,24},{20,28},{17,25},{21,29},{18,26},{22,30},{19,27},{23,31}} | collective-permute-start | bytes 1179656 | tf_op jit(solution)/shard_map/ppermute | solution.py:40
  70.9 32.8 %collective-permute-start.15 = (bf16[16,64,1152]{2,1,0:T(8,128)(2,1)S(1)}, bf16[16,64,1152]{2,1,0:T(8,128)(2,1)}, u32[]{:S(2)}, u32[]{:S(2)}) collective-permute-start(bf16[16,64,1152]{2,1,0:T(8,128)(2,1)S(1)} %pad_maximum_fusion.1.own_hbm), channel_id=1, source_target_pairs={{0,1},{1,0},{2,3},{3,2},{4,5},{5,4},{6,7},{7,6},{8,9},{9,8},{10,11... | collective-permute-start | bytes 7077896 | tf_op jit(solution)/shard_map/ppermute | solution.py:28
  80.1 11.8 %collective-permute-start.18 = (bf16[1,48,1920]{2,1,0:T(8,128)(2,1)S(1)}, bf16[1,48,1920]{2,1,0:T(8,128)(2,1)S(1)}, u32[]{:S(2)}, u32[]{:S(2)}) collective-permute-start(bf16[1,48,1920]{2,1,0:T(8,128)(2,1)S(1)} %bitcast.231), channel_id=1, source_target_pairs={{0,24},{4,28},{8,16},{12,20},{16,8},{20,12},{24,0},{28,4},{1,25},{... | collective-permute-start | bytes 552968 | tf_op jit(solution)/shard_map/ppermute | solution.py:37
  86.3 15.4 %collective-permute-start.17 = (bf16[1,48,1920]{2,1,0:T(8,128)(2,1)S(1)}, bf16[1,48,1920]{2,1,0:T(8,128)(2,1)S(1)}, u32[]{:S(2)}, u32[]{:S(2)}) collective-permute-start(bf16[1,48,1920]{2,1,0:T(8,128)(2,1)S(1)} %bitcast.232), channel_id=1, source_target_pairs={{0,16},{4,20},{8,24},{12,28},{16,0},{20,4},{24,8},{28,12},{1,17},{... | collective-permute-start | bytes 552968 | tf_op jit(solution)/shard_map/ppermute | solution.py:37
  86.3 16.1 %collective-permute-start.16 = (bf16[1,48,1920]{2,1,0:T(8,128)(2,1)S(1)}, bf16[1,48,1920]{2,1,0:T(8,128)(2,1)}, u32[]{:S(2)}, u32[]{:S(2)}) collective-permute-start(bf16[1,48,1920]{2,1,0:T(8,128)(2,1)S(1)} %bitcast.233), channel_id=1, source_target_pairs={{0,8},{4,12},{8,0},{12,4},{16,24},{20,28},{24,16},{28,20},{1,9},{5... | collective-permute-start | bytes 552968 | tf_op jit(solution)/shard_map/ppermute | solution.py:37
  86.9 16.8 %collective-permute-start.14 = (bf16[256,768]{1,0:T(8,128)(2,1)}, bf16[256,768]{1,0:T(8,128)(2,1)}, u32[]{:S(2)}, u32[]{:S(2)}) collective-permute-start(bf16[256,768]{1,0:T(8,128)(2,1)} %collective-permute-done.11), channel_id=1, source_target_pairs={{24,28},{28,24},{25,29},{29,25},{26,30},{30,26},{27,31},{31,27}} | collective-permute-start | bytes 1179656 | tf_op jit(solution)/shard_map/ppermute | solution.py:34
  105.5 30.2 %collective-permute-start.19 = (bf16[4,48,1920]{2,1,0:T(8,128)(2,1)S(1)}, bf16[4,48,1920]{2,1,0:T(8,128)(2,1)S(1)}, u32[]{:S(2)}, u32[]{:S(2)}) collective-permute-start(bf16[4,48,1920]{2,1,0:T(8,128)(2,1)S(1)} %pad_maximum_fusion.10), channel_id=1, source_target_pairs={{0,4},{4,0},{8,12},{12,8},{16,20},{20,16},{24,28},{28,24},{1,5},{5... | collective-permute-start | bytes 2211848 | tf_op jit(solution)/shard_map/ppermute | solution.py:34
  108.8 23.7 %collective-permute-start.22 = (bf16[1,2,96,768]{3,2,1,0:T(8,128)(2,1)}, bf16[1,2,96,768]{3,2,1,0:T(8,128)(2,1)S(1)}, u32[]{:S(2)}, u32[]{:S(2)}) collective-permute-start(bf16[1,2,96,768]{3,2,1,0:T(8,128)(2,1)} %maximum_bitcast_fusion), channel_id=1, source_target_pairs={{0,24},{4,28},{8,16},{12,20},{16,8},{20,12},{24,0},{28,4},{1,25},{... | collective-permute-start | bytes 884744 | tf_op jit(solution)/shard_map/ppermute | solution.py:37
  111.4 24.1 %collective-permute-start.21 = (bf16[1,2,96,768]{3,2,1,0:T(8,128)(2,1)}, bf16[1,2,96,768]{3,2,1,0:T(8,128)(2,1)S(1)}, u32[]{:S(2)}, u32[]{:S(2)}) collective-permute-start(bf16[1,2,96,768]{3,2,1,0:T(8,128)(2,1)} %maximum_bitcast_fusion), channel_id=1, source_target_pairs={{0,16},{4,20},{8,24},{12,28},{16,0},{20,4},{24,8},{28,12},{1,17},{... | collective-permute-start | bytes 884744 | tf_op jit(solution)/shard_map/ppermute | solution.py:37
  111.4 24.1 %collective-permute-start.20 = (bf16[1,2,96,768]{3,2,1,0:T(8,128)(2,1)}, bf16[1,2,96,768]{3,2,1,0:T(8,128)(2,1)S(1)}, u32[]{:S(2)}, u32[]{:S(2)}) collective-permute-start(bf16[1,2,96,768]{3,2,1,0:T(8,128)(2,1)} %maximum_bitcast_fusion), channel_id=1, source_target_pairs={{0,8},{4,12},{8,0},{12,4},{16,24},{20,28},{24,16},{28,20},{1,9},{5... | collective-permute-start | bytes 884744 | tf_op jit(solution)/shard_map/ppermute | solution.py:37
  135.8 32.7 %collective-permute-start.23 = (bf16[8,48,1920]{2,1,0:T(8,128)(2,1)S(1)}, bf16[8,48,1920]{2,1,0:T(8,128)(2,1)S(1)}, u32[]{:S(2)}, u32[]{:S(2)}) collective-permute-start(bf16[8,48,1920]{2,1,0:T(8,128)(2,1)S(1)} %pad_maximum_fusion.3), channel_id=1, source_target_pairs={{0,2},{1,3},{2,0},{3,1},{4,6},{5,7},{6,4},{7,5},{8,10},{9,11},{10,... | collective-permute-start | bytes 4423688 | tf_op jit(solution)/shard_map/ppermute | solution.py:31
  137.1 26.2 %collective-permute-start.24 = (bf16[4,2,96,768]{3,2,1,0:T(8,128)(2,1)S(1)}, bf16[4,2,96,768]{3,2,1,0:T(8,128)(2,1)}, u32[]{:S(2)}, u32[]{:S(2)}) collective-permute-start(bf16[4,2,96,768]{3,2,1,0:T(8,128)(2,1)S(1)} %pad_maximum_fusion.5), channel_id=1, source_target_pairs={{0,4},{4,0},{8,12},{12,8},{16,20},{20,16},{24,28},{28,24},{1,5},{5... | collective-permute-start | bytes 3538952 | tf_op jit(solution)/shard_map/ppermute | solution.py:34
  170.5 9.1 %collective-permute-start.25 = (bf16[16,48,1920]{2,1,0:T(8,128)(2,1)}, bf16[16,48,1920]{2,1,0:T(8,128)(2,1)}, u32[]{:S(2)}, u32[]{:S(2)}) collective-permute-start(bf16[16,48,1920]{2,1,0:T(8,128)(2,1)} %pad_maximum_fusion.one_own), channel_id=1, source_target_pairs={{0,1},{1,0},{2,3},{3,2},{4,5},{5,4},{6,7},{7,6},{8,9},{9,8},{10,11... | collective-permute-start | bytes 8847368 | tf_op jit(solution)/shard_map/ppermute | solution.py:28
  170.5 8.5 %collective-permute-start.26 = (bf16[16,96,768]{2,1,0:T(8,128)(2,1)S(1)}, bf16[16,96,768]{2,1,0:T(8,128)(2,1)}, u32[]{:S(2)}, u32[]{:S(2)}) collective-permute-start(bf16[16,96,768]{2,1,0:T(8,128)(2,1)S(1)} %bitcast.223), channel_id=1, source_target_pairs={{0,1},{1,0},{2,3},{3,2},{4,5},{5,4},{6,7},{7,6},{8,9},{9,8},{10,11... | collective-permute-start | bytes 7077896 | tf_op jit(solution)/shard_map/ppermute | solution.py:28
  206.4 15.0 %collective-permute-start.28 = (bf16[768,1536]{1,0:T(8,128)(2,1)}, bf16[768,1536]{1,0:T(8,128)(2,1)}, u32[]{:S(2)}, u32[]{:S(2)}) collective-permute-start(bf16[768,1536]{1,0:T(8,128)(2,1)} %convolution_convert_fusion), channel_id=1, source_target_pairs={{0,1},{1,0},{2,3},{3,2},{4,5},{5,4},{6,7},{7,6},{8,9},{9,8},{10,11... | collective-permute-start | bytes 7077896 | tf_op jit(solution)/shard_map/ppermute | solution.py:28
  211.1 13.9 %collective-permute-start.27 = (bf16[1536,768]{1,0:T(8,128)(2,1)}, bf16[1536,768]{1,0:T(8,128)(2,1)}, u32[]{:S(2)}, u32[]{:S(2)}) collective-permute-start(bf16[1536,768]{1,0:T(8,128)(2,1)} %convolution_convert_fusion.2), channel_id=1, source_target_pairs={{0,1},{1,0},{2,3},{3,2},{4,5},{5,4},{6,7},{7,6},{8,9},{9,8},{10,11... | collective-permute-start | bytes 7077896 | tf_op jit(solution)/shard_map/ppermute | solution.py:28
  228.4 28.3 %collective-permute-start.29 = (bf16[8,96,768]{2,1,0:T(8,128)(2,1)}, bf16[8,96,768]{2,1,0:T(8,128)(2,1)}, u32[]{:S(2)}, u32[]{:S(2)}) collective-permute-start(bf16[8,96,768]{2,1,0:T(8,128)(2,1)} %get-tuple-element.230), channel_id=1, source_target_pairs={{0,2},{1,3},{2,0},{3,1},{4,6},{5,7},{6,4},{7,5},{8,10},{9,11},{10,... | collective-permute-start | bytes 3538952 | tf_op jit(solution)/shard_map/ppermute | solution.py:31
  229.7 28.1 %collective-permute-start.30 = (bf16[4,2,48,1536]{3,2,1,0:T(8,128)(2,1)}, bf16[4,2,48,1536]{3,2,1,0:T(8,128)(2,1)}, u32[]{:S(2)}, u32[]{:S(2)}) collective-permute-start(bf16[4,2,48,1536]{3,2,1,0:T(8,128)(2,1)} %get-tuple-element.231), channel_id=1, source_target_pairs={{0,4},{4,0},{8,12},{12,8},{16,20},{20,16},{24,28},{28,24},{1,5},{5... | collective-permute-start | bytes 3538952 | tf_op jit(solution)/shard_map/ppermute | solution.py:34
  233.5 10.8 %collective-permute-start.31 = (bf16[8,2,48,384]{3,2,1,0:T(8,128)(2,1)}, bf16[8,2,48,384]{3,2,1,0:T(8,128)(2,1)S(1)}, u32[]{:S(2)}, u32[]{:S(2)}) collective-permute-start(bf16[8,2,48,384]{3,2,1,0:T(8,128)(2,1)} %bitcast.237), channel_id=1, source_target_pairs={{0,1},{1,0},{2,3},{3,2},{4,5},{5,4},{6,7},{7,6},{8,9},{9,8},{10,11... | collective-permute-start | bytes 1769480 | tf_op jit(solution)/shard_map/ppermute | solution.py:28
  275.8 24.2 %collective-permute-start.33 = (bf16[2,48,1536]{2,1,0:T(8,128)(2,1)S(1)}, bf16[2,48,1536]{2,1,0:T(8,128)(2,1)S(1)}, u32[]{:S(2)}, u32[]{:S(2)}) collective-permute-start(bf16[2,48,1536]{2,1,0:T(8,128)(2,1)S(1)} %get-tuple-element.250), channel_id=1, source_target_pairs={{0,8},{4,12},{8,0},{12,4},{16,24},{20,28},{24,16},{28,20},{1,9},{5... | collective-permute-start | bytes 884744 | tf_op jit(solution)/shard_map/ppermute | solution.py:37
  275.8 40.6 %collective-permute-start.34 = (bf16[2,48,1536]{2,1,0:T(8,128)(2,1)S(1)}, bf16[2,48,1536]{2,1,0:T(8,128)(2,1)}, u32[]{:S(2)}, u32[]{:S(2)}) collective-permute-start(bf16[2,48,1536]{2,1,0:T(8,128)(2,1)S(1)} %get-tuple-element.251), channel_id=1, source_target_pairs={{0,16},{4,20},{8,24},{12,28},{16,0},{20,4},{24,8},{28,12},{1,17},{... | collective-permute-start | bytes 884744 | tf_op jit(solution)/shard_map/ppermute | solution.py:37
  298.2 37.4 %collective-permute-start.35 = (bf16[2,48,1536]{2,1,0:T(8,128)(2,1)}, bf16[2,48,1536]{2,1,0:T(8,128)(2,1)S(1)}, u32[]{:S(2)}, u32[]{:S(2)}) collective-permute-start(bf16[2,48,1536]{2,1,0:T(8,128)(2,1)} %get-tuple-element.252), channel_id=1, source_target_pairs={{0,24},{4,28},{8,16},{12,20},{16,8},{20,12},{24,0},{28,4},{1,25},{... | collective-permute-start | bytes 884744 | tf_op jit(solution)/shard_map/ppermute | solution.py:37
  298.2 37.4 %collective-permute-start.36 = (bf16[8,48,384]{2,1,0:T(8,128)(2,1)}, bf16[8,48,384]{2,1,0:T(8,128)(2,1)S(1)}, u32[]{:S(2)}, u32[]{:S(2)}) collective-permute-start(bf16[8,48,384]{2,1,0:T(8,128)(2,1)} %get-tuple-element.253), channel_id=1, source_target_pairs={{0,2},{1,3},{2,0},{3,1},{4,6},{5,7},{6,4},{7,5},{8,10},{9,11},{10,... | collective-permute-start | bytes 884744 | tf_op jit(solution)/shard_map/ppermute | solution.py:31
  299.4 36.3 %collective-permute-start.37 = (bf16[256,768]{1,0:T(8,128)(2,1)}, bf16[256,768]{1,0:T(8,128)(2,1)S(1)}, u32[]{:S(2)}, u32[]{:S(2)}) collective-permute-start(bf16[256,768]{1,0:T(8,128)(2,1)} %get-tuple-element.254), channel_id=1, source_target_pairs={{24,28},{28,24},{25,29},{29,25},{26,30},{30,26},{27,31},{31,27}} | collective-permute-start | bytes 1179656 | tf_op jit(solution)/shard_map/ppermute | solution.py:34
  300.1 35.6 %collective-permute-start.38 = (bf16[256,768]{1,0:T(8,128)(2,1)}, bf16[256,768]{1,0:T(8,128)(2,1)S(1)}, u32[]{:S(2)}, u32[]{:S(2)}) collective-permute-start(bf16[256,768]{1,0:T(8,128)(2,1)} %get-tuple-element.255), channel_id=1, source_target_pairs={{16,20},{20,16},{24,28},{28,24},{17,21},{21,17},{25,29},{29,25},{1... | collective-permute-start | bytes 1179656 | tf_op jit(solution)/shard_map/ppermute | solution.py:34
  316.5 19.2 %collective-permute-start.32 = (bf16[4,96,768]{2,1,0:T(8,128)(2,1)}, bf16[4,96,768]{2,1,0:T(8,128)(2,1)S(1)}, u32[]{:S(2)}, u32[]{:S(2)}) collective-permute-start(bf16[4,96,768]{2,1,0:T(8,128)(2,1)} %get-tuple-element.249), channel_id=1, source_target_pairs={{0,4},{4,0},{8,12},{12,8},{16,20},{20,16},{24,28},{28,24},{1,5},{5... | collective-permute-start | bytes 1769480 | tf_op jit(solution)/shard_map/ppermute | solution.py:34
  366.1 13.1 %collective-permute-start.39 = (bf16[256,768]{1,0:T(8,128)(2,1)}, bf16[256,768]{1,0:T(8,128)(2,1)}, u32[]{:S(2)}, u32[]{:S(2)}) collective-permute-start(bf16[256,768]{1,0:T(8,128)(2,1)} %add_convert_fusion.12), channel_id=1, source_target_pairs={{24,16},{28,20},{25,17},{29,21},{26,18},{30,22},{27,19},{31,23}} | collective-permute-start | bytes 1179656 | tf_op jit(solution)/shard_map/ppermute | solution.py:43
  382.8 51.7 %collective-permute-start.41 = (bf16[8,2,48,640]{3,2,1,0:T(8,128)(2,1)}, bf16[8,2,48,640]{3,2,1,0:T(8,128)(2,1)}, u32[]{:S(2)}, u32[]{:S(2)}) collective-permute-start(bf16[8,2,48,640]{3,2,1,0:T(8,128)(2,1)} %bitcast.49), channel_id=1, source_target_pairs={{0,1},{1,0},{2,3},{3,2},{4,5},{5,4},{6,7},{7,6},{8,9},{9,8},{10,11... | collective-permute-start | bytes 2949128 | tf_op jit(solution)/shard_map/ppermute | solution.py:28
  387.9 17.1 %collective-permute-start.45 = (bf16[96,768]{1,0:T(8,128)(2,1)S(1)}, bf16[96,768]{1,0:T(8,128)(2,1)S(1)}, u32[]{:S(2)}, u32[]{:S(2)}) collective-permute-start(bf16[96,768]{1,0:T(8,128)(2,1)S(1)} %copy-done.31), channel_id=1, source_target_pairs={{0,8},{4,12},{8,0},{12,4},{16,24},{20,28},{24,16},{28,20},{1,9},{5... | collective-permute-start | bytes 442376 | tf_op jit(solution)/shard_map/ppermute | solution.py:37
  399.3 15.1 %collective-permute-start.46 = (bf16[96,768]{1,0:T(8,128)(2,1)S(1)}, bf16[96,768]{1,0:T(8,128)(2,1)S(1)}, u32[]{:S(2)}, u32[]{:S(2)}) collective-permute-start(bf16[96,768]{1,0:T(8,128)(2,1)S(1)} %copy-done.30), channel_id=1, source_target_pairs={{0,16},{4,20},{8,24},{12,28},{16,0},{20,4},{24,8},{28,12},{1,17},{... | collective-permute-start | bytes 442376 | tf_op jit(solution)/shard_map/ppermute | solution.py:37
  403.4 21.0 %collective-permute-start.47 = (bf16[96,768]{1,0:T(8,128)(2,1)S(1)}, bf16[96,768]{1,0:T(8,128)(2,1)S(1)}, u32[]{:S(2)}, u32[]{:S(2)}) collective-permute-start(bf16[96,768]{1,0:T(8,128)(2,1)S(1)} %copy-done.29), channel_id=1, source_target_pairs={{0,24},{4,28},{8,16},{12,20},{16,8},{20,12},{24,0},{28,4},{1,25},{... | collective-permute-start | bytes 442376 | tf_op jit(solution)/shard_map/ppermute | solution.py:37
  403.4 31.1 %collective-permute-start.40 = (bf16[8,2,56,512]{3,2,1,0:T(8,128)(2,1)}, bf16[8,2,56,512]{3,2,1,0:T(8,128)(2,1)}, u32[]{:S(2)}, u32[]{:S(2)}) collective-permute-start(bf16[8,2,56,512]{3,2,1,0:T(8,128)(2,1)} %fusion.29), channel_id=1, source_target_pairs={{0,1},{1,0},{2,3},{3,2},{4,5},{5,4},{6,7},{7,6},{8,9},{9,8},{10,11... | collective-permute-start | bytes 2752520 | tf_op jit(solution)/shard_map/ppermute | solution.py:28
  405.1 20.7 %collective-permute-start.48 = (bf16[48,1536]{1,0:T(8,128)(2,1)S(1)}, bf16[48,1536]{1,0:T(8,128)(2,1)S(1)}, u32[]{:S(2)}, u32[]{:S(2)}) collective-permute-start(bf16[48,1536]{1,0:T(8,128)(2,1)S(1)} %copy-done.43), channel_id=1, source_target_pairs={{0,2},{1,3},{2,0},{3,1},{4,6},{5,7},{6,4},{7,5},{8,10},{9,11},{10,... | collective-permute-start | bytes 442376 | tf_op jit(solution)/shard_map/ppermute | solution.py:31
  414.3 12.9 %collective-permute-start.49 = (bf16[4,48,384]{2,1,0:T(8,128)(2,1)S(1)}, bf16[4,48,384]{2,1,0:T(8,128)(2,1)S(1)}, u32[]{:S(2)}, u32[]{:S(2)}) collective-permute-start(bf16[4,48,384]{2,1,0:T(8,128)(2,1)S(1)} %copy-done.42), channel_id=1, source_target_pairs={{0,4},{4,0},{8,12},{12,8},{16,20},{20,16},{24,28},{28,24},{1,5},{5... | collective-permute-start | bytes 442376 | tf_op jit(solution)/shard_map/ppermute | solution.py:34
  424.4 10.1 %collective-permute-start.44 = (bf16[256,768]{1,0:T(8,128)(2,1)}, bf16[256,768]{1,0:T(8,128)(2,1)}, u32[]{:S(2)}, u32[]{:S(2)}) collective-permute-start(bf16[256,768]{1,0:T(8,128)(2,1)} %get-tuple-element.364), channel_id=1, source_target_pairs={{4,0},{12,8},{20,16},{28,24},{5,1},{13,9},{21,17},{29,25},{6,2},{1... | collective-permute-start | bytes 1179656 | tf_op jit(solution)/shard_map/ppermute | solution.py:34
  425.8 8.7 %collective-permute-start.42 = (bf16[256,768]{1,0:T(8,128)(2,1)}, bf16[256,768]{1,0:T(8,128)(2,1)}, u32[]{:S(2)}, u32[]{:S(2)}) collective-permute-start(bf16[256,768]{1,0:T(8,128)(2,1)} %get-tuple-element.365), channel_id=1, source_target_pairs={{8,12},{12,8},{16,20},{20,16},{24,28},{28,24},{9,13},{13,9},{17,21... | collective-permute-start | bytes 1179656 | tf_op jit(solution)/shard_map/ppermute | solution.py:34
  427.3 7.2 %collective-permute-start.43 = (bf16[256,768]{1,0:T(8,128)(2,1)}, bf16[256,768]{1,0:T(8,128)(2,1)}, u32[]{:S(2)}, u32[]{:S(2)}) collective-permute-start(bf16[256,768]{1,0:T(8,128)(2,1)} %add_convert_fusion.11), channel_id=1, source_target_pairs={{16,8},{20,12},{24,16},{28,20},{17,9},{21,13},{25,17},{29,21},{18,... | collective-permute-start | bytes 1179656 | tf_op jit(solution)/shard_map/ppermute | solution.py:43
  438.3 21.0 %collective-permute-start.66 = (f32[24,1536]{1,0:T(8,128)S(1)}, f32[24,1536]{1,0:T(8,128)S(1)}, u32[]{:S(2)}, u32[]{:S(2)}) collective-permute-start(f32[24,1536]{1,0:T(8,128)S(1)} %dynamic-slice_bitcast_fusion.18), channel_id=1, source_target_pairs={{0,1},{1,0},{2,3},{3,2},{4,5},{5,4},{6,7},{7,6},{8,9},{9,8},{10,11... | collective-permute-start | bytes 442376 | tf_op jit(solution)/shard_map/ppermute | solution.py:28
  442.3 18.0 %collective-permute-start.53 = (bf16[48,384]{1,0:T(8,128)(2,1)}, bf16[48,384]{1,0:T(8,128)(2,1)S(1)}, u32[]{:S(2)}, u32[]{:S(2)}) collective-permute-start(bf16[48,384]{1,0:T(8,128)(2,1)} %get-tuple-element.314), channel_id=1, source_target_pairs={{0,8},{4,12},{8,0},{12,4},{16,24},{20,28},{24,16},{28,20},{1,9},{5... | collective-permute-start | bytes 110600 | tf_op jit(solution)/shard_map/ppermute | solution.py:37
  452.4 12.5 %collective-permute-start.54 = (bf16[48,384]{1,0:T(8,128)(2,1)}, bf16[48,384]{1,0:T(8,128)(2,1)S(1)}, u32[]{:S(2)}, u32[]{:S(2)}) collective-permute-start(bf16[48,384]{1,0:T(8,128)(2,1)} %get-tuple-element.315), channel_id=1, source_target_pairs={{0,16},{4,20},{8,24},{12,28},{16,0},{20,4},{24,8},{28,12},{1,17},{... | collective-permute-start | bytes 110600 | tf_op jit(solution)/shard_map/ppermute | solution.py:37
  455.8 13.9 %collective-permute-start.52 = (bf16[256,768]{1,0:T(8,128)(2,1)}, bf16[256,768]{1,0:T(8,128)(2,1)}, u32[]{:S(2)}, u32[]{:S(2)}) collective-permute-start(bf16[256,768]{1,0:T(8,128)(2,1)} %add_convert_fusion.10), channel_id=1, source_target_pairs={{8,0},{12,4},{16,8},{20,12},{24,16},{28,20},{9,1},{13,5},{17,9},{2... | collective-permute-start | bytes 1179656 | tf_op jit(solution)/shard_map/ppermute | solution.py:43
  457.3 12.7 %collective-permute-start.50 = (bf16[8,56,512]{2,1,0:T(8,128)(2,1)}, bf16[8,56,512]{2,1,0:T(8,128)(2,1)}, u32[]{:S(2)}, u32[]{:S(2)}) collective-permute-start(bf16[8,56,512]{2,1,0:T(8,128)(2,1)} %get-tuple-element.311), channel_id=1, source_target_pairs={{0,2},{1,3},{2,0},{3,1},{4,6},{5,7},{6,4},{7,5},{8,10},{9,11},{10,... | collective-permute-start | bytes 1376264 | tf_op jit(solution)/shard_map/ppermute | solution.py:31
  459.3 12.9 %collective-permute-start.51 = (bf16[4,2,48,640]{3,2,1,0:T(8,128)(2,1)S(1)}, bf16[4,2,48,640]{3,2,1,0:T(8,128)(2,1)}, u32[]{:S(2)}, u32[]{:S(2)}) collective-permute-start(bf16[4,2,48,640]{3,2,1,0:T(8,128)(2,1)S(1)} %get-tuple-element.312), channel_id=1, source_target_pairs={{0,4},{4,0},{8,12},{12,8},{16,20},{20,16},{24,28},{28,24},{1,5},{5... | collective-permute-start | bytes 1474568 | tf_op jit(solution)/shard_map/ppermute | solution.py:34
  460.3 9.3 %collective-permute-start.55 = (bf16[48,384]{1,0:T(8,128)(2,1)S(1)}, bf16[48,384]{1,0:T(8,128)(2,1)}, u32[]{:S(2)}, u32[]{:S(2)}) collective-permute-start(bf16[48,384]{1,0:T(8,128)(2,1)S(1)} %get-tuple-element.316), channel_id=1, source_target_pairs={{0,24},{4,28},{8,16},{12,20},{16,8},{20,12},{24,0},{28,4},{1,25},{... | collective-permute-start | bytes 110600 | tf_op jit(solution)/shard_map/ppermute | solution.py:37
  477.3 6.4 %collective-permute-start.65 = (f32[24,384]{1,0:T(8,128)S(1)}, f32[24,384]{1,0:T(8,128)S(1)}, u32[]{:S(2)}, u32[]{:S(2)}) collective-permute-start(f32[24,384]{1,0:T(8,128)S(1)} %dynamic-slice_bitcast_fusion.38), channel_id=1, source_target_pairs={{0,1},{1,0},{2,3},{3,2},{4,5},{5,4},{6,7},{7,6},{8,9},{9,8},{10,11... | collective-permute-start | bytes 110600 | tf_op jit(solution)/shard_map/ppermute | solution.py:28
  477.3 7.4 %collective-permute-start.57 = (bf16[2,48,640]{2,1,0:T(8,128)(2,1)S(1)}, bf16[2,48,640]{2,1,0:T(8,128)(2,1)S(1)}, u32[]{:S(2)}, u32[]{:S(2)}) collective-permute-start(bf16[2,48,640]{2,1,0:T(8,128)(2,1)S(1)} %get-tuple-element.326), channel_id=1, source_target_pairs={{0,8},{4,12},{8,0},{12,4},{16,24},{20,28},{24,16},{28,20},{1,9},{5... | collective-permute-start | bytes 368648 | tf_op jit(solution)/shard_map/ppermute | solution.py:37
  479.8 12.3 %collective-permute-start.58 = (bf16[2,48,640]{2,1,0:T(8,128)(2,1)S(1)}, bf16[2,48,640]{2,1,0:T(8,128)(2,1)S(1)}, u32[]{:S(2)}, u32[]{:S(2)}) collective-permute-start(bf16[2,48,640]{2,1,0:T(8,128)(2,1)S(1)} %get-tuple-element.327), channel_id=1, source_target_pairs={{0,16},{4,20},{8,24},{12,28},{16,0},{20,4},{24,8},{28,12},{1,17},{... | collective-permute-start | bytes 368648 | tf_op jit(solution)/shard_map/ppermute | solution.py:37
  480.8 11.3 %collective-permute-start.59 = (bf16[2,48,640]{2,1,0:T(8,128)(2,1)S(1)}, bf16[2,48,640]{2,1,0:T(8,128)(2,1)S(1)}, u32[]{:S(2)}, u32[]{:S(2)}) collective-permute-start(bf16[2,48,640]{2,1,0:T(8,128)(2,1)S(1)} %get-tuple-element.328), channel_id=1, source_target_pairs={{0,24},{4,28},{8,16},{12,20},{16,8},{20,12},{24,0},{28,4},{1,25},{... | collective-permute-start | bytes 368648 | tf_op jit(solution)/shard_map/ppermute | solution.py:37
  482.2 9.9 %collective-permute-start.56 = (bf16[4,56,512]{2,1,0:T(8,128)(2,1)S(1)}, bf16[4,56,512]{2,1,0:T(8,128)(2,1)S(1)}, u32[]{:S(2)}, u32[]{:S(2)}) collective-permute-start(bf16[4,56,512]{2,1,0:T(8,128)(2,1)S(1)} %get-tuple-element.325), channel_id=1, source_target_pairs={{0,4},{4,0},{8,12},{12,8},{16,20},{20,16},{24,28},{28,24},{1,5},{5... | collective-permute-start | bytes 688136 | tf_op jit(solution)/shard_map/ppermute | solution.py:34
  492.3 6.4 %collective-permute-start.60 = (bf16[56,512]{1,0:T(8,128)(2,1)S(1)}, bf16[56,512]{1,0:T(8,128)(2,1)S(1)}, u32[]{:S(2)}, u32[]{:S(2)}) collective-permute-start(bf16[56,512]{1,0:T(8,128)(2,1)S(1)} %get-tuple-element.335), channel_id=1, source_target_pairs={{0,8},{4,12},{8,0},{12,4},{16,24},{20,28},{24,16},{28,20},{1,9},{5... | collective-permute-start | bytes 172040 | tf_op jit(solution)/shard_map/ppermute | solution.py:37
  494.8 6.6 %collective-permute-start.61 = (bf16[56,512]{1,0:T(8,128)(2,1)S(1)}, bf16[56,512]{1,0:T(8,128)(2,1)S(1)}, u32[]{:S(2)}, u32[]{:S(2)}) collective-permute-start(bf16[56,512]{1,0:T(8,128)(2,1)S(1)} %get-tuple-element.336), channel_id=1, source_target_pairs={{0,16},{4,20},{8,24},{12,28},{16,0},{20,4},{24,8},{28,12},{1,17},{... | collective-permute-start | bytes 172040 | tf_op jit(solution)/shard_map/ppermute | solution.py:37
  494.8 6.6 %collective-permute-start.62 = (bf16[56,512]{1,0:T(8,128)(2,1)S(1)}, bf16[56,512]{1,0:T(8,128)(2,1)S(1)}, u32[]{:S(2)}, u32[]{:S(2)}) collective-permute-start(bf16[56,512]{1,0:T(8,128)(2,1)S(1)} %get-tuple-element.337), channel_id=1, source_target_pairs={{0,24},{4,28},{8,16},{12,20},{16,8},{20,12},{24,0},{28,4},{1,25},{... | collective-permute-start | bytes 172040 | tf_op jit(solution)/shard_map/ppermute | solution.py:37
  497.2 4.2 collective-permute-start.63
  (81 other events, 933.2 us)

commit v4 on v3

--- a/solution.py
+++ b/solution.py
@@ -70,8 +70,16 @@
     return a.astype(F32) + b.astype(F32)
 
 
-def z_parts(at, g):
-    return pick(g, at.z, 0), [pick(g, at.z ^ n, 0) for n in (1, 2, 3)]
+def joined(mine, got, index, axis):
+    return plus(pick(mine, index, axis), pick(got, index, axis)).astype(BF)
+
+
+def halve(bit, mine, got, axis):
+    return joined(mine, got, bit, axis), joined(mine, got, 1 - bit, axis)
+
+
+def z_parts(at, mine, got):
+    return joined(mine, got, at.z, 0), [joined(mine, got, at.z ^ n, 0) for n in (1, 2, 3)]
 
 
 def z_move(at, parts):
@@ -186,6 +194,7 @@
         in_specs=[smem, vmem, vmem],
         out_specs=[vmem] * 4 + [smem],
         out_shape=[jax.ShapeDtypeStruct(shape, F32) for shape in shapes] + [jax.ShapeDtypeStruct((tiles,), jnp.int32)],
+        name="tables",
         scratch_shapes=[pltpu.VMEM((8, 128), F32)],
     )(leaf.reshape(1), seg, parent)
 
@@ -197,32 +206,44 @@
     return copies
 
 
-def placed(ref, count, size, table, row):
-    return [
-        ref.at[pl.ds(pl.multiple_of(table[row, n] * size, size), size), :] for n in range(count)
-    ]
+def placed(blocks, ref, size, table, row):
+    pieces = []
+    for hbm in blocks:
+        for n in range(hbm.shape[0]):
+            place = pl.multiple_of(table[row, len(pieces)] * size, size)
+            pieces.append((hbm.at[n, pl.ds(0, size), :], ref.at[pl.ds(place, size), :]))
+    return pieces
+
+
+def tiled(sources, ref, rows):
+    return [(src, ref.at[pl.ds(n * rows, rows), :]) for n, src in enumerate(sources)]
 
 
 def project_kernel(
-    count, size, first_rows, table_ref, x_ref, mask_ref, embed_ref, gain_ref, own_hbm, other_hbm, cos_ref, sin_ref,
-    a_ref, q_ref, k_ref, v_ref, own_ref, other_ref, sems,
+    blocks, sources, size, rows, table_ref, mask_ref, embed_ref, gain_ref, cos_ref, sin_ref, *refs,
 ):
+    own_hbm, other_hbm, tiles = refs[:blocks], refs[blocks : 2 * blocks], refs[2 * blocks : 2 * blocks + sources]
+    q_ref, k_ref, v_ref, x_ref, own_ref, other_ref, sems = refs[2 * blocks + sources :]
     tile = pl.program_id(0)
+    step = k_ref.shape[0]
 
     @pl.when(tile == 0)
     def _():
-        pieces = []
-        for hbm, ref in ((own_hbm, own_ref), (other_hbm, other_ref)):
-            spots = placed(ref, count, size, table_ref, 0)
-            pieces += [(hbm.at[n, pl.ds(0, size), :], spots[n]) for n in range(count)]
-        for copy in fetch(pieces, sems):
+        pieces = tiled([tiles[0]] + list(tiles), x_ref, rows)
+        count = len(pieces)
+        pieces += placed(own_hbm, own_ref, size, table_ref, 0) + placed(other_hbm, other_ref, size, table_ref, 0)
+        copies = fetch(pieces, sems)
+        for copy in copies[:count]:
             copy.wait()
-
-    x = jnp.where(mask_ref[...] > 0, embed_ref[...], x_ref[...].astype(F32))
+        masked = column(mask_ref[...].astype(F32)) > 0
+        x_ref[rows : 2 * rows, :] = jnp.where(masked, embed_ref[...], x_ref[rows : 2 * rows, :].astype(F32)).astype(BF)
+        for copy in copies[count:]:
+            copy.wait()
+
+    x = x_ref[pl.ds(pl.multiple_of(tile * step, step), step), :].astype(F32)
     centred = x - jnp.mean(x, axis=-1, keepdims=True)
     spread = jnp.mean(centred * centred, axis=-1, keepdims=True)
     a = (centred * lax.rsqrt(spread + EPSILON) * gain_ref[...]).astype(BF)
-    a_ref[...] = a
     cosine, sine = cos_ref[...], sin_ref[...]
     half = own_ref.shape[1] // 3
     for n, w_ref in enumerate((own_ref, other_ref)):
@@ -233,82 +254,85 @@
         values = jnp.dot(a, w_ref[:, 2 * half :], preferred_element_type=F32)
         v_ref[:, base : base + half] = values.astype(BF)
 
-    @pl.when(tile * x_ref.shape[0] < first_rows)
+    @pl.when(tile * step < 2 * rows)
     def _():
-        rows = q_ref.shape[0]
+        lines = q_ref.shape[0]
         for n, w_ref in enumerate((own_ref, other_ref)):
             base = n * half
-            q = jnp.dot(a[:rows], w_ref[:, :half], preferred_element_type=F32)
-            for g, part in enumerate(turn(q, cosine[:rows], sine[:rows])):
+            q = jnp.dot(a[:lines], w_ref[:, :half], preferred_element_type=F32)
+            for g, part in enumerate(turn(q, cosine[:lines], sine[:lines])):
                 q_ref[:, base + g * 128 : base + (g + 1) * 128] = part.astype(BF)
 
 
-def project(table, x_all, mask, embed, gain, own, other, cosine, sine, rows):
-    total, width = x_all.shape
+def project(table, tiles, mask, embed, gain, own, other, cosine, sine):
+    rows, width = tiles[0].shape
+    total = (len(tiles) + 1) * rows
     step = next(n for n in (3 * rows, 2 * rows, rows) if total % n == 0)
     q_step = min(step, 2 * rows)
     last_q = 2 * rows // q_step - 1
-    count = own.shape[0]
-    size = width // count
-    columns = own.shape[2]
-    whole = lambda shape: spec(shape, lambda t, i: (0, 0))
+    count = sum(v.shape[0] for v in own)
+    columns = own[0].shape[2]
+    whole = lambda v: spec(v.shape, lambda t, i: (0, 0))
     moved = lambda n: spec((step, n), lambda t, i: (t, 0))
     out = lambda n: jax.ShapeDtypeStruct((n, width), BF)
     anywhere = pl.BlockSpec(memory_space=pl.ANY)
+    far = list(own) + list(other) + list(tiles)
     return pl.pallas_call(
-        functools.partial(project_kernel, count, size, 2 * rows),
+        functools.partial(project_kernel, len(own), len(tiles), width // count, rows),
         grid_spec=pltpu.PrefetchScalarGridSpec(
             num_scalar_prefetch=1,
             grid=(total // step,),
-            in_specs=[
-                moved(width), moved(1), whole((1, width)), whole((1, width)), anywhere, anywhere, moved(128), moved(128),
-            ],
+            in_specs=[whole(mask), whole(embed), whole(gain), moved(128), moved(128)] + [anywhere] * len(far),
             out_specs=[
-                moved(width),
                 spec((q_step, width), lambda t, i: (jnp.minimum(t, last_q), 0)),
                 moved(width),
                 moved(width),
             ],
             scratch_shapes=[
+                pltpu.VMEM((total, width), BF),
                 pltpu.VMEM((width, columns), BF),
                 pltpu.VMEM((width, columns), BF),
-                pltpu.SemaphoreType.DMA((2 * count,)),
+                pltpu.SemaphoreType.DMA((2 * count + len(tiles) + 1,)),
             ],
         ),
-        out_shape=[out(total), out(2 * rows), out(total), out(total)],
+        out_shape=[out(2 * rows), out(total), out(total)],
         compiler_params=pltpu.CompilerParams(vmem_limit_bytes=VMEM_LIMIT),
         cost_estimate=pl.CostEstimate(
             flops=2 * total * width * 2 * width + 4 * rows * width * width,
-            bytes_accessed=2 * (4 * total * width + 3 * width * width),
+            bytes_accessed=2 * (3 * total * width + 3 * width * width),
             transcendentals=0,
         ),
-    )(table, x_all, mask, embed, gain, own, other, cosine, sine)
+        name="project",
+    )(table, mask, embed, gain, cosine, sine, *far)
 
 
 def middle_kernel(
-    count, size, chunk, table_ref, o_ref, x_ref, mask_ref, embed_ref, dy_ref, gain_ref, up_b_ref, down_b_ref,
-    one_own, one_other, two_own, two_other,
-    y_ref, b_ref, g_ref, du_ref, dh_low_ref, do_ref, dh_ref, dgain_ref, dup_b_ref, ddown_b_ref,
-    out_ref, up_ref, down_ref, sems,
+    blocks_one, blocks_two, size, chunk, table_ref, o_ref, x_ref, mask_ref, embed_ref, dy_ref, gain_ref, up_b_ref,
+    down_b_ref, *refs,
 ):
+    refs = list(refs)
+    take = lambda n: [refs.pop(0) for _ in range(n)]
+    ones, twos = (take(blocks_one), take(blocks_one)), (take(blocks_two), take(blocks_two))
+    y_ref, b_ref, g_ref, du_ref, dh_low_ref, do_ref, dh_ref, dgain_ref, dup_b_ref, ddown_b_ref = take(10)
+    out_ref, up_ref, down_ref, sems = refs
     cut = out_ref.shape[1] // 2
     units = up_ref.shape[2]
     pieces_out, pieces_up, pieces_down = [], [], []
-    for n, (one, two) in enumerate(((one_own, two_own), (one_other, two_other))):
-        column = pl.multiple_of(table_ref[3, n] * cut, cut)
-        for j in range(count):
-            spot = pl.multiple_of(table_ref[1, j] * size, size)
-            pieces_out.append(
-                (one.at[j, :, pl.ds(0, cut)], out_ref.at[pl.ds(spot, size), pl.ds(column, cut)])
-            )
-            spot = pl.multiple_of(table_ref[0, j] * size, size)
-            pieces_up.append((one.at[j, :, pl.ds(cut, units)], up_ref.at[n, pl.ds(spot, size), :]))
-            spot = pl.multiple_of(table_ref[2, j] * chunk, chunk)
-            pieces_down.append((two.at[j], down_ref.at[n, pl.ds(spot, chunk), :]))
+    for n in range(2):
+        columns = pl.ds(pl.multiple_of(table_ref[3, n] * cut, cut), cut)
+        spots = [(hbm, j) for hbm in ones[n] for j in range(hbm.shape[0])]
+        for place, (hbm, j) in enumerate(spots):
+            to = pl.ds(pl.multiple_of(table_ref[1, place] * size, size), size)
+            pieces_out.append((hbm.at[j, :, pl.ds(0, cut)], out_ref.at[to, columns]))
+            to = pl.ds(pl.multiple_of(table_ref[0, place] * size, size), size)
+            pieces_up.append((hbm.at[j, :, pl.ds(cut, units)], up_ref.at[n, to, :]))
+        pieces_down += placed(twos[n], down_ref.at[n], chunk, table_ref, 2)
     copies = fetch(pieces_out + pieces_up + pieces_down, sems)
-    for copy in copies[: 2 * count]:
+    for copy in copies[: len(pieces_out)]:
         copy.wait()
-    x = jnp.where(mask_ref[...] > 0, embed_ref[...], x_ref[...].astype(F32))
+    x = x_ref[...].astype(F32)
+    masked = column(mask_ref[...].astype(F32)) > 0
+    x = jnp.concatenate([x, jnp.where(masked, embed_ref[...], x)], axis=0)
     h = x + jnp.dot(o_ref[...], out_ref[...], preferred_element_type=F32)
     centred = h - jnp.mean(h, axis=-1, keepdims=True)
     spread = jnp.mean(centred * centred, axis=-1, keepdims=True)
@@ -318,7 +342,7 @@
     b_ref[...] = b
     dy = dy_ref[...]
     ddown_b_ref[...] = jnp.sum(dy.astype(F32), axis=0, keepdims=True)
-    for copy in copies[2 * count :]:
+    for copy in copies[len(pieces_out) :]:
         copy.wait()
     y = h + down_b_ref[...]
     db = None
@@ -348,22 +372,23 @@
 
 def middle(table, o, x, mask, embed, dy, gain, up_b, down_b, one, two):
     rows, width = o.shape
-    count, size, columns = one[0].shape
-    chunk = two[0].shape[1]
+    count = sum(v.shape[0] for v in one[0])
+    size, columns = one[0][0].shape[1:]
+    chunk = two[0][0].shape[1]
     units = columns - width // 2
-    anywhere = pl.BlockSpec(memory_space=pl.ANY)
     full = lambda shape: spec(shape, lambda t, i: (0, 0))
+    near = (o, x, mask, embed, dy, gain, up_b, down_b)
+    far = list(one[0]) + list(one[1]) + list(two[0]) + list(two[1])
     shapes = [
         ((rows, width), BF), ((rows, width), BF), ((rows, 2 * units), BF), ((rows, 2 * units), BF), ((rows, width), BF),
         ((rows, width), BF), ((rows, width), F32), ((1, width), F32), ((2, units), F32), ((1, width), F32),
     ]
     return pl.pallas_call(
-        functools.partial(middle_kernel, count, size, chunk),
+        functools.partial(middle_kernel, len(one[0]), len(two[0]), size, chunk),
         grid_spec=pltpu.PrefetchScalarGridSpec(
             num_scalar_prefetch=1,
             grid=(1,),
-            in_specs=[full((rows, v.shape[1]) if v is x or v is mask else v.shape) for v in (o, x, mask, embed, dy, gain, up_b, down_b)]
-            + [anywhere] * 4,
+            in_specs=[full(v.shape) for v in near] + [pl.BlockSpec(memory_space=pl.ANY)] * len(far),
             out_specs=[full(shape) for shape, _ in shapes],
             scratch_shapes=[
                 pltpu.VMEM((width, width), BF),
@@ -379,7 +404,8 @@
             bytes_accessed=4 * (width * width + 4 * units * width),
             transcendentals=2 * rows * units,
         ),
-    )(table, o, x, mask, embed, dy, gain, up_b, down_b, one[0], one[1], two[0], two[1])
+        name="middle",
+    )(table, *near, *far)
 
 
 def matmul_t(a, b):
@@ -491,6 +517,7 @@
             bytes_accessed=4 * (total + rows) * width,
             transcendentals=2 * rows * total * width // HEAD_DIM,
         ),
+        name="attend",
     )(flags, qcol, krow, q, k, v)
 
 
@@ -607,53 +634,77 @@
             bytes_accessed=8 * (there + rows) * width,
             transcendentals=2 * rows * there * width // HEAD_DIM,
         ),
+        name="attend_back_near" if near else "attend_back_far",
     )(flags, qrow, kcol, q, k, v, o, g, lse, cosine, sine, *([part] if near else []))
 
 
-def fold_kernel(
-    count, size, rows, first, table_ref, dk_ref, dv_ref, x_ref, mask_ref, embed_ref, gain_ref, own_hbm, other_hbm, *refs,
-):
-    near = first == 0
+def t_matmul(a, b):
+    return lax.dot_general(a, b, (((0,), (0,)), ((), ())), preferred_element_type=F32)
+
+
+def fold_kernel(near, blocks, sources, size, rows, table_ref, mask_ref, embed_ref, gain_ref, dk_ref, dv_ref, *refs):
     refs = list(refs)
-    dq_ref, dh_ref = refs[:2] if near else (None, None)
-    outs = refs[2:] if near else refs
+    take = lambda n: [refs.pop(0) for _ in range(n)]
     if near:
-        da_ref, dgain_ref, clean_ref, noisy_ref, dembed_ref, acc_ref, own_ref, other_ref, sems = outs
+        dq_ref, dh_ref, part_ref = take(3)
+    own_hbm, other_hbm, tiles = take(blocks), take(blocks), take(sources)
+    if near:
+        da_ref, dgain_ref, clean_ref, noisy_ref, dembed_ref = take(5)
+        piece_refs = take(4)
     else:
-        da_ref, dgain_ref, acc_ref, own_ref, other_ref, sems = outs
+        da_ref, dgain_ref, part_ref = take(3)
+    acc_ref, x_ref, own_ref, other_ref, sems = refs[:5]
+    dkv_ref, dwq_ref = refs[5:] if near else (part_ref, None)
     tile = pl.program_id(0)
+    width = x_ref.shape[1]
+    half = own_ref.shape[1] // 3
+    cuts = [slice(n * half, (n + 1) * half) for n in range(3)]
 
     @pl.when(tile == 0)
     def _():
-        pieces = []
-        for hbm, ref in ((own_hbm, own_ref), (other_hbm, other_ref)):
-            spots = placed(ref, count, size, table_ref, 0)
-            pieces += [(hbm.at[n, pl.ds(0, size), :], spots[n]) for n in range(count)]
-        for copy in fetch(pieces, sems):
+        pieces = tiled(([tiles[0]] if near else []) + tiles, x_ref, rows)
+        count = len(pieces)
+        pieces += placed(own_hbm, own_ref, size, table_ref, 0) + placed(other_hbm, other_ref, size, table_ref, 0)
+        copies = fetch(pieces, sems)
+        dgain_ref[...] = jnp.zeros_like(dgain_ref)
+        if near:
+            dkv_ref[...] = part_ref[...]
+            dwq_ref[...] = jnp.zeros_like(dwq_ref)
+        else:
+            dkv_ref[...] = jnp.zeros_like(dkv_ref)
+        for copy in copies[:count]:
             copy.wait()
-        dgain_ref[...] = jnp.zeros_like(dgain_ref)
-
-    half = own_ref.shape[1] // 3
-    cuts = [slice(n * half, (n + 1) * half) for n in range(3)]
+        if near:
+            masked = column(mask_ref[...].astype(F32)) > 0
+            x_ref[rows : 2 * rows, :] = jnp.where(
+                masked, embed_ref[...], x_ref[rows : 2 * rows, :].astype(F32)
+            ).astype(BF)
+        for copy in copies[count:]:
+            copy.wait()
+
+    x = x_ref[pl.ds(pl.multiple_of(tile * rows, rows), rows), :].astype(F32)
+    centred = x - jnp.mean(x, axis=-1, keepdims=True)
+    scale = lax.rsqrt(jnp.mean(centred * centred, axis=-1, keepdims=True) + EPSILON)
+    hat = centred * scale
+    a = (hat * gain_ref[...]).astype(BF)
+    dk, dv = dk_ref[...], dv_ref[...]
+    dkv_ref[:, :width] += t_matmul(a, dk)
+    dkv_ref[:, width:] += t_matmul(a, dv)
     da = None
     for n, w_ref in enumerate((own_ref, other_ref)):
-        part = matmul_t(dk_ref[:, cuts[n]], w_ref[:, cuts[1]]) + matmul_t(dv_ref[:, cuts[n]], w_ref[:, cuts[2]])
+        part = matmul_t(dk[:, cuts[n]], w_ref[:, cuts[1]]) + matmul_t(dv[:, cuts[n]], w_ref[:, cuts[2]])
         da = part if da is None else da + part
     acc_ref[...] = da
     if near:
 
         @pl.when(tile < 2)
         def _():
-            acc_ref[...] += matmul_t(dq_ref[:, cuts[0]], own_ref[:, cuts[0]]) + matmul_t(
-                dq_ref[:, cuts[1]], other_ref[:, cuts[0]]
-            )
+            dq = dq_ref[...]
+            acc_ref[...] += matmul_t(dq[:, cuts[0]], own_ref[:, cuts[0]]) + matmul_t(dq[:, cuts[1]], other_ref[:, cuts[0]])
+            dwq_ref[...] += t_matmul(a, dq)
 
     da = acc_ref[...]
     da_ref[...] = da.astype(BF)
-    x = jnp.where(mask_ref[...] > 0, embed_ref[...], x_ref[...].astype(F32))
-    centred = x - jnp.mean(x, axis=-1, keepdims=True)
-    scale = lax.rsqrt(jnp.mean(centred * centred, axis=-1, keepdims=True) + EPSILON)
-    hat = centred * scale
     dgain_ref[...] += jnp.sum(da * hat, axis=0, keepdims=True)
     if near:
 
@@ -665,49 +716,63 @@
         def _():
             noisy = dh_ref[...] + norm_back(hat, scale, gain_ref[...], da)
             noisy_ref[...] = noisy
-            dembed_ref[...] = jnp.sum(jnp.where(mask_ref[...] > 0, noisy, 0.0), axis=0, keepdims=True)
-
-
-def fold(table, first, last, dk, dv, x_all, mask, embed, gain, own, other, rows, dq=None, dh=None):
-    width = x_all.shape[1]
-    there = (last - first) * rows
-    near = first == 0
-    count = own.shape[0]
-    size = width // count
-    columns = own.shape[2]
+            masked = column(mask_ref[...].astype(F32)) > 0
+            dembed_ref[...] = jnp.sum(jnp.where(masked, noisy, 0.0), axis=0, keepdims=True)
+
+        @pl.when(tile == pl.num_programs(0) - 1)
+        def _():
+            third = half // 3
+            for n in range(2):
+                base = n * half
+                first_ref, second_ref = piece_refs[2 * n], piece_refs[2 * n + 1]
+                first_ref[:, :half] = dwq_ref[:, base : base + half].astype(BF)
+                first_ref[:, half:] = dkv_ref[:, base : base + third].astype(BF)
+                second_ref[:, : half - third] = dkv_ref[:, base + third : base + half].astype(BF)
+                second_ref[:, half - third :] = dkv_ref[:, width + base : width + base + half].astype(BF)
+
+
+def fold(table, tiles, dk, dv, mask, embed, gain, own, other, near=None):
+    rows, width = tiles[0].shape
+    there = dk.shape[0]
+    count = sum(v.shape[0] for v in own)
+    columns = own[0].shape[2]
     whole = lambda shape: spec(shape, lambda t, i: (0, 0))
-    moved = lambda n: spec((rows, n), lambda t, i: (t, 0))
-    shifted = lambda n: spec((rows, n), lambda t, i: (t + first, 0))
-    early = lambda n: spec((rows, n), lambda t, i: (jnp.minimum(t, 1), 0))
-    second = lambda n: spec((rows, n), lambda t, i: (1, 0))
+    moved = spec((rows, width), lambda t, i: (t, 0))
     anywhere = pl.BlockSpec(memory_space=pl.ANY)
-    line = jax.ShapeDtypeStruct((1, width), F32)
-    tile = jax.ShapeDtypeStruct((rows, width), F32)
+    line = ((1, width), F32)
+    part = ((width, 2 * width), F32)
+    pieces = [((width, columns * n // 9), BF) for n in (4, 5)] * 2
+    fixed = [line] + ([((rows, width), F32)] * 2 + [line] + pieces if near else [part])
+    extra = [spec((rows, width), lambda t, i: (jnp.minimum(t, 1), 0)), spec((rows, width), lambda t, i: (1, 0)), whole(part[0])]
+    far = list(own) + list(other) + list(tiles)
     return pl.pallas_call(
-        functools.partial(fold_kernel, count, size, rows, first),
+        functools.partial(fold_kernel, near is not None, len(own), len(tiles), width // count, rows),
         grid_spec=pltpu.PrefetchScalarGridSpec(
             num_scalar_prefetch=1,
-            grid=(last - first,),
-            in_specs=[
-                moved(width), moved(width), shifted(width), shifted(1), whole((1, width)), whole((1, width)), anywhere, anywhere,
-            ] + ([early(width), second(width)] if near else []),
-            out_specs=[moved(width), whole((1, width))]
-            + ([whole((rows, width)), whole((rows, width)), whole((1, width))] if near else []),
+            grid=(there // rows,),
+            in_specs=[whole(v.shape) for v in (mask, embed, gain)]
+            + [moved, moved]
+            + (extra if near else [])
+            + [anywhere] * len(far),
+            out_specs=[moved] + [whole(shape) for shape, _ in fixed],
             scratch_shapes=[
                 pltpu.VMEM((rows, width), F32),
+                pltpu.VMEM((there, width), BF),
                 pltpu.VMEM((width, columns), BF),
                 pltpu.VMEM((width, columns), BF),
-                pltpu.SemaphoreType.DMA((2 * count,)),
-            ],
+                pltpu.SemaphoreType.DMA((2 * count + len(tiles) + 1,)),
+            ]
+            + ([pltpu.VMEM(part[0], F32), pltpu.VMEM((width, width), F32)] if near else []),
         ),
-        out_shape=[jax.ShapeDtypeStruct((there, width), BF), line] + ([tile, tile, line] if near else []),
+        out_shape=[jax.ShapeDtypeStruct((there, width), BF)] + [jax.ShapeDtypeStruct(shape, kind) for shape, kind in fixed],
         compiler_params=pltpu.CompilerParams(vmem_limit_bytes=VMEM_LIMIT),
         cost_estimate=pl.CostEstimate(
-            flops=4 * there * width * width,
-            bytes_accessed=2 * (4 * there * width + 3 * width * width),
+            flops=8 * there * width * width,
+            bytes_accessed=2 * (4 * there * width + 9 * width * width),
             transcendentals=0,
         ),
-    )(table, dk, dv, x_all, mask, embed, gain, own, other, *([dq, dh] if near else []))
+        name="fold_near" if near else "fold_far",
+    )(table, mask, embed, gain, dk, dv, *(near or ()), *far)
 
 
 def normalise(values):
@@ -793,7 +858,7 @@
         columns = jnp.where(jnp.arange(16) % 2 == 0, at.core, 1 - at.core)
         return jnp.stack([first, first ^ (8 * at.core), yzx.reshape(16), columns]).astype(jnp.int32)
 
-    def first_gather(self, hid, w_qkv, w_out, w_up, w_down, vectors):
+    def first_gather(self, hid, w_qkv, w_out, w_up, w_down, vectors, early):
         at = self.at
         few, chunk, cut = w_qkv.shape[0], w_down.shape[0], w_out.shape[1] // 2
         qkv_a, qkv_b = halves_of_heads(w_qkv)
@@ -805,35 +870,40 @@
         )[None]
         beside = at.swap_y(hid, [(i, i + 1) for i in range(0, 8, 2)])
         down_two = at.swap_x(w_down)
-        block, hid_up = tie(block, hid)
-        line = z_gather(at, block)
-        line, hid_up = tie(line, hid_up)
-        first_hop = at.up(hid_up, 0, 2)
-        plane = jnp.concatenate([line, at.swap_y(line)], axis=0)
         up_a, up_b = halves_of_units(w_up, chunk)
         one_a = jnp.concatenate([w_out[:, :cut], up_a], axis=1)
         one_b = jnp.concatenate([w_out[:, cut:], up_b], axis=1)
+        block, hid_up, one_a, one_b = tie(block, hid, one_a, one_b)
+        line = z_gather(at, block)
         one = to_column_half(at, one_a, one_b)[None]
+        line, hid_up, one, beside, down_two, early = tie(line, hid_up, one, beside, down_two, early)
+        first_hop = at.up(hid_up, 0, 2)
+        plane = jnp.concatenate([line, at.swap_y(line)], axis=0)
+        one_line = [one, at.swap_z(one, 1)]
         down_two = jnp.stack([w_down, down_two])[None]
-        first_hop, plane, beside, one, down_two = tie(first_hop, plane, beside, one, down_two)
-        other = at.swap_x(plane)
+        first_hop, plane, one_line, down_two = tie(first_hop, plane, one_line, down_two)
+        far = at.swap_x(plane)
+        other = [at.swap_core(plane)]
         second_hop = at.up(first_hop, 1, 2)
         first_over = at.swap_y(first_hop, [(i, i ^ 1) for i in range(2, 8)])
-        second_hop, first_over, one = tie(second_hop, first_over, one)
+        second_hop, first_over, other, one_line = tie(second_hop, first_over, other, one_line)
         third_hop = at.up(second_hop, 2, 2)
         second_over = at.swap_y(second_hop, [(i, i ^ 1) for i in range(4, 8)])
-        qkv = jnp.concatenate([plane, other], axis=0)
-        third_hop, second_over, qkv, one = tie(third_hop, second_over, qkv, one)
+        one_line.append(at.swap_z(one_line[0], 2))
+        third_hop, second_over, far, one_line = tie(third_hop, second_over, far, one_line)
         third_over = at.swap_y(third_hop, [(i, i ^ 1) for i in range(6, 8)])
-        qkv_both = (qkv, at.swap_core(qkv))
-        line = z_gather(at, one)
-        third_over, qkv_both, line = tie(third_over, qkv_both, line)
+        other.append(at.swap_core(far))
+        one_line.append(at.swap_z(one_line[0], 3))
         m = 2 * few
-        vec = jnp.concatenate([qkv[:, m, : vectors.shape[0]], qkv[:, m + 8, : vectors.shape[0]]], axis=1)
+        n = vectors.shape[0]
+        vec = jnp.concatenate([v[:, at_row, :n] for at_row in (m, m + 8) for v in (plane, far)], axis=0)
+        vec = jnp.concatenate([vec[:16], vec[16:]], axis=1)
         order = (self.places()[0][None, :] == jnp.arange(16)[:, None]).astype(BF)
         vec = mm(order, vec).reshape(32, -1)
+        third_over, other, one_line, vec, down_two = tie(third_over, other, one_line, vec, down_two)
+        line = jnp.concatenate(one_line, axis=0)
         lower = [first_hop, first_over, beside, second_hop, second_over, third_hop, third_over]
-        return lower, qkv_both, vec, (line, down_two)
+        return lower, ((plane, far), tuple(other)), vec, (line, down_two), early
 
     def second_start(self, state):
         line, down_two = state
@@ -842,13 +912,13 @@
     def second_go_on(self, state):
         plane, line = state
         at = self.at
-        one = jnp.concatenate([plane, at.swap_x(plane)], axis=0)
-        down = jnp.concatenate([line, at.swap_y(line)], axis=0)
-        return one, down.reshape((16,) + down.shape[2:])
+        near = line.reshape((8,) + line.shape[2:])
+        one = (plane, at.swap_x(plane)), [at.swap_core(plane)]
+        down = (near, at.swap_y(near)), [at.swap_core(near)]
+        return one, down
 
     def second_end(self, state):
-        one, down = state
-        return (one, self.at.swap_core(one)), (down, self.at.swap_core(down))
+        return [(own, tuple(other + [self.at.swap_core(own[1])])) for own, other in state]
 
     def unit_bias(self, bias, chunk):
         a, b = halves_of_units(bias[None], chunk)
@@ -862,115 +932,101 @@
     def backward(self, run):
         at = self.at
         rows = self.rows
-        cores = lambda g: (8, 2, g.shape[0] // 16, g.shape[1])
-        down_other, up_other = run.feed_other()
-        down_got, up_got = at.swap_core(down_other), at.swap_core(up_other)
-        down_own, up_own, out_own, out_other = run.feed_own(self)
-        down = plus(down_own, down_got).astype(BF).reshape(cores(down_own))
-        up = plus(up_own, up_got).astype(BF)
-        up = up.reshape((4, 2, 2, up.shape[0] // 16, up.shape[1]))
-        down_keep, down_send = choose(at.x, down, 1)
-        up_keep, up_send = choose(at.y, up, 1)
-        (down_keep, down_send, up_keep, up_send, out_own, out_other, run.grad_mixed) = tie(
-            down_keep, down_send, up_keep, up_send, out_own, out_other, run.grad_mixed
+        lower_z = lambda s: [(i, i ^ 1) for i in range(2 * s, 8)]
+        down_other, rest_other = run.feed_other(self)
+        down_got, rest_got = at.swap_core(down_other), at.swap_core(rest_other)
+        down_own, rest_own = run.feed_own(self)
+        by_x = lambda g: g.reshape(8, 2, g.shape[0] // 16, g.shape[1])
+        by_y = lambda g: g.reshape(4, 2, 2, g.shape[0] // 16, g.shape[1])
+        split_y = lambda g: g.reshape((4, 2) + g.shape[1:])
+        down_keep, down_send = halve(at.x, by_x(down_own), by_x(down_got), 1)
+        rest_keep, rest_send = halve(at.y, by_y(rest_own), by_y(rest_got), 1)
+        down_keep, down_send, rest_keep, rest_send, run.grad_mixed = tie(
+            down_keep, down_send, rest_keep, rest_send, run.grad_mixed
         )
-        down_got, up_got, out_got = at.swap_x(down_send), at.swap_y(up_send), at.swap_core(out_other)
+        down_got, rest_got = at.swap_x(down_send), at.swap_y(rest_send)
         far = run.far_tiles()
-        down_got, up_got, out_got, far = tie(down_got, up_got, out_got, far)
-        far_da, far_gain = run.far_fold(far)
-        down = plus(down_keep, down_got).astype(BF)
-        down = down.reshape((4, 2) + down.shape[1:])
-        down_keep, down_send = choose(at.y, down, 1)
-        up = plus(up_keep, up_got).astype(BF)
-        up_keep, up_send = z_parts(at, up)
-        out = plus(out_own, out_got).astype(BF)
-        out_keep, out_send = choose(at.x, out, 1)
+        down_got, rest_got, far = tie(down_got, rest_got, far)
+        down_keep, down_send = halve(at.y, split_y(down_keep), split_y(down_got), 1)
+        rest_keep, rest_send = z_parts(at, rest_keep, rest_got)
+        down_keep, down_send, rest_keep, rest_send, far = tie(down_keep, down_send, rest_keep, rest_send, far)
+        down_got = at.swap_y(down_send)
+        far_da, far_gain, far_part = run.far_fold(far)
         tiles = [far_da[n * rows : (n + 1) * rows] for n in range(4)]
-        (down_keep, down_send, up_keep, up_send, out_keep, out_send, tiles, far) = tie(
-            down_keep, down_send, up_keep, up_send, out_keep, out_send, tiles, far
-        )
-        down_got, up_got, out_got = at.swap_y(down_send), z_move(at, up_send), at.swap_x(out_send)
-        third = at.swap_y(tiles[3], [(i, i ^ 1) for i in range(6, 8)])
-        second = at.swap_y(tiles[1], [(i, i ^ 1) for i in range(4, 8)])
+        over = jnp.concatenate([tiles[1], tiles[3]], axis=0)
+        down_got, tiles, over, far = tie(down_got, tiles, over, far)
+        over = at.swap_y(over, lower_z(2))
+        rest_got = z_move(at, rest_send)
         near = run.near_tiles(far)
-        down_got, up_got, out_got, third, second, near, tiles = tie(
-            down_got, up_got, out_got, third, second, near, tiles
-        )
-        down = plus(down_keep, down_got).astype(BF)
-        down_keep, down_send = z_parts(at, down)
-        up = z_total(up_keep, up_got).astype(BF)
-        up_keep, up_send = choose(at.x, up, 0)
-        out = plus(out_keep, out_got).astype(BF)
-        out = out.reshape((4, 2) + out.shape[1:])
-        out_keep, out_send = choose(at.y, out, 1)
-        cur = plus(tiles[2], third).astype(BF)
-        (down_keep, down_send, up_keep, up_send, out_keep, out_send, cur, near) = tie(
-            down_keep, down_send, up_keep, up_send, out_keep, out_send, cur, near
+        rest_got, over, near, tiles, down_got = tie(rest_got, over, near, tiles, down_got)
+        down_keep, down_send = z_parts(at, down_keep, down_got)
+        rest = z_total(rest_keep, rest_got).astype(BF)
+        rest_keep, rest_send = choose(at.x, rest, 0)
+        cur = plus(tiles[2], over[rows:]).astype(BF)
+        down_keep, down_send, rest_keep, rest_send, cur, near = tie(
+            down_keep, down_send, rest_keep, rest_send, cur, near
         )
         cur = at.down(cur, 3, 3)
-        down_got, up_got, out_got = z_move(at, down_send), at.swap_x(up_send), at.swap_y(out_send)
-        near_da, clean, vec = run.near_fold(near, far_gain)
-        near_da, clean, vec, cur = tie(near_da, clean, vec, cur)
-        first = at.swap_y(near_da[3 * rows : 4 * rows], [(i, i ^ 1) for i in range(2, 8)])
-        beside = at.swap_y(near_da[4 * rows : 5 * rows], [(i, i - 1) for i in range(1, 8, 2)])
-        cur = (plus(tiles[0], second) + cur.astype(F32)).astype(BF)
-        other = run.qkv_other(vec, self)
-        other, cur = tie(other, cur)
+        down_got, rest_got = z_move(at, down_send), at.swap_x(rest_send)
+        near_da, clean, vec, pieces = run.near_fold(near, far_gain, far_part)
+        near_da, pieces, cur, down_got, rest_got = tie(near_da, pieces, cur, down_got, rest_got)
+        cur = (plus(tiles[0], over[:rows]) + cur.astype(F32)).astype(BF)
+        own, other = self.qkv_pieces(pieces, vec)
+        across = near_da[3 * rows :]
+        across, cur, own, other = tie(across, cur, own, other)
+        first = at.swap_y(across[:rows], lower_z(1))
+        beside = at.swap_y(across[rows:], [(i, i - 1) for i in range(1, 8, 2)])
         cur = at.down(cur, 2, 3)
-        other_got = [at.swap_core(v) for v in other]
-        own = run.qkv_own(vec, self)
-        other_got, own, first, cur, beside, down_got, up_got, out_got = tie(
-            other_got, own, first, cur, beside, down_got, up_got, out_got
-        )
-        a, b = (plus(v, got).astype(BF) for v, got in zip(own, other_got))
-        b = b.reshape((4, 2) + b.shape[1:])
-        a_keep, a_send = choose(at.x, a, 1)
-        b_keep, b_send = choose(at.y, b, 1)
+        a_got, b_got = (at.swap_core(v) for v in other)
+        sum_down = z_total(down_keep, down_got)
+        rest = plus(rest_keep, rest_got)
+        first, cur, beside, a_got, b_got = tie(first, cur, beside, a_got, b_got)
+        a_keep, a_send = halve(at.x, own[0], a_got, 1)
+        b_keep, b_send = halve(at.y, split_y(own[1]), split_y(b_got), 1)
         cur = (plus(near_da[2 * rows : 3 * rows], first) + cur.astype(F32)).astype(BF)
-        out = plus(out_keep, out_got).astype(BF)
-        out_keep, out_send = z_parts(at, out)
-        a_keep, a_send, b_keep, b_send, cur, out_send = tie(a_keep, a_send, b_keep, b_send, cur, out_send)
-        a_got, b_got, cur, out_got = at.swap_x(a_send), at.swap_y(b_send), at.down(cur, 1, 3), z_move(at, out_send)
-        sum_down = z_total(down_keep, down_got)
-        sum_up = self.join_units(plus(up_keep, up_got), run.chunk)
-        a_got, b_got, cur, out_got = tie(a_got, b_got, cur, out_got)
-        a = plus(a_keep, a_got).astype(BF)
-        a = a.reshape((4, 2) + a.shape[1:])
-        a_keep, a_send = choose(at.y, a, 1)
-        b_keep, b_send = z_parts(at, plus(b_keep, b_got).astype(BF))
+        a_keep, a_send, b_keep, b_send, cur, rest = tie(a_keep, a_send, b_keep, b_send, cur, rest)
+        a_got, b_got, cur = at.swap_x(a_send), at.swap_y(b_send), at.down(cur, 1, 3)
+        sum_out, sum_up = self.join_rest(rest, run.chunk, run.width)
+        a_got, b_got, cur, sum_out, sum_up, sum_down = tie(a_got, b_got, cur, sum_out, sum_up, sum_down)
+        a_keep, a_send = halve(at.y, split_y(a_keep), split_y(a_got), 1)
+        b_keep, b_send = z_parts(at, b_keep, b_got)
         a_keep, a_send, b_keep, b_send = tie(a_keep, a_send, b_keep, b_send)
         a_got, b_got = at.swap_y(a_send), z_move(at, b_send)
         grad_hidden = run.last(clean + cur.astype(F32) + beside.astype(F32))
-        sum_out = jnp.concatenate(from_column_half(at, z_total(out_keep, out_got)), axis=1)
-        a_got, b_got = tie(a_got, b_got)
-        a_keep, a_send = z_parts(at, plus(a_keep, a_got).astype(BF))
+        a_got, b_got, grad_hidden = tie(a_got, b_got, grad_hidden)
+        a_keep, a_send = z_parts(at, a_keep, a_got)
         b_keep, b_send = choose(at.x, z_total(b_keep, b_got).astype(BF), 0)
         a_keep, a_send, b_keep, b_send = tie(a_keep, a_send, b_keep, b_send)
         a_got, b_got = z_move(at, a_send), at.swap_x(b_send)
         a_got, b_got = tie(a_got, b_got)
         m = run.few * 2
         a, b = z_total(a_keep, a_got), plus(b_keep, b_got)
-        rest = jnp.concatenate([a[:m], b], axis=1)
-        sum_qkv = heads_of_halves(*from_column_half(at, rest))
+        sum_qkv = heads_of_halves(*from_column_half(at, jnp.concatenate([a[:m], b], axis=1)))
         return sum_down, sum_up, sum_out, sum_qkv, a[m, : run.vectors], grad_hidden
 
-    def join_units(self, g, chunk):
-        return units_of_halves(*from_column_half(self.at, g), chunk)
-
-    def out_pieces(self, g):
-        half = g.shape[0] // 2
-        g = jnp.where(self.core == 0, g, jnp.concatenate([g[half:], g[:half]], axis=0))
-        g = g.reshape(8, 2, g.shape[0] // 16, 2, g.shape[1] // 2)
-        return choose(self.core, g, 3)
-
-    def qkv_pieces(self, q, k, v, vec, other):
-        m = q.shape[0] // 16
-        a = jnp.concatenate([q, k[:, : k.shape[1] // 3]], axis=1).reshape(8, 2, m, -1)
-        b = jnp.concatenate([k[:, k.shape[1] // 3 :], v], axis=1).reshape(8, 2, m, -1)
+    def join_rest(self, g, chunk, width):
+        a, b = from_column_half(self.at, g)
+        cut = width // 2
+        out = jnp.concatenate([a[:, :cut], b[:, :cut]], axis=1)
+        return out, units_of_halves(a[:, cut:], b[:, cut:], chunk)
+
+    def rest_pieces(self, out, up, other):
+        half = out.shape[0] // 2
+        core = 1 - self.core if other else self.core
+        out = lax.dynamic_slice_in_dim(out, core * half, half, axis=1)
+        out = jnp.where(self.core == 0, out, jnp.concatenate([out[half:], out[:half]], axis=0))
+        return jnp.concatenate([out.astype(BF), up], axis=1)
+
+    def qkv_pieces(self, pieces, vec):
+        cut = [v.reshape(8, 2, v.shape[0] // 16, v.shape[1]) for v in pieces]
         n = vec.shape[1]
-        rows = pick(vec.astype(BF).reshape(8, 2, 2, n), 1 - self.core if other else self.core, 2)[:, :, None]
-        rows = jnp.pad(rows, ((0, 0), (0, 0), (0, 7), (0, a.shape[3] - n)))
-        return [jnp.concatenate([a, rows], axis=2), b]
+        vec = vec.astype(BF).reshape(8, 2, 2, n)
+        found = []
+        for h, core in enumerate((self.core, 1 - self.core)):
+            rows = pick(vec, core, 2)[:, :, None]
+            rows = jnp.pad(rows, ((0, 0), (0, 0), (0, 7), (0, cut[0].shape[3] - n)))
+            found.append((jnp.concatenate([cut[2 * h], rows], axis=2), cut[2 * h + 1]))
+        return found
 
 
 AXES = ("leaf", "fsdp")
@@ -988,12 +1044,12 @@
     def places(self):
         return jnp.array([[0, 0], [0, 0], [0, 0], [0, 1]], jnp.int32)
 
-    def first_gather(self, hid, w_qkv, w_out, w_up, w_down, vectors):
+    def first_gather(self, hid, w_qkv, w_out, w_up, w_down, vectors, early):
         tree = lax.all_gather(hid, "leaf", axis=0, tiled=False)
         lower = [pick(tree, jnp.maximum(leaf, 0), 0) for leaf, _ in self.lower(self.leaf)]
         every = lambda w: lax.all_gather(w, AXES, axis=0, tiled=True)
-        qkv = tuple(v[None] for v in halves_of_heads(every(w_qkv)))
-        return lower, qkv, every(vectors[None]), (every(w_out), every(w_up), every(w_down))
+        qkv = tuple((v[None],) for v in halves_of_heads(every(w_qkv)))
+        return lower, qkv, every(vectors[None]), (every(w_out), every(w_up), every(w_down)), early
 
     def second_start(self, state):
         return state
@@ -1005,10 +1061,10 @@
         out_w, up_w, down_w = state
         half, cut = down_w.shape[0] // 2, out_w.shape[1] // 2
         one = tuple(
-            jnp.concatenate([out_w[:, n * cut : (n + 1) * cut], up_w[:, n * half : (n + 1) * half]], axis=1)[None]
+            (jnp.concatenate([out_w[:, n * cut : (n + 1) * cut], up_w[:, n * half : (n + 1) * half]], axis=1)[None],)
             for n in range(2)
         )
-        return one, tuple(down_w[None, n * half : (n + 1) * half] for n in range(2))
+        return one, tuple((down_w[None, n * half : (n + 1) * half],) for n in range(2))
 
     def unit_bias(self, bias, chunk):
         half = bias.shape[0] // 2
@@ -1020,31 +1076,28 @@
     def scatter(self, g):
         return lax.psum_scatter(g.astype(F32), AXES, scatter_dimension=0, tiled=True)
 
-    def out_pieces(self, g):
-        return g, g
-
-    def qkv_pieces(self, q, k, v, vec, other):
-        return [jnp.concatenate([q, k, v], axis=1), vec]
+    def rest_pieces(self, out, up, other):
+        cut = out.shape[1] // 2
+        return jnp.concatenate([out[:, cut:] if other else out[:, :cut], up.astype(F32)], axis=1)
 
     def backward(self, run):
         rows = self.rows
-        down_other, up_other = run.feed_other()
-        down_own, up_own, out, _ = run.feed_own(self)
+        down_other, rest_other = run.feed_other(self)
+        down_own, rest_own = run.feed_own(self)
         far = run.far_tiles()
-        far_da, far_gain = run.far_fold(far)
+        far_da, far_gain, far_part = run.far_fold(far)
         near = run.near_tiles(far)
-        near_da, clean, vec = run.near_fold(near, far_gain)
-        own, vec = run.qkv_own(vec, self)
-        other, _ = run.qkv_other(vec, self)
+        near_da, clean, vec, pieces = run.near_fold(near, far_gain, far_part)
         tiles = jnp.concatenate([near_da[:rows], near_da[2 * rows :], far_da], axis=0)
         tiles = tiles.reshape((self.leaves, rows) + tiles.shape[1:])
         order = [pick(tiles, (self.leaf - n) % self.leaves, 0) for n in range(self.leaves)]
         total = lax.psum_scatter(jnp.concatenate(order, axis=0), "leaf", scatter_dimension=0, tiled=True)
+        cut = run.width // 2
         return (
             self.scatter(jnp.concatenate([down_own, down_other], axis=0)),
-            self.scatter(jnp.concatenate([up_own, up_other], axis=1)),
-            self.scatter(out),
-            self.scatter(heads_of_halves(own, other)),
+            self.scatter(jnp.concatenate([rest_own[:, cut:], rest_other[:, cut:]], axis=1)),
+            self.scatter(jnp.concatenate([rest_own[:, :cut], rest_other[:, :cut]], axis=1)),
+            self.scatter(heads_of_halves(*(jnp.concatenate(pieces[n : n + 2], axis=1) for n in (0, 2)))),
             self.scatter(vec)[0],
             run.last(total.astype(F32)),
         )
@@ -1090,21 +1143,20 @@
     cosine = jnp.cos(angles)
     sine = jnp.sin(angles) * jnp.where((lanes % HEAD_DIM) < HEAD_DIM // 2, -1.0, 1.0)
     places = net.places()
-    mask = jnp.pad(noise_mask[0].astype(F32)[:, None], ((rows, (tiles - 2) * rows), (0, 0)))
 
     vectors = jnp.concatenate([ln1_gain, ln2_gain, down_bias, mask_embed, up_bias])
-    lower, qkv_w, vec, coming = net.first_gather(hid, w_qkv, w_out, w_up, w_down, vectors)
+    lower, qkv_w, vec, coming, (cosine, sine) = net.first_gather(
+        hid, w_qkv, w_out, w_up, w_down, vectors, (cosine, sine)
+    )
     gain_one, gain_two, down_b, embed = (
         vec[:, n * few : (n + 1) * few].reshape(1, width).astype(F32) for n in range(4)
     )
     up_b = jnp.concatenate(net.unit_bias(vec[:, 4 * few :].reshape(-1).astype(F32), chunk), axis=0)
-    x_all = jnp.concatenate([hid, hid] + lower, axis=0)
-    x_all, coming, cosine, sine = tie(x_all, coming, cosine, sine)
     coming = net.second_start(coming)
-    a_all, query, key, value = project(
-        places, x_all, mask, embed, gain_one, qkv_w[0], qkv_w[1], cosine, sine, rows
+    query, key, value = project(
+        places, [hid] + lower, noise_mask, embed, gain_one, qkv_w[0], qkv_w[1], cosine, sine
     )
-    coming, query, a_all = tie(coming, query, a_all)
+    coming, query = tie(coming, query)
     coming = net.second_go_on(coming)
     mixed, log_norm = attend(flags, query_cols, key_rows, query, key, value, rows)
     coming, mixed = tie(coming, mixed)
@@ -1113,20 +1165,18 @@
     grad_two = cotangent[0].reshape(2 * rows, width)
     (
         output, normed_two, act, grad_pre, grad_one, grad_mixed, grad_after, grad_gain_two, grad_up_b, grad_down_b,
-    ) = middle(places, mixed, x_all, mask, embed, grad_two, gain_two, up_b, down_b, one_w, down_w)
+    ) = middle(places, mixed, hid, noise_mask, embed, grad_two, gain_two, up_b, down_b, one_w, down_w)
     output = output.reshape(1, 2, rows, width)
     units = act.shape[1] // 2
 
     run = Backward()
-    run.chunk, run.few, run.vectors, run.grad_mixed = chunk, few, vectors.shape[0], grad_mixed
+    run.chunk, run.few, run.vectors, run.grad_mixed, run.width = chunk, few, vectors.shape[0], grad_mixed, width
     cut = net.near
 
-    def feed_other():
-        return t_mm(act[:, units:], grad_two).astype(BF), t_mm(normed_two, grad_pre[:, units:]).astype(BF)
-
-    def feed_own(net):
-        down, up = t_mm(act[:, :units], grad_two).astype(BF), t_mm(normed_two, grad_pre[:, :units]).astype(BF)
-        return (down, up) + tuple(net.out_pieces(t_mm(mixed, grad_one).astype(BF)))
+    def feed(n, net):
+        at = slice(n * units, (n + 1) * units)
+        down, up = t_mm(act[:, at], grad_two).astype(BF), t_mm(normed_two, grad_pre[:, at]).astype(BF)
+        return down, net.rest_pieces(t_mm(mixed, grad_one), up, n == 1)
 
     def far_tiles():
         return attend_back(
@@ -1134,30 +1184,21 @@
         )
 
     def far_fold(far):
-        run.far = far
-        return fold(places, cut, tiles, far[1], far[2], x_all, mask, embed, gain_one, qkv_w[0], qkv_w[1], rows)
+        return fold(places, lower[cut - 2 :], far[1], far[2], noise_mask, embed, gain_one, qkv_w[0], qkv_w[1])
 
     def near_tiles(far):
-        run.far = far
         return attend_back(
             0, cut, flags, query_rows, key_cols, query, key, value, mixed, run.grad_mixed, norm_rows, cosine, sine, rows, far[0]
         )
 
-    def near_fold(near, far_gain):
-        run.near = near
-        da, gain, clean, run.noisy, grad_embed = fold(
-            places, 0, cut, near[1], near[2], x_all, mask, embed, gain_one, qkv_w[0], qkv_w[1], rows, near[0], grad_after
+    def near_fold(near, far_gain, far_part):
+        da, gain, clean, run.noisy, grad_embed, *pieces = fold(
+            places, [hid] + lower[: cut - 2], near[1], near[2], noise_mask, embed, gain_one, qkv_w[0], qkv_w[1],
+            (near[0], grad_after, far_part),
         )
         parts = (gain + far_gain, grad_gain_two, grad_down_b, grad_embed, net.unit_bias_back(grad_up_b[:1], grad_up_b[1:], chunk))
         vec = jnp.concatenate([v.reshape(devices, -1) for v in parts], axis=1)
-        run.keys, run.values = (jnp.concatenate([run.near[n], run.far[n]], axis=0) for n in (1, 2))
-        return da, clean, vec
-
-    def qkv_half(n, vec, net):
-        at = slice(n * half, (n + 1) * half)
-        q = t_mm(a_all[: 2 * rows], run.near[0][:, at]).astype(BF)
-        k, v = (t_mm(a_all, g[:, at]).astype(BF) for g in (run.keys, run.values))
-        return net.qkv_pieces(q, k, v, vec, n == 1)
+        return da, clean, vec, pieces
 
     def last(total):
         hat, scale = normalise(hid.astype(F32))
@@ -1165,10 +1206,9 @@
         clean = grad_after[:rows] + norm_back(hat, scale, gain_one, total)
         return (clean + jnp.where(masked, 0.0, run.noisy)).astype(BF)[None]
 
-    run.feed_other, run.feed_own, run.far_tiles, run.far_fold = feed_other, feed_own, far_tiles, far_fold
-    run.near_tiles, run.near_fold, run.last = near_tiles, near_fold, last
-    run.qkv_own = lambda vec, net: qkv_half(0, vec, net)
-    run.qkv_other = lambda vec, net: qkv_half(1, vec, net)
+    run.feed_own = lambda net: feed(0, net)
+    run.feed_other = lambda net: feed(1, net)
+    run.far_tiles, run.far_fold, run.near_tiles, run.near_fold, run.last = far_tiles, far_fold, near_tiles, near_fold, last
     sum_down, sum_up, sum_out, sum_qkv, sum_vec, grad_hidden = net.backward(run)
     piece = lambda n: sum_vec[n * few : (n + 1) * few]
     return (

time: 511 us -> 454 us (0.89)
  local copies, waits for them, and re-layouts: 59.8 us -> 29.8 us
  waiting for transfers between devices: 131 us -> 111 us
  matrix products: 30.8 us -> 12.2 us
  Pallas kernels: 115 us -> 125 us
    ppermute x24 -> x21, waiting for transfers between devices: 64.7 us -> 31.5 us  [swap_z(): return lax.ppermute(v, 'leaf', [(i, i ^ 2 * n) for i in range(8)])]
    dot_general x11 -> x5, matrix products: 30.6 us -> 12 us  [t_mm(): lax.dot_general(a, b, (((0,), (0,)), ((), ())), preferred_element_type=F32)]
    ppermute x3, waiting for transfers between devices: 0.14 us -> 17 us  [down(): lax.ppermute(v, 'leaf', [(i, i - 2) for i in range(2 * first, 2 * last +...]
    ppermute x16 -> x14, waiting for transfers between devices: 22.8 us -> 37.2 us  [swap_y(): return lax.ppermute(v, 'leaf', pairs or [(i, i ^ 1) for i in range(8)])]
    ppermute x8 -> x7, waiting for transfers between devices: 35.7 us -> 22 us  [swap_x(): return lax.ppermute(v, 'fsdp', [(i, i ^ 2) for i in range(4)])]
    pallas_call x4, Pallas kernels: 66.4 us -> 76.2 us  [the longest x2 36.6 us: fold(): pl.pallas_call(functools.partial(fold_kernel, near is not None, len(own),...]
    squeeze x18 -> x4, local copies, waits for them, and re-layouts: 9.31 us -> 0.1 us  [pick(): return lax.dynamic_index_in_dim(v, index, axis, keepdims=False)]
    unnamed x167 -> x106, local copies, waits for them, and re-layouts: 16.8 us -> 8.37 us
  transfers between devices with their start and end apart: 67 -> 62, of which waited for: 24 -> 19; matrix products, arithmetic and copies ran while one was open for 16% -> 9% of each run, Pallas kernels for 13% -> 23%
where the time goes in v4:
time: 454 us; the launch traced here: 448 us
  Pallas kernels  125 us (28%)
  starting transfers between devices  124 us (27%)
  waiting for transfers between devices  111 us (24%)
  other arithmetic  44 us (10%)
  local copies, waits for them, and re-layouts  29.8 us (7%)
  matrix products  12.2 us (3%)
    ppermute x21, starting transfers between devices, swap_z(): return lax.ppermute(v, 'leaf', [(i, i ^ 2 * n) for i in range(8)])  84.3 us
    ppermute x14, waiting for transfers between devices, swap_y(): return lax.ppermute(v, 'leaf', pairs or [(i, i ^ 1) for i in range(8)])  37.2 us
    pallas_call x2, Pallas kernels, fold(): pl.pallas_call(functools.partial(fold_kernel, near is not None, len(own),...  36.6 us
    ppermute x21, waiting for transfers between devices, swap_z(): return lax.ppermute(v, 'leaf', [(i, i ^ 2 * n) for i in range(8)])  31.5 us
    pallas_call x2, Pallas kernels, attend_back(): pl.pallas_call(functools.partial(attend_back_kernel, rows, first, last),...  30.1 us
    pallas_call x1, Pallas kernels, middle(): pl.pallas_call(functools.partial(middle_kernel, len(one[0]), len(two[0]),...  22.2 us
    ppermute x7, waiting for transfers between devices, swap_x(): return lax.ppermute(v, 'fsdp', [(i, i ^ 2) for i in range(4)])  22 us
    convert_element_type x14, other arithmetic, joined(): return plus(pick(mine, index, axis), pick(got, index, axis)).astype(BF)  20.2 us
  transfers between devices with their start and end apart: 62, of which 19 were waited for; matrix products, arithmetic and copies ran while one was open for 9% of the time, Pallas kernels for 23%

profile of v4, /device:TPU:0, one launch (start us, length us, event | category | flops | bytes accessed | tf_op | source)
XLA Modules:
  0.0 447.5 jit_solution(1949406941436307460)
XLA Ops:
  0.7 3.5 concatenate.114
  6.0 2.6 collective-permute-start.6
  8.6 3.4 collective-permute-start.5
  13.8 2.7 tables.1
  16.5 2.0 slice_reduce_fusion
  18.7 5.9 %fusion.8 = (f32[2304,128]{1,0:T(8,128)}, f32[2304,128]{1,0:T(8,128)}) fusion(f32[128]{0:T(128)S(1)} %get-tuple-element.456, f32[128]{0:T(128)S(1)} %get-tuple-element.457, f32[2304]{0:T(1024)S(1)} %slice_reduce_fusion), kind=kLoop, calls=%fused_computation.21 | loop fusion | flops 589824 | bytes 2369536 | tf_op jit(solution)/shard_map/mul | solution.py:1144
  24.6 3.6 collective-permute-start.3
  29.1 4.1 collective-permute-done.3
  33.2 8.2 %collective-permute-done.2 = bf16[1,64,1152]{2,1,0:T(8,128)(2,1)S(1)} collective-permute-done((bf16[1,64,1152]{2,1,0:T(8,128)(2,1)S(1)}, bf16[1,64,1152]{2,1,0:T(8,128)(2,1)S(1)}, u32[]{:S(2)}, u32[]{:S(2)}) %collective-permute-start.2) | collective-permute-done | bytes 147488 | tf_op jit(solution)/shard_map/ppermute | solution.py:37
  41.6 4.7 %collective-permute-start.7 = (bf16[256,768]{1,0:T(8,128)(2,1)S(1)}, bf16[256,768]{1,0:T(8,128)(2,1)}, u32[]{:S(2)}, u32[]{:S(2)}) collective-permute-start(bf16[256,768]{1,0:T(8,128)(2,1)S(1)} %bitcast.199), channel_id=1, source_target_pairs={{0,8},{4,12},{8,16},{12,20},{16,24},{20,28},{1,9},{5,13},{9,17},{1... | collective-permute-start | bytes 1179656 | tf_op jit(solution)/shard_map/ppermute | solution.py:40
  46.3 10.1 %collective-permute-done.8 = bf16[4,64,1152]{2,1,0:T(8,128)(2,1)S(1)} collective-permute-done((bf16[4,64,1152]{2,1,0:T(8,128)(2,1)S(1)}, bf16[4,64,1152]{2,1,0:T(8,128)(2,1)S(1)}, u32[]{:S(2)}, u32[]{:S(2)}) %collective-permute-start.8) | collective-permute-done | bytes 589856 | tf_op jit(solution)/shard_map/ppermute | solution.py:34
  57.3 1.4 collective-permute-start.11
  61.6 19.7 %collective-permute-start.16 = (bf16[1,48,1920]{2,1,0:T(8,128)(2,1)S(1)}, bf16[1,48,1920]{2,1,0:T(8,128)(2,1)S(1)}, u32[]{:S(2)}, u32[]{:S(2)}) collective-permute-start(bf16[1,48,1920]{2,1,0:T(8,128)(2,1)S(1)} %bitcast.207), channel_id=1, source_target_pairs={{0,16},{4,20},{8,24},{12,28},{16,0},{20,4},{24,8},{28,12},{1,17},{... | collective-permute-start | bytes 552968 | tf_op jit(solution)/shard_map/ppermute | solution.py:37
  81.4 3.7 collective-permute-done.15.refs_1_.refs_4_
  85.1 2.5 collective-permute-done.16
  90.1 1.7 collective-permute-start.17
  91.9 8.1 %collective-permute-start.19 = (bf16[1,48,1920]{2,1,0:T(8,128)(2,1)S(1)}, bf16[1,48,1920]{2,1,0:T(8,128)(2,1)S(1)}, u32[]{:S(2)}, u32[]{:S(2)}) collective-permute-start(bf16[1,48,1920]{2,1,0:T(8,128)(2,1)S(1)} %bitcast.208), channel_id=1, source_target_pairs={{0,24},{4,28},{8,16},{12,20},{16,8},{20,12},{24,0},{28,4},{1,25},{... | collective-permute-start | bytes 552968 | tf_op jit(solution)/shard_map/ppermute | solution.py:37
  100.3 4.2 collective-permute-done.19
  104.5 4.8 %collective-permute-start.23 = (bf16[1,2,96,768]{3,2,1,0:T(8,128)(2,1)S(1)}, bf16[1,2,96,768]{3,2,1,0:T(8,128)(2,1)S(1)}, u32[]{:S(2)}, u32[]{:S(2)}) collective-permute-start(bf16[1,2,96,768]{3,2,1,0:T(8,128)(2,1)S(1)} %maximum_bitcast_fusion), channel_id=1, source_target_pairs={{0,24},{4,28},{8,16},{12,20},{16,8},{20,12},{24,0},{28,4},{1,25},{... | collective-permute-start | bytes 884744 | tf_op jit(solution)/shard_map/ppermute | solution.py:37
  111.5 1.6 collective-permute-start.20
  113.1 17.4 %project.1 = (bf16[512,768]{1,0:T(8,128)(2,1)}, bf16[2304,768]{1,0:T(8,128)(2,1)}, bf16[2304,768]{1,0:T(8,128)(2,1)}) custom-call(s32[4,16]{1,0:T(4,128)} %pad_add_fusion.table_ref, s32[1,256]{1,0:T(1,128)} %mask_ref.7, f32[1,768]{1,0:T(1,128)} %reshape.599.embed_ref, f32[1,768]{1,0:T(1,128)} %reshape.600.gain_ref, ...), custom_call_target="tpu_custom_call" | custom-call | flops 6039797760 | bytes 14155776 | tf_op jit(solution)/shard_map/project/pallas_call | solution.py:280
  131.2 1.6 collective-permute-start.24
  132.9 2.7 collective-permute-start.26
  135.6 15.7 %attend.1 = (bf16[512,768]{1,0:T(8,128)(2,1)}, f32[512,128]{1,0:T(8,128)}) custom-call(s32[9]{0:T(128)} %get-tuple-element.233.flag_ref, f32[512,8]{1,0:T(8,128)} %get-tuple-element.234.qcol_ref, f32[8,2304]{1,0:T(8,128)} %get-tuple-element.235.krow_ref, bf16[512,768]{1,0:T(8,128)(2,1)} %get-tuple-element.236.q_ref, ...), custom_call_target="tpu_custom_call" | custom-call | flops 7247757312 | bytes 7864320 | tf_op jit(solution)/shard_map/attend/pallas_call | solution.py:495
  151.3 10.9 %collective-permute-done.26.refs_5_ = bf16[8,96,768]{2,1,0:T(8,128)(2,1)} collective-permute-done((bf16[8,96,768]{2,1,0:T(8,128)(2,1)S(1)}, bf16[8,96,768]{2,1,0:T(8,128)(2,1)}, u32[]{:S(2)}, u32[]{:S(2)}) %collective-permute-start.26) | collective-permute-done | bytes 1179680 | tf_op jit(solution)/shard_map/ppermute | solution.py:34
  162.2 3.8 collective-permute-done.24.refs_1_
  168.7 2.6 collective-permute-done.29.refs_7_
  171.3 22.2 %middle.1 = (bf16[512,768]{1,0:T(8,128)(2,1)}, bf16[512,768]{1,0:T(8,128)(2,1)}, bf16[512,3072]{1,0:T(8,128)(2,1)}, bf16[512,3072]{1,0:T(8,128)(2,1)}, bf16[512,...) custom-call(s32[4,16]{1,0:T(4,128)} %pad_add_fusion.table_ref, ...), custom_call_target="tpu_custom_call" | custom-call | flops 10871635968 | bytes 21233664 | tf_op jit(solution)/shard_map/middle/pallas_call | solution.py:386
  193.6 2.1 fusion.82
  195.7 2.6 convolution_convert_fusion
  198.8 1.8 pad_maximum_fusion.1
  202.0 2.9 convolution_convert_fusion.2
  205.1 3.1 convolution_convert_fusion.1
  210.3 1.4 convolution_convert_fusion.3
  211.8 1.5 copy-done.3
  213.2 3.3 fusion.10
  216.5 2.9 fusion.7
  219.4 1.8 fusion.6
  221.2 2.8 collective-permute-start.33
  225.6 1.5 collective-permute-start.32
  228.9 10.6 %attend_back_far.1 = (f32[768,512]{1,0:T(8,128)}, bf16[1024,768]{1,0:T(8,128)(2,1)}, bf16[1024,768]{1,0:T(8,128)(2,1)}) custom-call(s32[9]{0:T(128)} %get-tuple-element.233.flag_ref, f32[8,512]{1,0:T(8,128)} %get-tuple-element.256.qrow_ref, f32[2304,8]{1,0:T(8,128)} %get-tuple-element.197.kcol_ref, bf16[512,768]{1,0:T(8,128)(2,1)} %get-tuple-element.236.q_ref, ...), custom_call_target="tpu_custom_call" | custom-call | flops 8053063680 | bytes 7864320 | tf_op jit(solution)/shard_map/attend_back_far/pallas_call | solution.py:615
  239.5 14.5 %collective-permute-done.32 = bf16[8,96,768]{2,1,0:T(8,128)(2,1)} collective-permute-done((bf16[8,96,768]{2,1,0:T(8,128)(2,1)}, bf16[8,96,768]{2,1,0:T(8,128)(2,1)}, u32[]{:S(2)}, u32[]{:S(2)}) %collective-permute-start.32) | collective-permute-done | bytes 1179680 | tf_op jit(solution)/shard_map/ppermute | solution.py:31
  254.0 3.1 collective-permute-done.33
  259.5 2.5 fusion.36
  262.2 13.7 %collective-permute-start.35 = (bf16[2,48,1920]{2,1,0:T(8,128)(2,1)S(1)}, bf16[2,48,1920]{2,1,0:T(8,128)(2,1)S(1)}, u32[]{:S(2)}, u32[]{:S(2)}) collective-permute-start(bf16[2,48,1920]{2,1,0:T(8,128)(2,1)S(1)} %get-tuple-element.270), channel_id=1, source_target_pairs={{0,16},{4,20},{8,24},{12,28},{16,0},{20,4},{24,8},{28,12},{1,17},{... | collective-permute-start | bytes 1105928 | tf_op jit(solution)/shard_map/ppermute | solution.py:37
  276.0 14.4 %fold_far.1 = (bf16[1024,768]{1,0:T(8,128)(2,1)}, f32[1,768]{1,0:T(1,128)}, f32[768,1536]{1,0:T(8,128)}) custom-call(s32[4,16]{1,0:T(4,128)} %pad_add_fusion.table_ref, s32[1,256]{1,0:T(1,128)} %mask_ref.7, f32[1,768]{1,0:T(1,128)} %reshape.599.embed_ref, f32[1,768]{1,0:T(1,128)} %reshape.600.gain_ref, bf16[1024,768]{1,0:T(8,128)(2,1)} %get-tuple-element.273.dk_ref, ...), custom_call_target="tpu_custom_call" | custom-call | flops 4831838208 | bytes 16908288 | tf_op jit(solution)/shard_map/fold_far/pallas_call | solution.py:748
  290.4 1.5 fusion.71
  292.6 19.5 %attend_back_near.1 = (bf16[512,768]{1,0:T(8,128)(2,1)}, bf16[1280,768]{1,0:T(8,128)(2,1)}, bf16[1280,768]{1,0:T(8,128)(2,1)}) custom-call(s32[9]{0:T(128)} %get-tuple-element.233.flag_ref, f32[8,512]{1,0:T(8,128)} %get-tuple-element.256.qrow_ref, f32[2304,8]{1,0:T(8,128)} %get-tuple-element.197.kcol_ref, bf16[512,768]{1,0:T(8,128)(2,1)} %get-tuple-element.236.q_ref, ...), custom_call_target="tpu_custom_call" | custom-call | flops 10066329600 | bytes 9437184 | tf_op jit(solution)/shard_map/attend_back_near/pallas_call | solution.py:615
  313.3 12.4 %collective-permute-start.40 = (bf16[96,768]{1,0:T(8,128)(2,1)}, bf16[96,768]{1,0:T(8,128)(2,1)S(1)}, u32[]{:S(2)}, u32[]{:S(2)}) collective-permute-start(bf16[96,768]{1,0:T(8,128)(2,1)} %get-tuple-element.306), channel_id=1, source_target_pairs={{0,8},{4,12},{8,0},{12,4},{16,24},{20,28},{24,16},{28,20},{1,9},{5... | collective-permute-start | bytes 442376 | tf_op jit(solution)/shard_map/ppermute | solution.py:37
  325.7 7.0 %collective-permute-start.41 = (bf16[96,768]{1,0:T(8,128)(2,1)S(1)}, bf16[96,768]{1,0:T(8,128)(2,1)S(1)}, u32[]{:S(2)}, u32[]{:S(2)}) collective-permute-start(bf16[96,768]{1,0:T(8,128)(2,1)S(1)} %get-tuple-element.307), channel_id=1, source_target_pairs={{0,16},{4,20},{8,24},{12,28},{16,0},{20,4},{24,8},{28,12},{1,17},{... | collective-permute-start | bytes 442376 | tf_op jit(solution)/shard_map/ppermute | solution.py:37
  332.8 1.5 collective-permute-start.43
  335.0 22.2 %fold_near.1 = (bf16[1280,768]{1,0:T(8,128)(2,1)}, f32[1,768]{1,0:T(1,128)}, f32[256,768]{1,0:T(8,128)}, f32[256,768]{1,0:T(8,128)}, f32[1,768]{1,0:T(1,128)}, /...) custom-call(s32[4,16]{1,0:T(4,128)} %pad_add_fusion.table_ref, ...), custom_call_target="tpu_custom_call" | custom-call | flops 6039797760 | bytes 18481152 | tf_op jit(solution)/shard_map/fold_near/pallas_call | solution.py:748
  368.8 13.1 %collective-permute-done.46 = bf16[256,768]{1,0:T(8,128)(2,1)S(1)} collective-permute-done((bf16[256,768]{1,0:T(8,128)(2,1)S(1)}, bf16[256,768]{1,0:T(8,128)(2,1)S(1)}, u32[]{:S(2)}, u32[]{:S(2)}) %collective-permute-start.46) | collective-permute-done | bytes 393248 | tf_op jit(solution)/shard_map/ppermute | solution.py:34
  382.9 2.1 fusion.29
  386.3 1.9 add_convert_fusion.10
  394.7 17.0 %collective-permute-done.51 = bf16[256,768]{1,0:T(8,128)(2,1)} collective-permute-done((bf16[256,768]{1,0:T(8,128)(2,1)}, bf16[256,768]{1,0:T(8,128)(2,1)}, u32[]{:S(2)}, u32[]{:S(2)}) %collective-permute-start.51) | collective-permute-done | bytes 393248 | tf_op jit(solution)/shard_map/ppermute | solution.py:43
  413.7 1.7 fusion.70
  415.6 4.1 collective-permute-start.54
  419.7 4.6 %collective-permute-start.55 = (bf16[2,48,640]{2,1,0:T(8,128)(2,1)S(1)}, bf16[2,48,640]{2,1,0:T(8,128)(2,1)S(1)}, u32[]{:S(2)}, u32[]{:S(2)}) collective-permute-start(bf16[2,48,640]{2,1,0:T(8,128)(2,1)S(1)} %get-tuple-element.349), channel_id=1, source_target_pairs={{0,16},{4,20},{8,24},{12,28},{16,0},{20,4},{24,8},{28,12},{1,17},{... | collective-permute-start | bytes 368648 | tf_op jit(solution)/shard_map/ppermute | solution.py:37
  425.7 7.6 %collective-permute-done.55 = bf16[2,48,640]{2,1,0:T(8,128)(2,1)S(1)} collective-permute-done((bf16[2,48,640]{2,1,0:T(8,128)(2,1)S(1)}, bf16[2,48,640]{2,1,0:T(8,128)(2,1)S(1)}, u32[]{:S(2)}, u32[]{:S(2)}) %collective-permute-start.55) | collective-permute-done | bytes 122912 | tf_op jit(solution)/shard_map/ppermute | solution.py:37
  433.5 1.5 collective-permute-start.60
  434.9 1.9 collective-permute-start.57
  437.9 1.4 collective-permute-start.59
  439.4 3.2 collective-permute-done.58
  (323 shorter events, 59.7 us)
Async XLA Ops:
  5.5 13.0 %collective-permute-start = (bf16[32,1152]{1,0:T(8,128)(2,1)S(1)}, bf16[32,1152]{1,0:T(8,128)(2,1)S(1)}, u32[]{:S(2)}, u32[]{:S(2)}) collective-permute-start(bf16[32,1152]{1,0:T(8,128)(2,1)S(1)} %fusion.47), channel_id=1, source_target_pairs={{0,1},{1,0},{2,3},{3,2},{4,5},{5,4},{6,7},{7,6},{8,9},{9,8},{10,11... | collective-permute-start | bytes 221192 | tf_op jit(solution)/shard_map/ppermute | solution.py:28
  6.0 35.5 %collective-permute-start.6 = (bf16[96,768]{1,0:T(8,128)(2,1)S(1)}, bf16[96,768]{1,0:T(8,128)(2,1)S(1)}, u32[]{:S(2)}, u32[]{:S(2)}) collective-permute-start(bf16[96,768]{1,0:T(8,128)(2,1)S(1)} %copy-done.23), channel_id=1, source_target_pairs={{0,2},{1,3},{2,0},{3,1},{4,6},{5,7},{6,4},{7,5},{8,10},{9,11},{10,... | collective-permute-start | bytes 442376 | tf_op jit(solution)/shard_map/ppermute | solution.py:31
  8.6 32.9 %collective-permute-start.5 = (bf16[256,768]{1,0:T(8,128)(2,1)S(1)}, bf16[256,768]{1,0:T(8,128)(2,1)S(1)}, u32[]{:S(2)}, u32[]{:S(2)}) collective-permute-start(bf16[256,768]{1,0:T(8,128)(2,1)S(1)} %bitcast.198), channel_id=1, source_target_pairs={{0,4},{8,12},{16,20},{24,28},{1,5},{9,13},{17,21},{25,29},{2,6},{1... | collective-permute-start | bytes 1179656 | tf_op jit(solution)/shard_map/ppermute | solution.py:34
  18.6 9.6 %collective-permute-start.4 = (bf16[24,1920]{1,0:T(8,128)(2,1)S(1)}, bf16[24,1920]{1,0:T(8,128)(2,1)S(1)}, u32[]{:S(2)}, u32[]{:S(2)}) collective-permute-start(bf16[24,1920]{1,0:T(8,128)(2,1)S(1)} %get-tuple-element.425), channel_id=1, source_target_pairs={{0,1},{1,0},{2,3},{3,2},{4,5},{5,4},{6,7},{7,6},{8,9},{9,8},{10,11... | collective-permute-start | bytes 276488 | tf_op jit(solution)/shard_map/ppermute | solution.py:28
  24.6 8.5 %collective-permute-start.3 = (bf16[1,64,1152]{2,1,0:T(8,128)(2,1)S(1)}, bf16[1,64,1152]{2,1,0:T(8,128)(2,1)S(1)}, u32[]{:S(2)}, u32[]{:S(2)}) collective-permute-start(bf16[1,64,1152]{2,1,0:T(8,128)(2,1)S(1)} %maximum_bitcast_fusion.1), channel_id=1, source_target_pairs={{0,24},{4,28},{8,16},{12,20},{16,8},{20,12},{24,0},{28,4},{1,25},{... | collective-permute-start | bytes 442376 | tf_op jit(solution)/shard_map/ppermute | solution.py:37
  28.2 13.1 %collective-permute-start.2 = (bf16[1,64,1152]{2,1,0:T(8,128)(2,1)S(1)}, bf16[1,64,1152]{2,1,0:T(8,128)(2,1)S(1)}, u32[]{:S(2)}, u32[]{:S(2)}) collective-permute-start(bf16[1,64,1152]{2,1,0:T(8,128)(2,1)S(1)} %maximum_bitcast_fusion.1), channel_id=1, source_target_pairs={{0,16},{4,20},{8,24},{12,28},{16,0},{20,4},{24,8},{28,12},{1,17},{... | collective-permute-start | bytes 442376 | tf_op jit(solution)/shard_map/ppermute | solution.py:37
  28.2 13.1 %collective-permute-start.1 = (bf16[1,64,1152]{2,1,0:T(8,128)(2,1)S(1)}, bf16[1,64,1152]{2,1,0:T(8,128)(2,1)S(1)}, u32[]{:S(2)}, u32[]{:S(2)}) collective-permute-start(bf16[1,64,1152]{2,1,0:T(8,128)(2,1)S(1)} %maximum_bitcast_fusion.1), channel_id=1, source_target_pairs={{0,8},{4,12},{8,0},{12,4},{16,24},{20,28},{24,16},{28,20},{1,9},{5... | collective-permute-start | bytes 442376 | tf_op jit(solution)/shard_map/ppermute | solution.py:37
  41.5 15.0 %collective-permute-start.8 = (bf16[4,64,1152]{2,1,0:T(8,128)(2,1)S(1)}, bf16[4,64,1152]{2,1,0:T(8,128)(2,1)S(1)}, u32[]{:S(2)}, u32[]{:S(2)}) collective-permute-start(bf16[4,64,1152]{2,1,0:T(8,128)(2,1)S(1)} %pad_maximum_fusion.6), channel_id=1, source_target_pairs={{0,4},{4,0},{8,12},{12,8},{16,20},{20,16},{24,28},{28,24},{1,5},{5... | collective-permute-start | bytes 1769480 | tf_op jit(solution)/shard_map/ppermute | solution.py:34
  41.6 15.0 %collective-permute-start.9 = (bf16[1,48,1920]{2,1,0:T(8,128)(2,1)S(1)}, bf16[1,48,1920]{2,1,0:T(8,128)(2,1)S(1)}, u32[]{:S(2)}, u32[]{:S(2)}) collective-permute-start(bf16[1,48,1920]{2,1,0:T(8,128)(2,1)S(1)} %bitcast.206), channel_id=1, source_target_pairs={{0,8},{4,12},{8,0},{12,4},{16,24},{20,28},{24,16},{28,20},{1,9},{5... | collective-permute-start | bytes 552968 | tf_op jit(solution)/shard_map/ppermute | solution.py:37
  41.6 15.0 %collective-permute-start.7 = (bf16[256,768]{1,0:T(8,128)(2,1)S(1)}, bf16[256,768]{1,0:T(8,128)(2,1)}, u32[]{:S(2)}, u32[]{:S(2)}) collective-permute-start(bf16[256,768]{1,0:T(8,128)(2,1)S(1)} %bitcast.199), channel_id=1, source_target_pairs={{0,8},{4,12},{8,16},{12,20},{16,24},{20,28},{1,9},{5,13},{9,17},{1... | collective-permute-start | bytes 1179656 | tf_op jit(solution)/shard_map/ppermute | solution.py:40
  56.6 56.5 %copy-start.4 = (bf16[8,64,1152]{2,1,0:T(8,128)(2,1)}, bf16[8,64,1152]{2,1,0:T(8,128)(2,1)S(1)}, u32[]{:S(2)}) copy-start(bf16[8,64,1152]{2,1,0:T(8,128)(2,1)S(1)} %pad_maximum_fusion.2.refs_0_.refs_3_) | copy-start | bytes 3538948
  56.6 3.5 collective-permute-start.12
  56.7 28.4 %collective-permute-start.15 = (bf16[8,64,1152]{2,1,0:T(8,128)(2,1)S(1)}, bf16[8,64,1152]{2,1,0:T(8,128)(2,1)S(1)}, u32[]{:S(2)}, u32[]{:S(2)}) collective-permute-start(bf16[8,64,1152]{2,1,0:T(8,128)(2,1)S(1)} %pad_maximum_fusion.2.refs_0_.refs_3_), channel_id=1, source_target_pairs={{0,2},{1,3},{2,0},{3,1},{4,6},{5,7},{6,4},{7,5},{8,10},{9,11},{10,... | collective-permute-start | bytes 3538952 | tf_op jit(solution)/shard_map/ppermute | solution.py:31
  57.3 2.8 collective-permute-start.11
  58.7 1.4 collective-permute-start.10
  60.1 27.5 %collective-permute-start.14 = (bf16[256,768]{1,0:T(8,128)(2,1)}, bf16[256,768]{1,0:T(8,128)(2,1)S(1)}, u32[]{:S(2)}, u32[]{:S(2)}) collective-permute-start(bf16[256,768]{1,0:T(8,128)(2,1)} %collective-permute-done.10.refs_8_.refs_4_), channel_id=1, source_target_pairs={{16,20},{20,16},{24,28},{28,24},{17,21},{21,17},{25,29},{29,25},{1... | collective-permute-start | bytes 1179656 | tf_op jit(solution)/shard_map/ppermute | solution.py:34
  60.8 26.8 %collective-permute-start.13 = (bf16[256,768]{1,0:T(8,128)(2,1)}, bf16[256,768]{1,0:T(8,128)(2,1)S(1)}, u32[]{:S(2)}, u32[]{:S(2)}) collective-permute-start(bf16[256,768]{1,0:T(8,128)(2,1)} %collective-permute-done.10.refs_8_.refs_4_), channel_id=1, source_target_pairs={{16,24},{20,28},{17,25},{21,29},{18,26},{22,30},{19,27},{23,31}} | collective-permute-start | bytes 1179656 | tf_op jit(solution)/shard_map/ppermute | solution.py:40
  61.6 26.0 %collective-permute-start.16 = (bf16[1,48,1920]{2,1,0:T(8,128)(2,1)S(1)}, bf16[1,48,1920]{2,1,0:T(8,128)(2,1)S(1)}, u32[]{:S(2)}, u32[]{:S(2)}) collective-permute-start(bf16[1,48,1920]{2,1,0:T(8,128)(2,1)S(1)} %bitcast.207), channel_id=1, source_target_pairs={{0,16},{4,20},{8,24},{12,28},{16,0},{20,4},{24,8},{28,12},{1,17},{... | collective-permute-start | bytes 552968 | tf_op jit(solution)/shard_map/ppermute | solution.py:37
  88.4 16.1 %collective-permute-start.18 = (bf16[8,64,1152]{2,1,0:T(8,128)(2,1)S(1)}, bf16[8,64,1152]{2,1,0:T(8,128)(2,1)}, u32[]{:S(2)}, u32[]{:S(2)}) collective-permute-start(bf16[8,64,1152]{2,1,0:T(8,128)(2,1)S(1)} %collective-permute-done.15.refs_1_.refs_4_), channel_id=1, source_target_pairs={{0,1},{1,0},{2,3},{3,2},{4,5},{5,4},{6,7},{7,6},{8,9},{9,8},{10,11... | collective-permute-start | bytes 3538952 | tf_op jit(solution)/shard_map/ppermute | solution.py:28
  90.1 14.3 %collective-permute-start.17 = (bf16[256,768]{1,0:T(8,128)(2,1)}, bf16[256,768]{1,0:T(8,128)(2,1)}, u32[]{:S(2)}, u32[]{:S(2)}) collective-permute-start(bf16[256,768]{1,0:T(8,128)(2,1)} %copy-done.41), channel_id=1, source_target_pairs={{24,28},{28,24},{25,29},{29,25},{26,30},{30,26},{27,31},{31,27}} | collective-permute-start | bytes 1179656 | tf_op jit(solution)/shard_map/ppermute | solution.py:34
  91.9 12.6 %collective-permute-start.19 = (bf16[1,48,1920]{2,1,0:T(8,128)(2,1)S(1)}, bf16[1,48,1920]{2,1,0:T(8,128)(2,1)S(1)}, u32[]{:S(2)}, u32[]{:S(2)}) collective-permute-start(bf16[1,48,1920]{2,1,0:T(8,128)(2,1)S(1)} %bitcast.208), channel_id=1, source_target_pairs={{0,24},{4,28},{8,16},{12,20},{16,8},{20,12},{24,0},{28,4},{1,25},{... | collective-permute-start | bytes 552968 | tf_op jit(solution)/shard_map/ppermute | solution.py:37
  104.5 26.1 %collective-permute-start.23 = (bf16[1,2,96,768]{3,2,1,0:T(8,128)(2,1)S(1)}, bf16[1,2,96,768]{3,2,1,0:T(8,128)(2,1)S(1)}, u32[]{:S(2)}, u32[]{:S(2)}) collective-permute-start(bf16[1,2,96,768]{3,2,1,0:T(8,128)(2,1)S(1)} %maximum_bitcast_fusion), channel_id=1, source_target_pairs={{0,24},{4,28},{8,16},{12,20},{16,8},{20,12},{24,0},{28,4},{1,25},{... | collective-permute-start | bytes 884744 | tf_op jit(solution)/shard_map/ppermute | solution.py:37
  109.3 21.5 %collective-permute-start.22 = (bf16[1,2,96,768]{3,2,1,0:T(8,128)(2,1)S(1)}, bf16[1,2,96,768]{3,2,1,0:T(8,128)(2,1)S(1)}, u32[]{:S(2)}, u32[]{:S(2)}) collective-permute-start(bf16[1,2,96,768]{3,2,1,0:T(8,128)(2,1)S(1)} %maximum_bitcast_fusion), channel_id=1, source_target_pairs={{0,16},{4,20},{8,24},{12,28},{16,0},{20,4},{24,8},{28,12},{1,17},{... | collective-permute-start | bytes 884744 | tf_op jit(solution)/shard_map/ppermute | solution.py:37
  109.3 21.5 %collective-permute-start.21 = (bf16[1,2,96,768]{3,2,1,0:T(8,128)(2,1)S(1)}, bf16[1,2,96,768]{3,2,1,0:T(8,128)(2,1)S(1)}, u32[]{:S(2)}, u32[]{:S(2)}) collective-permute-start(bf16[1,2,96,768]{3,2,1,0:T(8,128)(2,1)S(1)} %maximum_bitcast_fusion), channel_id=1, source_target_pairs={{0,8},{4,12},{8,0},{12,4},{16,24},{20,28},{24,16},{28,20},{1,9},{5... | collective-permute-start | bytes 884744 | tf_op jit(solution)/shard_map/ppermute | solution.py:37
  111.5 19.5 %collective-permute-start.20 = (bf16[4,48,1920]{2,1,0:T(8,128)(2,1)S(1)}, bf16[4,48,1920]{2,1,0:T(8,128)(2,1)S(1)}, u32[]{:S(2)}, u32[]{:S(2)}) collective-permute-start(bf16[4,48,1920]{2,1,0:T(8,128)(2,1)S(1)} %pad_maximum_fusion.5), channel_id=1, source_target_pairs={{0,4},{4,0},{8,12},{12,8},{16,20},{20,16},{24,28},{28,24},{1,5},{5... | collective-permute-start | bytes 2211848 | tf_op jit(solution)/shard_map/ppermute | solution.py:34
  131.1 31.1 %collective-permute-start.25 = (bf16[8,48,1920]{2,1,0:T(8,128)(2,1)S(1)}, bf16[8,48,1920]{2,1,0:T(8,128)(2,1)S(1)}, u32[]{:S(2)}, u32[]{:S(2)}) collective-permute-start(bf16[8,48,1920]{2,1,0:T(8,128)(2,1)S(1)} %constant_dynamic-update-slice_fusion.refs_0_), channel_id=1, source_target_pairs={{0,1},{1,0},{2,3},{3,2},{4,5},{5,4},{6,7},{7,6},{8,9},{9,8},{10,11... | collective-permute-start | bytes 4423688 | tf_op jit(solution)/shard_map/ppermute | solution.py:28
  131.2 34.8 %collective-permute-start.24 = (bf16[8,48,1920]{2,1,0:T(8,128)(2,1)S(1)}, bf16[8,48,1920]{2,1,0:T(8,128)(2,1)}, u32[]{:S(2)}, u32[]{:S(2)}) collective-permute-start(bf16[8,48,1920]{2,1,0:T(8,128)(2,1)S(1)} %constant_dynamic-update-slice_fusion.refs_0_), channel_id=1, source_target_pairs={{0,2},{1,3},{2,0},{3,1},{4,6},{5,7},{6,4},{7,5},{8,10},{9,11},{10,... | collective-permute-start | bytes 4423688 | tf_op jit(solution)/shard_map/ppermute | solution.py:31
  132.7 18.6 %collective-permute-start.27 = (bf16[8,96,768]{2,1,0:T(8,128)(2,1)S(1)}, bf16[8,96,768]{2,1,0:T(8,128)(2,1)S(1)}, u32[]{:S(2)}, u32[]{:S(2)}) collective-permute-start(bf16[8,96,768]{2,1,0:T(8,128)(2,1)S(1)} %bitcast.213), channel_id=1, source_target_pairs={{0,1},{1,0},{2,3},{3,2},{4,5},{5,4},{6,7},{7,6},{8,9},{9,8},{10,11... | collective-permute-start | bytes 3538952 | tf_op jit(solution)/shard_map/ppermute | solution.py:28
  132.9 29.3 %collective-permute-start.26 = (bf16[8,96,768]{2,1,0:T(8,128)(2,1)S(1)}, bf16[8,96,768]{2,1,0:T(8,128)(2,1)}, u32[]{:S(2)}, u32[]{:S(2)}) collective-permute-start(bf16[8,96,768]{2,1,0:T(8,128)(2,1)S(1)} %bitcast.214), channel_id=1, source_target_pairs={{0,4},{4,0},{8,12},{12,8},{16,20},{20,16},{24,28},{28,24},{1,5},{5... | collective-permute-start | bytes 3538952 | tf_op jit(solution)/shard_map/ppermute | solution.py:34
  166.0 5.3 %collective-permute-start.28 = (bf16[8,48,1920]{2,1,0:T(8,128)(2,1)}, bf16[8,48,1920]{2,1,0:T(8,128)(2,1)}, u32[]{:S(2)}, u32[]{:S(2)}) collective-permute-start(bf16[8,48,1920]{2,1,0:T(8,128)(2,1)} %collective-permute-done.24.refs_1_), channel_id=1, source_target_pairs={{0,1},{1,0},{2,3},{3,2},{4,5},{5,4},{6,7},{7,6},{8,9},{9,8},{10,11... | collective-permute-start | bytes 4423688 | tf_op jit(solution)/shard_map/ppermute | solution.py:28
  166.0 5.3 %collective-permute-start.29 = (bf16[8,96,768]{2,1,0:T(8,128)(2,1)}, bf16[8,96,768]{2,1,0:T(8,128)(2,1)}, u32[]{:S(2)}, u32[]{:S(2)}) collective-permute-start(bf16[8,96,768]{2,1,0:T(8,128)(2,1)} %collective-permute-done.26.refs_5_), channel_id=1, source_target_pairs={{0,1},{1,0},{2,3},{3,2},{4,5},{5,4},{6,7},{7,6},{8,9},{9,8},{10,11... | collective-permute-start | bytes 3538952 | tf_op jit(solution)/shard_map/ppermute | solution.py:28
  200.6 16.0 %collective-permute-start.31 = (bf16[768,1920]{1,0:T(8,128)(2,1)}, bf16[768,1920]{1,0:T(8,128)(2,1)}, u32[]{:S(2)}, u32[]{:S(2)}) collective-permute-start(bf16[768,1920]{1,0:T(8,128)(2,1)} %pad_maximum_fusion.1), channel_id=1, source_target_pairs={{0,1},{1,0},{2,3},{3,2},{4,5},{5,4},{6,7},{7,6},{8,9},{9,8},{10,11... | collective-permute-start | bytes 8847368 | tf_op jit(solution)/shard_map/ppermute | solution.py:28
  204.8 6.9 %collective-permute-start.30 = (bf16[1536,768]{1,0:T(8,128)(2,1)}, bf16[1536,768]{1,0:T(8,128)(2,1)S(1)}, u32[]{:S(2)}, u32[]{:S(2)}) collective-permute-start(bf16[1536,768]{1,0:T(8,128)(2,1)} %convolution_convert_fusion.2), channel_id=1, source_target_pairs={{0,1},{1,0},{2,3},{3,2},{4,5},{5,4},{6,7},{7,6},{8,9},{9,8},{10,11... | collective-permute-start | bytes 7077896 | tf_op jit(solution)/shard_map/ppermute | solution.py:28
  221.2 35.9 %collective-permute-start.33 = (bf16[4,2,48,1920]{3,2,1,0:T(8,128)(2,1)}, bf16[4,2,48,1920]{3,2,1,0:T(8,128)(2,1)}, u32[]{:S(2)}, u32[]{:S(2)}) collective-permute-start(bf16[4,2,48,1920]{3,2,1,0:T(8,128)(2,1)} %fusion.7), channel_id=1, source_target_pairs={{0,4},{4,0},{8,12},{12,8},{16,20},{20,16},{24,28},{28,24},{1,5},{5... | collective-permute-start | bytes 4423688 | tf_op jit(solution)/shard_map/ppermute | solution.py:34
  225.6 28.3 %collective-permute-start.32 = (bf16[8,96,768]{2,1,0:T(8,128)(2,1)}, bf16[8,96,768]{2,1,0:T(8,128)(2,1)}, u32[]{:S(2)}, u32[]{:S(2)}) collective-permute-start(bf16[8,96,768]{2,1,0:T(8,128)(2,1)} %get-tuple-element.254), channel_id=1, source_target_pairs={{0,2},{1,3},{2,0},{3,1},{4,6},{5,7},{6,4},{7,5},{8,10},{9,11},{10,... | collective-permute-start | bytes 3538952 | tf_op jit(solution)/shard_map/ppermute | solution.py:31
  262.0 50.1 %collective-permute-start.34 = (bf16[2,48,1920]{2,1,0:T(8,128)(2,1)}, bf16[2,48,1920]{2,1,0:T(8,128)(2,1)S(1)}, u32[]{:S(2)}, u32[]{:S(2)}) collective-permute-start(bf16[2,48,1920]{2,1,0:T(8,128)(2,1)} %get-tuple-element.269), channel_id=1, source_target_pairs={{0,8},{4,12},{8,0},{12,4},{16,24},{20,28},{24,16},{28,20},{1,9},{5... | collective-permute-start | bytes 1105928 | tf_op jit(solution)/shard_map/ppermute | solution.py:37
  262.2 49.9 %collective-permute-start.35 = (bf16[2,48,1920]{2,1,0:T(8,128)(2,1)S(1)}, bf16[2,48,1920]{2,1,0:T(8,128)(2,1)S(1)}, u32[]{:S(2)}, u32[]{:S(2)}) collective-permute-start(bf16[2,48,1920]{2,1,0:T(8,128)(2,1)S(1)} %get-tuple-element.270), channel_id=1, source_target_pairs={{0,16},{4,20},{8,24},{12,28},{16,0},{20,4},{24,8},{28,12},{1,17},{... | collective-permute-start | bytes 1105928 | tf_op jit(solution)/shard_map/ppermute | solution.py:37
  275.9 36.2 %collective-permute-start.36 = (bf16[2,48,1920]{2,1,0:T(8,128)(2,1)S(1)}, bf16[2,48,1920]{2,1,0:T(8,128)(2,1)S(1)}, u32[]{:S(2)}, u32[]{:S(2)}) collective-permute-start(bf16[2,48,1920]{2,1,0:T(8,128)(2,1)S(1)} %get-tuple-element.271), channel_id=1, source_target_pairs={{0,24},{4,28},{8,16},{12,20},{16,8},{20,12},{24,0},{28,4},{1,25},{... | collective-permute-start | bytes 1105928 | tf_op jit(solution)/shard_map/ppermute | solution.py:37
  275.9 16.0 %collective-permute-start.37 = (bf16[4,96,768]{2,1,0:T(8,128)(2,1)S(1)}, bf16[4,96,768]{2,1,0:T(8,128)(2,1)S(1)}, u32[]{:S(2)}, u32[]{:S(2)}) collective-permute-start(bf16[4,96,768]{2,1,0:T(8,128)(2,1)S(1)} %fusion.27), channel_id=1, source_target_pairs={{0,4},{4,0},{8,12},{12,8},{16,20},{20,16},{24,28},{28,24},{1,5},{5... | collective-permute-start | bytes 1769480 | tf_op jit(solution)/shard_map/ppermute | solution.py:34
  291.9 20.2 %collective-permute-start.38 = (bf16[512,768]{1,0:T(8,128)(2,1)S(1)}, bf16[512,768]{1,0:T(8,128)(2,1)S(1)}, u32[]{:S(2)}, u32[]{:S(2)}) collective-permute-start(bf16[512,768]{1,0:T(8,128)(2,1)S(1)} %pad_maximum_fusion.4), channel_id=1, source_target_pairs={{16,20},{20,16},{24,28},{28,24},{17,21},{21,17},{25,29},{29,25},{1... | collective-permute-start | bytes 2359304 | tf_op jit(solution)/shard_map/ppermute | solution.py:34
  313.3 45.7 %collective-permute-start.40 = (bf16[96,768]{1,0:T(8,128)(2,1)}, bf16[96,768]{1,0:T(8,128)(2,1)S(1)}, u32[]{:S(2)}, u32[]{:S(2)}) collective-permute-start(bf16[96,768]{1,0:T(8,128)(2,1)} %get-tuple-element.306), channel_id=1, source_target_pairs={{0,8},{4,12},{8,0},{12,4},{16,24},{20,28},{24,16},{28,20},{1,9},{5... | collective-permute-start | bytes 442376 | tf_op jit(solution)/shard_map/ppermute | solution.py:37
  325.7 33.3 %collective-permute-start.41 = (bf16[96,768]{1,0:T(8,128)(2,1)S(1)}, bf16[96,768]{1,0:T(8,128)(2,1)S(1)}, u32[]{:S(2)}, u32[]{:S(2)}) collective-permute-start(bf16[96,768]{1,0:T(8,128)(2,1)S(1)} %get-tuple-element.307), channel_id=1, source_target_pairs={{0,16},{4,20},{8,24},{12,28},{16,0},{20,4},{24,8},{28,12},{1,17},{... | collective-permute-start | bytes 442376 | tf_op jit(solution)/shard_map/ppermute | solution.py:37
  332.8 26.3 %collective-permute-start.42 = (bf16[96,768]{1,0:T(8,128)(2,1)S(1)}, bf16[96,768]{1,0:T(8,128)(2,1)S(1)}, u32[]{:S(2)}, u32[]{:S(2)}) collective-permute-start(bf16[96,768]{1,0:T(8,128)(2,1)S(1)} %get-tuple-element.308), channel_id=1, source_target_pairs={{0,24},{4,28},{8,16},{12,20},{16,8},{20,12},{24,0},{28,4},{1,25},{... | collective-permute-start | bytes 442376 | tf_op jit(solution)/shard_map/ppermute | solution.py:37
  332.8 26.3 %collective-permute-start.43 = (bf16[48,1920]{1,0:T(8,128)(2,1)S(1)}, bf16[48,1920]{1,0:T(8,128)(2,1)S(1)}, u32[]{:S(2)}, u32[]{:S(2)}) collective-permute-start(bf16[48,1920]{1,0:T(8,128)(2,1)S(1)} %get-tuple-element.309), channel_id=1, source_target_pairs={{0,2},{1,3},{2,0},{3,1},{4,6},{5,7},{6,4},{7,5},{8,10},{9,11},{10,... | collective-permute-start | bytes 552968 | tf_op jit(solution)/shard_map/ppermute | solution.py:31
  334.3 24.9 %collective-permute-start.39 = (bf16[256,768]{1,0:T(8,128)(2,1)S(1)}, bf16[256,768]{1,0:T(8,128)(2,1)S(1)}, u32[]{:S(2)}, u32[]{:S(2)}) collective-permute-start(bf16[256,768]{1,0:T(8,128)(2,1)S(1)} %add_convert_fusion.12), channel_id=1, source_target_pairs={{24,16},{28,20},{25,17},{29,21},{26,18},{30,22},{27,19},{31,23}} | collective-permute-start | bytes 1179656 | tf_op jit(solution)/shard_map/ppermute | solution.py:43
  335.0 23.8 %copy-start.25 = (bf16[8,2,2,24]{3,2,0,1:T(2,128)(2,1)S(1)}, bf16[8,2,2,24]{3,2,0,1:T(2,128)(2,1)}, u32[]{:S(2)}) copy-start(bf16[8,2,2,24]{3,2,0,1:T(2,128)(2,1)} %copy.164) | copy-start | bytes 4612
  363.4 18.6 %collective-permute-start.48 = (bf16[8,2,48,640]{3,2,1,0:T(8,128)(2,1)}, bf16[8,2,48,640]{3,2,1,0:T(8,128)(2,1)}, u32[]{:S(2)}, u32[]{:S(2)}) collective-permute-start(bf16[8,2,48,640]{3,2,1,0:T(8,128)(2,1)} %bitcast.42), channel_id=1, source_target_pairs={{0,1},{1,0},{2,3},{3,2},{4,5},{5,4},{6,7},{7,6},{8,9},{9,8},{10,11... | collective-permute-start | bytes 2949128 | tf_op jit(solution)/shard_map/ppermute | solution.py:28
  363.9 18.0 %collective-permute-start.47 = (bf16[8,2,56,512]{3,2,0,1:T(8,128)(2,1)}, bf16[8,2,56,512]{3,2,0,1:T(8,128)(2,1)S(1)}, u32[]{:S(2)}, u32[]{:S(2)}) collective-permute-start(bf16[8,2,56,512]{3,2,0,1:T(8,128)(2,1)} %fusion.16), channel_id=1, source_target_pairs={{0,1},{1,0},{2,3},{3,2},{4,5},{5,4},{6,7},{7,6},{8,9},{9,8},{10,11... | collective-permute-start | bytes 2752520 | tf_op jit(solution)/shard_map/ppermute | solution.py:28
  364.5 4.3 collective-permute-start.45
  365.4 16.5 %collective-permute-start.46 = (bf16[256,768]{1,0:T(8,128)(2,1)S(1)}, bf16[256,768]{1,0:T(8,128)(2,1)S(1)}, u32[]{:S(2)}, u32[]{:S(2)}) collective-permute-start(bf16[256,768]{1,0:T(8,128)(2,1)S(1)} %get-tuple-element.412), channel_id=1, source_target_pairs={{4,0},{12,8},{20,16},{28,24},{5,1},{13,9},{21,17},{29,25},{6,2},{1... | collective-permute-start | bytes 1179656 | tf_op jit(solution)/shard_map/ppermute | solution.py:34
  366.7 15.2 %collective-permute-start.44 = (bf16[256,768]{1,0:T(8,128)(2,1)S(1)}, bf16[256,768]{1,0:T(8,128)(2,1)S(1)}, u32[]{:S(2)}, u32[]{:S(2)}) collective-permute-start(bf16[256,768]{1,0:T(8,128)(2,1)S(1)} %get-tuple-element.413), channel_id=1, source_target_pairs={{8,12},{12,8},{16,20},{20,16},{24,28},{28,24},{9,13},{13,9},{17,21... | collective-permute-start | bytes 1179656 | tf_op jit(solution)/shard_map/ppermute | solution.py:34
  389.2 2.8 collective-permute-start.52
  390.1 21.5 %collective-permute-start.51 = (bf16[256,768]{1,0:T(8,128)(2,1)}, bf16[256,768]{1,0:T(8,128)(2,1)}, u32[]{:S(2)}, u32[]{:S(2)}) collective-permute-start(bf16[256,768]{1,0:T(8,128)(2,1)} %add_convert_fusion.10), channel_id=1, source_target_pairs={{8,0},{12,4},{16,8},{20,12},{24,16},{28,20},{9,1},{13,5},{17,9},{2... | collective-permute-start | bytes 1179656 | tf_op jit(solution)/shard_map/ppermute | solution.py:43
  391.4 20.2 %collective-permute-start.49 = (bf16[8,56,512]{2,1,0:T(8,128)(2,1)}, bf16[8,56,512]{2,1,0:T(8,128)(2,1)}, u32[]{:S(2)}, u32[]{:S(2)}) collective-permute-start(bf16[8,56,512]{2,1,0:T(8,128)(2,1)} %get-tuple-element.336), channel_id=1, source_target_pairs={{0,2},{1,3},{2,0},{3,1},{4,6},{5,7},{6,4},{7,5},{8,10},{9,11},{10,... | collective-permute-start | bytes 1376264 | tf_op jit(solution)/shard_map/ppermute | solution.py:31
  392.0 19.7 %collective-permute-start.50 = (bf16[4,2,48,640]{3,2,1,0:T(8,128)(2,1)}, bf16[4,2,48,640]{3,2,1,0:T(8,128)(2,1)S(1)}, u32[]{:S(2)}, u32[]{:S(2)}) collective-permute-start(bf16[4,2,48,640]{3,2,1,0:T(8,128)(2,1)} %fusion.29), channel_id=1, source_target_pairs={{0,4},{4,0},{8,12},{12,8},{16,20},{20,16},{24,28},{28,24},{1,5},{5... | collective-permute-start | bytes 1474568 | tf_op jit(solution)/shard_map/ppermute | solution.py:34
  415.6 10.1 %collective-permute-start.54 = (bf16[2,48,640]{2,1,0:T(8,128)(2,1)S(1)}, bf16[2,48,640]{2,1,0:T(8,128)(2,1)S(1)}, u32[]{:S(2)}, u32[]{:S(2)}) collective-permute-start(bf16[2,48,640]{2,1,0:T(8,128)(2,1)S(1)} %get-tuple-element.348), channel_id=1, source_target_pairs={{0,8},{4,12},{8,0},{12,4},{16,24},{20,28},{24,16},{28,20},{1,9},{5... | collective-permute-start | bytes 368648 | tf_op jit(solution)/shard_map/ppermute | solution.py:37
  419.7 13.6 %collective-permute-start.55 = (bf16[2,48,640]{2,1,0:T(8,128)(2,1)S(1)}, bf16[2,48,640]{2,1,0:T(8,128)(2,1)S(1)}, u32[]{:S(2)}, u32[]{:S(2)}) collective-permute-start(bf16[2,48,640]{2,1,0:T(8,128)(2,1)S(1)} %get-tuple-element.349), channel_id=1, source_target_pairs={{0,16},{4,20},{8,24},{12,28},{16,0},{20,4},{24,8},{28,12},{1,17},{... | collective-permute-start | bytes 368648 | tf_op jit(solution)/shard_map/ppermute | solution.py:37
  424.3 9.0 %collective-permute-start.56 = (bf16[2,48,640]{2,1,0:T(8,128)(2,1)S(1)}, bf16[2,48,640]{2,1,0:T(8,128)(2,1)S(1)}, u32[]{:S(2)}, u32[]{:S(2)}) collective-permute-start(bf16[2,48,640]{2,1,0:T(8,128)(2,1)S(1)} %get-tuple-element.350), channel_id=1, source_target_pairs={{0,24},{4,28},{8,16},{12,20},{16,8},{20,12},{24,0},{28,4},{1,25},{... | collective-permute-start | bytes 368648 | tf_op jit(solution)/shard_map/ppermute | solution.py:37
  424.3 9.0 %collective-permute-start.53 = (bf16[4,56,512]{2,1,0:T(8,128)(2,1)S(1)}, bf16[4,56,512]{2,1,0:T(8,128)(2,1)S(1)}, u32[]{:S(2)}, u32[]{:S(2)}) collective-permute-start(bf16[4,56,512]{2,1,0:T(8,128)(2,1)S(1)} %fusion.38), channel_id=1, source_target_pairs={{0,4},{4,0},{8,12},{12,8},{16,20},{20,16},{24,28},{28,24},{1,5},{5... | collective-permute-start | bytes 688136 | tf_op jit(solution)/shard_map/ppermute | solution.py:34
  433.5 10.5 %collective-permute-start.60 = (bf16[48,640]{1,0:T(8,128)(2,1)S(1)}, bf16[48,640]{1,0:T(8,128)(2,1)S(1)}, u32[]{:S(2)}, u32[]{:S(2)}) collective-permute-start(bf16[48,640]{1,0:T(8,128)(2,1)S(1)} %get-tuple-element.366), channel_id=1, source_target_pairs={{0,2},{1,3},{2,0},{3,1},{4,6},{5,7},{6,4},{7,5},{8,10},{9,11},{10,... | collective-permute-start | bytes 184328 | tf_op jit(solution)/shard_map/ppermute | solution.py:31
  434.9 4.5 %collective-permute-start.57 = (bf16[56,512]{1,0:T(8,128)(2,1)S(1)}, bf16[56,512]{1,0:T(8,128)(2,1)S(1)}, u32[]{:S(2)}, u32[]{:S(2)}) collective-permute-start(bf16[56,512]{1,0:T(8,128)(2,1)S(1)} %get-tuple-element.363), channel_id=1, source_target_pairs={{0,8},{4,12},{8,0},{12,4},{16,24},{20,28},{24,16},{28,20},{1,9},{5... | collective-permute-start | bytes 172040 | tf_op jit(solution)/shard_map/ppermute | solution.py:37
  436.8 5.8 %collective-permute-start.58 = (bf16[56,512]{1,0:T(8,128)(2,1)S(1)}, bf16[56,512]{1,0:T(8,128)(2,1)S(1)}, u32[]{:S(2)}, u32[]{:S(2)}) collective-permute-start(bf16[56,512]{1,0:T(8,128)(2,1)S(1)} %get-tuple-element.364), channel_id=1, source_target_pairs={{0,16},{4,20},{8,24},{12,28},{16,0},{20,4},{24,8},{28,12},{1,17},{... | collective-permute-start | bytes 172040 | tf_op jit(solution)/shard_map/ppermute | solution.py:37
  437.9 6.1 %collective-permute-start.59 = (bf16[56,512]{1,0:T(8,128)(2,1)S(1)}, bf16[56,512]{1,0:T(8,128)(2,1)S(1)}, u32[]{:S(2)}, u32[]{:S(2)}) collective-permute-start(bf16[56,512]{1,0:T(8,128)(2,1)S(1)} %get-tuple-element.365), channel_id=1, source_target_pairs={{0,24},{4,28},{8,16},{12,20},{16,8},{20,12},{24,0},{28,4},{1,25},{... | collective-permute-start | bytes 172040 | tf_op jit(solution)/shard_map/ppermute | solution.py:37
  444.7 1.4 collective-permute-start.61
  (45 other events, 367.0 us)
